TPU v7x, 32 devices: a whole 2x2x4 slice. The times are simulated.
32 devices in a mesh: grp: 2 (over x), seq: 16 (over z, y, core).
Axes of the slice: x: 2, y: 2, z: 4, core: 2. Of those that a mesh axis runs over, the one named last changes fastest.
Arguments:
- alignment: bfloat16 [64, 128, 768], P(('grp', 'seq')), parts along dimension 0, may hold values from -20 to 20
- protein_id: int32 [256], P('grp'), parts along dimension 0, may hold values from 0 to 3, never falling along the last dimension, each value on 1 to 64 neighbouring positions
- row_depth: int32 [8], P('grp'), parts along dimension 0, may hold values from 8 to 32, as said below
- row_gain: float32 [768], replicated, may hold values from 0.1 to 1.9
- row_query: bfloat16 [768, 768], replicated, may hold values from -40 to 40
- row_key: bfloat16 [768, 768], replicated, may hold values from -0.21875 to 0.21875
- row_value: bfloat16 [768, 768], replicated, may hold values from -0.21875 to 0.21875
- row_output: bfloat16 [768, 768], replicated, may hold values from -0.21875 to 0.21875
- column_gain: float32 [768], replicated, may hold values from 0.1 to 1.9
- column_query: bfloat16 [768, 768], replicated, may hold values from -40 to 40
- column_key: bfloat16 [768, 768], replicated, may hold values from -0.21875 to 0.21875
- column_value: bfloat16 [768, 768], replicated, may hold values from -0.21875 to 0.21875
- column_output: bfloat16 [768, 768], replicated, may hold values from -0.21875 to 0.21875
Outputs:
- layer_out: bfloat16 [64, 128, 768], P(('grp', 'seq')), parts along dimension 0
There are 2 independent parts, one for each index of `grp`. A program takes and returns all parts, laid end to end along the dimension named above; an argument that names none is the same for every part. Nothing has to cross between parts.
Inputs may be any that keep to these rules, and one draw needn't show every extreme that they name: `row_depth`: row 0 is real for every protein; one protein of each pack has all 32 rows real. `protein_id`: proteins occupy contiguous column ranges in order, each 1 to 64 columns.
All inputs are finite; a program needn't handle non-finite values.
Results may differ from a plain program's by a relative error of at most 0.011.
Values may be sent and summed in bfloat16 or wider, within the bound.
No kernel may reach another device: no remote copies, remote signals or barrier semaphores. Data moves between devices by JAX's collectives and lax.ppermute only.
A program may use at most 64 MiB of HBM per device.

v0:
```python
import math

import jax
import jax.numpy as jnp
from jax import lax
from jax.sharding import PartitionSpec as P

H = 12


def layer_norm(values, gain):
    full = values.astype(jnp.float32)
    middle = jnp.mean(full, axis=-1, keepdims=True)
    spread = jnp.mean((full - middle) ** 2, axis=-1, keepdims=True)
    return ((full - middle) * lax.rsqrt(spread + 1e-05) * gain).astype(jnp.bfloat16)


def project(normed, weight):
    shape = normed.shape
    flattened = normed.reshape(-1, shape[-1])
    return (
        jnp.dot(flattened, weight, preferred_element_type=jnp.float32)
        .astype(jnp.bfloat16)
        .reshape(shape[:-1] + (weight.shape[1],))
    )


def column_depth(protein_id, row_depth):
    onehot = protein_id[:, None] == jnp.arange(row_depth.shape[0], dtype=jnp.int32)[None, :]
    return jnp.sum(jnp.where(onehot, row_depth[None, :], 0), axis=1)


def per_device(
    alignment,
    protein_id,
    row_depth,
    row_gain,
    row_query,
    row_key,
    row_value,
    row_output,
    column_gain,
    column_query,
    column_key,
    column_value,
    column_output,
):
    rows_dev, columns, width = alignment.shape
    devices = lax.axis_size("seq")
    position = lax.axis_index("seq")
    total_rows = rows_dev * devices
    head_count = H
    head_size = width // head_count
    tile_cols = columns // devices
    depth_col = column_depth(protein_id, row_depth)
    row_ids = position * rows_dev + jnp.arange(rows_dev, dtype=jnp.int32)
    valid = row_ids[:, None] < depth_col[None, :]
    mask_bf = valid.astype(jnp.bfloat16)[:, :, None]
    normed_row = layer_norm(alignment, row_gain)
    query_a = (project(normed_row, row_query) * mask_bf).reshape(
        rows_dev, columns, head_count, head_size
    )
    key_a = (project(normed_row, row_key) * mask_bf).reshape(
        rows_dev, columns, head_count, head_size
    )
    value_a = project(normed_row, row_value).reshape(rows_dev, columns, head_count, head_size)
    scale = 1.0 / (math.sqrt(head_size) * math.sqrt(total_rows))
    tied = (
        lax.psum_scatter(
            jnp.einsum("rihe,rjhe->ihj", query_a, key_a, preferred_element_type=jnp.float32),
            "seq",
            scatter_dimension=0,
            tiled=True,
        )
        * scale
    )
    prot_query = lax.dynamic_slice_in_dim(protein_id, position * tile_cols, tile_cols, 0)
    same_prot = prot_query[:, None, None] == protein_id[None, None, :]
    tied = jnp.where(same_prot, tied, -1000000000.0)
    row_weights = jax.nn.softmax(tied, axis=-1).astype(jnp.bfloat16)
    row_mixed = (
        jnp.einsum(
            "ihj,rjhe->rihe",
            lax.all_gather(row_weights, "seq", axis=0, tiled=True),
            value_a,
            preferred_element_type=jnp.float32,
        )
        .astype(jnp.bfloat16)
        .reshape(rows_dev, columns, width)
    )
    after_row = (
        alignment.astype(jnp.float32)
        + jnp.dot(
            row_mixed.reshape(-1, width), row_output, preferred_element_type=jnp.float32
        ).reshape(rows_dev, columns, width)
    ).astype(jnp.bfloat16)
    normed_col = layer_norm(after_row, column_gain)
    moved = lax.all_to_all(normed_col, "seq", split_axis=1, concat_axis=0, tiled=True)
    query_b = project(moved, column_query)
    key_b = project(moved, column_key)
    value_b = project(moved, column_value)
    query_b = query_b.reshape(total_rows, tile_cols, head_count, head_size)
    key_b = key_b.reshape(total_rows, tile_cols, head_count, head_size)
    value_b = value_b.reshape(total_rows, tile_cols, head_count, head_size)
    depth_tile = lax.dynamic_slice_in_dim(depth_col, position * tile_cols, tile_cols, 0)
    key_valid = jnp.arange(total_rows, dtype=jnp.int32)[None, :] < depth_tile[:, None]
    col_scores = jnp.einsum(
        "rche,sche->chrs", query_b, key_b, preferred_element_type=jnp.float32
    ) / math.sqrt(head_size)
    col_scores = jnp.where(key_valid[:, None, None, :], col_scores, -1000000000.0)
    col_weights = jax.nn.softmax(col_scores, axis=-1).astype(jnp.bfloat16)
    col_mixed = jnp.einsum(
        "chrs,sche->rche", col_weights, value_b, preferred_element_type=jnp.float32
    ).astype(jnp.bfloat16)
    col_mixed = col_mixed.reshape(total_rows, tile_cols, width)
    returned = lax.all_to_all(col_mixed, "seq", split_axis=0, concat_axis=1, tiled=True)
    layer_out = after_row.astype(jnp.float32) + jnp.dot(
        returned.reshape(-1, width), column_output, preferred_element_type=jnp.float32
    ).reshape(rows_dev, columns, width)
    return layer_out.astype(jnp.bfloat16)


def solution(mesh):
    return jax.shard_map(
        per_device,
        mesh=mesh,
        in_specs=(
            P(("grp", "seq"), None, None),
            P("grp"),
            P("grp"),
            P(),
            P(),
            P(),
            P(),
            P(),
            P(),
            P(),
            P(),
            P(),
            P(),
        ),
        out_specs=P(("grp", "seq"), None, None),
        check_vma=False,
    )
```

profile of v0, /device:TPU:0, one launch (start us, length us, event | category | flops | bytes accessed | tf_op | source)
XLA Modules:
  0.0 158.1 jit_solution(10954076205752719301)
XLA Ops:
  6.5 1.3 convert_reduce_fusion
  7.8 1.2 fusion.15
  9.1 1.2 fusion.17
  10.3 0.5 convolution_convert_fusion.5
  10.8 0.2 copy.75
  11.0 0.1 reshape.141
  11.1 1.7 %convolution_convert_fusion.4 = bf16[256,768]{1,0:T(8,128)(2,1)S(1)} fusion(bf16[256,768]{1,0:T(8,128)(2,1)S(1)} %bitcast.61, bf16[768,768]{1,0:T(8,128)(2,1)} %param.17), kind=kOutput, calls=%fused_computation.17 | convolution fusion | flops 302186496 | bytes 1966080 | tf_op jit(solution)/shard_map/dot_general | solution.py:22
  12.8 0.0 copy-start.6
  12.9 0.2 copy.76
  13.0 0.1 reshape.142
  13.2 0.3 copy-done.6
  13.5 0.0 copy-done.7
  13.5 0.1 select_reduce_fusion
  13.6 0.1 compare_convert_fusion
  13.7 0.1 broadcast_multiply_fusion.1
  13.7 0.3 convolution_bitcast_fusion
  14.1 1.4 copy.79
  15.5 0.0 reduce-scatter.2.cloned.1.call-update
  15.5 0.1 dynamic_slice.6
  15.6 0.5 convolution_convert_fusion.6
  16.1 0.2 copy.74
  16.2 0.1 reshape_reshape.13
  16.3 0.1 broadcast_compare_fusion
  16.4 59.4 %reduce-scatter.2.cloned.1.call-done = f32[8,12,128]{2,1,0:T(8,128)} async-done(((f32[128,12,128]{2,1,0:T(8,128)}), f32[8,12,128]{2,1,0:T(8,128)}) %reduce-scatter.2.cloned.1.call-update) | async-done | bytes 49168 | tf_op jit(solution)/shard_map/reduce_scatter | solution.py:69
  75.8 1.0 fusion.38
  76.8 0.1 divide_convert_fusion.2
  76.9 20.5 %all_gather.3 = bf16[128,12,128]{2,0,1:T(8,128)(2,1)S(1)} all-gather(bf16[8,12,128]{2,0,1:T(8,128)(2,1)S(1)} %copy.80), channel_id=1, replica_groups=mesh['grp'=2,'seq'=16] {'seq'}, dimensions={0}, use_global_device_ids=true | all-gather | bytes 417792 | tf_op jit(solution)/shard_map/all_gather | solution.py:84
  97.5 0.4 fusion.8
  97.9 0.6 fusion.39
  98.5 0.2 multiply_reduce_fusion
  98.8 0.2 multiply_convert_fusion
  99.0 1.2 copy.84
  100.1 3.6 %all-to-all-start = ((bf16[2,128,768]{2,0,1:T(2,128)(2,1)}), bf16[2,128,768]{2,0,1:T(2,128)(2,1)S(1)}, u32[]{:S(2)}, u32[]{:S(2)}) async-start(bf16[2,128,768]{2,0,1:T(2,128)(2,1)} %copy.84), calls=%async_computation.1 | async-start | bytes 786432 | tf_op jit(solution)/shard_map/all_to_all | solution.py:98
  103.7 0.1 dynamic_slice.7
  103.7 0.1 iota_compare_fusion
  103.8 12.0 %all-to-all-done = bf16[2,128,768]{2,0,1:T(2,128)(2,1)S(1)} async-done(((bf16[2,128,768]{2,0,1:T(2,128)(2,1)}), bf16[2,128,768]{2,0,1:T(2,128)(2,1)S(1)}, u32[]{:S(2)}, u32[]{:S(2)}) %all-to-all-start) | async-done | bytes 393248 | tf_op jit(solution)/shard_map/all_to_all | solution.py:98
  115.9 1.7 %convolution_convert_fusion.2 = bf16[256,768]{1,0:T(8,128)(2,1)S(1)} fusion(bf16[256,768]{1,0:T(8,128)(2,1)S(1)} %bitcast.63, bf16[768,768]{1,0:T(8,128)(2,1)} %param.22), kind=kOutput, calls=%fused_computation.15 | convolution fusion | flops 302186496 | bytes 1966080 | tf_op jit(solution)/shard_map/dot_general | solution.py:22
  117.7 1.6 %reshape_reshape.15 = bf16[32,8,12,64]{3,2,1,0:T(8,128)(2,1)} reshape(bf16[256,768]{1,0:T(8,128)(2,1)S(1)} %convolution_convert_fusion.2) | data formatting | bytes 786432 | tf_op jit(solution)/shard_map/reshape;reshape | solution.py:102
  119.3 1.7 %convolution_convert_fusion.1 = bf16[256,768]{1,0:T(8,128)(2,1)S(1)} fusion(bf16[256,768]{1,0:T(8,128)(2,1)S(1)} %bitcast.64, bf16[768,768]{1,0:T(8,128)(2,1)} %param.23), kind=kOutput, calls=%fused_computation.14 | convolution fusion | flops 302186496 | bytes 1966080 | tf_op jit(solution)/shard_map/dot_general | solution.py:22
  121.0 1.6 reshape_reshape.16
  122.6 1.7 %convolution_convert_fusion.3 = bf16[256,768]{1,0:T(8,128)(2,1)S(1)} fusion(bf16[256,768]{1,0:T(8,128)(2,1)S(1)} %bitcast.65, bf16[768,768]{1,0:T(8,128)(2,1)} %param.24), kind=kOutput, calls=%fused_computation.16 | convolution fusion | flops 302186496 | bytes 1966080 | tf_op jit(solution)/shard_map/dot_general | solution.py:22
  124.3 1.6 reshape_reshape.14
  125.9 4.2 %fusion.40 = (f32[8,12,32]{2,1,0:T(8,128)S(1)}, f32[8,12,32,32]{2,3,1,0:T(8,128)}) fusion(bf16[32,8,12,64]{3,2,1,0:T(8,128)(2,1)} %reshape_reshape.16, bf16[32,8,12,64]{3,2,1,0:T(8,128)(2,1)} %reshape_reshape.15, pred[8,32]{1,0:T(8,128)(4,1)S(1)} %iota_compare_fusion), kind=kOutput, calls=%fused_computation.68 | convolution fusion | flops 12976159 | bytes 1192192 | tf_op jit(solution)/shard_map/sub | solution.py:111
  130.1 2.1 %fusion.4 = bf16[32,8,12,64]{3,0,2,1:T(8,128)(2,1)S(1)} fusion(f32[8,12,32,32]{2,3,1,0:T(8,128)} %get-tuple-element.12, bf16[32,8,12,64]{3,2,1,0:T(8,128)(2,1)S(1)} %copy-done.4, f32[8,12,32]{2,1,0:T(8,128)S(1)} %get-tuple-element.11), kind=kOutput, calls=%fused_computation.7 | convolution fusion | flops 12976128 | bytes 1191936 | tf_op jit(solution)/shard_map/chrs,sche->rche/dot_general | solution.py:112
  132.3 0.3 copy.91
  132.6 0.6 reshape.144
  133.3 15.5 %all_to_all.30 = bf16[32,8,768]{2,1,0:T(8,128)(2,1)S(1)} all-to-all(bf16[32,8,768]{2,1,0:T(8,128)(2,1)S(1)} %reshape.144), channel_id=1, replica_groups=mesh['grp'=2,'seq'=16] {'seq'}, dimensions={0} | all-to-all | bytes 786432 | tf_op jit(solution)/shard_map/all_to_all | solution.py:116
  148.7 2.5 %fusion.7 = bf16[2,128,768]{2,1,0:T(8,128)(2,1)} fusion(f32[2,128,768]{2,1,0:T(8,128)S(1)} %get-tuple-element.10, bf16[768,768]{1,0:T(8,128)(2,1)} %param.25, bf16[2,16,8,768]{3,2,0,1:T(8,128)(2,1)S(1)} %bitcast.72), kind=kOutput, calls=%fused_computation.13 | convolution fusion | flops 302383104 | bytes 2752512 | tf_op jit(solution)/shard_map/dot_general | solution.py:117
  (24 shorter events, 0.2 us)
Async XLA Ops:
  6.5 91.4 %copy-start = (bf16[768,768]{1,0:T(8,128)(2,1)S(1)}, bf16[768,768]{1,0:T(8,128)(2,1)}, u32[]{:S(2)}) copy-start(bf16[768,768]{1,0:T(8,128)(2,1)} %param.20) | copy-start | bytes 3538948
  6.5 3.8 %copy-start.2 = (bf16[768,768]{1,0:T(8,128)(2,1)S(1)}, bf16[768,768]{1,0:T(8,128)(2,1)}, u32[]{:S(2)}) copy-start(bf16[768,768]{1,0:T(8,128)(2,1)} %param.18) | copy-start | bytes 3538948
  6.5 69.2 %reduce-scatter.2.cloned.1.call-start = ((), (), s32[]{:S(2)}) async-start(), calls=%async_computation.3 | async-start | bytes 1114112 | tf_op jit(solution)/shard_map/reduce_scatter | solution.py:69
  12.8 0.7 copy-start.6
  12.8 0.7 copy-start.7
  14.1 1.5 copy-start.3
  76.9 21.0 %copy-start.1 = (bf16[2,128,768]{2,1,0:T(8,128)(2,1)S(1)}, bf16[2,128,768]{2,1,0:T(8,128)(2,1)}, u32[]{:S(2)}) copy-start(bf16[2,128,768]{2,1,0:T(8,128)(2,1)} %param.13) | copy-start | bytes 1179652
  97.9 0.8 copy-start.5
  100.1 15.7 %all-to-all-start = ((bf16[2,128,768]{2,0,1:T(2,128)(2,1)}), bf16[2,128,768]{2,0,1:T(2,128)(2,1)S(1)}, u32[]{:S(2)}, u32[]{:S(2)}) async-start(bf16[2,128,768]{2,0,1:T(2,128)(2,1)} %copy.84), calls=%async_computation.1 | async-start | bytes 786432 | tf_op jit(solution)/shard_map/all_to_all | solution.py:98
  125.9 4.2 %copy-start.4 = (bf16[32,8,12,64]{3,2,1,0:T(8,128)(2,1)S(1)}, bf16[32,8,12,64]{3,2,1,0:T(8,128)(2,1)}, u32[]{:S(2)}) copy-start(bf16[32,8,12,64]{3,2,1,0:T(8,128)(2,1)} %reshape_reshape.14) | copy-start | bytes 1179652
Sparse Core Ops, SparseCore 0:
  15.6 60.1 reduce-scatter.1
where the time goes:
time: 159 us; the launch traced here: 158 us
  waiting for transfers between devices  71.4 us (45%)
  blocking collectives  36 us (23%)
  matrix products  18.1 us (11%)
  between operations  13.7 us (9%)
  local copies, waits for them, and re-layouts  9.7 us (6%)
  other arithmetic  5.64 us (4%)
  starting transfers between devices  3.56 us (2%)
    reduce_scatter x1, waiting for transfers between devices, per_device(): lax.psum_scatter(jnp.einsum('rihe,rjhe->ihj', query_a, key_a, preferred_e...  59.4 us
    all_gather x1, blocking collectives, per_device(): lax.all_gather(row_weights, 'seq', axis=0, tiled=True)  20.5 us
    all_to_all x1, blocking collectives, per_device(): lax.all_to_all(col_mixed, 'seq', split_axis=0, concat_axis=1, tiled=True)  15.5 us
    all_to_all x1, waiting for transfers between devices, per_device(): lax.all_to_all(normed_col, 'seq', split_axis=1, concat_axis=0, tiled=True)  12 us
    dot_general x6, matrix products, project(): jnp.dot(flattened, weight, preferred_element_type=jnp.float32)  7.94 us
    sub x1, matrix products, per_device(): col_weights = jax.nn.softmax(col_scores, axis=-1).astype(jnp.bfloat16)  4.24 us
    all_to_all x1, starting transfers between devices, per_device(): lax.all_to_all(normed_col, 'seq', split_axis=1, concat_axis=0, tiled=True)  3.55 us
  transfers between devices with their start and end apart: 2, of which 2 were waited for; matrix products, arithmetic and copies ran while one was open for 1% of the time, Pallas kernels for 0%

commit v1 on v0

--- a/solution.py
+++ b/solution.py
@@ -65,26 +65,37 @@
     )
     value_a = project(normed_row, row_value).reshape(rows_dev, columns, head_count, head_size)
     scale = 1.0 / (math.sqrt(head_size) * math.sqrt(total_rows))
-    tied = (
-        lax.psum_scatter(
-            jnp.einsum("rihe,rjhe->ihj", query_a, key_a, preferred_element_type=jnp.float32),
-            "seq",
-            scatter_dimension=0,
-            tiled=True,
-        )
-        * scale
+    fold = columns // 2
+    partial = jnp.einsum("rihe,rjhe->ihj", query_a, key_a, preferred_element_type=jnp.float32)
+    same = protein_id[:, None] == protein_id[None, :]
+    folded = jnp.where(same[:, None, :fold], partial[..., :fold], partial[..., fold:])
+    blocks = lax.all_to_all(
+        folded.reshape(devices, tile_cols, head_count * fold),
+        "seq",
+        split_axis=0,
+        concat_axis=0,
+        tiled=True,
     )
-    prot_query = lax.dynamic_slice_in_dim(protein_id, position * tile_cols, tile_cols, 0)
-    same_prot = prot_query[:, None, None] == protein_id[None, None, :]
-    tied = jnp.where(same_prot, tied, -1000000000.0)
+    tied = jnp.sum(blocks, axis=0).reshape(tile_cols, head_count, fold) * scale
+    same_tile = lax.dynamic_slice_in_dim(same, position * tile_cols, tile_cols, 0)
+    same_folded = same_tile[:, :fold] | same_tile[:, fold:]
+    tied = jnp.where(same_folded[:, None, :], tied, -1000000000.0)
     row_weights = jax.nn.softmax(tied, axis=-1).astype(jnp.bfloat16)
+    gathered = lax.all_to_all(
+        jnp.broadcast_to(
+            row_weights.reshape(1, tile_cols, head_count * fold),
+            (devices, tile_cols, head_count * fold),
+        ),
+        "seq",
+        split_axis=0,
+        concat_axis=0,
+        tiled=True,
+    ).reshape(columns, head_count, fold)
+    weights = jnp.where(
+        same[:, None, :], jnp.concatenate([gathered, gathered], axis=-1), jnp.bfloat16(0)
+    )
     row_mixed = (
-        jnp.einsum(
-            "ihj,rjhe->rihe",
-            lax.all_gather(row_weights, "seq", axis=0, tiled=True),
-            value_a,
-            preferred_element_type=jnp.float32,
-        )
+        jnp.einsum("ihj,rjhe->rihe", weights, value_a, preferred_element_type=jnp.float32)
         .astype(jnp.bfloat16)
         .reshape(rows_dev, columns, width)
     )

time: 159 us -> 99.5 us (0.63)
  waiting for transfers between devices: 71.4 us -> 31.8 us
  blocking collectives: 36 us -> 15.5 us
  between operations: 13.7 us -> 0.38 us
  starting transfers between devices: 3.56 us -> 14.8 us
  local copies, waits for them, and re-layouts: 9.7 us -> 12.9 us
    reduce_scatter x1 -> x0, waiting for transfers between devices: 59.4 us -> none  [per_device(): lax.psum_scatter(jnp.einsum('rihe,rjhe->ihj', query_a, key_a, preferred_e...]
    all_gather x1 -> x0, blocking collectives: 20.5 us -> none  [per_device(): lax.all_gather(row_weights, 'seq', axis=0, tiled=True)]
    all_to_all x0 -> x2, waiting for transfers between devices: none -> 20 us  [the longest x1 11.9 us: per_device(): lax.all_to_all(folded.reshape(devices, tile_cols, head_count * fold), 'se...]
    all_to_all x0 -> x2, starting transfers between devices: none -> 11 us  [the longest x1 7.51 us: per_device(): lax.all_to_all(folded.reshape(devices, tile_cols, head_count * fold), 'se...]
  transfers between devices with their start and end apart: 2 -> 3, of which waited for: 2 -> 3; matrix products, arithmetic and copies ran while one was open for 1% -> 1% of each run, Pallas kernels for 0% -> 0%
where the time goes in v1:
time: 99.5 us; the launch traced here: 98.7 us
  waiting for transfers between devices  31.8 us (32%)
  matrix products  16.8 us (17%)
  blocking collectives  15.5 us (16%)
  starting transfers between devices  14.8 us (15%)
  local copies, waits for them, and re-layouts  12.9 us (13%)
  other arithmetic  6.52 us (7%)
    all_to_all x1, blocking collectives, per_device(): lax.all_to_all(col_mixed, 'seq', split_axis=0, concat_axis=1, tiled=True)  15.5 us
    all_to_all x1, waiting for transfers between devices, per_device(): lax.all_to_all(folded.reshape(devices, tile_cols, head_count * fold), 'se...  11.9 us
    all_to_all x1, waiting for transfers between devices, per_device(): lax.all_to_all(normed_col, 'seq', split_axis=1, concat_axis=0, tiled=True)  11.8 us
    all_to_all x1, waiting for transfers between devices, per_device(): lax.all_to_all(jnp.broadcast_to(row_weights.reshape(1, tile_cols, head_co...  8.09 us
    all_to_all x1, starting transfers between devices, per_device(): lax.all_to_all(folded.reshape(devices, tile_cols, head_count * fold), 'se...  7.51 us
    dot_general x6, matrix products, project(): jnp.dot(flattened, weight, preferred_element_type=jnp.float32)  6.68 us
    sub x1, matrix products, per_device(): col_weights = jax.nn.softmax(col_scores, axis=-1).astype(jnp.bfloat16)  4.24 us
    all_to_all x1, starting transfers between devices, per_device(): lax.all_to_all(normed_col, 'seq', split_axis=1, concat_axis=0, tiled=True)  3.73 us
  transfers between devices with their start and end apart: 3, of which 3 were waited for; matrix products, arithmetic and copies ran while one was open for 1% of the time, Pallas kernels for 0%

profile of v1, /device:TPU:0, one launch (start us, length us, event | category | flops | bytes accessed | tf_op | source)
XLA Modules:
  0.0 98.7 jit_solution(8152733996387298316)
XLA Ops:
  0.0 1.3 %convert_reduce_fusion = f32[2,128]{1,0:T(2,128)S(1)} fusion(bf16[2,128,768]{2,1,0:T(8,128)(2,1)} %param.13), kind=kLoop, calls=%fused_computation.23 | loop fusion | flops 392960 | bytes 394240 | tf_op jit(solution)/shard_map/reduce_sum | solution.py:13
  1.3 1.2 %fusion.13 = f32[2,128]{1,0:T(2,128)S(1)} fusion(bf16[2,128,768]{2,1,0:T(8,128)(2,1)} %param.13, f32[2,128]{1,0:T(2,128)S(1)} %broadcast_multiply_fusion.4), kind=kLoop, calls=%fused_computation.28 | loop fusion | flops 786176 | bytes 395264 | tf_op jit(solution)/shard_map/reduce_sum | solution.py:14
  2.5 1.2 %fusion.15 = bf16[2,128,768]{2,1,0:T(8,128)(2,1)S(1)} fusion(bf16[2,128,768]{2,1,0:T(8,128)(2,1)} %param.13, f32[768]{0:T(1024)} %param.16, f32[2,128]{1,0:T(2,128)S(1)} %add_rsqrt_fusion.1, f32[2,128]{1,0:T(2,128)S(1)} %broadcast_multiply_fusion.4), kind=kLoop, calls=%fused_computation.30 | loop fusion | flops 983040 | bytes 791552 | tf_op jit(solution)/shard_map/convert_element_type | solution.py:15
  3.8 0.5 convolution_convert_fusion.5
  4.3 0.2 copy.85
  4.5 0.1 reshape.173
  4.6 1.0 copy-done.3
  5.5 0.5 convolution_convert_fusion.4
  6.1 0.2 copy.86
  6.2 0.1 reshape.174
  6.4 0.3 copy-done.7
  7.0 0.3 convolution_bitcast_fusion
  7.4 0.5 copy.89
  7.9 1.0 %reshape.175 = f32[16,8,768]{2,1,0:T(8,128)} reshape(f32[128,12,64]{2,1,0:T(8,128)S(1)} %copy.89) | data formatting | bytes 786432 | tf_op jit(solution)/shard_map/reshape | solution.py:73
  8.9 7.5 %all-to-all-start = ((f32[16,8,768]{2,1,0:T(8,128)}), f32[16,8,768]{2,1,0:T(8,128)S(1)}, u32[]{:S(2)}, u32[]{:S(2)}) async-start(f32[16,8,768]{2,1,0:T(8,128)} %reshape.175), calls=%async_computation | async-start | bytes 786432 | tf_op jit(solution)/shard_map/all_to_all | solution.py:72
  16.6 0.1 broadcast_in_dim.64
  16.7 11.9 %all-to-all-done = f32[16,8,768]{2,1,0:T(8,128)S(1)} async-done(((f32[16,8,768]{2,1,0:T(8,128)}), f32[16,8,768]{2,1,0:T(8,128)S(1)}, u32[]{:S(2)}, u32[]{:S(2)}) %all-to-all-start) | async-done | bytes 393248 | tf_op jit(solution)/shard_map/all_to_all | solution.py:72
  28.9 1.2 %fusion.1 = f32[8,12,64]{2,1,0:T(8,128)S(1)} fusion(f32[8,12,64]{2,1,0:T(8,128)S(1)} %mul.79, f32[8,12]{1,0:T(8,128)S(1)} %select_reduce_fusion, pred[8,64]{1,0:T(8,128)(4,1)S(1)} %copy.84), kind=kOutput, calls=%fused_computation.1 | output fusion | flops 12447 | bytes 50048 | tf_op jit(solution)/shard_map/div | solution.py:83
  30.1 0.1 div.43
  30.4 0.7 broadcast_in_dim.97
  31.1 3.5 %all-to-all-start.1 = ((bf16[16,8,768]{2,1,0:T(8,128)(2,1)}), bf16[16,8,768]{2,1,0:T(8,128)(2,1)S(1)}, u32[]{:S(2)}, u32[]{:S(2)}) async-start(bf16[16,8,768]{2,1,0:T(8,128)(2,1)} %broadcast_in_dim.97), calls=%async_computation.1 | async-start | bytes 393216 | tf_op jit(solution)/shard_map/all_to_all | solution.py:84
  34.6 0.1 copy.83
  34.8 0.5 convolution_convert_fusion.6
  35.3 0.2 copy.82
  35.4 0.1 reshape_reshape.13
  35.5 8.1 %all-to-all-done.1 = bf16[16,8,768]{2,1,0:T(8,128)(2,1)S(1)} async-done(((bf16[16,8,768]{2,1,0:T(8,128)(2,1)}), bf16[16,8,768]{2,1,0:T(8,128)(2,1)S(1)}, u32[]{:S(2)}, u32[]{:S(2)}) %all-to-all-start.1) | async-done | bytes 196640 | tf_op jit(solution)/shard_map/all_to_all | solution.py:84
  43.6 0.3 reshape.176
  44.0 0.4 fusion.20
  44.4 0.4 fusion.8
  44.9 0.5 copy-done.1
  45.4 0.6 fusion.38
  46.0 0.2 multiply_reduce_fusion
  46.3 0.2 multiply_convert_fusion
  46.4 1.2 %copy.94 = bf16[2,128,768]{2,0,1:T(2,128)(2,1)} copy(bf16[2,128,768]{2,1,0:T(8,128)(2,1)S(1)} %multiply_convert_fusion) | data formatting | bytes 786432 | tf_op jit(solution)/shard_map/convert_element_type | solution.py:15
  47.6 3.7 %all-to-all-start.2 = ((bf16[2,128,768]{2,0,1:T(2,128)(2,1)}), bf16[2,128,768]{2,0,1:T(2,128)(2,1)S(1)}, u32[]{:S(2)}, u32[]{:S(2)}) async-start(bf16[2,128,768]{2,0,1:T(2,128)(2,1)} %copy.94), calls=%async_computation.2 | async-start | bytes 786432 | tf_op jit(solution)/shard_map/all_to_all | solution.py:109
  51.5 11.8 %all-to-all-done.2 = bf16[2,128,768]{2,0,1:T(2,128)(2,1)S(1)} async-done(((bf16[2,128,768]{2,0,1:T(2,128)(2,1)}), bf16[2,128,768]{2,0,1:T(2,128)(2,1)S(1)}, u32[]{:S(2)}, u32[]{:S(2)}) %all-to-all-start.2) | async-done | bytes 393248 | tf_op jit(solution)/shard_map/all_to_all | solution.py:109
  63.4 1.7 %convolution_convert_fusion.2 = bf16[256,768]{1,0:T(8,128)(2,1)S(1)} fusion(bf16[256,768]{1,0:T(8,128)(2,1)S(1)} %bitcast.60, bf16[768,768]{1,0:T(8,128)(2,1)} %param.22), kind=kOutput, calls=%fused_computation.15 | convolution fusion | flops 302186496 | bytes 1966080 | tf_op jit(solution)/shard_map/dot_general | solution.py:22
  65.1 1.6 %reshape_reshape.15 = bf16[32,8,12,64]{3,2,1,0:T(8,128)(2,1)} reshape(bf16[256,768]{1,0:T(8,128)(2,1)S(1)} %convolution_convert_fusion.2) | data formatting | bytes 786432 | tf_op jit(solution)/shard_map/reshape;reshape | solution.py:113
  66.7 1.7 %convolution_convert_fusion.1 = bf16[256,768]{1,0:T(8,128)(2,1)S(1)} fusion(bf16[256,768]{1,0:T(8,128)(2,1)S(1)} %bitcast.61, bf16[768,768]{1,0:T(8,128)(2,1)} %param.23), kind=kOutput, calls=%fused_computation.14 | convolution fusion | flops 302186496 | bytes 1966080 | tf_op jit(solution)/shard_map/dot_general | solution.py:22
  68.5 1.6 %reshape_reshape.16 = bf16[32,8,12,64]{3,2,1,0:T(8,128)(2,1)} reshape(bf16[256,768]{1,0:T(8,128)(2,1)S(1)} %convolution_convert_fusion.1) | data formatting | bytes 786432 | tf_op jit(solution)/shard_map/reshape;reshape | solution.py:114
  70.1 1.7 %convolution_convert_fusion.3 = bf16[256,768]{1,0:T(8,128)(2,1)S(1)} fusion(bf16[256,768]{1,0:T(8,128)(2,1)S(1)} %bitcast.62, bf16[768,768]{1,0:T(8,128)(2,1)} %param.24), kind=kOutput, calls=%fused_computation.16 | convolution fusion | flops 302186496 | bytes 1966080 | tf_op jit(solution)/shard_map/dot_general | solution.py:22
  71.8 1.6 %reshape_reshape.14 = bf16[32,8,12,64]{3,2,1,0:T(8,128)(2,1)} reshape(bf16[256,768]{1,0:T(8,128)(2,1)S(1)} %convolution_convert_fusion.3) | data formatting | bytes 786432 | tf_op jit(solution)/shard_map/reshape;reshape | solution.py:115
  73.4 4.2 %fusion.39 = (f32[8,12,32]{2,1,0:T(8,128)S(1)}, f32[8,12,32,32]{2,3,1,0:T(8,128)}) fusion(bf16[32,8,12,64]{3,2,1,0:T(8,128)(2,1)} %reshape_reshape.16, bf16[32,8,12,64]{3,2,1,0:T(8,128)(2,1)} %reshape_reshape.15, pred[8,32]{1,0:T(8,128)(4,1)S(1)} %iota_compare_fusion), kind=kOutput, calls=%fused_computation.72 | convolution fusion | flops 12976159 | bytes 1192192 | tf_op jit(solution)/shard_map/sub | solution.py:122
  77.6 2.1 %fusion.4 = bf16[32,8,12,64]{3,0,2,1:T(8,128)(2,1)S(1)} fusion(f32[8,12,32,32]{2,3,1,0:T(8,128)} %get-tuple-element.10, bf16[32,8,12,64]{3,2,1,0:T(8,128)(2,1)S(1)} %copy-done.5, f32[8,12,32]{2,1,0:T(8,128)S(1)} %get-tuple-element.9), kind=kOutput, calls=%fused_computation.7 | convolution fusion | flops 12976128 | bytes 1191936 | tf_op jit(solution)/shard_map/chrs,sche->rche/dot_general | solution.py:123
  79.8 0.3 copy.101
  80.1 0.6 reshape.178
  80.7 15.5 %all_to_all.40 = bf16[32,8,768]{2,1,0:T(8,128)(2,1)S(1)} all-to-all(bf16[32,8,768]{2,1,0:T(8,128)(2,1)S(1)} %reshape.178), channel_id=1, replica_groups=mesh['grp'=2,'seq'=16] {'seq'}, dimensions={0} | all-to-all | bytes 786432 | tf_op jit(solution)/shard_map/all_to_all | solution.py:127
  96.2 2.5 %fusion.7 = bf16[2,128,768]{2,1,0:T(8,128)(2,1)} fusion(f32[2,128,768]{2,1,0:T(8,128)S(1)} %get-tuple-element.8, bf16[768,768]{1,0:T(8,128)(2,1)} %param.25, bf16[2,16,8,768]{3,2,0,1:T(8,128)(2,1)S(1)} %bitcast.69), kind=kOutput, calls=%fused_computation.13 | convolution fusion | flops 302383104 | bytes 2752512 | tf_op jit(solution)/shard_map/dot_general | solution.py:128
  (42 shorter events, 1.2 us)
Async XLA Ops:
  0.0 44.9 %copy-start = (bf16[768,768]{1,0:T(8,128)(2,1)S(1)}, bf16[768,768]{1,0:T(8,128)(2,1)}, u32[]{:S(2)}) copy-start(bf16[768,768]{1,0:T(8,128)(2,1)} %param.20) | copy-start | bytes 3538948
  0.0 3.8 %copy-start.2 = (bf16[768,768]{1,0:T(8,128)(2,1)S(1)}, bf16[768,768]{1,0:T(8,128)(2,1)}, u32[]{:S(2)}) copy-start(bf16[768,768]{1,0:T(8,128)(2,1)} %param.18) | copy-start | bytes 3538948
  4.3 1.3 %copy-start.3 = (bf16[768,768]{1,0:T(8,128)(2,1)S(1)}, bf16[768,768]{1,0:T(8,128)(2,1)}, u32[]{:S(2)}) copy-start(bf16[768,768]{1,0:T(8,128)(2,1)} %param.17) | copy-start | bytes 3538948
  6.0 0.7 copy-start.7
  6.0 0.7 copy-start.8
  8.9 25.9 %copy-start.4 = (bf16[768,768]{1,0:T(8,128)(2,1)S(1)}, bf16[768,768]{1,0:T(8,128)(2,1)}, u32[]{:S(2)}) copy-start(bf16[768,768]{1,0:T(8,128)(2,1)} %param.19) | copy-start | bytes 3538948
  8.9 19.7 %all-to-all-start = ((f32[16,8,768]{2,1,0:T(8,128)}), f32[16,8,768]{2,1,0:T(8,128)S(1)}, u32[]{:S(2)}, u32[]{:S(2)}) async-start(f32[16,8,768]{2,1,0:T(8,128)} %reshape.175), calls=%async_computation | async-start | bytes 786432 | tf_op jit(solution)/shard_map/all_to_all | solution.py:72
  31.1 12.5 %all-to-all-start.1 = ((bf16[16,8,768]{2,1,0:T(8,128)(2,1)}), bf16[16,8,768]{2,1,0:T(8,128)(2,1)S(1)}, u32[]{:S(2)}, u32[]{:S(2)}) async-start(bf16[16,8,768]{2,1,0:T(8,128)(2,1)} %broadcast_in_dim.97), calls=%async_computation.1 | async-start | bytes 393216 | tf_op jit(solution)/shard_map/all_to_all | solution.py:84
  44.4 1.0 %copy-start.1 = (bf16[2,128,768]{2,1,0:T(8,128)(2,1)S(1)}, bf16[2,128,768]{2,1,0:T(8,128)(2,1)}, u32[]{:S(2)}) copy-start(bf16[2,128,768]{2,1,0:T(8,128)(2,1)} %param.13) | copy-start | bytes 1179652
  45.4 0.8 copy-start.6
  47.6 15.7 %all-to-all-start.2 = ((bf16[2,128,768]{2,0,1:T(2,128)(2,1)}), bf16[2,128,768]{2,0,1:T(2,128)(2,1)S(1)}, u32[]{:S(2)}, u32[]{:S(2)}) async-start(bf16[2,128,768]{2,0,1:T(2,128)(2,1)} %copy.94), calls=%async_computation.2 | async-start | bytes 786432 | tf_op jit(solution)/shard_map/all_to_all | solution.py:109
  73.4 4.2 %copy-start.5 = (bf16[32,8,12,64]{3,2,1,0:T(8,128)(2,1)S(1)}, bf16[32,8,12,64]{3,2,1,0:T(8,128)(2,1)}, u32[]{:S(2)}) copy-start(bf16[32,8,12,64]{3,2,1,0:T(8,128)(2,1)} %reshape_reshape.14) | copy-start | bytes 1179652

commit v2 on v0

v2 whole, which is shorter than its diff:
```python
import functools
import math

import jax
import jax.numpy as jnp
from jax import lax
from jax.experimental import pallas as pl
from jax.experimental.pallas import tpu as pltpu
from jax.sharding import PartitionSpec as P

H = 12
EPS = 1e-05
NEG = -1000000000.0
F32 = jnp.float32
BF16 = jnp.bfloat16
LIMIT = 48 << 20


def call(kernel, out_shape, ins, outs, scratch, cost, name):
    spaces = {"v": pltpu.VMEM, "s": pltpu.SMEM, "a": pl.ANY}
    return pl.pallas_call(
        kernel,
        out_shape=out_shape,
        in_specs=[pl.BlockSpec(memory_space=spaces[c]) for c in ins],
        out_specs=[pl.BlockSpec(memory_space=spaces[c]) for c in outs],
        scratch_shapes=scratch,
        compiler_params=pltpu.CompilerParams(vmem_limit_bytes=LIMIT),
        cost_estimate=pl.CostEstimate(flops=cost[0], bytes_accessed=cost[1], transcendentals=cost[2]),
        name=name,
    )


def norm(full, gain):
    middle = jnp.mean(full, axis=-1, keepdims=True)
    spread = jnp.mean((full - middle) ** 2, axis=-1, keepdims=True)
    return (full - middle) * lax.rsqrt(spread + EPS) * gain


def dot(a, b):
    return jnp.dot(a, b, preferred_element_type=F32)


def dot_t(a, b):
    return lax.dot_general(a, b, (((1,), (1,)), ((), ())), preferred_element_type=F32)


def iota(shape, dim):
    return lax.broadcasted_iota(jnp.int32, shape, dim)


def to_column(row, size):
    eye = iota((size, size), 0) == iota((size, size), 1)
    return jnp.sum(jnp.where(eye, jnp.broadcast_to(row, (size, size)), 0.0), axis=1, keepdims=True)


def half_masks(width):
    low = (iota((1, width), 1) % 128) < 64
    return jnp.where(low, 1.0, 0.0), jnp.where(low, 0.0, 1.0)


def row_scores_kernel(
    depth_ref, place_ref, x_ref, gain_ref, prot_ref, wq_ref, wk_ref, part_ref, normed_ref, same_ref
):
    columns = prot_ref.shape[1]
    tokens, width = x_ref.shape
    rows = tokens // columns
    normed = norm(x_ref[...].astype(F32), gain_ref[...]).astype(BF16)
    normed_ref[...] = normed
    prot = prot_ref[...].astype(F32)
    depth = jnp.zeros((1, columns), F32)
    for p in range(depth_ref.shape[0]):
        depth = jnp.where(prot == float(p), depth_ref[p].astype(F32), depth)
    prot_col = to_column(prot, columns)
    depth_col = to_column(depth, columns)
    same = jnp.broadcast_to(prot_col, (columns, columns)) == jnp.broadcast_to(prot, (columns, columns))
    same_f = jnp.where(same, 1.0, 0.0)
    same_ref[...] = same_f
    low = iota((columns, columns), 1) < 64
    first = jnp.where(low, same_f, pltpu.roll(same_f, 64, 1)) > 0.5
    valid = [
        jnp.where((place_ref[0] * rows + r).astype(F32) < depth_col, 1.0, 0.0) for r in range(rows)
    ]
    valid = jnp.concatenate(valid, axis=0)
    even, odd = half_masks(256)
    for n in range(width // 256):
        cols = slice(256 * n, 256 * n + 256)
        query = dot(normed, wq_ref[:, cols]).astype(BF16).astype(F32) * valid
        key = (dot(normed, wk_ref[:, cols]) * valid).astype(BF16)
        query_even, query_odd = (query * even).astype(BF16), (query * odd).astype(BF16)
        for q in range(2):
            lanes = slice(128 * q, 128 * q + 128)

            def side(array, lanes=lanes):
                return jnp.concatenate(
                    [array[r * columns : (r + 1) * columns, lanes] for r in range(rows)], axis=1
                )

            both = jnp.concatenate([side(query_even), side(query_odd)], axis=0)
            logits = dot_t(both, side(key))
            one, two = logits[:columns], logits[columns:]
            folded = jnp.where(
                low,
                jnp.where(first, one, pltpu.roll(one, 64, 1)),
                jnp.where(first, pltpu.roll(two, 64, 1), two),
            )
            part_ref[:, 256 * n + 128 * q : 256 * n + 128 * q + 128] = folded


def project_kernel(x_ref, w_ref, out_ref):
    out_ref[...] = dot(x_ref[...], w_ref[...]).astype(BF16)


def row_softmax_kernel(scale, place_ref, blocks_ref, same_ref, out_ref, mask_ref):
    devices, tile, width = blocks_ref.shape
    same = same_ref[...]
    mask_ref[...] = jnp.maximum(same, pltpu.roll(same, 64, 1))
    live = mask_ref[pl.ds(place_ref[0] * tile, tile), :] > 0.5
    low = iota((tile, 128), 1) < 64
    total = blocks_ref[0]
    for d in range(1, devices):
        total = total + blocks_ref[d]
    pieces = []
    for p in range(width // 128):
        tied = jnp.where(live, total[:, 128 * p : 128 * p + 128] * scale, NEG)
        top_low = jnp.max(jnp.where(low, tied, 2 * NEG), axis=1, keepdims=True)
        top_high = jnp.max(jnp.where(low, 2 * NEG, tied), axis=1, keepdims=True)
        value = jnp.exp(tied - jnp.where(low, top_low, top_high))
        sum_low = jnp.sum(jnp.where(low, value, 0.0), axis=1, keepdims=True)
        sum_high = jnp.sum(jnp.where(low, 0.0, value), axis=1, keepdims=True)
        pieces.append(value / jnp.where(low, sum_low, sum_high))
    out_ref[...] = jnp.broadcast_to(
        jnp.concatenate(pieces, axis=1).astype(BF16)[None], (devices, tile, width)
    )


def row_output_kernel(
    folded_ref, same_ref, value_ref, x_ref, w_ref, gain_ref, after_ref, normed_ref, mixed_ref
):
    columns = same_ref.shape[0]
    tokens, width = x_ref.shape
    rows = tokens // columns
    folded = folded_ref[...].reshape(columns, width).astype(F32)
    same = same_ref[...] > 0.5
    low = iota((columns, columns), 1) < 64
    even, odd = half_masks(128 * rows)
    even, odd = even.astype(BF16), odd.astype(BF16)
    for p in range(width // 128):
        lanes = slice(128 * p, 128 * p + 128)
        piece = folded[:, lanes]
        turned = pltpu.roll(piece, 64, 1)
        one = jnp.where(same, jnp.where(low, piece, turned), 0.0)
        two = jnp.where(same, jnp.where(low, turned, piece), 0.0)
        weights = jnp.concatenate([one, two], axis=1).astype(BF16)
        value = jnp.concatenate(
            [value_ref[r * columns : (r + 1) * columns, lanes] for r in range(rows)], axis=1
        )
        value = jnp.concatenate([value * even, value * odd], axis=0)
        mixed = dot(weights, value).astype(BF16)
        for r in range(rows):
            mixed_ref[r * columns : (r + 1) * columns, lanes] = mixed[:, 128 * r : 128 * r + 128]
    after = (x_ref[...].astype(F32) + dot(mixed_ref[...], w_ref[...])).astype(BF16)
    after_ref[...] = after
    normed = norm(after.astype(F32), gain_ref[...])
    if len(normed_ref.shape) == 2:
        normed_ref[...] = normed.astype(BF16)
    else:
        devices, _, tile, _ = normed_ref.shape
        for d in range(devices):
            for r in range(rows):
                start = r * columns + d * tile
                normed_ref[d, r] = normed[start : start + tile].astype(BF16)


def column_kernel(scale, tile, depth_ref, prot_ref, place_ref, x_ref, wq_ref, wk_ref, wv_ref, out_ref):
    tokens, width = x_ref.shape
    x = x_ref[...]
    lane = iota((1, tokens), 1)
    depth = jnp.zeros((1, tokens), jnp.int32)
    for c in range(tile):
        depth = jnp.where(lane % tile == c, depth_ref[prot_ref[place_ref[0] * tile + c]], depth)
    live = (iota((tokens, tokens), 0) % tile == iota((tokens, tokens), 1) % tile) & (
        iota((tokens, tokens), 1) // tile < depth
    )
    even, odd = half_masks(256)
    for n in range(width // 256):
        cols = slice(256 * n, 256 * n + 256)
        query = dot(x, wq_ref[:, cols]).astype(BF16).astype(F32)
        key = dot(x, wk_ref[:, cols]).astype(BF16)
        value = dot(x, wv_ref[:, cols])
        query_sides = [(query * side).astype(BF16) for side in (even, odd)]
        value_sides = [(value * side).astype(BF16) for side in (even, odd)]
        for q in range(2):
            lanes = slice(128 * q, 128 * q + 128)
            mixed = jnp.zeros((tokens, 128), F32)
            for s in range(2):
                scores = dot_t(query_sides[s][:, lanes], key[:, lanes]) * scale
                scores = jnp.where(live, scores, NEG)
                top = jnp.max(scores, axis=1, keepdims=True)
                weight = jnp.exp(scores - top)
                weight = weight / jnp.sum(weight, axis=1, keepdims=True)
                mixed = mixed + dot(weight.astype(BF16), value_sides[s][:, lanes])
            out_ref[:, 256 * n + 128 * q : 256 * n + 128 * q + 128] = mixed.astype(BF16)


def column_output_kernel(x_ref, w_ref, after_ref, out_ref, total_ref):
    rows, columns, width = out_ref.shape
    if len(x_ref.shape) == 2:
        total = dot(x_ref[...], w_ref[...]) + after_ref[...].astype(F32)
        out_ref[...] = total.astype(BF16).reshape(rows, columns, width)
    else:
        devices, _, tile, _ = x_ref.shape
        total = dot(x_ref[...].reshape(rows * columns, width), w_ref[...])
        for d in range(devices):
            for r in range(rows):
                start, block = r * columns + d * tile, (d * rows + r) * tile
                total_ref[start : start + tile] = total[block : block + tile]
        total = total_ref[...] + after_ref[...].astype(F32)
        out_ref[...] = total.astype(BF16).reshape(rows, columns, width)


def exchange(array):
    return lax.all_to_all(array, "seq", split_axis=0, concat_axis=0, tiled=True)


def per_device(
    alignment,
    protein_id,
    row_depth,
    row_gain,
    row_query,
    row_key,
    row_value,
    row_output,
    column_gain,
    column_query,
    column_key,
    column_value,
    column_output,
):
    rows, columns, width = alignment.shape
    devices = lax.axis_size("seq")
    place = lax.axis_index("seq").astype(jnp.int32)[None]
    total_rows = rows * devices
    head_size = width // H
    tile = columns // devices
    tokens = rows * columns
    blocked = tile % 8 == 0
    x = alignment.reshape(tokens, width)
    shape = jax.ShapeDtypeStruct
    square = 2 * tokens * width * width

    partial, normed, same = call(
        row_scores_kernel,
        (shape((columns, width), F32), shape((tokens, width), BF16), shape((columns, columns), F32)),
        "ssvvvvv",
        "vvv",
        [],
        (2 * square, 4 * width * width, tokens),
        "row_scores",
    )(row_depth, place, x, row_gain[None], protein_id[None], row_query, row_key)
    blocks = exchange(partial.reshape(devices, tile, width))
    (value,) = call(
        project_kernel, (shape((tokens, width), BF16),), "vv", "v", [], (square, 2 * width * width, 0), "row_value"
    )(normed, row_value)
    (weights,) = call(
        functools.partial(row_softmax_kernel, 1.0 / (math.sqrt(head_size) * math.sqrt(total_rows))),
        (shape((devices, tile, width), BF16),),
        "svv",
        "v",
        [pltpu.VMEM((columns, columns), F32)],
        (columns * width, 6 * columns * width, tile * width),
        "row_softmax",
    )(place, blocks, same)
    folded = exchange(weights)
    normed_shape = (devices, rows, tile, width) if blocked else (tokens, width)
    after, normed = call(
        row_output_kernel,
        (shape((tokens, width), BF16), shape(normed_shape, BF16)),
        "vvvvvv",
        "vv",
        [pltpu.VMEM((tokens, width), BF16)],
        (square, 2 * width * width, tokens),
        "row_output",
    )(folded, same, value, x, row_output, column_gain[None])
    if not blocked:
        normed = normed.reshape(rows, devices, tile, width).transpose(1, 0, 2, 3)
    moved = exchange(normed).reshape(tokens, width)
    (mixed,) = call(
        functools.partial(column_kernel, 1.0 / math.sqrt(head_size), tile),
        (shape((tokens, width), BF16),),
        "sssvvvv",
        "v",
        [],
        (4 * square, 6 * width * width, H * tokens * tokens),
        "column_attention",
    )(row_depth, protein_id, place, moved, column_query, column_key, column_value)
    returned = exchange(mixed.reshape(devices, rows, tile, width))
    if not blocked:
        returned = returned.transpose(1, 0, 2, 3).reshape(tokens, width)
    (out,) = call(
        column_output_kernel,
        (shape((rows, columns, width), BF16),),
        "vvv",
        "v",
        [pltpu.VMEM((tokens, width), F32)],
        (square, 2 * width * width, 0),
        "column_output",
    )(returned, column_output, after)
    return out


def solution(mesh):
    return jax.shard_map(
        per_device,
        mesh=mesh,
        in_specs=(P(("grp", "seq"), None, None), P("grp"), P("grp")) + (P(),) * 10,
        out_specs=P(("grp", "seq"), None, None),
        check_vma=False,
    )
```

time: 159 us -> 79.8 us (0.50)
  waiting for transfers between devices: 71.4 us -> 7.44 us
  matrix products: 18.1 us -> 0 us
  blocking collectives: 36 us -> 49.8 us
  between operations: 13.7 us -> 0.15 us
  Pallas kernels: 0 us -> 10.3 us
  other arithmetic: 5.64 us -> 0 us
  local copies, waits for them, and re-layouts: 9.7 us -> 7.84 us
    reduce_scatter x1 -> x0, waiting for transfers between devices: 59.4 us -> none  [per_device(): lax.psum_scatter(jnp.einsum('rihe,rjhe->ihj', query_a, key_a, preferred_e...]
    all_to_all x1 -> x3, blocking collectives: 15.5 us -> 49.8 us  [exchange(): return lax.all_to_all(array, 'seq', split_axis=0, concat_axis=0, tiled=True)]
    all_gather x1 -> x0, blocking collectives: 20.5 us -> none  [per_device(): lax.all_gather(row_weights, 'seq', axis=0, tiled=True)]
    dot_general x11 -> x0, matrix products: 13.9 us -> none  [the longest x6 7.94 us: project(): jnp.dot(flattened, weight, preferred_element_type=jnp.float32)]
    pallas_call x0 -> x6, Pallas kernels: none -> 10.3 us  [the longest x1 4.45 us: per_device(): call(functools.partial(column_kernel, 1.0 / math.sqrt(head_size), tile),...]
    unnamed x17 -> x34, local copies, waits for them, and re-layouts: 0.4 us -> 7.15 us
    another operation x4 -> x0, local copies, waits for them, and re-layouts: 4.84 us -> none  [the longest x1 1.6 us: per_device(): query_b = query_b.reshape(total_rows, tile_cols, head_count, head_size)]
    all_to_all x1, waiting for transfers between devices: 12 us -> 7.44 us  [exchange(): return lax.all_to_all(array, 'seq', split_axis=0, concat_axis=0, tiled=True)]
  transfers between devices with their start and end apart: 2 -> 1, of which waited for: 2 -> 1; matrix products, arithmetic and copies ran while one was open for 1% -> 0% of each run, Pallas kernels for 0% -> 1%
where the time goes in v2:
time: 79.8 us; the launch traced here: 79.2 us
  blocking collectives  49.8 us (62%)
  Pallas kernels  10.3 us (13%)
  local copies, waits for them, and re-layouts  7.84 us (10%)
  waiting for transfers between devices  7.44 us (9%)
  starting transfers between devices  3.66 us (5%)
    all_to_all x3, blocking collectives, exchange(): return lax.all_to_all(array, 'seq', split_axis=0, concat_axis=0, tiled=True)  49.8 us
    all_to_all x1, waiting for transfers between devices, exchange(): return lax.all_to_all(array, 'seq', split_axis=0, concat_axis=0, tiled=True)  7.44 us
    unnamed x34, local copies, waits for them, and re-layouts  7.15 us
    pallas_call x1, Pallas kernels, per_device(): call(functools.partial(column_kernel, 1.0 / math.sqrt(head_size), tile),...  4.45 us
    all_to_all x1, starting transfers between devices, exchange(): return lax.all_to_all(array, 'seq', split_axis=0, concat_axis=0, tiled=True)  3.66 us
    pallas_call x1, Pallas kernels, per_device(): call(row_scores_kernel, (shape((columns, width), F32), shape((tokens, wid...  2.26 us
  transfers between devices with their start and end apart: 1, of which 1 were waited for; matrix products, arithmetic and copies ran while one was open for 0% of the time, Pallas kernels for 1%

profile of v2, /device:TPU:0, one launch (start us, length us, event | category | flops | bytes accessed | tf_op | source)
XLA Modules:
  0.0 79.2 jit_solution(17918831212133312451)
XLA Ops:
  0.0 0.7 broadcast_in_dim.13.gain_ref
  0.7 0.0 copy-start
  0.7 1.0 %copy-done = bf16[2,128,768]{2,1,0:T(8,128)(2,1)S(1)} copy-done((bf16[2,128,768]{2,1,0:T(8,128)(2,1)S(1)}, bf16[2,128,768]{2,1,0:T(8,128)(2,1)}, u32[]{:S(2)}) %copy-start) | copy-done | bytes 393240
  1.7 0.0 copy-start.2
  1.7 1.3 %copy-done.2 = bf16[768,768]{1,0:T(8,128)(2,1)S(1)} copy-done((bf16[768,768]{1,0:T(8,128)(2,1)S(1)}, bf16[768,768]{1,0:T(8,128)(2,1)}, u32[]{:S(2)}) %copy-start.2) | copy-done | bytes 1179672
  3.0 0.0 copy-start.3
  3.0 1.3 %copy-done.3 = bf16[768,768]{1,0:T(8,128)(2,1)S(1)} copy-done((bf16[768,768]{1,0:T(8,128)(2,1)S(1)}, bf16[768,768]{1,0:T(8,128)(2,1)}, u32[]{:S(2)}) %copy-start.3) | copy-done | bytes 1179672
  4.2 0.0 copy-start.9
  4.2 0.7 copy-done.9
  4.9 0.0 copy-start.11
  4.9 0.7 copy-done.11
  5.5 2.3 %row_scores.1 = (f32[128,768]{1,0:T(8,128)S(1)}, bf16[256,768]{1,0:T(8,128)(2,1)S(1)}, f32[128,128]{1,0:T(8,128)S(1)}) custom-call(s32[4]{0:T(128)S(1)} %copy-done.9, s32[1]{0:T(128)} %bitcast.place_ref, bf16[256,768]{1,0:T(8,128)(2,1)S(1)} %bitcast.6, f32[1,768]{1,0:T(1,128)S(1)} %broadcast_in_dim.13.gain_ref, s32[1,128]{1,0:T(1,128)S(1)} %bitcast.11, ...), custom_call_target="tpu_custom_call" | custom-call | flops 603979776 | bytes 2359296 | tf_op jit(solution)/shard_map/row_scores/pallas_call | solution.py:252
  7.8 0.0 copy-start.7
  7.8 0.0 copy-start.16
  7.8 0.0 copy-start.6
  7.8 19.5 %all_to_all.20.blocks_ref = f32[16,8,768]{2,1,0:T(8,128)S(1)} all-to-all(f32[16,8,768]{2,1,0:T(8,128)S(1)} %bitcast.8), channel_id=1, replica_groups=mesh['grp'=2,'seq'=16] {'seq'}, dimensions={0} | all-to-all | bytes 786432 | tf_op jit(solution)/shard_map/all_to_all | solution.py:222
  27.4 0.0 copy-done.7
  27.4 0.9 %row_softmax.1 = bf16[16,8,768]{2,1,0:T(8,128)(2,1)} custom-call(s32[1]{0:T(128)} %bitcast.place_ref, f32[16,8,768]{2,1,0:T(8,128)S(1)} %all_to_all.20.blocks_ref, f32[128,128]{1,0:T(8,128)S(1)} %get-tuple-element.11.same_ref), custom_call_target="tpu_custom_call" | custom-call | flops 98304 | bytes 589824 | tf_op jit(solution)/shard_map/row_softmax/pallas_call | solution.py:265
  28.3 0.0 copy-start.1
  28.3 0.0 copy-start.4
  28.3 3.7 %all-to-all-start.1 = ((bf16[16,8,768]{2,1,0:T(8,128)(2,1)}), bf16[16,8,768]{2,1,0:T(8,128)(2,1)S(1)}, u32[]{:S(2)}, u32[]{:S(2)}) async-start(bf16[16,8,768]{2,1,0:T(8,128)(2,1)} %row_softmax.1), calls=%async_computation.1 | async-start | bytes 393216 | tf_op jit(solution)/shard_map/all_to_all | solution.py:222
  32.0 0.0 copy-done.16
  32.0 0.0 copy-done.6
  32.0 0.0 copy-start.8
  32.0 1.0 %copy-done.8 = bf16[256,768]{1,0:T(8,128)(2,1)S(1)} copy-done((bf16[256,768]{1,0:T(8,128)(2,1)S(1)}, bf16[256,768]{1,0:T(8,128)(2,1)}, u32[]{:S(2)}) %copy-start.8) | copy-done | bytes 393240
  33.0 0.5 row_value.1.value_ref
  33.5 0.0 copy-start.10
  33.5 0.0 copy-start.12
  33.5 7.4 %all-to-all-done.1.folded_ref = bf16[16,8,768]{2,1,0:T(8,128)(2,1)S(1)} async-done(((bf16[16,8,768]{2,1,0:T(8,128)(2,1)}), bf16[16,8,768]{2,1,0:T(8,128)(2,1)S(1)}, u32[]{:S(2)}, u32[]{:S(2)}) %all-to-all-start.1) | async-done | bytes 196640 | tf_op jit(solution)/shard_map/all_to_all | solution.py:222
  41.0 0.0 copy-done.1
  41.0 0.0 copy-done.4
  41.0 0.0 copy-start.13
  41.0 0.0 copy-start.14
  41.0 1.0 %row_output.1 = (bf16[256,768]{1,0:T(8,128)(2,1)S(1)}, bf16[16,2,8,768]{3,2,1,0:T(8,128)(2,1)S(1)}) custom-call(bf16[16,8,768]{2,1,0:T(8,128)(2,1)S(1)} %all-to-all-done.1.folded_ref, f32[128,128]{1,0:T(8,128)S(1)} %get-tuple-element.11.same_ref, bf16[256,768]{1,0:T(8,128)(2,1)S(1)} %row_value.1.value_ref, bf16[256,768]{1,0:T(8,128)(2,1)S(1)} %bitcast.7, ...), custom_call_target="tpu_custom_call" | custom-call | flops 301989888 | bytes 1179648 | tf_op jit(solution)/shard_map/row_output/pallas_call | solution.py:276
  42.0 14.8 %all_to_all.21 = bf16[16,2,8,768]{3,2,1,0:T(8,128)(2,1)S(1)} all-to-all(bf16[16,2,8,768]{3,2,1,0:T(8,128)(2,1)S(1)} %get-tuple-element.13), channel_id=1, replica_groups=mesh['grp'=2,'seq'=16] {'seq'}, dimensions={0} | all-to-all | bytes 786432 | tf_op jit(solution)/shard_map/all_to_all | solution.py:222
  56.8 0.0 copy-done.10
  56.8 0.0 copy-done.12
  56.8 0.0 copy-done.13
  56.8 0.0 copy-done.14
  56.8 0.0 copy-start.15
  56.8 1.3 %copy-done.15 = bf16[768,768]{1,0:T(8,128)(2,1)S(1)} copy-done((bf16[768,768]{1,0:T(8,128)(2,1)S(1)}, bf16[768,768]{1,0:T(8,128)(2,1)}, u32[]{:S(2)}) %copy-start.15) | copy-done | bytes 1179672
  58.1 0.0 copy-start.5
  58.1 4.5 %column_attention.1 = bf16[256,768]{1,0:T(8,128)(2,1)S(1)} custom-call(s32[4]{0:T(128)S(1)} %copy-done.10, s32[128]{0:T(128)S(1)} %copy-done.12, s32[1]{0:T(128)} %bitcast.place_ref, bf16[256,768]{1,0:T(8,128)(2,1)S(1)} %bitcast.9, bf16[768,768]{1,0:T(8,128)(2,1)S(1)} %copy-done.13, bf16[768,768]{1,0:T(8,128)(2,1)S(1)} %copy-done.14, ...), custom_call_target="tpu_custom_call" | custom-call | flops 1207959552 | bytes 3538944 | tf_op jit(solution)/shard_map/column_attention/pallas_call | solution.py:288
  62.5 15.5 %all_to_all.22.x_ref = bf16[16,2,8,768]{3,2,1,0:T(8,128)(2,1)S(1)} all-to-all(bf16[16,2,8,768]{3,2,1,0:T(8,128)(2,1)S(1)} %bitcast.10), channel_id=1, replica_groups=mesh['grp'=2,'seq'=16] {'seq'}, dimensions={0} | all-to-all | bytes 786432 | tf_op jit(solution)/shard_map/all_to_all | solution.py:222
  78.0 0.0 copy-done.5
  78.0 1.2 %column_output.1 = bf16[2,128,768]{2,1,0:T(8,128)(2,1)} custom-call(bf16[16,2,8,768]{3,2,1,0:T(8,128)(2,1)S(1)} %all_to_all.22.x_ref, bf16[768,768]{1,0:T(8,128)(2,1)S(1)} %copy-done.5, bf16[256,768]{1,0:T(8,128)(2,1)S(1)} %get-tuple-element.14.after_ref), custom_call_target="tpu_custom_call" | custom-call | flops 301989888 | bytes 1179648 | tf_op jit(solution)/shard_map/column_output/pallas_call | solution.py:300
  (1 shorter events, 0.0 us)
Async XLA Ops:
  0.7 1.0 %copy-start = (bf16[2,128,768]{2,1,0:T(8,128)(2,1)S(1)}, bf16[2,128,768]{2,1,0:T(8,128)(2,1)}, u32[]{:S(2)}) copy-start(bf16[2,128,768]{2,1,0:T(8,128)(2,1)} %param.13) | copy-start | bytes 1179652
  1.7 1.3 %copy-start.2 = (bf16[768,768]{1,0:T(8,128)(2,1)S(1)}, bf16[768,768]{1,0:T(8,128)(2,1)}, u32[]{:S(2)}) copy-start(bf16[768,768]{1,0:T(8,128)(2,1)} %wq_ref.2) | copy-start | bytes 3538948
  3.0 1.3 %copy-start.3 = (bf16[768,768]{1,0:T(8,128)(2,1)S(1)}, bf16[768,768]{1,0:T(8,128)(2,1)}, u32[]{:S(2)}) copy-start(bf16[768,768]{1,0:T(8,128)(2,1)} %wk_ref.2) | copy-start | bytes 3538948
  4.2 0.7 copy-start.9
  4.9 0.7 copy-start.11
  7.8 19.6 %copy-start.7 = (bf16[256,768]{1,0:T(8,128)(2,1)}, bf16[256,768]{1,0:T(8,128)(2,1)S(1)}, u32[]{:S(2)}) copy-start(bf16[256,768]{1,0:T(8,128)(2,1)S(1)} %get-tuple-element.12.x_ref) | copy-start | bytes 1179652
  7.8 24.2 %copy-start.16 = (f32[768]{0:T(1024)S(1)}, f32[768]{0:T(1024)}, u32[]{:S(2)}) copy-start(f32[768]{0:T(1024)} %param.21) | copy-start | bytes 9220
  7.8 24.2 %copy-start.6 = (bf16[768,768]{1,0:T(8,128)(2,1)S(1)}, bf16[768,768]{1,0:T(8,128)(2,1)}, u32[]{:S(2)}) copy-start(bf16[768,768]{1,0:T(8,128)(2,1)} %w_ref.3) | copy-start | bytes 3538948
  28.3 12.7 %copy-start.1 = (bf16[2,128,768]{2,1,0:T(8,128)(2,1)S(1)}, bf16[2,128,768]{2,1,0:T(8,128)(2,1)}, u32[]{:S(2)}) copy-start(bf16[2,128,768]{2,1,0:T(8,128)(2,1)} %param.13) | copy-start | bytes 1179652
  28.3 12.7 %copy-start.4 = (bf16[768,768]{1,0:T(8,128)(2,1)S(1)}, bf16[768,768]{1,0:T(8,128)(2,1)}, u32[]{:S(2)}) copy-start(bf16[768,768]{1,0:T(8,128)(2,1)} %w_ref.4) | copy-start | bytes 3538948
  28.3 12.7 %all-to-all-start.1 = ((bf16[16,8,768]{2,1,0:T(8,128)(2,1)}), bf16[16,8,768]{2,1,0:T(8,128)(2,1)S(1)}, u32[]{:S(2)}, u32[]{:S(2)}) async-start(bf16[16,8,768]{2,1,0:T(8,128)(2,1)} %row_softmax.1), calls=%async_computation.1 | async-start | bytes 393216 | tf_op jit(solution)/shard_map/all_to_all | solution.py:222
  32.0 1.0 %copy-start.8 = (bf16[256,768]{1,0:T(8,128)(2,1)S(1)}, bf16[256,768]{1,0:T(8,128)(2,1)}, u32[]{:S(2)}) copy-start(bf16[256,768]{1,0:T(8,128)(2,1)} %copy-done.7) | copy-start | bytes 1179652
  33.5 23.3 %copy-start.10 = (s32[4]{0:T(128)S(1)}, s32[4]{0:T(128)}, u32[]{:S(2)}) copy-start(s32[4]{0:T(128)} %depth_ref.3) | copy-start | bytes 52
  33.5 23.3 %copy-start.12 = (s32[128]{0:T(128)S(1)}, s32[128]{0:T(128)}, u32[]{:S(2)}) copy-start(s32[128]{0:T(128)} %prot_ref.1) | copy-start | bytes 1540
  41.0 15.8 %copy-start.13 = (bf16[768,768]{1,0:T(8,128)(2,1)S(1)}, bf16[768,768]{1,0:T(8,128)(2,1)}, u32[]{:S(2)}) copy-start(bf16[768,768]{1,0:T(8,128)(2,1)} %wq_ref.3) | copy-start | bytes 3538948
  41.0 15.8 %copy-start.14 = (bf16[768,768]{1,0:T(8,128)(2,1)S(1)}, bf16[768,768]{1,0:T(8,128)(2,1)}, u32[]{:S(2)}) copy-start(bf16[768,768]{1,0:T(8,128)(2,1)} %wk_ref.3) | copy-start | bytes 3538948
  56.8 1.3 %copy-start.15 = (bf16[768,768]{1,0:T(8,128)(2,1)S(1)}, bf16[768,768]{1,0:T(8,128)(2,1)}, u32[]{:S(2)}) copy-start(bf16[768,768]{1,0:T(8,128)(2,1)} %wv_ref.1) | copy-start | bytes 3538948
  58.1 19.9 %copy-start.5 = (bf16[768,768]{1,0:T(8,128)(2,1)S(1)}, bf16[768,768]{1,0:T(8,128)(2,1)}, u32[]{:S(2)}) copy-start(bf16[768,768]{1,0:T(8,128)(2,1)} %w_ref.5) | copy-start | bytes 3538948

commit v3 on v2

--- a/solution.py
+++ b/solution.py
@@ -13,10 +13,12 @@
 NEG = -1000000000.0
 F32 = jnp.float32
 BF16 = jnp.bfloat16
-LIMIT = 48 << 20
-
-
-def call(kernel, out_shape, ins, outs, scratch, cost, name):
+LIMIT = 20 << 20
+LARGE = 56 << 20
+PLANE = 4
+
+
+def call(kernel, out_shape, ins, outs, scratch, cost, name, limit=LIMIT):
     spaces = {"v": pltpu.VMEM, "s": pltpu.SMEM, "a": pl.ANY}
     return pl.pallas_call(
         kernel,
@@ -24,7 +26,7 @@
         in_specs=[pl.BlockSpec(memory_space=spaces[c]) for c in ins],
         out_specs=[pl.BlockSpec(memory_space=spaces[c]) for c in outs],
         scratch_shapes=scratch,
-        compiler_params=pltpu.CompilerParams(vmem_limit_bytes=LIMIT),
+        compiler_params=pltpu.CompilerParams(vmem_limit_bytes=limit),
         cost_estimate=pl.CostEstimate(flops=cost[0], bytes_accessed=cost[1], transcendentals=cost[2]),
         name=name,
     )
@@ -59,14 +61,42 @@
 
 
 def row_scores_kernel(
-    depth_ref, place_ref, x_ref, gain_ref, prot_ref, wq_ref, wk_ref, part_ref, normed_ref, same_ref
+    depth_hbm,
+    place_ref,
+    x_hbm,
+    gain_hbm,
+    prot_hbm,
+    wq_hbm,
+    wk_hbm,
+    keep_ref,
+    send_ref,
+    normed_ref,
+    same_ref,
+    depth_ref,
+    x_ref,
+    gain_ref,
+    prot_ref,
+    wq_ref,
+    wk_ref,
+    sems,
 ):
-    columns = prot_ref.shape[1]
+    columns = prot_ref.shape[0]
     tokens, width = x_ref.shape
     rows = tokens // columns
-    normed = norm(x_ref[...].astype(F32), gain_ref[...]).astype(BF16)
+    pairs = [(x_hbm, x_ref), (gain_hbm, gain_ref), (prot_hbm, prot_ref), (depth_hbm, depth_ref)]
+    for n in range(width // 256):
+        for source, target in ((wq_hbm, wq_ref), (wk_hbm, wk_ref)):
+            pairs.append((source.at[:, 256 * n : 256 * n + 256], target.at[:, 256 * n : 256 * n + 256]))
+    copies = [pltpu.make_async_copy(a, b, sems.at[i]) for i, (a, b) in enumerate(pairs)]
+    for copy in copies:
+        copy.start()
+    for copy in copies[:2]:
+        copy.wait()
+    normed = norm(x_ref[...].astype(F32), gain_ref[...].reshape(1, width)).astype(BF16)
     normed_ref[...] = normed
-    prot = prot_ref[...].astype(F32)
+    for copy in copies[2:4]:
+        copy.wait()
+    prot = prot_ref[...].reshape(1, columns).astype(F32)
     depth = jnp.zeros((1, columns), F32)
     for p in range(depth_ref.shape[0]):
         depth = jnp.where(prot == float(p), depth_ref[p].astype(F32), depth)
@@ -82,9 +112,13 @@
     ]
     valid = jnp.concatenate(valid, axis=0)
     even, odd = half_masks(256)
+    quarter = columns // PLANE
+    core = (place_ref[0] % 2) == 0
     for n in range(width // 256):
         cols = slice(256 * n, 256 * n + 256)
+        copies[4 + 2 * n].wait()
         query = dot(normed, wq_ref[:, cols]).astype(BF16).astype(F32) * valid
+        copies[5 + 2 * n].wait()
         key = (dot(normed, wk_ref[:, cols]) * valid).astype(BF16)
         query_even, query_odd = (query * even).astype(BF16), (query * odd).astype(BF16)
         for q in range(2):
@@ -103,50 +137,84 @@
                 jnp.where(first, one, pltpu.roll(one, 64, 1)),
                 jnp.where(first, pltpu.roll(two, 64, 1), two),
             )
-            part_ref[:, 256 * n + 128 * q : 256 * n + 128 * q + 128] = folded
+            out = slice(256 * n + 128 * q, 256 * n + 128 * q + 128)
+            for y in range(PLANE // 2):
+                start = 2 * y * quarter
+                left, right = folded[start : start + quarter], folded[start + quarter : start + 2 * quarter]
+                keep_ref[y, :, out] = jnp.where(core, left, right)
+                send_ref[y, :, out] = jnp.where(core, right, left)
+
+
+def core_sum_kernel(place_ref, mine_ref, other_ref, keep_ref, send_ref):
+    row = (place_ref[0] // 2) % 2
+    keep_ref[...] = mine_ref[row] + other_ref[row]
+    send_ref[...] = mine_ref[1 - row] + other_ref[1 - row]
+
+
+def add_kernel(*refs):
+    total = refs[0][...] + refs[1][...]
+    if len(refs) == 5:
+        total = total + (refs[2][...] + refs[3][...])
+    refs[-1][...] = total
 
 
 def project_kernel(x_ref, w_ref, out_ref):
     out_ref[...] = dot(x_ref[...], w_ref[...]).astype(BF16)
 
 
-def row_softmax_kernel(scale, place_ref, blocks_ref, same_ref, out_ref, mask_ref):
-    devices, tile, width = blocks_ref.shape
+def row_softmax_kernel(scale, place_ref, *refs):
+    part_refs, (same_ref, out_ref, mask_ref) = refs[:-3], refs[-3:]
+    tile, width = out_ref.shape
     same = same_ref[...]
     mask_ref[...] = jnp.maximum(same, pltpu.roll(same, 64, 1))
-    live = mask_ref[pl.ds(place_ref[0] * tile, tile), :] > 0.5
+    live = mask_ref[pl.ds((place_ref[0] % PLANE) * tile, tile), :] > 0.5
     low = iota((tile, 128), 1) < 64
-    total = blocks_ref[0]
-    for d in range(1, devices):
-        total = total + blocks_ref[d]
-    pieces = []
     for p in range(width // 128):
-        tied = jnp.where(live, total[:, 128 * p : 128 * p + 128] * scale, NEG)
+        lanes = slice(128 * p, 128 * p + 128)
+        parts = [part[:, lanes] for part in part_refs]
+        while len(parts) > 1:
+            parts = [a + b for a, b in zip(parts[::2], parts[1::2])]
+        tied = jnp.where(live, parts[0] * scale, NEG)
         top_low = jnp.max(jnp.where(low, tied, 2 * NEG), axis=1, keepdims=True)
         top_high = jnp.max(jnp.where(low, 2 * NEG, tied), axis=1, keepdims=True)
         value = jnp.exp(tied - jnp.where(low, top_low, top_high))
         sum_low = jnp.sum(jnp.where(low, value, 0.0), axis=1, keepdims=True)
         sum_high = jnp.sum(jnp.where(low, 0.0, value), axis=1, keepdims=True)
-        pieces.append(value / jnp.where(low, sum_low, sum_high))
-    out_ref[...] = jnp.broadcast_to(
-        jnp.concatenate(pieces, axis=1).astype(BF16)[None], (devices, tile, width)
-    )
+        out_ref[:, lanes] = (value / jnp.where(low, sum_low, sum_high)).astype(BF16)
 
 
 def row_output_kernel(
-    folded_ref, same_ref, value_ref, x_ref, w_ref, gain_ref, after_ref, normed_ref, mixed_ref
+    place_ref,
+    piece0_ref,
+    piece1_ref,
+    piece2_ref,
+    piece3_ref,
+    same_ref,
+    value_ref,
+    x_ref,
+    w_ref,
+    gain_ref,
+    after_ref,
+    normed_ref,
+    mixed_ref,
+    folded_ref,
 ):
     columns = same_ref.shape[0]
     tokens, width = x_ref.shape
     rows = tokens // columns
-    folded = folded_ref[...].reshape(columns, width).astype(F32)
+    mine = place_ref[0] % PLANE
+    quarter = columns // PLANE
+    spot = [mine, mine + 1 - 2 * (mine % 2), (mine + 2) % 4]
+    spot.append(spot[1] + spot[2] - mine)
+    for where, piece in zip(spot, (piece0_ref, piece1_ref, piece2_ref, piece3_ref)):
+        folded_ref[pl.ds(pl.multiple_of(where * quarter, quarter), quarter), :] = piece[...].astype(F32)
     same = same_ref[...] > 0.5
     low = iota((columns, columns), 1) < 64
     even, odd = half_masks(128 * rows)
     even, odd = even.astype(BF16), odd.astype(BF16)
     for p in range(width // 128):
         lanes = slice(128 * p, 128 * p + 128)
-        piece = folded[:, lanes]
+        piece = folded_ref[:, lanes]
         turned = pltpu.roll(piece, 64, 1)
         one = jnp.where(same, jnp.where(low, piece, turned), 0.0)
         two = jnp.where(same, jnp.where(low, turned, piece), 0.0)
@@ -218,6 +286,11 @@
         out_ref[...] = total.astype(BF16).reshape(rows, columns, width)
 
 
+def swap(array, offset):
+    devices = lax.axis_size("seq")
+    return lax.ppermute(array, "seq", [(i, i ^ offset) for i in range(devices)])
+
+
 def exchange(array):
     return lax.all_to_all(array, "seq", split_axis=0, concat_axis=0, tiled=True)
 
@@ -249,39 +322,63 @@
     shape = jax.ShapeDtypeStruct
     square = 2 * tokens * width * width
 
-    partial, normed, same = call(
+    quarter = columns // PLANE
+    half = shape((PLANE // 2, quarter, width), F32)
+    part = shape((quarter, width), F32)
+    keep, send, normed, same = call(
         row_scores_kernel,
-        (shape((columns, width), F32), shape((tokens, width), BF16), shape((columns, columns), F32)),
-        "ssvvvvv",
-        "vvv",
-        [],
+        (half, half, shape((tokens, width), BF16), shape((columns, columns), F32)),
+        "asaaaaa",
+        "vvvv",
+        [
+            pltpu.SMEM(row_depth.shape, jnp.int32),
+            pltpu.VMEM((tokens, width), BF16),
+            pltpu.VMEM((width,), F32),
+            pltpu.VMEM((columns,), jnp.int32),
+            pltpu.VMEM((width, width), BF16),
+            pltpu.VMEM((width, width), BF16),
+            pltpu.SemaphoreType.DMA((4 + 2 * (width // 256),)),
+        ],
         (2 * square, 4 * width * width, tokens),
         "row_scores",
-    )(row_depth, place, x, row_gain[None], protein_id[None], row_query, row_key)
-    blocks = exchange(partial.reshape(devices, tile, width))
+        LARGE,
+    )(row_depth, place, x, row_gain, protein_id, row_query, row_key)
     (value,) = call(
         project_kernel, (shape((tokens, width), BF16),), "vv", "v", [], (square, 2 * width * width, 0), "row_value"
     )(normed, row_value)
+    keep, send = call(
+        core_sum_kernel, (part, part), "svv", "vv", [], (columns * width, 6 * columns * width, 0), "core_sum"
+    )(place, keep, swap(send, 1))
+    parts = [keep, swap(send, 2)]
+    stride, planes = PLANE, devices // PLANE
+    while planes > 1:
+        ways = 4 if planes % 4 == 0 else 2
+        (total,) = call(
+            add_kernel, (part,), "v" * len(parts), "v", [], (columns * width, 6 * columns * width, 0), "add"
+        )(*parts)
+        parts = [total] + [swap(total, stride * w) for w in range(1, ways)]
+        stride, planes = stride * ways, planes // ways
     (weights,) = call(
         functools.partial(row_softmax_kernel, 1.0 / (math.sqrt(head_size) * math.sqrt(total_rows))),
-        (shape((devices, tile, width), BF16),),
-        "svv",
+        (shape((quarter, width), BF16),),
+        "s" + "v" * len(parts) + "v",
         "v",
         [pltpu.VMEM((columns, columns), F32)],
-        (columns * width, 6 * columns * width, tile * width),
+        (columns * width, 6 * columns * width, quarter * width),
         "row_softmax",
-    )(place, blocks, same)
-    folded = exchange(weights)
+    )(place, *parts, same)
+    across = swap(weights, 2)
+    pieces = (weights, swap(weights, 1), across, swap(across, 1))
     normed_shape = (devices, rows, tile, width) if blocked else (tokens, width)
     after, normed = call(
         row_output_kernel,
         (shape((tokens, width), BF16), shape(normed_shape, BF16)),
-        "vvvvvv",
+        "s" + "v" * 9,
         "vv",
-        [pltpu.VMEM((tokens, width), BF16)],
+        [pltpu.VMEM((tokens, width), BF16), pltpu.VMEM((columns, width), F32)],
         (square, 2 * width * width, tokens),
         "row_output",
-    )(folded, same, value, x, row_output, column_gain[None])
+    )(place, *pieces, same, value, x, row_output, column_gain[None])
     if not blocked:
         normed = normed.reshape(rows, devices, tile, width).transpose(1, 0, 2, 3)
     moved = exchange(normed).reshape(tokens, width)

time: 79.8 us -> 72.4 us (0.907)
  blocking collectives: 49.8 us -> 32.5 us
  waiting for transfers between devices: 7.44 us -> 14.1 us
  starting transfers between devices: 3.66 us -> 9.59 us
  local copies, waits for them, and re-layouts: 7.84 us -> 2.81 us
  Pallas kernels: 10.3 us -> 13 us
    all_to_all x3 -> x2, blocking collectives: 49.8 us -> 32.5 us  [exchange(): return lax.all_to_all(array, 'seq', split_axis=0, concat_axis=0, tiled=True)]
    ppermute x0 -> x8, waiting for transfers between devices: none -> 14.1 us  [swap(): return lax.ppermute(array, 'seq', [(i, i ^ offset) for i in range(devices)])]
    ppermute x0 -> x8, starting transfers between devices: none -> 9.59 us  [swap(): return lax.ppermute(array, 'seq', [(i, i ^ offset) for i in range(devices)])]
    all_to_all x1 -> x0, waiting for transfers between devices: 7.44 us -> none  [exchange(): return lax.all_to_all(array, 'seq', split_axis=0, concat_axis=0, tiled=True)]
    unnamed x34 -> x26, local copies, waits for them, and re-layouts: 7.15 us -> 2.81 us
    all_to_all x1 -> x0, starting transfers between devices: 3.66 us -> none  [exchange(): return lax.all_to_all(array, 'seq', split_axis=0, concat_axis=0, tiled=True)]
    pallas_call x1 -> x3, Pallas kernels: 2.26 us -> 5.51 us  [the longest x1 5.47 us: per_device(): call(row_scores_kernel, (half, half, shape((tokens, width), BF16), shape(...]
  transfers between devices with their start and end apart: 1 -> 8, of which waited for: 1 -> 5; matrix products, arithmetic and copies ran while one was open for 0% -> 0% of each run, Pallas kernels for 1% -> 1%
where the time goes in v3:
time: 72.4 us; the launch traced here: 72.1 us
  blocking collectives  32.5 us (45%)
  waiting for transfers between devices  14.1 us (19%)
  Pallas kernels  13 us (18%)
  starting transfers between devices  9.59 us (13%)
  local copies, waits for them, and re-layouts  2.81 us (4%)
    all_to_all x2, blocking collectives, exchange(): return lax.all_to_all(array, 'seq', split_axis=0, concat_axis=0, tiled=True)  32.5 us
    ppermute x8, waiting for transfers between devices, swap(): return lax.ppermute(array, 'seq', [(i, i ^ offset) for i in range(devices)])  14.1 us
    ppermute x8, starting transfers between devices, swap(): return lax.ppermute(array, 'seq', [(i, i ^ offset) for i in range(devices)])  9.59 us
    pallas_call x1, Pallas kernels, per_device(): call(row_scores_kernel, (half, half, shape((tokens, width), BF16), shape(...  5.47 us
    pallas_call x1, Pallas kernels, per_device(): call(functools.partial(column_kernel, 1.0 / math.sqrt(head_size), tile),...  4.46 us
    unnamed x26, local copies, waits for them, and re-layouts  2.81 us
  transfers between devices with their start and end apart: 8, of which 5 were waited for; matrix products, arithmetic and copies ran while one was open for 0% of the time, Pallas kernels for 1%

profile of v3, /device:TPU:0, one launch (start us, length us, event | category | flops | bytes accessed | tf_op | source)
XLA Modules:
  0.0 72.1 jit_solution(15864090372065473285)
XLA Ops:
  0.0 0.0 copy-start.12
  0.0 0.0 copy-start.11
  0.0 5.5 %row_scores.1 = (f32[2,32,768]{2,1,0:T(8,128)}, f32[2,32,768]{2,1,0:T(8,128)}, bf16[256,768]{1,0:T(8,128)(2,1)}, f32[128,128]{1,0:T(8,128)}) custom-call(s32[4]{0:T(128)} %depth_ref.1, s32[1]{0:T(128)} %bitcast.place_ref, bf16[256,768]{1,0:T(8,128)(2,1)} %bitcast.4, f32[768]{0:T(1024)} %gain_hbm.1, s32[128]{0:T(128)} %prot_ref.1, bf16[768,768]{1,0:T(8,128)(2,1)} %wq_hbm.1, ...), custom_call_target="tpu_custom_call" | custom-call | flops 603979776 | bytes 2359296 | tf_op jit(solution)/shard_map/row_scores/pallas_call | solution.py:328
  5.5 0.0 copy-start.2
  5.5 0.5 collective-permute-start
  6.0 1.3 %collective-permute-done.other_ref = f32[2,32,768]{2,1,0:T(8,128)S(1)} collective-permute-done((f32[2,32,768]{2,1,0:T(8,128)}, f32[2,32,768]{2,1,0:T(8,128)S(1)}, u32[]{:S(2)}, u32[]{:S(2)}) %collective-permute-start) | collective-permute-done | bytes 196640 | tf_op jit(solution)/shard_map/ppermute | solution.py:291
  7.3 0.0 copy-start.6
  7.3 0.9 %copy-done.6 = f32[2,32,768]{2,1,0:T(8,128)S(1)} copy-done((f32[2,32,768]{2,1,0:T(8,128)S(1)}, f32[2,32,768]{2,1,0:T(8,128)}, u32[]{:S(2)}) %copy-start.6) | copy-done | bytes 196632
  8.3 2.9 %collective-permute-start.1 = (f32[32,768]{1,0:T(8,128)S(1)}, f32[32,768]{1,0:T(8,128)S(1)}, u32[]{:S(2)}, u32[]{:S(2)}) collective-permute-start(f32[32,768]{1,0:T(8,128)S(1)} %get-tuple-element.16), channel_id=1, source_target_pairs={{0,2},{1,3},{2,0},{3,1},{4,6},{5,7},{6,4},{7,5},{8,10},{9,11},{10,... | collective-permute-start | bytes 294920 | tf_op jit(solution)/shard_map/ppermute | solution.py:291
  11.2 3.1 %collective-permute-done.1.refs_1_ = f32[32,768]{1,0:T(8,128)S(1)} collective-permute-done((f32[32,768]{1,0:T(8,128)S(1)}, f32[32,768]{1,0:T(8,128)S(1)}, u32[]{:S(2)}, u32[]{:S(2)}) %collective-permute-start.1) | collective-permute-done | bytes 98336 | tf_op jit(solution)/shard_map/ppermute | solution.py:291
  14.3 3.9 %collective-permute-start.4 = (f32[32,768]{1,0:T(8,128)S(1)}, f32[32,768]{1,0:T(8,128)S(1)}, u32[]{:S(2)}, u32[]{:S(2)}) collective-permute-start(f32[32,768]{1,0:T(8,128)S(1)} %add.1.refs_0_), channel_id=1, source_target_pairs={{0,12},{1,13},{2,14},{3,15},{4,8},{5,9},{6,10},{7,11},{8,4},{9,5},... | collective-permute-start | bytes 294920 | tf_op jit(solution)/shard_map/ppermute | solution.py:291
  18.2 0.0 collective-permute-start.3
  18.2 0.6 collective-permute-start.2
  18.8 3.1 %collective-permute-done.4.refs_3_ = f32[32,768]{1,0:T(8,128)S(1)} collective-permute-done((f32[32,768]{1,0:T(8,128)S(1)}, f32[32,768]{1,0:T(8,128)S(1)}, u32[]{:S(2)}, u32[]{:S(2)}) %collective-permute-start.4) | collective-permute-done | bytes 98336 | tf_op jit(solution)/shard_map/ppermute | solution.py:291
  21.9 4.0 %collective-permute-done.3.refs_2_ = f32[32,768]{1,0:T(8,128)S(1)} collective-permute-done((f32[32,768]{1,0:T(8,128)S(1)}, f32[32,768]{1,0:T(8,128)S(1)}, u32[]{:S(2)}, u32[]{:S(2)}) %collective-permute-start.3) | collective-permute-done | bytes 98336 | tf_op jit(solution)/shard_map/ppermute | solution.py:291
  25.9 0.0 collective-permute-done.2.refs_1_
  25.9 0.0 copy-start.5
  26.0 0.8 %copy-done.5 = f32[128,128]{1,0:T(8,128)S(1)} copy-done((f32[128,128]{1,0:T(8,128)S(1)}, f32[128,128]{1,0:T(8,128)}, u32[]{:S(2)}) %copy-start.5) | copy-done | bytes 65560
  26.8 0.3 row_softmax.1.piece0_ref
  27.1 1.6 %collective-permute-start.6 = (bf16[32,768]{1,0:T(8,128)(2,1)S(1)}, bf16[32,768]{1,0:T(8,128)(2,1)S(1)}, u32[]{:S(2)}, u32[]{:S(2)}) collective-permute-start(bf16[32,768]{1,0:T(8,128)(2,1)S(1)} %row_softmax.1.piece0_ref), channel_id=1, source_target_pairs={{0,2},{1,3},{2,0},{3,1},{4,6},{5,7},{6,4},{7,5},{8,10},{9,11},{10,... | collective-permute-start | bytes 147464 | tf_op jit(solution)/shard_map/ppermute | solution.py:291
  28.7 0.0 collective-permute-start.5
  28.7 2.6 %collective-permute-done.6.piece2_ref = bf16[32,768]{1,0:T(8,128)(2,1)S(1)} collective-permute-done((bf16[32,768]{1,0:T(8,128)(2,1)S(1)}, bf16[32,768]{1,0:T(8,128)(2,1)S(1)}, u32[]{:S(2)}, u32[]{:S(2)}) %collective-permute-start.6) | collective-permute-done | bytes 49184 | tf_op jit(solution)/shard_map/ppermute | solution.py:291
  31.3 0.0 collective-permute-start.7
  31.3 0.0 copy-done.12
  31.3 0.0 copy-done.2
  31.3 0.0 copy-start.4
  31.3 1.0 %copy-done.4 = bf16[256,768]{1,0:T(8,128)(2,1)S(1)} copy-done((bf16[256,768]{1,0:T(8,128)(2,1)S(1)}, bf16[256,768]{1,0:T(8,128)(2,1)}, u32[]{:S(2)}) %copy-start.4) | copy-done | bytes 393240
  32.3 0.5 row_value.1.value_ref
  32.8 0.0 copy-start.7
  32.8 0.0 copy-start.8
  32.8 0.0 copy-start.9
  32.8 0.0 copy-start.10
  32.8 0.0 collective-permute-done.5.piece1_ref
  32.8 0.0 collective-permute-done.7.piece3_ref
  32.9 0.0 copy-done
  32.9 0.0 copy-done.3
  32.9 1.0 %row_output.1 = (bf16[256,768]{1,0:T(8,128)(2,1)S(1)}, bf16[16,2,8,768]{3,2,1,0:T(8,128)(2,1)S(1)}) custom-call(s32[1]{0:T(128)} %bitcast.place_ref, bf16[32,768]{1,0:T(8,128)(2,1)S(1)} %row_softmax.1.piece0_ref, bf16[32,768]{1,0:T(8,128)(2,1)S(1)} %collective-permute-done.5.piece1_ref, bf16[32,768]{1,0:T(8,128)(2,1)S(1)} %collective-permute-done.6.piece2_ref, ...), custom_call_target="tpu_custom_call" | custom-call | flops 301989888 | bytes 1179648 | tf_op jit(solution)/shard_map/row_output/pallas_call | solution.py:373
  33.9 17.0 %all_to_all.10 = bf16[16,2,8,768]{3,2,1,0:T(8,128)(2,1)S(1)} all-to-all(bf16[16,2,8,768]{3,2,1,0:T(8,128)(2,1)S(1)} %get-tuple-element.19), channel_id=1, replica_groups=mesh['grp'=2,'seq'=16] {'seq'}, dimensions={0} | all-to-all | bytes 786432 | tf_op jit(solution)/shard_map/all_to_all | solution.py:295
  50.9 0.0 copy-done.11
  50.9 0.0 copy-done.7
  50.9 0.0 copy-done.8
  50.9 0.0 copy-done.9
  50.9 0.0 copy-done.10
  50.9 0.0 copy-start.1
  50.9 4.5 %column_attention.1 = bf16[256,768]{1,0:T(8,128)(2,1)S(1)} custom-call(s32[4]{0:T(128)S(1)} %copy-done.7, s32[128]{0:T(128)S(1)} %copy-done.8, s32[1]{0:T(128)} %bitcast.place_ref, bf16[256,768]{1,0:T(8,128)(2,1)S(1)} %bitcast.6, bf16[768,768]{1,0:T(8,128)(2,1)S(1)} %copy-done.9, bf16[768,768]{1,0:T(8,128)(2,1)S(1)} %copy-done.10, ...), custom_call_target="tpu_custom_call" | custom-call | flops 1207959552 | bytes 3538944 | tf_op jit(solution)/shard_map/column_attention/pallas_call | solution.py:385
  55.4 15.5 %all_to_all.11.x_ref = bf16[16,2,8,768]{3,2,1,0:T(8,128)(2,1)S(1)} all-to-all(bf16[16,2,8,768]{3,2,1,0:T(8,128)(2,1)S(1)} %bitcast.7), channel_id=1, replica_groups=mesh['grp'=2,'seq'=16] {'seq'}, dimensions={0} | all-to-all | bytes 786432 | tf_op jit(solution)/shard_map/all_to_all | solution.py:295
  70.9 0.0 copy-done.1
  70.9 1.2 %column_output.1 = bf16[2,128,768]{2,1,0:T(8,128)(2,1)} custom-call(bf16[16,2,8,768]{3,2,1,0:T(8,128)(2,1)S(1)} %all_to_all.11.x_ref, bf16[768,768]{1,0:T(8,128)(2,1)S(1)} %copy-done.1, bf16[256,768]{1,0:T(8,128)(2,1)S(1)} %get-tuple-element.20.after_ref), custom_call_target="tpu_custom_call" | custom-call | flops 301989888 | bytes 1179648 | tf_op jit(solution)/shard_map/column_output/pallas_call | solution.py:397
  (5 shorter events, 0.0 us)
Async XLA Ops:
  0.0 31.3 %copy-start.12 = (f32[768]{0:T(1024)S(1)}, f32[768]{0:T(1024)}, u32[]{:S(2)}) copy-start(f32[768]{0:T(1024)} %param.21) | copy-start | bytes 9220
  0.0 50.9 %copy-start.11 = (bf16[768,768]{1,0:T(8,128)(2,1)S(1)}, bf16[768,768]{1,0:T(8,128)(2,1)}, u32[]{:S(2)}) copy-start(bf16[768,768]{1,0:T(8,128)(2,1)} %wv_ref.1) | copy-start | bytes 3538948
  5.5 25.8 %copy-start.2 = (bf16[768,768]{1,0:T(8,128)(2,1)S(1)}, bf16[768,768]{1,0:T(8,128)(2,1)}, u32[]{:S(2)}) copy-start(bf16[768,768]{1,0:T(8,128)(2,1)} %w_ref.3) | copy-start | bytes 3538948
  5.5 1.8 %collective-permute-start = (f32[2,32,768]{2,1,0:T(8,128)}, f32[2,32,768]{2,1,0:T(8,128)S(1)}, u32[]{:S(2)}, u32[]{:S(2)}) collective-permute-start(f32[2,32,768]{2,1,0:T(8,128)} %get-tuple-element.14), channel_id=1, source_target_pairs={{0,1},{1,0},{2,3},{3,2},{4,5},{5,4},{6,7},{7,6},{8,9},{9,8},{10,11... | collective-permute-start | bytes 589832 | tf_op jit(solution)/shard_map/ppermute | solution.py:291
  7.3 0.9 %copy-start.6 = (f32[2,32,768]{2,1,0:T(8,128)S(1)}, f32[2,32,768]{2,1,0:T(8,128)}, u32[]{:S(2)}) copy-start(f32[2,32,768]{2,1,0:T(8,128)} %get-tuple-element.13.mine_ref) | copy-start | bytes 589828
  8.3 6.0 %collective-permute-start.1 = (f32[32,768]{1,0:T(8,128)S(1)}, f32[32,768]{1,0:T(8,128)S(1)}, u32[]{:S(2)}, u32[]{:S(2)}) collective-permute-start(f32[32,768]{1,0:T(8,128)S(1)} %get-tuple-element.16), channel_id=1, source_target_pairs={{0,2},{1,3},{2,0},{3,1},{4,6},{5,7},{6,4},{7,5},{8,10},{9,11},{10,... | collective-permute-start | bytes 294920 | tf_op jit(solution)/shard_map/ppermute | solution.py:291
  14.3 7.6 %collective-permute-start.4 = (f32[32,768]{1,0:T(8,128)S(1)}, f32[32,768]{1,0:T(8,128)S(1)}, u32[]{:S(2)}, u32[]{:S(2)}) collective-permute-start(f32[32,768]{1,0:T(8,128)S(1)} %add.1.refs_0_), channel_id=1, source_target_pairs={{0,12},{1,13},{2,14},{3,15},{4,8},{5,9},{6,10},{7,11},{8,4},{9,5},... | collective-permute-start | bytes 294920 | tf_op jit(solution)/shard_map/ppermute | solution.py:291
  18.2 7.7 %collective-permute-start.3 = (f32[32,768]{1,0:T(8,128)S(1)}, f32[32,768]{1,0:T(8,128)S(1)}, u32[]{:S(2)}, u32[]{:S(2)}) collective-permute-start(f32[32,768]{1,0:T(8,128)S(1)} %add.1.refs_0_), channel_id=1, source_target_pairs={{0,8},{1,9},{2,10},{3,11},{4,12},{5,13},{6,14},{7,15},{8,0},{9,1},... | collective-permute-start | bytes 294920 | tf_op jit(solution)/shard_map/ppermute | solution.py:291
  18.2 7.7 %collective-permute-start.2 = (f32[32,768]{1,0:T(8,128)S(1)}, f32[32,768]{1,0:T(8,128)S(1)}, u32[]{:S(2)}, u32[]{:S(2)}) collective-permute-start(f32[32,768]{1,0:T(8,128)S(1)} %add.1.refs_0_), channel_id=1, source_target_pairs={{0,4},{1,5},{2,6},{3,7},{4,0},{5,1},{6,2},{7,3},{8,12},{9,13},{10,... | collective-permute-start | bytes 294920 | tf_op jit(solution)/shard_map/ppermute | solution.py:291
  25.9 0.8 %copy-start.5 = (f32[128,128]{1,0:T(8,128)S(1)}, f32[128,128]{1,0:T(8,128)}, u32[]{:S(2)}) copy-start(f32[128,128]{1,0:T(8,128)} %get-tuple-element.17.refs_4_.same_ref) | copy-start | bytes 196612
  26.8 6.1 %copy-start = (bf16[2,128,768]{2,1,0:T(8,128)(2,1)S(1)}, bf16[2,128,768]{2,1,0:T(8,128)(2,1)}, u32[]{:S(2)}) copy-start(bf16[2,128,768]{2,1,0:T(8,128)(2,1)} %param.13) | copy-start | bytes 1179652
  26.8 6.1 %copy-start.3 = (bf16[768,768]{1,0:T(8,128)(2,1)S(1)}, bf16[768,768]{1,0:T(8,128)(2,1)}, u32[]{:S(2)}) copy-start(bf16[768,768]{1,0:T(8,128)(2,1)} %w_ref.4) | copy-start | bytes 3538948
  27.1 4.2 %collective-permute-start.6 = (bf16[32,768]{1,0:T(8,128)(2,1)S(1)}, bf16[32,768]{1,0:T(8,128)(2,1)S(1)}, u32[]{:S(2)}, u32[]{:S(2)}) collective-permute-start(bf16[32,768]{1,0:T(8,128)(2,1)S(1)} %row_softmax.1.piece0_ref), channel_id=1, source_target_pairs={{0,2},{1,3},{2,0},{3,1},{4,6},{5,7},{6,4},{7,5},{8,10},{9,11},{10,... | collective-permute-start | bytes 147464 | tf_op jit(solution)/shard_map/ppermute | solution.py:291
  28.7 4.1 %collective-permute-start.5 = (bf16[32,768]{1,0:T(8,128)(2,1)S(1)}, bf16[32,768]{1,0:T(8,128)(2,1)S(1)}, u32[]{:S(2)}, u32[]{:S(2)}) collective-permute-start(bf16[32,768]{1,0:T(8,128)(2,1)S(1)} %row_softmax.1.piece0_ref), channel_id=1, source_target_pairs={{0,1},{1,0},{2,3},{3,2},{4,5},{5,4},{6,7},{7,6},{8,9},{9,8},{10,11... | collective-permute-start | bytes 147464 | tf_op jit(solution)/shard_map/ppermute | solution.py:291
  31.3 1.6 %collective-permute-start.7 = (bf16[32,768]{1,0:T(8,128)(2,1)S(1)}, bf16[32,768]{1,0:T(8,128)(2,1)S(1)}, u32[]{:S(2)}, u32[]{:S(2)}) collective-permute-start(bf16[32,768]{1,0:T(8,128)(2,1)S(1)} %collective-permute-done.6.piece2_ref), channel_id=1, source_target_pairs={{0,1},{1,0},{2,3},{3,2},{4,5},{5,4},{6,7},{7,6},{8,9},{9,8},{10,11... | collective-permute-start | bytes 147464 | tf_op jit(solution)/shard_map/ppermute | solution.py:291
  31.3 1.0 %copy-start.4 = (bf16[256,768]{1,0:T(8,128)(2,1)S(1)}, bf16[256,768]{1,0:T(8,128)(2,1)}, u32[]{:S(2)}) copy-start(bf16[256,768]{1,0:T(8,128)(2,1)} %get-tuple-element.18.x_ref) | copy-start | bytes 1179652
  32.8 18.1 %copy-start.7 = (s32[4]{0:T(128)S(1)}, s32[4]{0:T(128)}, u32[]{:S(2)}) copy-start(s32[4]{0:T(128)} %depth_ref.1) | copy-start | bytes 52
  32.8 18.1 %copy-start.8 = (s32[128]{0:T(128)S(1)}, s32[128]{0:T(128)}, u32[]{:S(2)}) copy-start(s32[128]{0:T(128)} %prot_ref.1) | copy-start | bytes 1540
  32.8 18.1 %copy-start.9 = (bf16[768,768]{1,0:T(8,128)(2,1)S(1)}, bf16[768,768]{1,0:T(8,128)(2,1)}, u32[]{:S(2)}) copy-start(bf16[768,768]{1,0:T(8,128)(2,1)} %wq_ref.1) | copy-start | bytes 3538948
  32.8 18.1 %copy-start.10 = (bf16[768,768]{1,0:T(8,128)(2,1)S(1)}, bf16[768,768]{1,0:T(8,128)(2,1)}, u32[]{:S(2)}) copy-start(bf16[768,768]{1,0:T(8,128)(2,1)} %wk_ref.1) | copy-start | bytes 3538948
  50.9 20.0 %copy-start.1 = (bf16[768,768]{1,0:T(8,128)(2,1)S(1)}, bf16[768,768]{1,0:T(8,128)(2,1)}, u32[]{:S(2)}) copy-start(bf16[768,768]{1,0:T(8,128)(2,1)} %w_ref.5) | copy-start | bytes 3538948

commit v4 on v3

--- a/solution.py
+++ b/solution.py
@@ -14,19 +14,18 @@
 F32 = jnp.float32
 BF16 = jnp.bfloat16
 LIMIT = 20 << 20
-LARGE = 56 << 20
 PLANE = 4
 
 
-def call(kernel, out_shape, ins, outs, scratch, cost, name, limit=LIMIT):
-    spaces = {"v": pltpu.VMEM, "s": pltpu.SMEM, "a": pl.ANY}
+def call(kernel, out_shape, ins, outs, scratch, cost, name):
+    spaces = {"v": pltpu.VMEM, "s": pltpu.SMEM, "h": pltpu.HBM}
     return pl.pallas_call(
         kernel,
         out_shape=out_shape,
         in_specs=[pl.BlockSpec(memory_space=spaces[c]) for c in ins],
         out_specs=[pl.BlockSpec(memory_space=spaces[c]) for c in outs],
         scratch_shapes=scratch,
-        compiler_params=pltpu.CompilerParams(vmem_limit_bytes=limit),
+        compiler_params=pltpu.CompilerParams(vmem_limit_bytes=LIMIT),
         cost_estimate=pl.CostEstimate(flops=cost[0], bytes_accessed=cost[1], transcendentals=cost[2]),
         name=name,
     )
@@ -86,7 +85,7 @@
     pairs = [(x_hbm, x_ref), (gain_hbm, gain_ref), (prot_hbm, prot_ref), (depth_hbm, depth_ref)]
     for n in range(width // 256):
         for source, target in ((wq_hbm, wq_ref), (wk_hbm, wk_ref)):
-            pairs.append((source.at[:, 256 * n : 256 * n + 256], target.at[:, 256 * n : 256 * n + 256]))
+            pairs.append((source.at[256 * n : 256 * n + 256], target.at[256 * n : 256 * n + 256]))
     copies = [pltpu.make_async_copy(a, b, sems.at[i]) for i, (a, b) in enumerate(pairs)]
     for copy in copies:
         copy.start()
@@ -114,11 +113,11 @@
     even, odd = half_masks(256)
     quarter = columns // PLANE
     core = (place_ref[0] % 2) == 0
+    for copy in copies[4:]:
+        copy.wait()
     for n in range(width // 256):
         cols = slice(256 * n, 256 * n + 256)
-        copies[4 + 2 * n].wait()
         query = dot(normed, wq_ref[:, cols]).astype(BF16).astype(F32) * valid
-        copies[5 + 2 * n].wait()
         key = (dot(normed, wk_ref[:, cols]) * valid).astype(BF16)
         query_even, query_odd = (query * even).astype(BF16), (query * odd).astype(BF16)
         for q in range(2):
@@ -239,35 +238,63 @@
                 normed_ref[d, r] = normed[start : start + tile].astype(BF16)
 
 
-def column_kernel(scale, tile, depth_ref, prot_ref, place_ref, x_ref, wq_ref, wk_ref, wv_ref, out_ref):
+def column_kernel(
+    scale, tile, depth_ref, prot_ref, place_ref, x_ref, wq_ref, wk_ref, wv_ref, out_ref, mixed_ref
+):
     tokens, width = x_ref.shape
+    rows = tokens // tile
+    chunk = max(128, rows)
+    groups = chunk // rows
     x = x_ref[...]
-    lane = iota((1, tokens), 1)
-    depth = jnp.zeros((1, tokens), jnp.int32)
-    for c in range(tile):
-        depth = jnp.where(lane % tile == c, depth_ref[prot_ref[place_ref[0] * tile + c]], depth)
-    live = (iota((tokens, tokens), 0) % tile == iota((tokens, tokens), 1) % tile) & (
-        iota((tokens, tokens), 1) // tile < depth
-    )
+    here, there = iota((tokens, tokens), 0), iota((tokens, tokens), 1)
+    if tile > 1:
+        sort = jnp.where(there == (here % rows) * tile + here // rows, 1.0, 0.0).astype(BF16)
+        x = dot(sort, x).astype(BF16)
+    same = jnp.where(iota((256, 256), 0) == iota((256, 256), 1), 1.0, 0.0).astype(BF16)
+    group = (iota((1, 2 * chunk), 1) % chunk) // rows
+    mine = [jnp.where(group == g, 1.0, 0.0).astype(BF16) for g in range(groups)]
+    lives = []
+    for start in range(0, tokens, chunk):
+        depth = jnp.zeros((1, 2 * chunk), jnp.int32)
+        for g in range(groups):
+            column = place_ref[0] * tile + start // rows + g
+            depth = jnp.where(group == g, depth_ref[prot_ref[column]], depth)
+        lives.append(iota((rows, 2 * chunk), 0) < depth)
     even, odd = half_masks(256)
+    even, odd = even * scale, odd * scale
+    packs, values = [], []
     for n in range(width // 256):
         cols = slice(256 * n, 256 * n + 256)
         query = dot(x, wq_ref[:, cols]).astype(BF16).astype(F32)
         key = dot(x, wk_ref[:, cols]).astype(BF16)
-        value = dot(x, wv_ref[:, cols])
-        query_sides = [(query * side).astype(BF16) for side in (even, odd)]
-        value_sides = [(value * side).astype(BF16) for side in (even, odd)]
+        sides = [(query * side).astype(BF16) for side in (even, odd)]
         for q in range(2):
             lanes = slice(128 * q, 128 * q + 128)
-            mixed = jnp.zeros((tokens, 128), F32)
-            for s in range(2):
-                scores = dot_t(query_sides[s][:, lanes], key[:, lanes]) * scale
-                scores = jnp.where(live, scores, NEG)
-                top = jnp.max(scores, axis=1, keepdims=True)
-                weight = jnp.exp(scores - top)
-                weight = weight / jnp.sum(weight, axis=1, keepdims=True)
-                mixed = mixed + dot(weight.astype(BF16), value_sides[s][:, lanes])
-            out_ref[:, 256 * n + 128 * q : 256 * n + 128 * q + 128] = mixed.astype(BF16)
+            for j, live in enumerate(lives):
+                part = slice(j * chunk, j * chunk + chunk)
+                both = jnp.concatenate([side[part, lanes] for side in sides], axis=0)
+                scores = dot_t(key[part, lanes], both)
+                packed = scores[:rows]
+                for g in range(1, groups):
+                    packed = jnp.where(group == g, scores[g * rows : (g + 1) * rows], packed)
+                packs.append(jnp.where(live, packed, NEG))
+        values.append(dot_t(same, dot(x, wv_ref[:, cols]).astype(BF16)).astype(BF16))
+    packs = [jnp.exp(packed - jnp.max(packed, axis=0, keepdims=True)) for packed in packs]
+    packs = [
+        (packed * (1.0 / jnp.sum(packed, axis=0, keepdims=True))).astype(BF16) for packed in packs
+    ]
+    for n, value in enumerate(values):
+        for q in range(2):
+            for j in range(len(lives)):
+                part = slice(j * chunk, j * chunk + chunk)
+                weight = packs[(2 * n + q) * len(lives) + j]
+                spread = jnp.concatenate([weight * m for m in mine], axis=0)
+                for s in range(2):
+                    first = 128 * q + 64 * s
+                    mixed = dot(value[first : first + 64, part], spread[:, s * chunk : (s + 1) * chunk])
+                    mixed_ref[256 * n + first : 256 * n + first + 64, part] = mixed.astype(BF16)
+    back = jnp.where(there == (here % tile) * rows + here // tile, 1.0, 0.0).astype(BF16)
+    out_ref[...] = dot_t(back, mixed_ref[...]).astype(BF16)
 
 
 def column_output_kernel(x_ref, w_ref, after_ref, out_ref, total_ref):
@@ -284,6 +311,10 @@
                 total_ref[start : start + tile] = total[block : block + tile]
         total = total_ref[...] + after_ref[...].astype(F32)
         out_ref[...] = total.astype(BF16).reshape(rows, columns, width)
+
+
+def hbm(array):
+    return pltpu.with_memory_space_constraint(array, pltpu.HBM)
 
 
 def swap(array, offset):
@@ -328,7 +359,7 @@
     keep, send, normed, same = call(
         row_scores_kernel,
         (half, half, shape((tokens, width), BF16), shape((columns, columns), F32)),
-        "asaaaaa",
+        "hshhhhh",
         "vvvv",
         [
             pltpu.SMEM(row_depth.shape, jnp.int32),
@@ -341,8 +372,8 @@
         ],
         (2 * square, 4 * width * width, tokens),
         "row_scores",
-        LARGE,
-    )(row_depth, place, x, row_gain, protein_id, row_query, row_key)
+    )(hbm(row_depth), place, hbm(x), hbm(row_gain), hbm(protein_id), hbm(row_query), hbm(row_key))
+    column_value, normed = lax.optimization_barrier((column_value, normed))
     (value,) = call(
         project_kernel, (shape((tokens, width), BF16),), "vv", "v", [], (square, 2 * width * width, 0), "row_value"
     )(normed, row_value)
@@ -387,7 +418,7 @@
         (shape((tokens, width), BF16),),
         "sssvvvv",
         "v",
-        [],
+        [pltpu.VMEM((width, tokens), BF16)],
         (4 * square, 6 * width * width, H * tokens * tokens),
         "column_attention",
     )(row_depth, protein_id, place, moved, column_query, column_key, column_value)

time: 72.4 us -> 67 us (0.925)
  Pallas kernels: 13 us -> 10.1 us
  local copies, waits for them, and re-layouts: 2.81 us -> 0.06 us
    unnamed x26 -> x20, local copies, waits for them, and re-layouts: 2.81 us -> 0.06 us
    pallas_call x1, Pallas kernels: 5.47 us -> 3.39 us  [per_device(): call(row_scores_kernel, (half, half, shape((tokens, width), BF16), shape(...]
    pallas_call x1, Pallas kernels: 4.46 us -> 3.65 us  [per_device(): call(functools.partial(column_kernel, 1.0 / math.sqrt(head_size), tile),...]
  transfers between devices with their start and end apart: 8 -> 8, of which waited for: 5 -> 6; matrix products, arithmetic and copies ran while one was open for 0% -> 0% of each run, Pallas kernels for 1% -> 1%
where the time goes in v4:
time: 67 us; the launch traced here: 66.8 us
  blocking collectives  32.4 us (48%)
  waiting for transfers between devices  14.5 us (22%)
  Pallas kernels  10.1 us (15%)
  starting transfers between devices  9.58 us (14%)
    all_to_all x2, blocking collectives, exchange(): return lax.all_to_all(array, 'seq', split_axis=0, concat_axis=0, tiled=True)  32.4 us
    ppermute x8, waiting for transfers between devices, swap(): return lax.ppermute(array, 'seq', [(i, i ^ offset) for i in range(devices)])  14.5 us
    ppermute x8, starting transfers between devices, swap(): return lax.ppermute(array, 'seq', [(i, i ^ offset) for i in range(devices)])  9.58 us
    pallas_call x1, Pallas kernels, per_device(): call(functools.partial(column_kernel, 1.0 / math.sqrt(head_size), tile),...  3.65 us
    pallas_call x1, Pallas kernels, per_device(): call(row_scores_kernel, (half, half, shape((tokens, width), BF16), shape(...  3.39 us
  transfers between devices with their start and end apart: 8, of which 6 were waited for; matrix products, arithmetic and copies ran while one was open for 0% of the time, Pallas kernels for 1%

profile of v4, /device:TPU:0, one launch (start us, length us, event | category | flops | bytes accessed | tf_op | source)
XLA Modules:
  0.0 66.8 jit_solution(2707993946543353816)
XLA Ops:
  0.0 0.0 copy-start.8
  0.0 3.4 %row_scores.1 = (f32[2,32,768]{2,1,0:T(8,128)S(1)}, f32[2,32,768]{2,1,0:T(8,128)S(1)}, bf16[256,768]{1,0:T(8,128)(2,1)S(1)}, f32[128,128]{1,0:T(8,128)S(1)}) custom-call(s32[4]{0:T(128)} %depth_ref.1, s32[1]{0:T(128)} %bitcast.place_ref, bf16[256,768]{1,0:T(8,128)(2,1)} %bitcast.4, f32[768]{0:T(1024)} %gain_hbm.1, s32[128]{0:T(128)} %prot_ref.1, ...), custom_call_target="tpu_custom_call" | custom-call | flops 603979776 | bytes 2359296 | tf_op jit(solution)/shard_map/row_scores/pallas_call | solution.py:359
  3.4 0.0 copy-start.9
  3.4 0.0 copy-start.2
  3.4 0.5 collective-permute-start
  3.9 1.1 %collective-permute-done.other_ref = f32[2,32,768]{2,1,0:T(8,128)S(1)} collective-permute-done((f32[2,32,768]{2,1,0:T(8,128)S(1)}, f32[2,32,768]{2,1,0:T(8,128)S(1)}, u32[]{:S(2)}, u32[]{:S(2)}) %collective-permute-start) | collective-permute-done | bytes 196640 | tf_op jit(solution)/shard_map/ppermute | solution.py:322
  5.0 3.0 %collective-permute-start.1 = (f32[32,768]{1,0:T(8,128)S(1)}, f32[32,768]{1,0:T(8,128)S(1)}, u32[]{:S(2)}, u32[]{:S(2)}) collective-permute-start(f32[32,768]{1,0:T(8,128)S(1)} %get-tuple-element.18), channel_id=1, source_target_pairs={{0,2},{1,3},{2,0},{3,1},{4,6},{5,7},{6,4},{7,5},{8,10},{9,11},{10,... | collective-permute-start | bytes 294920 | tf_op jit(solution)/shard_map/ppermute | solution.py:322
  8.0 3.1 %collective-permute-done.1.refs_1_ = f32[32,768]{1,0:T(8,128)S(1)} collective-permute-done((f32[32,768]{1,0:T(8,128)S(1)}, f32[32,768]{1,0:T(8,128)S(1)}, u32[]{:S(2)}, u32[]{:S(2)}) %collective-permute-start.1) | collective-permute-done | bytes 98336 | tf_op jit(solution)/shard_map/ppermute | solution.py:322
  11.1 3.9 %collective-permute-start.4 = (f32[32,768]{1,0:T(8,128)S(1)}, f32[32,768]{1,0:T(8,128)S(1)}, u32[]{:S(2)}, u32[]{:S(2)}) collective-permute-start(f32[32,768]{1,0:T(8,128)S(1)} %add.1.refs_0_), channel_id=1, source_target_pairs={{0,12},{1,13},{2,14},{3,15},{4,8},{5,9},{6,10},{7,11},{8,4},{9,5},... | collective-permute-start | bytes 294920 | tf_op jit(solution)/shard_map/ppermute | solution.py:322
  15.0 0.0 collective-permute-start.3
  15.0 0.6 collective-permute-start.2
  15.6 3.1 %collective-permute-done.4.refs_3_ = f32[32,768]{1,0:T(8,128)S(1)} collective-permute-done((f32[32,768]{1,0:T(8,128)S(1)}, f32[32,768]{1,0:T(8,128)S(1)}, u32[]{:S(2)}, u32[]{:S(2)}) %collective-permute-start.4) | collective-permute-done | bytes 98336 | tf_op jit(solution)/shard_map/ppermute | solution.py:322
  18.7 4.0 %collective-permute-done.3.refs_2_ = f32[32,768]{1,0:T(8,128)S(1)} collective-permute-done((f32[32,768]{1,0:T(8,128)S(1)}, f32[32,768]{1,0:T(8,128)S(1)}, u32[]{:S(2)}, u32[]{:S(2)}) %collective-permute-start.3) | collective-permute-done | bytes 98336 | tf_op jit(solution)/shard_map/ppermute | solution.py:322
  22.7 0.0 collective-permute-done.2.refs_1_
  22.7 0.0 copy-start
  22.7 0.0 copy-start.3
  22.7 0.3 row_softmax.1.piece0_ref
  23.1 1.6 %collective-permute-start.6 = (bf16[32,768]{1,0:T(8,128)(2,1)S(1)}, bf16[32,768]{1,0:T(8,128)(2,1)S(1)}, u32[]{:S(2)}, u32[]{:S(2)}) collective-permute-start(bf16[32,768]{1,0:T(8,128)(2,1)S(1)} %row_softmax.1.piece0_ref), channel_id=1, source_target_pairs={{0,2},{1,3},{2,0},{3,1},{4,6},{5,7},{6,4},{7,5},{8,10},{9,11},{10,... | collective-permute-start | bytes 147464 | tf_op jit(solution)/shard_map/ppermute | solution.py:322
  24.6 0.0 collective-permute-start.5
  24.6 2.6 %collective-permute-done.6.piece2_ref = bf16[32,768]{1,0:T(8,128)(2,1)S(1)} collective-permute-done((bf16[32,768]{1,0:T(8,128)(2,1)S(1)}, bf16[32,768]{1,0:T(8,128)(2,1)S(1)}, u32[]{:S(2)}, u32[]{:S(2)}) %collective-permute-start.6) | collective-permute-done | bytes 49184 | tf_op jit(solution)/shard_map/ppermute | solution.py:322
  27.2 0.0 collective-permute-start.7
  27.2 0.0 copy-done.9
  27.2 0.0 copy-done.2
  27.2 0.5 row_value.1.value_ref
  27.7 0.0 copy-start.4
  27.7 0.0 copy-start.5
  27.7 0.0 copy-start.6
  27.8 0.0 copy-start.7
  27.8 0.0 collective-permute-done.5.piece1_ref
  27.8 0.7 collective-permute-done.7.piece3_ref
  28.4 0.0 copy-done
  28.4 0.0 copy-done.3
  28.4 1.0 %row_output.1 = (bf16[256,768]{1,0:T(8,128)(2,1)S(1)}, bf16[16,2,8,768]{3,2,1,0:T(8,128)(2,1)S(1)}) custom-call(s32[1]{0:T(128)} %bitcast.place_ref, bf16[32,768]{1,0:T(8,128)(2,1)S(1)} %row_softmax.1.piece0_ref, bf16[32,768]{1,0:T(8,128)(2,1)S(1)} %collective-permute-done.5.piece1_ref, bf16[32,768]{1,0:T(8,128)(2,1)S(1)} %collective-permute-done.6.piece2_ref, ...), custom_call_target="tpu_custom_call" | custom-call | flops 301989888 | bytes 1179648 | tf_op jit(solution)/shard_map/row_output/pallas_call | solution.py:404
  29.5 16.9 %all_to_all.10 = bf16[16,2,8,768]{3,2,1,0:T(8,128)(2,1)S(1)} all-to-all(bf16[16,2,8,768]{3,2,1,0:T(8,128)(2,1)S(1)} %get-tuple-element.22), channel_id=1, replica_groups=mesh['grp'=2,'seq'=16] {'seq'}, dimensions={0} | all-to-all | bytes 786432 | tf_op jit(solution)/shard_map/all_to_all | solution.py:326
  46.3 0.0 copy-done.8
  46.3 0.0 copy-done.4
  46.3 0.0 copy-done.5
  46.3 0.0 copy-done.6
  46.3 0.0 copy-done.7
  46.4 0.0 copy-start.1
  46.4 3.7 %column_attention.1 = bf16[256,768]{1,0:T(8,128)(2,1)S(1)} custom-call(s32[4]{0:T(128)S(1)} %copy-done.4, s32[128]{0:T(128)S(1)} %copy-done.5, s32[1]{0:T(128)} %bitcast.place_ref, bf16[256,768]{1,0:T(8,128)(2,1)S(1)} %bitcast.6, bf16[768,768]{1,0:T(8,128)(2,1)S(1)} %copy-done.6, bf16[768,768]{1,0:T(8,128)(2,1)S(1)} %copy-done.7, bf16[768,768]{1,0:T(8,128)(2,1)S(1)} %copy-done.8), custom_call_target="tpu_custom_call" | custom-call | flops 1207959552 | bytes 3538944 | tf_op jit(solution)/shard_map/column_attention/pallas_call | solution.py:416
  50.0 15.5 %all_to_all.11.x_ref = bf16[16,2,8,768]{3,2,1,0:T(8,128)(2,1)S(1)} all-to-all(bf16[16,2,8,768]{3,2,1,0:T(8,128)(2,1)S(1)} %bitcast.7), channel_id=1, replica_groups=mesh['grp'=2,'seq'=16] {'seq'}, dimensions={0} | all-to-all | bytes 786432 | tf_op jit(solution)/shard_map/all_to_all | solution.py:326
  65.5 0.0 copy-done.1
  65.6 1.2 %column_output.1 = bf16[2,128,768]{2,1,0:T(8,128)(2,1)} custom-call(bf16[16,2,8,768]{3,2,1,0:T(8,128)(2,1)S(1)} %all_to_all.11.x_ref, bf16[768,768]{1,0:T(8,128)(2,1)S(1)} %copy-done.1, bf16[256,768]{1,0:T(8,128)(2,1)S(1)} %get-tuple-element.24.after_ref), custom_call_target="tpu_custom_call" | custom-call | flops 301989888 | bytes 1179648 | tf_op jit(solution)/shard_map/column_output/pallas_call | solution.py:428
  (3 shorter events, 0.0 us)
Async XLA Ops:
  0.0 46.3 %copy-start.8 = (bf16[768,768]{1,0:T(8,128)(2,1)S(1)}, bf16[768,768]{1,0:T(8,128)(2,1)}, u32[]{:S(2)}) copy-start(bf16[768,768]{1,0:T(8,128)(2,1)} %wv_ref) | copy-start | bytes 3538948
  3.4 23.8 %copy-start.9 = (f32[768]{0:T(1024)S(1)}, f32[768]{0:T(1024)}, u32[]{:S(2)}) copy-start(f32[768]{0:T(1024)} %param.21) | copy-start | bytes 9220
  3.4 23.8 %copy-start.2 = (bf16[768,768]{1,0:T(8,128)(2,1)S(1)}, bf16[768,768]{1,0:T(8,128)(2,1)}, u32[]{:S(2)}) copy-start(bf16[768,768]{1,0:T(8,128)(2,1)} %w_ref.3) | copy-start | bytes 3538948
  3.4 1.6 %collective-permute-start = (f32[2,32,768]{2,1,0:T(8,128)S(1)}, f32[2,32,768]{2,1,0:T(8,128)S(1)}, u32[]{:S(2)}, u32[]{:S(2)}) collective-permute-start(f32[2,32,768]{2,1,0:T(8,128)S(1)} %get-tuple-element.16), channel_id=1, source_target_pairs={{0,1},{1,0},{2,3},{3,2},{4,5},{5,4},{6,7},{7,6},{8,9},{9,8},{10,11... | collective-permute-start | bytes 589832 | tf_op jit(solution)/shard_map/ppermute | solution.py:322
  5.0 6.1 %collective-permute-start.1 = (f32[32,768]{1,0:T(8,128)S(1)}, f32[32,768]{1,0:T(8,128)S(1)}, u32[]{:S(2)}, u32[]{:S(2)}) collective-permute-start(f32[32,768]{1,0:T(8,128)S(1)} %get-tuple-element.18), channel_id=1, source_target_pairs={{0,2},{1,3},{2,0},{3,1},{4,6},{5,7},{6,4},{7,5},{8,10},{9,11},{10,... | collective-permute-start | bytes 294920 | tf_op jit(solution)/shard_map/ppermute | solution.py:322
  11.1 7.6 %collective-permute-start.4 = (f32[32,768]{1,0:T(8,128)S(1)}, f32[32,768]{1,0:T(8,128)S(1)}, u32[]{:S(2)}, u32[]{:S(2)}) collective-permute-start(f32[32,768]{1,0:T(8,128)S(1)} %add.1.refs_0_), channel_id=1, source_target_pairs={{0,12},{1,13},{2,14},{3,15},{4,8},{5,9},{6,10},{7,11},{8,4},{9,5},... | collective-permute-start | bytes 294920 | tf_op jit(solution)/shard_map/ppermute | solution.py:322
  15.0 7.7 %collective-permute-start.3 = (f32[32,768]{1,0:T(8,128)S(1)}, f32[32,768]{1,0:T(8,128)S(1)}, u32[]{:S(2)}, u32[]{:S(2)}) collective-permute-start(f32[32,768]{1,0:T(8,128)S(1)} %add.1.refs_0_), channel_id=1, source_target_pairs={{0,8},{1,9},{2,10},{3,11},{4,12},{5,13},{6,14},{7,15},{8,0},{9,1},... | collective-permute-start | bytes 294920 | tf_op jit(solution)/shard_map/ppermute | solution.py:322
  15.0 7.7 %collective-permute-start.2 = (f32[32,768]{1,0:T(8,128)S(1)}, f32[32,768]{1,0:T(8,128)S(1)}, u32[]{:S(2)}, u32[]{:S(2)}) collective-permute-start(f32[32,768]{1,0:T(8,128)S(1)} %add.1.refs_0_), channel_id=1, source_target_pairs={{0,4},{1,5},{2,6},{3,7},{4,0},{5,1},{6,2},{7,3},{8,12},{9,13},{10,... | collective-permute-start | bytes 294920 | tf_op jit(solution)/shard_map/ppermute | solution.py:322
  22.7 5.7 %copy-start = (bf16[2,128,768]{2,1,0:T(8,128)(2,1)S(1)}, bf16[2,128,768]{2,1,0:T(8,128)(2,1)}, u32[]{:S(2)}) copy-start(bf16[2,128,768]{2,1,0:T(8,128)(2,1)} %param.13) | copy-start | bytes 1179652
  22.7 5.7 %copy-start.3 = (bf16[768,768]{1,0:T(8,128)(2,1)S(1)}, bf16[768,768]{1,0:T(8,128)(2,1)}, u32[]{:S(2)}) copy-start(bf16[768,768]{1,0:T(8,128)(2,1)} %w_ref.4) | copy-start | bytes 3538948
  23.1 4.2 %collective-permute-start.6 = (bf16[32,768]{1,0:T(8,128)(2,1)S(1)}, bf16[32,768]{1,0:T(8,128)(2,1)S(1)}, u32[]{:S(2)}, u32[]{:S(2)}) collective-permute-start(bf16[32,768]{1,0:T(8,128)(2,1)S(1)} %row_softmax.1.piece0_ref), channel_id=1, source_target_pairs={{0,2},{1,3},{2,0},{3,1},{4,6},{5,7},{6,4},{7,5},{8,10},{9,11},{10,... | collective-permute-start | bytes 147464 | tf_op jit(solution)/shard_map/ppermute | solution.py:322
  24.6 3.1 %collective-permute-start.5 = (bf16[32,768]{1,0:T(8,128)(2,1)S(1)}, bf16[32,768]{1,0:T(8,128)(2,1)S(1)}, u32[]{:S(2)}, u32[]{:S(2)}) collective-permute-start(bf16[32,768]{1,0:T(8,128)(2,1)S(1)} %row_softmax.1.piece0_ref), channel_id=1, source_target_pairs={{0,1},{1,0},{2,3},{3,2},{4,5},{5,4},{6,7},{7,6},{8,9},{9,8},{10,11... | collective-permute-start | bytes 147464 | tf_op jit(solution)/shard_map/ppermute | solution.py:322
  27.2 1.2 %collective-permute-start.7 = (bf16[32,768]{1,0:T(8,128)(2,1)S(1)}, bf16[32,768]{1,0:T(8,128)(2,1)S(1)}, u32[]{:S(2)}, u32[]{:S(2)}) collective-permute-start(bf16[32,768]{1,0:T(8,128)(2,1)S(1)} %collective-permute-done.6.piece2_ref), channel_id=1, source_target_pairs={{0,1},{1,0},{2,3},{3,2},{4,5},{5,4},{6,7},{7,6},{8,9},{9,8},{10,11... | collective-permute-start | bytes 147464 | tf_op jit(solution)/shard_map/ppermute | solution.py:322
  27.7 18.6 %copy-start.4 = (s32[4]{0:T(128)S(1)}, s32[4]{0:T(128)}, u32[]{:S(2)}) copy-start(s32[4]{0:T(128)} %depth_ref.1) | copy-start | bytes 52
  27.7 18.6 %copy-start.5 = (s32[128]{0:T(128)S(1)}, s32[128]{0:T(128)}, u32[]{:S(2)}) copy-start(s32[128]{0:T(128)} %prot_ref.1) | copy-start | bytes 1540
  27.7 18.6 %copy-start.6 = (bf16[768,768]{1,0:T(8,128)(2,1)S(1)}, bf16[768,768]{1,0:T(8,128)(2,1)}, u32[]{:S(2)}) copy-start(bf16[768,768]{1,0:T(8,128)(2,1)} %wq_ref.1) | copy-start | bytes 3538948
  27.8 18.6 %copy-start.7 = (bf16[768,768]{1,0:T(8,128)(2,1)S(1)}, bf16[768,768]{1,0:T(8,128)(2,1)}, u32[]{:S(2)}) copy-start(bf16[768,768]{1,0:T(8,128)(2,1)} %wk_ref.1) | copy-start | bytes 3538948
  46.4 19.2 %copy-start.1 = (bf16[768,768]{1,0:T(8,128)(2,1)S(1)}, bf16[768,768]{1,0:T(8,128)(2,1)}, u32[]{:S(2)}) copy-start(bf16[768,768]{1,0:T(8,128)(2,1)} %w_ref.5) | copy-start | bytes 3538948

commit v5 on v3

v5 whole, which is shorter than its diff:
```python
import functools
import math

import jax
import jax.numpy as jnp
from jax import lax
from jax.experimental import pallas as pl
from jax.experimental.pallas import tpu as pltpu
from jax.sharding import PartitionSpec as P

H = 12
EPS = 1e-05
NEG = -1000000000.0
F32 = jnp.float32
BF16 = jnp.bfloat16
LIMIT = 20 << 20
PLANE = 4


def call(kernel, out_shape, ins, outs, scratch, cost, name):
    spaces = {"v": pltpu.VMEM, "s": pltpu.SMEM, "h": pltpu.HBM, "a": pl.ANY}
    return pl.pallas_call(
        kernel,
        out_shape=out_shape,
        in_specs=[pl.BlockSpec(memory_space=spaces[c]) for c in ins],
        out_specs=[pl.BlockSpec(memory_space=spaces[c]) for c in outs],
        scratch_shapes=scratch,
        compiler_params=pltpu.CompilerParams(vmem_limit_bytes=LIMIT),
        cost_estimate=pl.CostEstimate(flops=cost[0], bytes_accessed=cost[1], transcendentals=cost[2]),
        name=name,
    )


def norm(full, gain):
    middle = jnp.mean(full, axis=-1, keepdims=True)
    spread = jnp.mean((full - middle) ** 2, axis=-1, keepdims=True)
    return (full - middle) * lax.rsqrt(spread + EPS) * gain


def dot(a, b):
    return jnp.dot(a, b, preferred_element_type=F32)


def dot_t(a, b):
    return lax.dot_general(a, b, (((1,), (1,)), ((), ())), preferred_element_type=F32)


def iota(shape, dim):
    return lax.broadcasted_iota(jnp.int32, shape, dim)


def flat(ref):
    return jnp.concatenate([ref[p] for p in range(ref.shape[0])], axis=1)


def to_column(row, size):
    eye = iota((size, size), 0) == iota((size, size), 1)
    return jnp.sum(jnp.where(eye, jnp.broadcast_to(row, (size, size)), 0.0), axis=1, keepdims=True)


def half_masks(width):
    low = (iota((1, width), 1) % 128) < 64
    return jnp.where(low, 1.0, 0.0), jnp.where(low, 0.0, 1.0)


def row_scores_kernel(
    depth_hbm,
    place_ref,
    x_hbm,
    gain_hbm,
    prot_hbm,
    wq_hbm,
    wk_hbm,
    keep_ref,
    send_ref,
    normed_ref,
    same_ref,
    depth_ref,
    x_ref,
    gain_ref,
    prot_ref,
    wq_ref,
    wk_ref,
    sems,
):
    columns = prot_ref.shape[0]
    tokens, width = x_ref.shape
    rows = tokens // columns
    pairs = [(x_hbm, x_ref), (gain_hbm, gain_ref), (prot_hbm, prot_ref), (depth_hbm, depth_ref)]
    for n in range(width // 256):
        for source, target in ((wq_hbm, wq_ref), (wk_hbm, wk_ref)):
            pairs.append((source.at[256 * n : 256 * n + 256], target.at[256 * n : 256 * n + 256]))
    copies = [pltpu.make_async_copy(a, b, sems.at[i]) for i, (a, b) in enumerate(pairs)]
    for copy in copies:
        copy.start()
    for copy in copies[:2]:
        copy.wait()
    normed = norm(x_ref[...].astype(F32), gain_ref[...].reshape(1, width)).astype(BF16)
    normed_ref[...] = normed
    for copy in copies[2:4]:
        copy.wait()
    prot = prot_ref[...].reshape(1, columns).astype(F32)
    depth = jnp.zeros((1, columns), F32)
    for p in range(depth_ref.shape[0]):
        depth = jnp.where(prot == float(p), depth_ref[p].astype(F32), depth)
    prot_col = to_column(prot, columns)
    depth_col = to_column(depth, columns)
    same = jnp.broadcast_to(prot_col, (columns, columns)) == jnp.broadcast_to(prot, (columns, columns))
    same_f = jnp.where(same, 1.0, 0.0)
    same_ref[...] = same_f
    low = iota((columns, columns), 1) < 64
    first = jnp.where(low, same_f, pltpu.roll(same_f, 64, 1)) > 0.5
    valid = [
        jnp.where((place_ref[0] * rows + r).astype(F32) < depth_col, 1.0, 0.0) for r in range(rows)
    ]
    valid = jnp.concatenate(valid, axis=0)
    even, odd = half_masks(256)
    quarter = columns // PLANE
    core = (place_ref[0] % 2) == 0
    for copy in copies[4:]:
        copy.wait()
    for n in range(width // 256):
        cols = slice(256 * n, 256 * n + 256)
        query = dot(normed, wq_ref[:, cols]).astype(BF16).astype(F32) * valid
        key = (dot(normed, wk_ref[:, cols]) * valid).astype(BF16)
        query_even, query_odd = (query * even).astype(BF16), (query * odd).astype(BF16)
        for q in range(2):
            lanes = slice(128 * q, 128 * q + 128)

            def side(array, lanes=lanes):
                return jnp.concatenate(
                    [array[r * columns : (r + 1) * columns, lanes] for r in range(rows)], axis=1
                )

            both = jnp.concatenate([side(query_even), side(query_odd)], axis=0)
            logits = dot_t(both, side(key))
            one, two = logits[:columns], logits[columns:]
            folded = jnp.where(
                low,
                jnp.where(first, one, pltpu.roll(one, 64, 1)),
                jnp.where(first, pltpu.roll(two, 64, 1), two),
            )
            out = slice(256 * n + 128 * q, 256 * n + 128 * q + 128)
            for y in range(PLANE // 2):
                start = 2 * y * quarter
                left, right = folded[start : start + quarter], folded[start + quarter : start + 2 * quarter]
                keep_ref[y, :, out] = jnp.where(core, left, right)
                send_ref[y, :, out] = jnp.where(core, right, left)


def core_sum_kernel(place_ref, mine_ref, other_ref, keep_ref, send_ref):
    row = (place_ref[0] // 2) % 2
    keep_ref[...] = mine_ref[row] + other_ref[row]
    send_ref[...] = mine_ref[1 - row] + other_ref[1 - row]


def add_kernel(*refs):
    total = refs[0][...] + refs[1][...]
    if len(refs) == 5:
        total = total + (refs[2][...] + refs[3][...])
    refs[-1][...] = total


def row_value_kernel(columns, place_ref, x_ref, w_ref, mine_ref, other_ref, out_ref, spread_ref):
    core = place_ref[0] % 2
    out_ref[...] = dot(x_ref[...], w_ref[...]).astype(BF16)
    rows = x_ref.shape[0] // columns
    quarter = columns // PLANE
    for source, index in ((mine_ref, core), (other_ref, 1 - core)):
        for r in range(rows):
            for y in range(2):
                start = pl.multiple_of(r * columns + y * columns // 2 + quarter * core, quarter)
                piece = source[pl.ds(start, quarter), :].astype(F32)
                target = pl.ds(2 * rows * quarter * y + index * rows + r, quarter, stride=2 * rows)
                for p in range(piece.shape[1] // 128):
                    spread_ref[p, target, :] = piece[:, 128 * p : 128 * p + 128]


def row_softmax_kernel(scale, place_ref, *refs):
    part_refs, (same_ref, out_ref, mask_ref) = refs[:-3], refs[-3:]
    tile, width = out_ref.shape
    same = same_ref[...]
    mask_ref[...] = jnp.maximum(same, pltpu.roll(same, 64, 1))
    live = mask_ref[pl.ds((place_ref[0] % PLANE) * tile, tile), :] > 0.5
    low = iota((tile, 128), 1) < 64
    for p in range(width // 128):
        lanes = slice(128 * p, 128 * p + 128)
        parts = [part[:, lanes] for part in part_refs]
        while len(parts) > 1:
            parts = [a + b for a, b in zip(parts[::2], parts[1::2])]
        tied = jnp.where(live, parts[0] * scale, NEG)
        top_low = jnp.max(jnp.where(low, tied, 2 * NEG), axis=1, keepdims=True)
        top_high = jnp.max(jnp.where(low, 2 * NEG, tied), axis=1, keepdims=True)
        value = jnp.exp(tied - jnp.where(low, top_low, top_high))
        sum_low = jnp.sum(jnp.where(low, value, 0.0), axis=1, keepdims=True)
        sum_high = jnp.sum(jnp.where(low, 0.0, value), axis=1, keepdims=True)
        out_ref[:, lanes] = (value / jnp.where(low, sum_low, sum_high)).astype(BF16)


def row_output_kernel(
    place_ref,
    mine_ref,
    across_ref,
    same_ref,
    value_ref,
    other_ref,
    x_ref,
    w_ref,
    gain_ref,
    after_ref,
    *refs,
):
    outs, (mixed_ref, folded_ref, normed_ref) = refs[:-3], refs[-3:]
    columns = same_ref.shape[0]
    tokens, width = after_ref.shape
    rows = tokens // columns
    quarter, local = columns // PLANE, columns // 2
    place = place_ref[0]
    core, line, plane = place % 2, (place // 2) % 2, place // PLANE
    folded_ref[pl.ds(pl.multiple_of(line * quarter, quarter), quarter), :] = mine_ref[...].astype(F32)
    folded_ref[pl.ds(pl.multiple_of((1 - line) * quarter, quarter), quarter), :] = across_ref[...].astype(F32)
    same = [
        same_ref[pl.ds(pl.multiple_of(y * local + core * quarter, quarter), quarter), :] for y in range(2)
    ]
    same = jnp.concatenate(same, axis=0) > 0.5
    low = iota((local, columns), 1) < 64
    even, odd = half_masks(256 * rows)
    even, odd = even.astype(BF16), odd.astype(BF16)
    spots = [core * rows + r for r in range(rows)] + [(1 - core) * rows + r for r in range(rows)]
    for p in range(width // 128):
        lanes = slice(128 * p, 128 * p + 128)
        piece = folded_ref[:, lanes]
        turned = pltpu.roll(piece, 64, 1)
        one = jnp.where(same, jnp.where(low, piece, turned), 0.0)
        two = jnp.where(same, jnp.where(low, turned, piece), 0.0)
        weights = jnp.concatenate([one, two], axis=1).astype(BF16)
        value = jnp.concatenate(
            [
                source[r * columns : (r + 1) * columns, lanes]
                for source in (value_ref, other_ref)
                for r in range(rows)
            ],
            axis=1,
        )
        value = jnp.concatenate([value * even, value * odd], axis=0)
        mixed = dot(weights, value)
        for i, spot in enumerate(spots):
            mixed_ref[p, pl.ds(spot, local, stride=2 * rows), :] = mixed[:, 128 * i : 128 * i + 128]
    after = (flat(x_ref) + dot(flat(mixed_ref).astype(BF16), w_ref[...])).astype(BF16)
    after_ref[...] = after
    normed_ref[...] = norm(after.astype(F32), gain_ref[...])
    size = tokens // len(outs)
    for s, out in enumerate(outs):
        start = pl.multiple_of(((plane + s) % len(outs)) * size, size)
        out[...] = normed_ref[pl.ds(start, size), :].astype(BF16)


def column_kernel(scale, planes, columns, depth_ref, prot_ref, place_ref, wq_ref, wk_ref, wv_ref, *refs):
    ins, (keep_ref, send_ref, all_ref, mixed_ref) = refs[: 2 * planes], refs[2 * planes :]
    size, width = ins[0].shape
    wide = width // 2
    slots, local = 2 * planes, columns // 2
    own = local // planes
    rows = size // own
    block = 4 if own % 4 == 0 else own
    piece = block * rows
    chunk = slots * piece
    chunks = own // block
    fold = piece // 8
    pair = 8 // rows
    place = place_ref[0]
    core, line, plane = place % 2, (place // 2) % 2, place // PLANE
    for g in range(chunks):
        for i, source in enumerate(ins):
            all_ref[g * chunk + i * piece : g * chunk + (i + 1) * piece, :] = source[g * piece : (g + 1) * piece, :]
    x = all_ref[...]
    heads = pl.ds(pl.multiple_of(core * wide, 128), wide)
    even, odd = half_masks(wide)
    query = dot(x, wq_ref[:, heads]).astype(BF16).astype(F32) * scale
    key = dot(x, wk_ref[:, heads]).astype(BF16)
    value = dot(x, wv_ref[:, heads]).astype(BF16)
    sides = [(query * side).astype(BF16) for side in (even, odd)]
    unit = jnp.where(iota((128, 128), 0) == iota((128, 128), 1), 1.0, 0.0).astype(BF16)
    lane = (iota((8, 2 * chunk), 1) % piece) // rows
    level = iota((8, 2 * chunk), 0)
    fits = level // rows == lane % pair
    mine = [jnp.where(lane // pair == v, 1.0, 0.0)[None] for v in range(fold)]
    lives = []
    for g in range(chunks):
        depth = jnp.zeros((8, 2 * chunk), jnp.int32)
        for c in range(block):
            index = plane * own + g * block + c
            column = index % (local // 2) + (local // 2) * line + local * (index // (local // 2))
            depth = jnp.where(lane == c, depth_ref[prot_ref[column]], depth)
        live = []
        for i in range(slots):
            away = ((plane + planes - i % planes) % planes) * 2 + (core if i < planes else 1 - core)
            live.append((fits & (level % rows + away * rows < depth))[None])
        lives.append(jnp.concatenate([jnp.where(l, 1.0, 0.0) for l in live], axis=0) > 0.5)
    packs, values = [], []
    for q in range(wide // 128):
        lanes = slice(128 * q, 128 * q + 128)
        for g in range(chunks):
            part = slice(g * chunk, g * chunk + chunk)
            both = jnp.concatenate([side[part, lanes] for side in sides], axis=0)
            scores = dot_t(key[part, lanes], both).reshape(slots, fold, 8, 2 * chunk)
            packed = scores[:, 0]
            for v in range(1, fold):
                packed = jnp.where(mine[v] > 0.5, scores[:, v], packed)
            packs.append(jnp.where(lives[g], packed, NEG))
        values.append(dot_t(unit, value[:, lanes]).astype(BF16))
    packs = [jnp.exp(packed - jnp.max(packed, axis=(0, 1), keepdims=True)) for packed in packs]
    packs = [packed * (1.0 / jnp.sum(packed, axis=(0, 1), keepdims=True)) for packed in packs]
    for q, value in enumerate(values):
        for g in range(chunks):
            part = slice(g * chunk, g * chunk + chunk)
            weight = packs[q * chunks + g]
            spread = jnp.stack([weight * m for m in mine], axis=1).reshape(chunk, 2 * chunk).astype(BF16)
            for s in range(2):
                mixed = dot(value[64 * s : 64 * s + 64, part], spread[:, s * chunk : (s + 1) * chunk])
                mixed_ref[128 * q + 64 * s : 128 * q + 64 * s + 64, part] = mixed.astype(BF16)
    turn = jnp.where(iota((chunk, chunk), 0) == iota((chunk, chunk), 1), 1.0, 0.0).astype(BF16)
    for g in range(chunks):
        mixed = dot_t(turn, mixed_ref[:, g * chunk : (g + 1) * chunk])
        for i in range(slots):
            target = keep_ref if i < planes else send_ref
            target[i % planes, g * piece : (g + 1) * piece, :] = mixed[i * piece : (i + 1) * piece].astype(BF16)


def join_kernel(place_ref, keep_ref, other_ref, *outs):
    wide = keep_ref.shape[2]
    core = place_ref[0] % 2

    def write(left, right):
        for s, out in enumerate(outs):
            out[:, :wide] = left[s]
            out[:, wide:] = right[s]

    @pl.when(core == 0)
    def _():
        write(keep_ref, other_ref)

    @pl.when(core == 1)
    def _():
        write(other_ref, keep_ref)


def column_output_kernel(place_ref, w_ref, after_ref, *refs):
    ins, (keep_ref, send_ref, total_ref) = refs[:-3], refs[-3:]
    rows, local, _ = keep_ref.shape
    core, plane = place_ref[0] % 2, place_ref[0] // PLANE
    size = ins[0].shape[0]
    total = dot(jnp.concatenate([source[...] for source in ins], axis=0), w_ref[...])
    for s in range(len(ins)):
        start = pl.multiple_of(((plane + s) % len(ins)) * size, size)
        for p in range(total.shape[1] // 128):
            total_ref[p, pl.ds(start, size), :] = total[s * size : (s + 1) * size, 128 * p : 128 * p + 128]
    for p in range(total.shape[1] // 128):
        lanes = slice(128 * p, 128 * p + 128)
        total_ref[p] = total_ref[p] + after_ref[:, lanes].astype(F32)
        for r in range(rows):
            for target, index in ((keep_ref, core), (send_ref, 1 - core)):
                row = total_ref[p, pl.ds(index * rows + r, local, stride=2 * rows), :]
                target[r, :, lanes] = row.astype(BF16)


def assemble_kernel(place_ref, mine_ref, other_ref, out_ref, sems):
    core = place_ref[0] % 2
    local = mine_ref.shape[1]
    quarter = local // 2
    copies = []
    for source, index in ((mine_ref, core), (other_ref, 1 - core)):
        for y in range(2):
            start = pl.multiple_of(y * local + index * quarter, quarter)
            copies.append(
                pltpu.make_async_copy(
                    source.at[:, y * quarter : (y + 1) * quarter, :],
                    out_ref.at[:, pl.ds(start, quarter), :],
                    sems.at[len(copies)],
                )
            )
    for copy in copies:
        copy.start()
    for copy in copies:
        copy.wait()


def hbm(array):
    return pltpu.with_memory_space_constraint(array, pltpu.HBM)


def swap(array, offset):
    devices = lax.axis_size("seq")
    return lax.ppermute(array, "seq", [(i, i ^ offset) for i in range(devices)])


def spin_pairs(step):
    planes = lax.axis_size("seq") // PLANE
    pairs = []
    for z in range(planes):
        for y in range(2):
            for k in range(2):
                pairs.append((z * PLANE + 2 * y + k, (z + step) % planes * PLANE + 2 * k + y))
    return pairs


def spin(array, step):
    return lax.ppermute(array, "seq", spin_pairs(step))


def spin_back(array, step):
    return lax.ppermute(array, "seq", [(b, a) for a, b in spin_pairs(step)])


def per_device(
    alignment,
    protein_id,
    row_depth,
    row_gain,
    row_query,
    row_key,
    row_value,
    row_output,
    column_gain,
    column_query,
    column_key,
    column_value,
    column_output,
):
    rows, columns, width = alignment.shape
    devices = lax.axis_size("seq")
    place = lax.axis_index("seq").astype(jnp.int32)[None]
    total_rows = rows * devices
    head_size = width // H
    tokens = rows * columns
    planes, local = devices // PLANE, columns // 2
    size = tokens // planes
    x = alignment.reshape(tokens, width)
    shape = jax.ShapeDtypeStruct
    square = 2 * tokens * width * width

    quarter = columns // PLANE
    half = shape((PLANE // 2, quarter, width), F32)
    part = shape((quarter, width), F32)
    keep, send, normed, same = call(
        row_scores_kernel,
        (half, half, shape((tokens, width), BF16), shape((columns, columns), F32)),
        "hshhhhh",
        "vvvv",
        [
            pltpu.SMEM(row_depth.shape, jnp.int32),
            pltpu.VMEM((tokens, width), BF16),
            pltpu.VMEM((width,), F32),
            pltpu.VMEM((columns,), jnp.int32),
            pltpu.VMEM((width, width), BF16),
            pltpu.VMEM((width, width), BF16),
            pltpu.SemaphoreType.DMA((4 + 2 * (width // 256),)),
        ],
        (2 * square, 4 * width * width, tokens),
        "row_scores",
    )(hbm(row_depth), place, hbm(x), hbm(row_gain), hbm(protein_id), hbm(row_query), hbm(row_key))
    column_query, column_key, column_value, late, normed = lax.optimization_barrier(
        (column_query, column_key, column_value, x, normed)
    )
    sibling = swap(late, 1)
    value, spread = call(
        functools.partial(row_value_kernel, columns),
        (shape((tokens, width), BF16), shape((width // 128, tokens, 128), F32)),
        "svvvv",
        "vv",
        [],
        (square, 2 * width * width, 0),
        "row_value",
    )(place, normed, row_value, late, sibling)
    value_other = swap(value, 1)
    keep, send = call(
        core_sum_kernel, (part, part), "svv", "vv", [], (columns * width, 6 * columns * width, 0), "core_sum"
    )(place, keep, swap(send, 1))
    parts = [keep, swap(send, 2)]
    stride, left = PLANE, planes
    while left > 1:
        ways = 4 if left % 4 == 0 else 2
        (total,) = call(
            add_kernel, (part,), "v" * len(parts), "v", [], (columns * width, 6 * columns * width, 0), "add"
        )(*parts)
        parts = [total] + [swap(total, stride * w) for w in range(1, ways)]
        stride, left = stride * ways, left // ways
    (weights,) = call(
        functools.partial(row_softmax_kernel, 1.0 / (math.sqrt(head_size) * math.sqrt(total_rows))),
        (shape((quarter, width), BF16),),
        "s" + "v" * len(parts) + "v",
        "v",
        [pltpu.VMEM((columns, columns), F32)],
        (columns * width, 6 * columns * width, quarter * width),
        "row_softmax",
    )(place, *parts, same)
    across = swap(weights, 2)
    after, *blocks = call(
        row_output_kernel,
        (shape((tokens, width), BF16),) + (shape((size, width), BF16),) * planes,
        "s" + "v" * 8,
        "v" * (1 + planes),
        [
            pltpu.VMEM((width // 128, tokens, 128), F32),
            pltpu.VMEM((local, width), F32),
            pltpu.VMEM((tokens, width), F32),
        ],
        (square, 2 * width * width, tokens),
        "row_output",
    )(place, weights, across, same, value, value_other, spread, row_output, column_gain[None])
    moved = [spin(block, s) for s, block in enumerate(blocks)]
    moved += [swap(block, 1) for block in moved]
    wide = width // 2
    halves = shape((planes, size, wide), BF16)
    keep, send = call(
        functools.partial(column_kernel, 1.0 / math.sqrt(head_size), planes, columns),
        (halves, halves),
        "sss" + "v" * (3 + 2 * planes),
        "vv",
        [pltpu.VMEM((2 * tokens, width), BF16), pltpu.VMEM((wide, 2 * tokens), BF16)],
        (4 * square, 6 * width * width, H * tokens * tokens // 4),
        "column_attention",
    )(row_depth, protein_id, place, column_query, column_key, column_value, *moved)
    joined = call(
        join_kernel,
        (shape((size, width), BF16),) * planes,
        "svv",
        "v" * planes,
        [],
        (tokens * width, 4 * tokens * width, 0),
        "join",
    )(place, keep, swap(send, 1))
    returned = [spin_back(block, s) for s, block in enumerate(joined)]
    half = shape((rows, local, width), BF16)
    keep, send = call(
        column_output_kernel,
        (half, half),
        "svv" + "v" * planes,
        "vv",
        [pltpu.VMEM((width // 128, tokens, 128), F32)],
        (square, 2 * width * width, 0),
        "column_output",
    )(place, column_output, after, *returned)
    (out,) = call(
        assemble_kernel,
        (shape((rows, columns, width), BF16),),
        "svv",
        "a",
        [pltpu.SemaphoreType.DMA((4,))],
        (tokens * width, 4 * tokens * width, 0),
        "assemble",
    )(place, keep, swap(send, 1))
    return out


def solution(mesh):
    return jax.shard_map(
        per_device,
        mesh=mesh,
        in_specs=(P(("grp", "seq"), None, None), P("grp"), P("grp")) + (P(),) * 10,
        out_specs=P(("grp", "seq"), None, None),
        check_vma=False,
    )
```

time: 72.4 us -> 65.5 us (0.905)
  blocking collectives: 32.5 us -> 0 us
  starting transfers between devices: 9.59 us -> 28.8 us
  waiting for transfers between devices: 14.1 us -> 26.6 us
  Pallas kernels: 13 us -> 9.72 us
  local copies, waits for them, and re-layouts: 2.81 us -> 0.06 us
    all_to_all x2 -> x0, blocking collectives: 32.5 us -> none  [exchange(): return lax.all_to_all(array, 'seq', split_axis=0, concat_axis=0, tiled=True)]
    ppermute x8 -> x14, starting transfers between devices: 9.59 us -> 20 us  [swap(): return lax.ppermute(array, 'seq', [(i, i ^ offset) for i in range(devices)])]
    ppermute x0 -> x8, waiting for transfers between devices: none -> 9.01 us  [the longest x4 7.84 us: spin_back(): return lax.ppermute(array, 'seq', [(b, a) for a, b in spin_pairs(step)])]
    ppermute x0 -> x8, starting transfers between devices: none -> 8.84 us  [the longest x4 4.55 us: spin(): return lax.ppermute(array, 'seq', spin_pairs(step))]
    ppermute x8 -> x14, waiting for transfers between devices: 14.1 us -> 17.6 us  [swap(): return lax.ppermute(array, 'seq', [(i, i ^ offset) for i in range(devices)])]
    unnamed x26 -> x20, local copies, waits for them, and re-layouts: 2.81 us -> 0.05 us
    pallas_call x1, Pallas kernels: 5.47 us -> 3.41 us  [per_device(): call(row_scores_kernel, (half, half, shape((tokens, width), BF16), shape(...]
    pallas_call x4 -> x6, Pallas kernels: 7.22 us -> 5.97 us  [the longest x1 2.82 us: per_device(): call(functools.partial(column_kernel, 1.0 / math.sqrt(head_size), planes,...]
  transfers between devices with their start and end apart: 8 -> 22, of which waited for: 5 -> 12; matrix products, arithmetic and copies ran while one was open for 0% -> 0% of each run, Pallas kernels for 1% -> 1%
where the time goes in v5:
time: 65.5 us; the launch traced here: 65.4 us
  starting transfers between devices  28.8 us (44%)
  waiting for transfers between devices  26.6 us (41%)
  Pallas kernels  9.72 us (15%)
    ppermute x14, starting transfers between devices, swap(): return lax.ppermute(array, 'seq', [(i, i ^ offset) for i in range(devices)])  20 us
    ppermute x14, waiting for transfers between devices, swap(): return lax.ppermute(array, 'seq', [(i, i ^ offset) for i in range(devices)])  17.6 us
    ppermute x4, waiting for transfers between devices, spin_back(): return lax.ppermute(array, 'seq', [(b, a) for a, b in spin_pairs(step)])  7.84 us
    ppermute x4, starting transfers between devices, spin(): return lax.ppermute(array, 'seq', spin_pairs(step))  4.55 us
    ppermute x4, starting transfers between devices, spin_back(): return lax.ppermute(array, 'seq', [(b, a) for a, b in spin_pairs(step)])  4.3 us
    pallas_call x1, Pallas kernels, per_device(): call(row_scores_kernel, (half, half, shape((tokens, width), BF16), shape(...  3.41 us
    pallas_call x1, Pallas kernels, per_device(): call(functools.partial(column_kernel, 1.0 / math.sqrt(head_size), planes,...  2.82 us
  transfers between devices with their start and end apart: 22, of which 12 were waited for; matrix products, arithmetic and copies ran while one was open for 0% of the time, Pallas kernels for 1%

profile of v5, /device:TPU:0, one launch (start us, length us, event | category | flops | bytes accessed | tf_op | source)
XLA Modules:
  0.0 65.4 jit_solution(4339811869061149106)
XLA Ops:
  0.0 3.4 %row_scores.1 = (f32[2,32,768]{2,1,0:T(8,128)S(1)}, f32[2,32,768]{2,1,0:T(8,128)S(1)}, bf16[256,768]{1,0:T(8,128)(2,1)S(1)}, f32[128,128]{1,0:T(8,128)S(1)}) custom-call(s32[4]{0:T(128)} %depth_ref.1, s32[1]{0:T(128)} %bitcast.place_ref, bf16[256,768]{1,0:T(8,128)(2,1)} %bitcast.2, f32[768]{0:T(1024)} %gain_hbm.1, s32[128]{0:T(128)} %prot_ref.1, ...), custom_call_target="tpu_custom_call" | custom-call | flops 603979776 | bytes 2359296 | tf_op jit(solution)/shard_map/row_scores/pallas_call | solution.py:445
  3.4 0.5 collective-permute-start.6
  4.0 0.1 collective-permute-start
  4.0 1.3 %collective-permute-done.6.other_ref = bf16[256,768]{1,0:T(8,128)(2,1)S(1)} collective-permute-done((bf16[256,768]{1,0:T(8,128)(2,1)S(1)}, bf16[256,768]{1,0:T(8,128)(2,1)S(1)}, u32[]{:S(2)}, u32[]{:S(2)}) %collective-permute-start.6) | collective-permute-done | bytes 393248 | tf_op jit(solution)/shard_map/ppermute | solution.py:394
  5.3 0.5 row_value.1
  5.8 0.0 copy-start.9
  5.8 0.0 copy-start.1
  5.8 0.4 collective-permute-start.7
  6.3 0.0 collective-permute-done.other_ref
  6.3 2.7 %collective-permute-start.1 = (f32[32,768]{1,0:T(8,128)S(1)}, f32[32,768]{1,0:T(8,128)S(1)}, u32[]{:S(2)}, u32[]{:S(2)}) collective-permute-start(f32[32,768]{1,0:T(8,128)S(1)} %get-tuple-element.34), channel_id=1, source_target_pairs={{0,2},{1,3},{2,0},{3,1},{4,6},{5,7},{6,4},{7,5},{8,10},{9,11},{10,... | collective-permute-start | bytes 294920 | tf_op jit(solution)/shard_map/ppermute | solution.py:394
  9.0 3.3 %collective-permute-done.1.refs_1_ = f32[32,768]{1,0:T(8,128)S(1)} collective-permute-done((f32[32,768]{1,0:T(8,128)S(1)}, f32[32,768]{1,0:T(8,128)S(1)}, u32[]{:S(2)}, u32[]{:S(2)}) %collective-permute-start.1) | collective-permute-done | bytes 98336 | tf_op jit(solution)/shard_map/ppermute | solution.py:394
  12.4 3.9 %collective-permute-start.4 = (f32[32,768]{1,0:T(8,128)S(1)}, f32[32,768]{1,0:T(8,128)S(1)}, u32[]{:S(2)}, u32[]{:S(2)}) collective-permute-start(f32[32,768]{1,0:T(8,128)S(1)} %add.1.refs_0_), channel_id=1, source_target_pairs={{0,12},{1,13},{2,14},{3,15},{4,8},{5,9},{6,10},{7,11},{8,4},{9,5},... | collective-permute-start | bytes 294920 | tf_op jit(solution)/shard_map/ppermute | solution.py:394
  16.3 0.6 collective-permute-start.2
  16.9 2.8 %collective-permute-done.4.refs_3_ = f32[32,768]{1,0:T(8,128)S(1)} collective-permute-done((f32[32,768]{1,0:T(8,128)S(1)}, f32[32,768]{1,0:T(8,128)S(1)}, u32[]{:S(2)}, u32[]{:S(2)}) %collective-permute-start.4) | collective-permute-done | bytes 98336 | tf_op jit(solution)/shard_map/ppermute | solution.py:394
  19.7 4.5 %collective-permute-done.3.refs_2_ = f32[32,768]{1,0:T(8,128)S(1)} collective-permute-done((f32[32,768]{1,0:T(8,128)S(1)}, f32[32,768]{1,0:T(8,128)S(1)}, u32[]{:S(2)}, u32[]{:S(2)}) %collective-permute-start.3) | collective-permute-done | bytes 98336 | tf_op jit(solution)/shard_map/ppermute | solution.py:394
  24.2 0.3 row_softmax.1.mine_ref
  24.6 1.6 %collective-permute-start.5 = (bf16[32,768]{1,0:T(8,128)(2,1)S(1)}, bf16[32,768]{1,0:T(8,128)(2,1)S(1)}, u32[]{:S(2)}, u32[]{:S(2)}) collective-permute-start(bf16[32,768]{1,0:T(8,128)(2,1)S(1)} %row_softmax.1.mine_ref), channel_id=1, source_target_pairs={{0,2},{1,3},{2,0},{3,1},{4,6},{5,7},{6,4},{7,5},{8,10},{9,11},{10,... | collective-permute-start | bytes 147464 | tf_op jit(solution)/shard_map/ppermute | solution.py:394
  26.1 2.6 %collective-permute-done.5.across_ref = bf16[32,768]{1,0:T(8,128)(2,1)S(1)} collective-permute-done((bf16[32,768]{1,0:T(8,128)(2,1)S(1)}, bf16[32,768]{1,0:T(8,128)(2,1)S(1)}, u32[]{:S(2)}, u32[]{:S(2)}) %collective-permute-start.5) | collective-permute-done | bytes 49184 | tf_op jit(solution)/shard_map/ppermute | solution.py:394
  28.7 0.0 collective-permute-done.7.other_ref
  28.7 0.0 copy-start.5
  28.7 0.0 copy-start.6
  28.7 0.0 copy-start.7
  28.8 1.2 %row_output.1 = (bf16[256,768]{1,0:T(8,128)(2,1)S(1)}, bf16[64,768]{1,0:T(8,128)(2,1)S(1)}, bf16[64,768]{1,0:T(8,128)(2,1)S(1)}, bf16[64,768]{1,0:T(8,128)(2,1)S(1)}, bf16[64,768]{1,0:T(8,128)(2,1)S(1)}) custom-call(s32[1]{0:T(128)} %bitcast.place_ref, bf16[32,768]{1,0:T(8,128)(2,1)S(1)} %row_softmax.1.mine_ref, ...), custom_call_target="tpu_custom_call" | custom-call | flops 301989888 | bytes 1179648 | tf_op jit(solution)/shard_map/row_output/pallas_call | solution.py:498
  30.0 0.7 %collective-permute-start.8 = (bf16[64,768]{1,0:T(8,128)(2,1)S(1)}, bf16[64,768]{1,0:T(8,128)(2,1)S(1)}, u32[]{:S(2)}, u32[]{:S(2)}) collective-permute-start(bf16[64,768]{1,0:T(8,128)(2,1)S(1)} %get-tuple-element.45), channel_id=1, source_target_pairs={{0,0},{1,2},{2,1},{3,3},{4,4},{5,6},{6,5},{7,7},{8,8},{9,10},{10,9... | collective-permute-start | bytes 294920 | tf_op jit(solution)/shard_map/ppermute | solution.py:408
  30.6 0.6 collective-permute-start.9
  31.2 2.6 %collective-permute-start.10 = (bf16[64,768]{1,0:T(8,128)(2,1)S(1)}, bf16[64,768]{1,0:T(8,128)(2,1)S(1)}, u32[]{:S(2)}, u32[]{:S(2)}) collective-permute-start(bf16[64,768]{1,0:T(8,128)(2,1)S(1)} %get-tuple-element.47), channel_id=1, source_target_pairs={{0,8},{1,10},{2,9},{3,11},{4,12},{5,14},{6,13},{7,15},{8,0},{9,2},... | collective-permute-start | bytes 294920 | tf_op jit(solution)/shard_map/ppermute | solution.py:408
  33.8 0.7 %collective-permute-start.11 = (bf16[64,768]{1,0:T(8,128)(2,1)S(1)}, bf16[64,768]{1,0:T(8,128)(2,1)S(1)}, u32[]{:S(2)}, u32[]{:S(2)}) collective-permute-start(bf16[64,768]{1,0:T(8,128)(2,1)S(1)} %get-tuple-element.48), channel_id=1, source_target_pairs={{0,12},{1,14},{2,13},{3,15},{4,0},{5,2},{6,1},{7,3},{8,4},{9,6},{1... | collective-permute-start | bytes 294920 | tf_op jit(solution)/shard_map/ppermute | solution.py:408
  34.5 0.0 collective-permute-done.8.refs_0_
  34.5 3.5 %collective-permute-start.12 = (bf16[64,768]{1,0:T(8,128)(2,1)S(1)}, bf16[64,768]{1,0:T(8,128)(2,1)S(1)}, u32[]{:S(2)}, u32[]{:S(2)}) collective-permute-start(bf16[64,768]{1,0:T(8,128)(2,1)S(1)} %collective-permute-done.8.refs_0_), channel_id=1, source_target_pairs={{0,1},{1,0},{2,3},{3,2},{4,5},{5,4},{6,7},{7,6},{8,9},{9,8},{10,11... | collective-permute-start | bytes 294920 | tf_op jit(solution)/shard_map/ppermute | solution.py:394
  38.0 2.4 %collective-permute-start.13 = (bf16[64,768]{1,0:T(8,128)(2,1)S(1)}, bf16[64,768]{1,0:T(8,128)(2,1)S(1)}, u32[]{:S(2)}, u32[]{:S(2)}) collective-permute-start(bf16[64,768]{1,0:T(8,128)(2,1)S(1)} %collective-permute-done.9.refs_1_), channel_id=1, source_target_pairs={{0,1},{1,0},{2,3},{3,2},{4,5},{5,4},{6,7},{7,6},{8,9},{9,8},{10,11... | collective-permute-start | bytes 294920 | tf_op jit(solution)/shard_map/ppermute | solution.py:394
  40.4 1.2 %collective-permute-done.10.refs_2_ = bf16[64,768]{1,0:T(8,128)(2,1)S(1)} collective-permute-done((bf16[64,768]{1,0:T(8,128)(2,1)S(1)}, bf16[64,768]{1,0:T(8,128)(2,1)S(1)}, u32[]{:S(2)}, u32[]{:S(2)}) %collective-permute-start.10) | collective-permute-done | bytes 98336 | tf_op jit(solution)/shard_map/ppermute | solution.py:408
  41.6 0.2 collective-permute-start.14
  41.8 0.6 collective-permute-start.15
  42.4 0.5 collective-permute-done.14.refs_6_
  42.9 0.5 collective-permute-done.15.refs_7_
  43.4 0.0 copy-start.3
  43.4 2.8 %column_attention.1 = (bf16[4,64,384]{2,1,0:T(8,128)(2,1)S(1)}, bf16[4,64,384]{2,1,0:T(8,128)(2,1)S(1)}) custom-call(s32[4]{0:T(128)S(1)} %copy-done.4, s32[128]{0:T(128)S(1)} %copy-done.5, s32[1]{0:T(128)} %bitcast.place_ref, bf16[768,768]{1,0:T(8,128)(2,1)S(1)} %copy-done.6, bf16[768,768]{1,0:T(8,128)(2,1)S(1)} %copy-done.7, ...), custom_call_target="tpu_custom_call" | custom-call | flops 1207959552 | bytes 3538944 | tf_op jit(solution)/shard_map/column_attention/pallas_call | solution.py:515
  46.2 0.4 collective-permute-start.16
  46.7 1.1 %collective-permute-done.16.other_ref = bf16[4,64,384]{2,1,0:T(8,128)(2,1)S(1)} collective-permute-done((bf16[4,64,384]{2,1,0:T(8,128)(2,1)S(1)}, bf16[4,64,384]{2,1,0:T(8,128)(2,1)S(1)}, u32[]{:S(2)}, u32[]{:S(2)}) %collective-permute-start.16) | collective-permute-done | bytes 196640 | tf_op jit(solution)/shard_map/ppermute | solution.py:394
  47.8 0.7 %collective-permute-start.17 = (bf16[64,768]{1,0:T(8,128)(2,1)S(1)}, bf16[64,768]{1,0:T(8,128)(2,1)S(1)}, u32[]{:S(2)}, u32[]{:S(2)}) collective-permute-start(bf16[64,768]{1,0:T(8,128)(2,1)S(1)} %get-tuple-element.51), channel_id=1, source_target_pairs={{0,0},{2,1},{1,2},{3,3},{4,4},{6,5},{5,6},{7,7},{8,8},{10,9},{9,10... | collective-permute-start | bytes 294920 | tf_op jit(solution)/shard_map/ppermute | solution.py:412
  48.5 2.8 %collective-permute-start.18 = (bf16[64,768]{1,0:T(8,128)(2,1)S(1)}, bf16[64,768]{1,0:T(8,128)(2,1)S(1)}, u32[]{:S(2)}, u32[]{:S(2)}) collective-permute-start(bf16[64,768]{1,0:T(8,128)(2,1)S(1)} %get-tuple-element.52), channel_id=1, source_target_pairs={{4,0},{6,1},{5,2},{7,3},{8,4},{10,5},{9,6},{11,7},{12,8},{14,9},{1... | collective-permute-start | bytes 294920 | tf_op jit(solution)/shard_map/ppermute | solution.py:412
  51.2 0.8 %collective-permute-start.19 = (bf16[64,768]{1,0:T(8,128)(2,1)S(1)}, bf16[64,768]{1,0:T(8,128)(2,1)S(1)}, u32[]{:S(2)}, u32[]{:S(2)}) collective-permute-start(bf16[64,768]{1,0:T(8,128)(2,1)S(1)} %get-tuple-element.53), channel_id=1, source_target_pairs={{8,0},{10,1},{9,2},{11,3},{12,4},{14,5},{13,6},{15,7},{0,8},{2,9},... | collective-permute-start | bytes 294920 | tf_op jit(solution)/shard_map/ppermute | solution.py:412
  52.1 1.4 %collective-permute-done.18.refs_1_ = bf16[64,768]{1,0:T(8,128)(2,1)S(1)} collective-permute-done((bf16[64,768]{1,0:T(8,128)(2,1)S(1)}, bf16[64,768]{1,0:T(8,128)(2,1)S(1)}, u32[]{:S(2)}, u32[]{:S(2)}) %collective-permute-start.18) | collective-permute-done | bytes 98336 | tf_op jit(solution)/shard_map/ppermute | solution.py:412
  53.5 6.5 %collective-permute-done.19.refs_2_ = bf16[64,768]{1,0:T(8,128)(2,1)S(1)} collective-permute-done((bf16[64,768]{1,0:T(8,128)(2,1)S(1)}, bf16[64,768]{1,0:T(8,128)(2,1)S(1)}, u32[]{:S(2)}, u32[]{:S(2)}) %collective-permute-start.19) | collective-permute-done | bytes 98336 | tf_op jit(solution)/shard_map/ppermute | solution.py:412
  59.9 0.7 %column_output.1 = (bf16[2,64,768]{2,1,0:T(8,128)(2,1)S(1)}, bf16[2,64,768]{2,1,0:T(8,128)(2,1)S(1)}) custom-call(s32[1]{0:T(128)} %bitcast.place_ref, bf16[768,768]{1,0:T(8,128)(2,1)S(1)} %copy-done.3, bf16[256,768]{1,0:T(8,128)(2,1)S(1)} %get-tuple-element.41.after_ref, bf16[64,768]{1,0:T(8,128)(2,1)S(1)} %collective-permute-done.17.refs_0_, ...), custom_call_target="tpu_custom_call" | custom-call | flops 301989888 | bytes 1179648 | tf_op jit(solution)/shard_map/column_output/pallas_call | solution.py:535
  60.6 2.9 %collective-permute-start.21 = (bf16[2,64,768]{2,1,0:T(8,128)(2,1)S(1)}, bf16[2,64,768]{2,1,0:T(8,128)(2,1)S(1)}, u32[]{:S(2)}, u32[]{:S(2)}) collective-permute-start(bf16[2,64,768]{2,1,0:T(8,128)(2,1)S(1)} %get-tuple-element.56), channel_id=1, source_target_pairs={{0,1},{1,0},{2,3},{3,2},{4,5},{5,4},{6,7},{7,6},{8,9},{9,8},{10,11... | collective-permute-start | bytes 589832 | tf_op jit(solution)/shard_map/ppermute | solution.py:394
  63.5 1.1 %collective-permute-done.21.other_ref = bf16[2,64,768]{2,1,0:T(8,128)(2,1)S(1)} collective-permute-done((bf16[2,64,768]{2,1,0:T(8,128)(2,1)S(1)}, bf16[2,64,768]{2,1,0:T(8,128)(2,1)S(1)}, u32[]{:S(2)}, u32[]{:S(2)}) %collective-permute-start.21) | collective-permute-done | bytes 196640 | tf_op jit(solution)/shard_map/ppermute | solution.py:394
  64.6 0.8 %assemble.1 = bf16[2,128,768]{2,1,0:T(8,128)(2,1)} custom-call(s32[1]{0:T(128)} %bitcast.place_ref, bf16[2,64,768]{2,1,0:T(8,128)(2,1)S(1)} %get-tuple-element.55.mine_ref, bf16[2,64,768]{2,1,0:T(8,128)(2,1)S(1)} %collective-permute-done.21.other_ref), custom_call_target="tpu_custom_call" | custom-call | flops 196608 | bytes 786432 | tf_op jit(solution)/shard_map/assemble/pallas_call | solution.py:544
  (27 shorter events, 0.1 us)
Async XLA Ops:
  0.0 3.4 %copy-start = (bf16[2,128,768]{2,1,0:T(8,128)(2,1)S(1)}, bf16[2,128,768]{2,1,0:T(8,128)(2,1)}, u32[]{:S(2)}) copy-start(bf16[2,128,768]{2,1,0:T(8,128)(2,1)} %param.13) | copy-start | bytes 1179652
  0.0 5.3 %copy-start.2 = (bf16[768,768]{1,0:T(8,128)(2,1)S(1)}, bf16[768,768]{1,0:T(8,128)(2,1)}, u32[]{:S(2)}) copy-start(bf16[768,768]{1,0:T(8,128)(2,1)} %w_ref.3) | copy-start | bytes 3538948
  3.4 1.9 %collective-permute-start.6 = (bf16[256,768]{1,0:T(8,128)(2,1)S(1)}, bf16[256,768]{1,0:T(8,128)(2,1)S(1)}, u32[]{:S(2)}, u32[]{:S(2)}) collective-permute-start(bf16[256,768]{1,0:T(8,128)(2,1)S(1)} %bitcast.3), channel_id=1, source_target_pairs={{0,1},{1,0},{2,3},{3,2},{4,5},{5,4},{6,7},{7,6},{8,9},{9,8},{10,11... | collective-permute-start | bytes 1179656 | tf_op jit(solution)/shard_map/ppermute | solution.py:394
  4.0 2.3 %collective-permute-start = (f32[2,32,768]{2,1,0:T(8,128)S(1)}, f32[2,32,768]{2,1,0:T(8,128)S(1)}, u32[]{:S(2)}, u32[]{:S(2)}) collective-permute-start(f32[2,32,768]{2,1,0:T(8,128)S(1)} %get-tuple-element.32), channel_id=1, source_target_pairs={{0,1},{1,0},{2,3},{3,2},{4,5},{5,4},{6,7},{7,6},{8,9},{9,8},{10,11... | collective-permute-start | bytes 589832 | tf_op jit(solution)/shard_map/ppermute | solution.py:394
  5.3 38.1 %copy-start.8 = (bf16[768,768]{1,0:T(8,128)(2,1)S(1)}, bf16[768,768]{1,0:T(8,128)(2,1)}, u32[]{:S(2)}) copy-start(bf16[768,768]{1,0:T(8,128)(2,1)} %wv_ref) | copy-start | bytes 3538948
  5.8 20.3 %copy-start.9 = (f32[768]{0:T(1024)S(1)}, f32[768]{0:T(1024)}, u32[]{:S(2)}) copy-start(f32[768]{0:T(1024)} %param.21) | copy-start | bytes 9220
  5.8 22.9 %copy-start.1 = (bf16[768,768]{1,0:T(8,128)(2,1)S(1)}, bf16[768,768]{1,0:T(8,128)(2,1)}, u32[]{:S(2)}) copy-start(bf16[768,768]{1,0:T(8,128)(2,1)} %w_ref.4) | copy-start | bytes 3538948
  5.8 22.9 %collective-permute-start.7 = (bf16[256,768]{1,0:T(8,128)(2,1)S(1)}, bf16[256,768]{1,0:T(8,128)(2,1)S(1)}, u32[]{:S(2)}, u32[]{:S(2)}) collective-permute-start(bf16[256,768]{1,0:T(8,128)(2,1)S(1)} %get-tuple-element.39.value_ref), channel_id=1, source_target_pairs={{0,1},{1,0},{2,3},{3,2},{4,5},{5,4},{6,7},{7,6},{8,9},{9,8},{10,11... | collective-permute-start | bytes 1179656 | tf_op jit(solution)/shard_map/ppermute | solution.py:394
  6.3 6.0 %collective-permute-start.1 = (f32[32,768]{1,0:T(8,128)S(1)}, f32[32,768]{1,0:T(8,128)S(1)}, u32[]{:S(2)}, u32[]{:S(2)}) collective-permute-start(f32[32,768]{1,0:T(8,128)S(1)} %get-tuple-element.34), channel_id=1, source_target_pairs={{0,2},{1,3},{2,0},{3,1},{4,6},{5,7},{6,4},{7,5},{8,10},{9,11},{10,... | collective-permute-start | bytes 294920 | tf_op jit(solution)/shard_map/ppermute | solution.py:394
  12.4 7.4 %collective-permute-start.4 = (f32[32,768]{1,0:T(8,128)S(1)}, f32[32,768]{1,0:T(8,128)S(1)}, u32[]{:S(2)}, u32[]{:S(2)}) collective-permute-start(f32[32,768]{1,0:T(8,128)S(1)} %add.1.refs_0_), channel_id=1, source_target_pairs={{0,12},{1,13},{2,14},{3,15},{4,8},{5,9},{6,10},{7,11},{8,4},{9,5},... | collective-permute-start | bytes 294920 | tf_op jit(solution)/shard_map/ppermute | solution.py:394
  16.3 8.0 %collective-permute-start.3 = (f32[32,768]{1,0:T(8,128)S(1)}, f32[32,768]{1,0:T(8,128)S(1)}, u32[]{:S(2)}, u32[]{:S(2)}) collective-permute-start(f32[32,768]{1,0:T(8,128)S(1)} %add.1.refs_0_), channel_id=1, source_target_pairs={{0,8},{1,9},{2,10},{3,11},{4,12},{5,13},{6,14},{7,15},{8,0},{9,1},... | collective-permute-start | bytes 294920 | tf_op jit(solution)/shard_map/ppermute | solution.py:394
  16.3 8.0 %collective-permute-start.2 = (f32[32,768]{1,0:T(8,128)S(1)}, f32[32,768]{1,0:T(8,128)S(1)}, u32[]{:S(2)}, u32[]{:S(2)}) collective-permute-start(f32[32,768]{1,0:T(8,128)S(1)} %add.1.refs_0_), channel_id=1, source_target_pairs={{0,4},{1,5},{2,6},{3,7},{4,0},{5,1},{6,2},{7,3},{8,12},{9,13},{10,... | collective-permute-start | bytes 294920 | tf_op jit(solution)/shard_map/ppermute | solution.py:394
  24.6 4.2 %collective-permute-start.5 = (bf16[32,768]{1,0:T(8,128)(2,1)S(1)}, bf16[32,768]{1,0:T(8,128)(2,1)S(1)}, u32[]{:S(2)}, u32[]{:S(2)}) collective-permute-start(bf16[32,768]{1,0:T(8,128)(2,1)S(1)} %row_softmax.1.mine_ref), channel_id=1, source_target_pairs={{0,2},{1,3},{2,0},{3,1},{4,6},{5,7},{6,4},{7,5},{8,10},{9,11},{10,... | collective-permute-start | bytes 147464 | tf_op jit(solution)/shard_map/ppermute | solution.py:394
  28.7 14.6 %copy-start.4 = (s32[4]{0:T(128)S(1)}, s32[4]{0:T(128)}, u32[]{:S(2)}) copy-start(s32[4]{0:T(128)} %depth_ref.1) | copy-start | bytes 52
  28.7 14.6 %copy-start.5 = (s32[128]{0:T(128)S(1)}, s32[128]{0:T(128)}, u32[]{:S(2)}) copy-start(s32[128]{0:T(128)} %prot_ref.1) | copy-start | bytes 1540
  28.7 14.6 %copy-start.6 = (bf16[768,768]{1,0:T(8,128)(2,1)S(1)}, bf16[768,768]{1,0:T(8,128)(2,1)}, u32[]{:S(2)}) copy-start(bf16[768,768]{1,0:T(8,128)(2,1)} %wq_ref) | copy-start | bytes 3538948
  28.7 14.6 %copy-start.7 = (bf16[768,768]{1,0:T(8,128)(2,1)S(1)}, bf16[768,768]{1,0:T(8,128)(2,1)}, u32[]{:S(2)}) copy-start(bf16[768,768]{1,0:T(8,128)(2,1)} %wk_ref) | copy-start | bytes 3538948
  30.0 4.6 %collective-permute-start.8 = (bf16[64,768]{1,0:T(8,128)(2,1)S(1)}, bf16[64,768]{1,0:T(8,128)(2,1)S(1)}, u32[]{:S(2)}, u32[]{:S(2)}) collective-permute-start(bf16[64,768]{1,0:T(8,128)(2,1)S(1)} %get-tuple-element.45), channel_id=1, source_target_pairs={{0,0},{1,2},{2,1},{3,3},{4,4},{5,6},{6,5},{7,7},{8,8},{9,10},{10,9... | collective-permute-start | bytes 294920 | tf_op jit(solution)/shard_map/ppermute | solution.py:408
  30.6 7.4 %collective-permute-start.9 = (bf16[64,768]{1,0:T(8,128)(2,1)S(1)}, bf16[64,768]{1,0:T(8,128)(2,1)S(1)}, u32[]{:S(2)}, u32[]{:S(2)}) collective-permute-start(bf16[64,768]{1,0:T(8,128)(2,1)S(1)} %get-tuple-element.46), channel_id=1, source_target_pairs={{0,4},{1,6},{2,5},{3,7},{4,8},{5,10},{6,9},{7,11},{8,12},{9,14},{1... | collective-permute-start | bytes 294920 | tf_op jit(solution)/shard_map/ppermute | solution.py:408
  31.2 10.4 %collective-permute-start.10 = (bf16[64,768]{1,0:T(8,128)(2,1)S(1)}, bf16[64,768]{1,0:T(8,128)(2,1)S(1)}, u32[]{:S(2)}, u32[]{:S(2)}) collective-permute-start(bf16[64,768]{1,0:T(8,128)(2,1)S(1)} %get-tuple-element.47), channel_id=1, source_target_pairs={{0,8},{1,10},{2,9},{3,11},{4,12},{5,14},{6,13},{7,15},{8,0},{9,2},... | collective-permute-start | bytes 294920 | tf_op jit(solution)/shard_map/ppermute | solution.py:408
  33.8 8.0 %collective-permute-start.11 = (bf16[64,768]{1,0:T(8,128)(2,1)S(1)}, bf16[64,768]{1,0:T(8,128)(2,1)S(1)}, u32[]{:S(2)}, u32[]{:S(2)}) collective-permute-start(bf16[64,768]{1,0:T(8,128)(2,1)S(1)} %get-tuple-element.48), channel_id=1, source_target_pairs={{0,12},{1,14},{2,13},{3,15},{4,0},{5,2},{6,1},{7,3},{8,4},{9,6},{1... | collective-permute-start | bytes 294920 | tf_op jit(solution)/shard_map/ppermute | solution.py:408
  34.5 7.9 %collective-permute-start.12 = (bf16[64,768]{1,0:T(8,128)(2,1)S(1)}, bf16[64,768]{1,0:T(8,128)(2,1)S(1)}, u32[]{:S(2)}, u32[]{:S(2)}) collective-permute-start(bf16[64,768]{1,0:T(8,128)(2,1)S(1)} %collective-permute-done.8.refs_0_), channel_id=1, source_target_pairs={{0,1},{1,0},{2,3},{3,2},{4,5},{5,4},{6,7},{7,6},{8,9},{9,8},{10,11... | collective-permute-start | bytes 294920 | tf_op jit(solution)/shard_map/ppermute | solution.py:394
  38.0 4.4 %collective-permute-start.13 = (bf16[64,768]{1,0:T(8,128)(2,1)S(1)}, bf16[64,768]{1,0:T(8,128)(2,1)S(1)}, u32[]{:S(2)}, u32[]{:S(2)}) collective-permute-start(bf16[64,768]{1,0:T(8,128)(2,1)S(1)} %collective-permute-done.9.refs_1_), channel_id=1, source_target_pairs={{0,1},{1,0},{2,3},{3,2},{4,5},{5,4},{6,7},{7,6},{8,9},{9,8},{10,11... | collective-permute-start | bytes 294920 | tf_op jit(solution)/shard_map/ppermute | solution.py:394
  41.6 1.3 %collective-permute-start.14 = (bf16[64,768]{1,0:T(8,128)(2,1)S(1)}, bf16[64,768]{1,0:T(8,128)(2,1)S(1)}, u32[]{:S(2)}, u32[]{:S(2)}) collective-permute-start(bf16[64,768]{1,0:T(8,128)(2,1)S(1)} %collective-permute-done.10.refs_2_), channel_id=1, source_target_pairs={{0,1},{1,0},{2,3},{3,2},{4,5},{5,4},{6,7},{7,6},{8,9},{9,8},{10,11... | collective-permute-start | bytes 294920 | tf_op jit(solution)/shard_map/ppermute | solution.py:394
  41.8 1.6 %collective-permute-start.15 = (bf16[64,768]{1,0:T(8,128)(2,1)S(1)}, bf16[64,768]{1,0:T(8,128)(2,1)S(1)}, u32[]{:S(2)}, u32[]{:S(2)}) collective-permute-start(bf16[64,768]{1,0:T(8,128)(2,1)S(1)} %collective-permute-done.11.refs_3_), channel_id=1, source_target_pairs={{0,1},{1,0},{2,3},{3,2},{4,5},{5,4},{6,7},{7,6},{8,9},{9,8},{10,11... | collective-permute-start | bytes 294920 | tf_op jit(solution)/shard_map/ppermute | solution.py:394
  43.4 16.5 %copy-start.3 = (bf16[768,768]{1,0:T(8,128)(2,1)S(1)}, bf16[768,768]{1,0:T(8,128)(2,1)}, u32[]{:S(2)}) copy-start(bf16[768,768]{1,0:T(8,128)(2,1)} %w_ref.5) | copy-start | bytes 3538948
  46.2 1.5 %collective-permute-start.16 = (bf16[4,64,384]{2,1,0:T(8,128)(2,1)S(1)}, bf16[4,64,384]{2,1,0:T(8,128)(2,1)S(1)}, u32[]{:S(2)}, u32[]{:S(2)}) collective-permute-start(bf16[4,64,384]{2,1,0:T(8,128)(2,1)S(1)} %get-tuple-element.50), channel_id=1, source_target_pairs={{0,1},{1,0},{2,3},{3,2},{4,5},{5,4},{6,7},{7,6},{8,9},{9,8},{10,11... | collective-permute-start | bytes 589832 | tf_op jit(solution)/shard_map/ppermute | solution.py:394
  47.8 4.3 %collective-permute-start.17 = (bf16[64,768]{1,0:T(8,128)(2,1)S(1)}, bf16[64,768]{1,0:T(8,128)(2,1)S(1)}, u32[]{:S(2)}, u32[]{:S(2)}) collective-permute-start(bf16[64,768]{1,0:T(8,128)(2,1)S(1)} %get-tuple-element.51), channel_id=1, source_target_pairs={{0,0},{2,1},{1,2},{3,3},{4,4},{6,5},{5,6},{7,7},{8,8},{10,9},{9,10... | collective-permute-start | bytes 294920 | tf_op jit(solution)/shard_map/ppermute | solution.py:412
  48.5 5.0 %collective-permute-start.18 = (bf16[64,768]{1,0:T(8,128)(2,1)S(1)}, bf16[64,768]{1,0:T(8,128)(2,1)S(1)}, u32[]{:S(2)}, u32[]{:S(2)}) collective-permute-start(bf16[64,768]{1,0:T(8,128)(2,1)S(1)} %get-tuple-element.52), channel_id=1, source_target_pairs={{4,0},{6,1},{5,2},{7,3},{8,4},{10,5},{9,6},{11,7},{12,8},{14,9},{1... | collective-permute-start | bytes 294920 | tf_op jit(solution)/shard_map/ppermute | solution.py:412
  51.2 8.7 %collective-permute-start.19 = (bf16[64,768]{1,0:T(8,128)(2,1)S(1)}, bf16[64,768]{1,0:T(8,128)(2,1)S(1)}, u32[]{:S(2)}, u32[]{:S(2)}) collective-permute-start(bf16[64,768]{1,0:T(8,128)(2,1)S(1)} %get-tuple-element.53), channel_id=1, source_target_pairs={{8,0},{10,1},{9,2},{11,3},{12,4},{14,5},{13,6},{15,7},{0,8},{2,9},... | collective-permute-start | bytes 294920 | tf_op jit(solution)/shard_map/ppermute | solution.py:412
  52.1 7.8 %collective-permute-start.20 = (bf16[64,768]{1,0:T(8,128)(2,1)S(1)}, bf16[64,768]{1,0:T(8,128)(2,1)S(1)}, u32[]{:S(2)}, u32[]{:S(2)}) collective-permute-start(bf16[64,768]{1,0:T(8,128)(2,1)S(1)} %get-tuple-element.54), channel_id=1, source_target_pairs={{12,0},{14,1},{13,2},{15,3},{0,4},{2,5},{1,6},{3,7},{4,8},{6,9},{5... | collective-permute-start | bytes 294920 | tf_op jit(solution)/shard_map/ppermute | solution.py:412
  60.6 4.0 %collective-permute-start.21 = (bf16[2,64,768]{2,1,0:T(8,128)(2,1)S(1)}, bf16[2,64,768]{2,1,0:T(8,128)(2,1)S(1)}, u32[]{:S(2)}, u32[]{:S(2)}) collective-permute-start(bf16[2,64,768]{2,1,0:T(8,128)(2,1)S(1)} %get-tuple-element.56), channel_id=1, source_target_pairs={{0,1},{1,0},{2,3},{3,2},{4,5},{5,4},{6,7},{7,6},{8,9},{9,8},{10,11... | collective-permute-start | bytes 589832 | tf_op jit(solution)/shard_map/ppermute | solution.py:394

commit v6 on v5

--- a/solution.py
+++ b/solution.py
@@ -117,6 +117,7 @@
     even, odd = half_masks(256)
     quarter = columns // PLANE
     core = (place_ref[0] % 2) == 0
+    own = keep_ref.shape[1]
     for copy in copies[4:]:
         copy.wait()
     for n in range(width // 256):
@@ -144,26 +145,32 @@
             for y in range(PLANE // 2):
                 start = 2 * y * quarter
                 left, right = folded[start : start + quarter], folded[start + quarter : start + 2 * quarter]
-                keep_ref[y, :, out] = jnp.where(core, left, right)
-                send_ref[y, :, out] = jnp.where(core, right, left)
-
-
-def core_sum_kernel(place_ref, mine_ref, other_ref, keep_ref, send_ref):
-    row = (place_ref[0] // 2) % 2
-    keep_ref[...] = mine_ref[row] + other_ref[row]
-    send_ref[...] = mine_ref[1 - row] + other_ref[1 - row]
+                for target, value in ((keep_ref, jnp.where(core, left, right)), (send_ref, jnp.where(core, right, left))):
+                    for i in range(quarter // own):
+                        target[y * (quarter // own) + i, :, out] = value[i * own : (i + 1) * own]
+
+
+def core_sum_kernel(place_ref, mine_ref, other_ref, *outs):
+    plane, planes = place_ref[0] // PLANE, len(outs)
+    for s, out in enumerate(outs):
+        index = (plane + s) % planes
+        out[...] = mine_ref[index] + other_ref[index]
 
 
 def add_kernel(*refs):
-    total = refs[0][...] + refs[1][...]
-    if len(refs) == 5:
-        total = total + (refs[2][...] + refs[3][...])
-    refs[-1][...] = total
-
-
-def row_value_kernel(columns, place_ref, x_ref, w_ref, mine_ref, other_ref, out_ref, spread_ref):
+    parts = [ref[...] for ref in refs[:-1]]
+    while len(parts) > 1:
+        parts = [a + b for a, b in zip(parts[::2], parts[1::2])]
+    refs[-1][...] = parts[0]
+
+
+def row_value_kernel(
+    columns, place_ref, x_ref, w_ref, gain_ref, mine_ref, other_ref, out_ref, next_ref, spread_ref
+):
     core = place_ref[0] % 2
     out_ref[...] = dot(x_ref[...], w_ref[...]).astype(BF16)
+    normed = norm(other_ref[...].astype(F32), gain_ref[...]).astype(BF16)
+    next_ref[...] = dot(normed, w_ref[...]).astype(BF16)
     rows = x_ref.shape[0] // columns
     quarter = columns // PLANE
     for source, index in ((mine_ref, core), (other_ref, 1 - core)):
@@ -176,19 +183,21 @@
                     spread_ref[p, target, :] = piece[:, 128 * p : 128 * p + 128]
 
 
-def row_softmax_kernel(scale, place_ref, *refs):
-    part_refs, (same_ref, out_ref, mask_ref) = refs[:-3], refs[-3:]
-    tile, width = out_ref.shape
+def row_softmax_kernel(scale, place_ref, mine_ref, other_ref, same_ref, out_ref, mask_ref):
+    own, width = out_ref.shape
+    columns = same_ref.shape[0]
+    quarter, local = columns // PLANE, columns // 2
+    line, plane = (place_ref[0] // 2) % 2, place_ref[0] // PLANE
     same = same_ref[...]
-    mask_ref[...] = jnp.maximum(same, pltpu.roll(same, 64, 1))
-    live = mask_ref[pl.ds((place_ref[0] % PLANE) * tile, tile), :] > 0.5
-    low = iota((tile, 128), 1) < 64
+    mask = jnp.maximum(same, pltpu.roll(same, 64, 1))
+    for i in range(columns // own):
+        mask_ref[i] = mask[i * own : (i + 1) * own]
+    first = plane * own
+    live = mask_ref[(first % quarter + quarter * line + local * (first // quarter)) // own] > 0.5
+    low = iota((own, 128), 1) < 64
     for p in range(width // 128):
         lanes = slice(128 * p, 128 * p + 128)
-        parts = [part[:, lanes] for part in part_refs]
-        while len(parts) > 1:
-            parts = [a + b for a, b in zip(parts[::2], parts[1::2])]
-        tied = jnp.where(live, parts[0] * scale, NEG)
+        tied = jnp.where(live, (mine_ref[:, lanes] + other_ref[:, lanes]) * scale, NEG)
         top_low = jnp.max(jnp.where(low, tied, 2 * NEG), axis=1, keepdims=True)
         top_high = jnp.max(jnp.where(low, 2 * NEG, tied), axis=1, keepdims=True)
         value = jnp.exp(tied - jnp.where(low, top_low, top_high))
@@ -198,27 +207,28 @@
 
 
 def row_output_kernel(
+    steps,
     place_ref,
-    mine_ref,
-    across_ref,
     same_ref,
     value_ref,
     other_ref,
     x_ref,
     w_ref,
     gain_ref,
-    after_ref,
     *refs,
 ):
-    outs, (mixed_ref, folded_ref, normed_ref) = refs[:-3], refs[-3:]
+    planes = (len(refs) - 4) // 2
+    pieces, after_ref, outs = refs[:planes], refs[planes], refs[planes + 1 : -3]
+    mixed_ref, folded_ref, normed_ref = refs[-3:]
     columns = same_ref.shape[0]
     tokens, width = after_ref.shape
     rows = tokens // columns
     quarter, local = columns // PLANE, columns // 2
     place = place_ref[0]
-    core, line, plane = place % 2, (place // 2) % 2, place // PLANE
-    folded_ref[pl.ds(pl.multiple_of(line * quarter, quarter), quarter), :] = mine_ref[...].astype(F32)
-    folded_ref[pl.ds(pl.multiple_of((1 - line) * quarter, quarter), quarter), :] = across_ref[...].astype(F32)
+    core, plane = place % 2, place // PLANE
+    own = local // planes
+    for s, piece in zip(steps, pieces):
+        folded_ref[(plane + planes - s) % planes] = piece[...].astype(F32)
     same = [
         same_ref[pl.ds(pl.multiple_of(y * local + core * quarter, quarter), quarter), :] for y in range(2)
     ]
@@ -229,7 +239,7 @@
     spots = [core * rows + r for r in range(rows)] + [(1 - core) * rows + r for r in range(rows)]
     for p in range(width // 128):
         lanes = slice(128 * p, 128 * p + 128)
-        piece = folded_ref[:, lanes]
+        piece = folded_ref[:, :, lanes].reshape(local, 128)
         turned = pltpu.roll(piece, 64, 1)
         one = jnp.where(same, jnp.where(low, piece, turned), 0.0)
         two = jnp.where(same, jnp.where(low, turned, piece), 0.0)
@@ -255,7 +265,8 @@
         out[...] = normed_ref[pl.ds(start, size), :].astype(BF16)
 
 
-def column_kernel(scale, planes, columns, depth_ref, prot_ref, place_ref, wq_ref, wk_ref, wv_ref, *refs):
+def column_kernel(scale, steps, columns, depth_ref, prot_ref, place_ref, wq_ref, wk_ref, wv_ref, *refs):
+    planes = len(steps)
     ins, (keep_ref, send_ref, all_ref, mixed_ref) = refs[: 2 * planes], refs[2 * planes :]
     size, width = ins[0].shape
     wide = width // 2
@@ -294,7 +305,7 @@
             depth = jnp.where(lane == c, depth_ref[prot_ref[column]], depth)
         live = []
         for i in range(slots):
-            away = ((plane + planes - i % planes) % planes) * 2 + (core if i < planes else 1 - core)
+            away = ((plane + planes - steps[i % planes]) % planes) * 2 + (core if i < planes else 1 - core)
             live.append((fits & (level % rows + away * rows < depth))[None])
         lives.append(jnp.concatenate([jnp.where(l, 1.0, 0.0) for l in live], axis=0) > 0.5)
     packs, values = [], []
@@ -345,16 +356,16 @@
         write(other_ref, keep_ref)
 
 
-def column_output_kernel(place_ref, w_ref, after_ref, *refs):
+def column_output_kernel(steps, place_ref, w_ref, after_ref, *refs):
     ins, (keep_ref, send_ref, total_ref) = refs[:-3], refs[-3:]
     rows, local, _ = keep_ref.shape
     core, plane = place_ref[0] % 2, place_ref[0] // PLANE
     size = ins[0].shape[0]
     total = dot(jnp.concatenate([source[...] for source in ins], axis=0), w_ref[...])
-    for s in range(len(ins)):
+    for i, s in enumerate(steps):
         start = pl.multiple_of(((plane + s) % len(ins)) * size, size)
         for p in range(total.shape[1] // 128):
-            total_ref[p, pl.ds(start, size), :] = total[s * size : (s + 1) * size, 128 * p : 128 * p + 128]
+            total_ref[p, pl.ds(start, size), :] = total[i * size : (i + 1) * size, 128 * p : 128 * p + 128]
     for p in range(total.shape[1] // 128):
         lanes = slice(128 * p, 128 * p + 128)
         total_ref[p] = total_ref[p] + after_ref[:, lanes].astype(F32)
@@ -402,6 +413,10 @@
             for k in range(2):
                 pairs.append((z * PLANE + 2 * y + k, (z + step) % planes * PLANE + 2 * k + y))
     return pairs
+
+
+def far_first(planes):
+    return sorted(range(planes), key=lambda s: (-min(s, planes - s), s))
 
 
 def spin(array, step):
@@ -435,13 +450,15 @@
     tokens = rows * columns
     planes, local = devices // PLANE, columns // 2
     size = tokens // planes
+    sum_steps = move_steps = back_steps = far_first(planes)
+    share_steps = far_first(planes)
+    share_steps = share_steps[1:] + share_steps[:1]
     x = alignment.reshape(tokens, width)
     shape = jax.ShapeDtypeStruct
     square = 2 * tokens * width * width
 
-    quarter = columns // PLANE
-    half = shape((PLANE // 2, quarter, width), F32)
-    part = shape((quarter, width), F32)
+    half = shape((planes, local // planes, width), F32)
+    part = shape((local // planes, width), F32)
     keep, send, normed, same = call(
         row_scores_kernel,
         (half, half, shape((tokens, width), BF16), shape((columns, columns), F32)),
@@ -462,58 +479,58 @@
     column_query, column_key, column_value, late, normed = lax.optimization_barrier(
         (column_query, column_key, column_value, x, normed)
     )
+    other = swap(send, 1)
     sibling = swap(late, 1)
-    value, spread = call(
+    pieces = call(
+        core_sum_kernel,
+        (part,) * planes,
+        "svv",
+        "v" * planes,
+        [],
+        (columns * width, 6 * columns * width, 0),
+        "core_sum",
+    )(place, keep, other)
+    (total,) = call(
+        add_kernel, (part,), "v" * planes, "v", [], (columns * width, 2 * columns * width, 0), "add"
+    )(*[spin(pieces[s], s) for s in sum_steps])
+    value, value_other, spread = call(
         functools.partial(row_value_kernel, columns),
-        (shape((tokens, width), BF16), shape((width // 128, tokens, 128), F32)),
-        "svvvv",
-        "vv",
+        (shape((tokens, width), BF16),) * 2 + (shape((width // 128, tokens, 128), F32),),
+        "svvvvv",
+        "vvv",
         [],
-        (square, 2 * width * width, 0),
+        (2 * square, 2 * width * width, 0),
         "row_value",
-    )(place, normed, row_value, late, sibling)
-    value_other = swap(value, 1)
-    keep, send = call(
-        core_sum_kernel, (part, part), "svv", "vv", [], (columns * width, 6 * columns * width, 0), "core_sum"
-    )(place, keep, swap(send, 1))
-    parts = [keep, swap(send, 2)]
-    stride, left = PLANE, planes
-    while left > 1:
-        ways = 4 if left % 4 == 0 else 2
-        (total,) = call(
-            add_kernel, (part,), "v" * len(parts), "v", [], (columns * width, 6 * columns * width, 0), "add"
-        )(*parts)
-        parts = [total] + [swap(total, stride * w) for w in range(1, ways)]
-        stride, left = stride * ways, left // ways
+    )(place, normed, row_value, row_gain[None], late, sibling)
     (weights,) = call(
         functools.partial(row_softmax_kernel, 1.0 / (math.sqrt(head_size) * math.sqrt(total_rows))),
-        (shape((quarter, width), BF16),),
-        "s" + "v" * len(parts) + "v",
+        (shape((local // planes, width), BF16),),
+        "svvv",
         "v",
-        [pltpu.VMEM((columns, columns), F32)],
-        (columns * width, 6 * columns * width, quarter * width),
+        [pltpu.VMEM((columns * planes // local, local // planes, columns), F32)],
+        (columns * width, 2 * columns * width, columns * width // 8),
         "row_softmax",
-    )(place, *parts, same)
-    across = swap(weights, 2)
+    )(place, total, swap(total, 1), same)
+    shared = [spin(weights, s) for s in share_steps]
     after, *blocks = call(
-        row_output_kernel,
+        functools.partial(row_output_kernel, share_steps),
         (shape((tokens, width), BF16),) + (shape((size, width), BF16),) * planes,
-        "s" + "v" * 8,
+        "s" + "v" * (6 + planes),
         "v" * (1 + planes),
         [
             pltpu.VMEM((width // 128, tokens, 128), F32),
-            pltpu.VMEM((local, width), F32),
+            pltpu.VMEM((planes, local // planes, width), F32),
             pltpu.VMEM((tokens, width), F32),
         ],
         (square, 2 * width * width, tokens),
         "row_output",
-    )(place, weights, across, same, value, value_other, spread, row_output, column_gain[None])
-    moved = [spin(block, s) for s, block in enumerate(blocks)]
+    )(place, same, value, value_other, spread, row_output, column_gain[None], *shared)
+    moved = [spin(blocks[s], s) for s in move_steps]
     moved += [swap(block, 1) for block in moved]
     wide = width // 2
     halves = shape((planes, size, wide), BF16)
     keep, send = call(
-        functools.partial(column_kernel, 1.0 / math.sqrt(head_size), planes, columns),
+        functools.partial(column_kernel, 1.0 / math.sqrt(head_size), move_steps, columns),
         (halves, halves),
         "sss" + "v" * (3 + 2 * planes),
         "vv",
@@ -530,10 +547,10 @@
         (tokens * width, 4 * tokens * width, 0),
         "join",
     )(place, keep, swap(send, 1))
-    returned = [spin_back(block, s) for s, block in enumerate(joined)]
+    returned = [spin_back(joined[move_steps.index(s)], s) for s in back_steps]
     half = shape((rows, local, width), BF16)
     keep, send = call(
-        column_output_kernel,
+        functools.partial(column_output_kernel, back_steps),
         (half, half),
         "svv" + "v" * planes,
         "vv",

time: 65.5 us -> 63.9 us (0.976)
  waiting for transfers between devices: 26.6 us -> 15.4 us
  starting transfers between devices: 28.8 us -> 37.8 us
    ppermute x4 -> x12, starting transfers between devices: 4.55 us -> 18.6 us  [spin(): return lax.ppermute(array, 'seq', spin_pairs(step))]
    ppermute x14 -> x9, waiting for transfers between devices: 17.6 us -> 5.5 us  [swap(): return lax.ppermute(array, 'seq', [(i, i ^ offset) for i in range(devices)])]
    ppermute x14 -> x9, starting transfers between devices: 20 us -> 16.4 us  [swap(): return lax.ppermute(array, 'seq', [(i, i ^ offset) for i in range(devices)])]
    ppermute x4 -> x12, waiting for transfers between devices: 1.17 us -> 2.75 us  [spin(): return lax.ppermute(array, 'seq', spin_pairs(step))]
    ppermute x4, starting transfers between devices: 4.3 us -> 2.8 us  [spin_back(): return lax.ppermute(array, 'seq', [(b, a) for a, b in spin_pairs(step)])]
    ppermute x4, waiting for transfers between devices: 7.84 us -> 7.19 us  [spin_back(): return lax.ppermute(array, 'seq', [(b, a) for a, b in spin_pairs(step)])]
  transfers between devices with their start and end apart: 22 -> 25, of which waited for: 12 -> 11; matrix products, arithmetic and copies ran while one was open for 0% -> 0% of each run, Pallas kernels for 1% -> 2%
where the time goes in v6:
time: 63.9 us; the launch traced here: 63.7 us
  starting transfers between devices  37.8 us (59%)
  waiting for transfers between devices  15.4 us (24%)
  Pallas kernels  10.1 us (16%)
    ppermute x12, starting transfers between devices, spin(): return lax.ppermute(array, 'seq', spin_pairs(step))  18.6 us
    ppermute x9, starting transfers between devices, swap(): return lax.ppermute(array, 'seq', [(i, i ^ offset) for i in range(devices)])  16.4 us
    ppermute x4, waiting for transfers between devices, spin_back(): return lax.ppermute(array, 'seq', [(b, a) for a, b in spin_pairs(step)])  7.19 us
    ppermute x9, waiting for transfers between devices, swap(): return lax.ppermute(array, 'seq', [(i, i ^ offset) for i in range(devices)])  5.5 us
    pallas_call x1, Pallas kernels, per_device(): call(row_scores_kernel, (half, half, shape((tokens, width), BF16), shape(...  3.41 us
    pallas_call x1, Pallas kernels, per_device(): call(functools.partial(column_kernel, 1.0 / math.sqrt(head_size), move_st...  2.82 us
    ppermute x4, starting transfers between devices, spin_back(): return lax.ppermute(array, 'seq', [(b, a) for a, b in spin_pairs(step)])  2.8 us
    ppermute x12, waiting for transfers between devices, spin(): return lax.ppermute(array, 'seq', spin_pairs(step))  2.75 us
  transfers between devices with their start and end apart: 25, of which 11 were waited for; matrix products, arithmetic and copies ran while one was open for 0% of the time, Pallas kernels for 2%

profile of v6, /device:TPU:0, one launch (start us, length us, event | category | flops | bytes accessed | tf_op | source)
XLA Modules:
  0.0 63.7 jit_solution(5068990536204083095)
XLA Ops:
  0.0 3.4 %row_scores.1 = (f32[4,16,768]{2,1,0:T(8,128)S(1)}, f32[4,16,768]{2,1,0:T(8,128)S(1)}, bf16[256,768]{1,0:T(8,128)(2,1)S(1)}, f32[128,128]{1,0:T(8,128)S(1)}) custom-call(s32[4]{0:T(128)} %depth_ref.1, s32[1]{0:T(128)} %bitcast.place_ref, bf16[256,768]{1,0:T(8,128)(2,1)} %bitcast.2, f32[768]{0:T(1024)} %gain_hbm.1, s32[128]{0:T(128)} %prot_ref.1, ...), custom_call_target="tpu_custom_call" | custom-call | flops 603979776 | bytes 2359296 | tf_op jit(solution)/shard_map/row_scores/pallas_call | solution.py:462
  3.4 0.5 collective-permute-start
  4.0 0.1 collective-permute-start.1
  4.0 1.6 %collective-permute-done.1.other_ref = f32[4,16,768]{2,1,0:T(8,128)S(1)} collective-permute-done((f32[4,16,768]{2,1,0:T(8,128)S(1)}, f32[4,16,768]{2,1,0:T(8,128)S(1)}, u32[]{:S(2)}, u32[]{:S(2)}) %collective-permute-start.1) | collective-permute-done | bytes 196640 | tf_op jit(solution)/shard_map/ppermute | solution.py:405
  5.6 4.0 %collective-permute-start.2 = (f32[16,768]{1,0:T(8,128)S(1)}, f32[16,768]{1,0:T(8,128)S(1)}, u32[]{:S(2)}, u32[]{:S(2)}) collective-permute-start(f32[16,768]{1,0:T(8,128)S(1)} %get-tuple-element.43), channel_id=1, source_target_pairs={{0,8},{1,10},{2,9},{3,11},{4,12},{5,14},{6,13},{7,15},{8,0},{9,2},... | collective-permute-start | bytes 147464 | tf_op jit(solution)/shard_map/ppermute | solution.py:423
  9.7 1.6 %collective-permute-start.3 = (f32[16,768]{1,0:T(8,128)S(1)}, f32[16,768]{1,0:T(8,128)S(1)}, u32[]{:S(2)}, u32[]{:S(2)}) collective-permute-start(f32[16,768]{1,0:T(8,128)S(1)} %get-tuple-element.44), channel_id=1, source_target_pairs={{0,4},{1,6},{2,5},{3,7},{4,8},{5,10},{6,9},{7,11},{8,12},{9,14},{1... | collective-permute-start | bytes 147464 | tf_op jit(solution)/shard_map/ppermute | solution.py:423
  11.2 2.2 %collective-permute-start.4 = (f32[16,768]{1,0:T(8,128)S(1)}, f32[16,768]{1,0:T(8,128)S(1)}, u32[]{:S(2)}, u32[]{:S(2)}) collective-permute-start(f32[16,768]{1,0:T(8,128)S(1)} %get-tuple-element.45), channel_id=1, source_target_pairs={{0,12},{1,14},{2,13},{3,15},{4,0},{5,2},{6,1},{7,3},{8,4},{9,6},{1... | collective-permute-start | bytes 147464 | tf_op jit(solution)/shard_map/ppermute | solution.py:423
  13.5 0.7 %collective-permute-start.5 = (f32[16,768]{1,0:T(8,128)S(1)}, f32[16,768]{1,0:T(8,128)S(1)}, u32[]{:S(2)}, u32[]{:S(2)}) collective-permute-start(f32[16,768]{1,0:T(8,128)S(1)} %get-tuple-element.46), channel_id=1, source_target_pairs={{0,0},{1,2},{2,1},{3,3},{4,4},{5,6},{6,5},{7,7},{8,8},{9,10},{10,9... | collective-permute-start | bytes 147464 | tf_op jit(solution)/shard_map/ppermute | solution.py:423
  14.1 2.0 %collective-permute-done.3.refs_1_ = f32[16,768]{1,0:T(8,128)S(1)} collective-permute-done((f32[16,768]{1,0:T(8,128)S(1)}, f32[16,768]{1,0:T(8,128)S(1)}, u32[]{:S(2)}, u32[]{:S(2)}) %collective-permute-start.3) | collective-permute-done | bytes 49184 | tf_op jit(solution)/shard_map/ppermute | solution.py:423
  16.2 0.4 collective-permute-done.4.refs_2_
  16.5 4.1 %collective-permute-start.6 = (f32[16,768]{1,0:T(8,128)S(1)}, f32[16,768]{1,0:T(8,128)S(1)}, u32[]{:S(2)}, u32[]{:S(2)}) collective-permute-start(f32[16,768]{1,0:T(8,128)S(1)} %add.1.mine_ref), channel_id=1, source_target_pairs={{0,1},{1,0},{2,3},{3,2},{4,5},{5,4},{6,7},{7,6},{8,9},{9,8},{10,11... | collective-permute-start | bytes 147464 | tf_op jit(solution)/shard_map/ppermute | solution.py:405
  20.7 0.9 %collective-permute-done.6.other_ref = f32[16,768]{1,0:T(8,128)S(1)} collective-permute-done((f32[16,768]{1,0:T(8,128)S(1)}, f32[16,768]{1,0:T(8,128)S(1)}, u32[]{:S(2)}, u32[]{:S(2)}) %collective-permute-start.6) | collective-permute-done | bytes 49184 | tf_op jit(solution)/shard_map/ppermute | solution.py:405
  21.5 0.3 row_softmax.1
  21.8 0.0 copy-start.1
  21.8 0.1 collective-permute-start.10
  21.9 0.6 collective-permute-start.7
  22.5 3.2 %collective-permute-start.8 = (bf16[16,768]{1,0:T(8,128)(2,1)S(1)}, bf16[16,768]{1,0:T(8,128)(2,1)S(1)}, u32[]{:S(2)}, u32[]{:S(2)}) collective-permute-start(bf16[16,768]{1,0:T(8,128)(2,1)S(1)} %row_softmax.1), channel_id=1, source_target_pairs={{0,12},{1,14},{2,13},{3,15},{4,0},{5,2},{6,1},{7,3},{8,4},{9,6},{1... | collective-permute-start | bytes 73736 | tf_op jit(solution)/shard_map/ppermute | solution.py:423
  25.8 0.7 %collective-permute-start.9 = (bf16[16,768]{1,0:T(8,128)(2,1)S(1)}, bf16[16,768]{1,0:T(8,128)(2,1)S(1)}, u32[]{:S(2)}, u32[]{:S(2)}) collective-permute-start(bf16[16,768]{1,0:T(8,128)(2,1)S(1)} %row_softmax.1), channel_id=1, source_target_pairs={{0,0},{1,2},{2,1},{3,3},{4,4},{5,6},{6,5},{7,7},{8,8},{9,10},{10,9... | collective-permute-start | bytes 73736 | tf_op jit(solution)/shard_map/ppermute | solution.py:423
  26.5 0.0 copy-start.8
  26.5 0.9 %row_value.1 = (bf16[256,768]{1,0:T(8,128)(2,1)S(1)}, bf16[256,768]{1,0:T(8,128)(2,1)S(1)}, f32[6,256,128]{2,1,0:T(8,128)S(1)}) custom-call(s32[1]{0:T(128)} %bitcast.place_ref, bf16[256,768]{1,0:T(8,128)(2,1)S(1)} %get-tuple-element.36.x_ref, bf16[768,768]{1,0:T(8,128)(2,1)S(1)} %copy-done.3, f32[1,768]{1,0:T(1,128)S(1)} %broadcast_in_dim.10.gain_ref, ...), custom_call_target="tpu_custom_call" | custom-call | flops 603979776 | bytes 1179648 | tf_op jit(solution)/shard_map/row_value/pallas_call | solution.py:496
  27.4 0.3 collective-permute-done.7.refs_0_
  27.7 0.0 copy-start.4
  27.7 0.0 copy-start.5
  27.7 1.2 %row_output.1 = (bf16[256,768]{1,0:T(8,128)(2,1)S(1)}, bf16[64,768]{1,0:T(8,128)(2,1)S(1)}, bf16[64,768]{1,0:T(8,128)(2,1)S(1)}, bf16[64,768]{1,0:T(8,128)(2,1)S(1)}, bf16[64,768]{1,0:T(8,128)(2,1)S(1)}) custom-call(s32[1]{0:T(128)} %bitcast.place_ref, f32[128,128]{1,0:T(8,128)S(1)} %get-tuple-element.34.same_ref, ...), custom_call_target="tpu_custom_call" | custom-call | flops 301989888 | bytes 1179648 | tf_op jit(solution)/shard_map/row_output/pallas_call | solution.py:515
  29.0 1.0 %collective-permute-start.11 = (bf16[64,768]{1,0:T(8,128)(2,1)S(1)}, bf16[64,768]{1,0:T(8,128)(2,1)S(1)}, u32[]{:S(2)}, u32[]{:S(2)}) collective-permute-start(bf16[64,768]{1,0:T(8,128)(2,1)S(1)} %get-tuple-element.51), channel_id=1, source_target_pairs={{0,8},{1,10},{2,9},{3,11},{4,12},{5,14},{6,13},{7,15},{8,0},{9,2},... | collective-permute-start | bytes 294920 | tf_op jit(solution)/shard_map/ppermute | solution.py:423
  30.0 3.3 %collective-permute-start.12 = (bf16[64,768]{1,0:T(8,128)(2,1)S(1)}, bf16[64,768]{1,0:T(8,128)(2,1)S(1)}, u32[]{:S(2)}, u32[]{:S(2)}) collective-permute-start(bf16[64,768]{1,0:T(8,128)(2,1)S(1)} %get-tuple-element.52), channel_id=1, source_target_pairs={{0,4},{1,6},{2,5},{3,7},{4,8},{5,10},{6,9},{7,11},{8,12},{9,14},{1... | collective-permute-start | bytes 294920 | tf_op jit(solution)/shard_map/ppermute | solution.py:423
  33.3 0.5 collective-permute-start.13
  33.8 0.7 %collective-permute-start.14 = (bf16[64,768]{1,0:T(8,128)(2,1)S(1)}, bf16[64,768]{1,0:T(8,128)(2,1)S(1)}, u32[]{:S(2)}, u32[]{:S(2)}) collective-permute-start(bf16[64,768]{1,0:T(8,128)(2,1)S(1)} %get-tuple-element.54), channel_id=1, source_target_pairs={{0,0},{1,2},{2,1},{3,3},{4,4},{5,6},{6,5},{7,7},{8,8},{9,10},{10,9... | collective-permute-start | bytes 294920 | tf_op jit(solution)/shard_map/ppermute | solution.py:423
  34.5 0.1 collective-permute-done.11.refs_0_
  34.5 7.0 %collective-permute-start.15 = (bf16[64,768]{1,0:T(8,128)(2,1)S(1)}, bf16[64,768]{1,0:T(8,128)(2,1)S(1)}, u32[]{:S(2)}, u32[]{:S(2)}) collective-permute-start(bf16[64,768]{1,0:T(8,128)(2,1)S(1)} %collective-permute-done.11.refs_0_), channel_id=1, source_target_pairs={{0,1},{1,0},{2,3},{3,2},{4,5},{5,4},{6,7},{7,6},{8,9},{9,8},{10,11... | collective-permute-start | bytes 294920 | tf_op jit(solution)/shard_map/ppermute | solution.py:405
  41.5 0.2 collective-permute-start.16
  41.7 0.3 collective-permute-start.17
  42.1 3.2 %collective-permute-start.18 = (bf16[64,768]{1,0:T(8,128)(2,1)S(1)}, bf16[64,768]{1,0:T(8,128)(2,1)S(1)}, u32[]{:S(2)}, u32[]{:S(2)}) collective-permute-start(bf16[64,768]{1,0:T(8,128)(2,1)S(1)} %collective-permute-done.14.refs_3_), channel_id=1, source_target_pairs={{0,1},{1,0},{2,3},{3,2},{4,5},{5,4},{6,7},{7,6},{8,9},{9,8},{10,11... | collective-permute-start | bytes 294920 | tf_op jit(solution)/shard_map/ppermute | solution.py:405
  45.2 0.9 %collective-permute-done.18.refs_7_ = bf16[64,768]{1,0:T(8,128)(2,1)S(1)} collective-permute-done((bf16[64,768]{1,0:T(8,128)(2,1)S(1)}, bf16[64,768]{1,0:T(8,128)(2,1)S(1)}, u32[]{:S(2)}, u32[]{:S(2)}) %collective-permute-start.18) | collective-permute-done | bytes 98336 | tf_op jit(solution)/shard_map/ppermute | solution.py:405
  46.2 2.8 %column_attention.1 = (bf16[4,64,384]{2,1,0:T(8,128)(2,1)S(1)}, bf16[4,64,384]{2,1,0:T(8,128)(2,1)S(1)}) custom-call(s32[4]{0:T(128)S(1)} %copy-done.4, s32[128]{0:T(128)S(1)} %copy-done.5, s32[1]{0:T(128)} %bitcast.place_ref, bf16[768,768]{1,0:T(8,128)(2,1)S(1)} %copy-done.6, bf16[768,768]{1,0:T(8,128)(2,1)S(1)} %copy-done.7, ...), custom_call_target="tpu_custom_call" | custom-call | flops 1207959552 | bytes 3538944 | tf_op jit(solution)/shard_map/column_attention/pallas_call | solution.py:532
  49.0 0.4 collective-permute-start.19
  49.5 1.1 %collective-permute-done.19.other_ref = bf16[4,64,384]{2,1,0:T(8,128)(2,1)S(1)} collective-permute-done((bf16[4,64,384]{2,1,0:T(8,128)(2,1)S(1)}, bf16[4,64,384]{2,1,0:T(8,128)(2,1)S(1)}, u32[]{:S(2)}, u32[]{:S(2)}) %collective-permute-start.19) | collective-permute-done | bytes 196640 | tf_op jit(solution)/shard_map/ppermute | solution.py:405
  50.6 0.1 collective-permute-start.20
  50.7 1.4 %collective-permute-start.21 = (bf16[64,768]{1,0:T(8,128)(2,1)S(1)}, bf16[64,768]{1,0:T(8,128)(2,1)S(1)}, u32[]{:S(2)}, u32[]{:S(2)}) collective-permute-start(bf16[64,768]{1,0:T(8,128)(2,1)S(1)} %get-tuple-element.58), channel_id=1, source_target_pairs={{4,0},{6,1},{5,2},{7,3},{8,4},{10,5},{9,6},{11,7},{12,8},{14,9},{1... | collective-permute-start | bytes 294920 | tf_op jit(solution)/shard_map/ppermute | solution.py:427
  52.1 0.7 %collective-permute-start.22 = (bf16[64,768]{1,0:T(8,128)(2,1)S(1)}, bf16[64,768]{1,0:T(8,128)(2,1)S(1)}, u32[]{:S(2)}, u32[]{:S(2)}) collective-permute-start(bf16[64,768]{1,0:T(8,128)(2,1)S(1)} %get-tuple-element.59), channel_id=1, source_target_pairs={{12,0},{14,1},{13,2},{15,3},{0,4},{2,5},{1,6},{3,7},{4,8},{6,9},{5... | collective-permute-start | bytes 294920 | tf_op jit(solution)/shard_map/ppermute | solution.py:427
  52.8 0.7 %collective-permute-start.23 = (bf16[64,768]{1,0:T(8,128)(2,1)S(1)}, bf16[64,768]{1,0:T(8,128)(2,1)S(1)}, u32[]{:S(2)}, u32[]{:S(2)}) collective-permute-start(bf16[64,768]{1,0:T(8,128)(2,1)S(1)} %get-tuple-element.60), channel_id=1, source_target_pairs={{0,0},{2,1},{1,2},{3,3},{4,4},{6,5},{5,6},{7,7},{8,8},{10,9},{9,10... | collective-permute-start | bytes 294920 | tf_op jit(solution)/shard_map/ppermute | solution.py:427
  53.4 4.4 %collective-permute-done.20.refs_0_ = bf16[64,768]{1,0:T(8,128)(2,1)S(1)} collective-permute-done((bf16[64,768]{1,0:T(8,128)(2,1)S(1)}, bf16[64,768]{1,0:T(8,128)(2,1)S(1)}, u32[]{:S(2)}, u32[]{:S(2)}) %collective-permute-start.20) | collective-permute-done | bytes 98336 | tf_op jit(solution)/shard_map/ppermute | solution.py:427
  57.8 0.0 collective-permute-done.21.refs_1_
  57.9 2.7 %collective-permute-done.22.refs_2_ = bf16[64,768]{1,0:T(8,128)(2,1)S(1)} collective-permute-done((bf16[64,768]{1,0:T(8,128)(2,1)S(1)}, bf16[64,768]{1,0:T(8,128)(2,1)S(1)}, u32[]{:S(2)}, u32[]{:S(2)}) %collective-permute-start.22) | collective-permute-done | bytes 98336 | tf_op jit(solution)/shard_map/ppermute | solution.py:427
  60.6 0.7 %column_output.1 = (bf16[2,64,768]{2,1,0:T(8,128)(2,1)S(1)}, bf16[2,64,768]{2,1,0:T(8,128)(2,1)S(1)}) custom-call(s32[1]{0:T(128)} %bitcast.place_ref, bf16[768,768]{1,0:T(8,128)(2,1)S(1)} %copy-done.2, bf16[256,768]{1,0:T(8,128)(2,1)S(1)} %get-tuple-element.47.after_ref, bf16[64,768]{1,0:T(8,128)(2,1)S(1)} %collective-permute-done.20.refs_0_, ...), custom_call_target="tpu_custom_call" | custom-call | flops 301989888 | bytes 1179648 | tf_op jit(solution)/shard_map/column_output/pallas_call | solution.py:552
  61.3 0.6 collective-permute-start.24
  61.8 1.1 %collective-permute-done.24.other_ref = bf16[2,64,768]{2,1,0:T(8,128)(2,1)S(1)} collective-permute-done((bf16[2,64,768]{2,1,0:T(8,128)(2,1)S(1)}, bf16[2,64,768]{2,1,0:T(8,128)(2,1)S(1)}, u32[]{:S(2)}, u32[]{:S(2)}) %collective-permute-start.24) | collective-permute-done | bytes 196640 | tf_op jit(solution)/shard_map/ppermute | solution.py:405
  62.9 0.8 %assemble.1 = bf16[2,128,768]{2,1,0:T(8,128)(2,1)} custom-call(s32[1]{0:T(128)} %bitcast.place_ref, bf16[2,64,768]{2,1,0:T(8,128)(2,1)S(1)} %get-tuple-element.61.mine_ref, bf16[2,64,768]{2,1,0:T(8,128)(2,1)S(1)} %collective-permute-done.24.other_ref), custom_call_target="tpu_custom_call" | custom-call | flops 196608 | bytes 786432 | tf_op jit(solution)/shard_map/assemble/pallas_call | solution.py:561
  (36 shorter events, 0.2 us)
Async XLA Ops:
  0.0 3.4 %copy-start = (bf16[2,128,768]{2,1,0:T(8,128)(2,1)S(1)}, bf16[2,128,768]{2,1,0:T(8,128)(2,1)}, u32[]{:S(2)}) copy-start(bf16[2,128,768]{2,1,0:T(8,128)(2,1)} %param.13) | copy-start | bytes 1179652
  0.0 20.6 %copy-start.9 = (f32[768]{0:T(1024)S(1)}, f32[768]{0:T(1024)}, u32[]{:S(2)}) copy-start(f32[768]{0:T(1024)} %gain_hbm.1) | copy-start | bytes 9220
  0.0 20.6 %copy-start.10 = (f32[768]{0:T(1024)S(1)}, f32[768]{0:T(1024)}, u32[]{:S(2)}) copy-start(f32[768]{0:T(1024)} %param.21) | copy-start | bytes 9220
  0.0 26.4 %copy-start.3 = (bf16[768,768]{1,0:T(8,128)(2,1)S(1)}, bf16[768,768]{1,0:T(8,128)(2,1)}, u32[]{:S(2)}) copy-start(bf16[768,768]{1,0:T(8,128)(2,1)} %w_ref.3) | copy-start | bytes 3538948
  3.4 23.0 %collective-permute-start = (bf16[256,768]{1,0:T(8,128)(2,1)S(1)}, bf16[256,768]{1,0:T(8,128)(2,1)S(1)}, u32[]{:S(2)}, u32[]{:S(2)}) collective-permute-start(bf16[256,768]{1,0:T(8,128)(2,1)S(1)} %bitcast.3), channel_id=1, source_target_pairs={{0,1},{1,0},{2,3},{3,2},{4,5},{5,4},{6,7},{7,6},{8,9},{9,8},{10,11... | collective-permute-start | bytes 1179656 | tf_op jit(solution)/shard_map/ppermute | solution.py:405
  4.0 1.6 %collective-permute-start.1 = (f32[4,16,768]{2,1,0:T(8,128)S(1)}, f32[4,16,768]{2,1,0:T(8,128)S(1)}, u32[]{:S(2)}, u32[]{:S(2)}) collective-permute-start(f32[4,16,768]{2,1,0:T(8,128)S(1)} %get-tuple-element.42), channel_id=1, source_target_pairs={{0,1},{1,0},{2,3},{3,2},{4,5},{5,4},{6,7},{7,6},{8,9},{9,8},{10,11... | collective-permute-start | bytes 589832 | tf_op jit(solution)/shard_map/ppermute | solution.py:405
  5.6 8.5 %collective-permute-start.2 = (f32[16,768]{1,0:T(8,128)S(1)}, f32[16,768]{1,0:T(8,128)S(1)}, u32[]{:S(2)}, u32[]{:S(2)}) collective-permute-start(f32[16,768]{1,0:T(8,128)S(1)} %get-tuple-element.43), channel_id=1, source_target_pairs={{0,8},{1,10},{2,9},{3,11},{4,12},{5,14},{6,13},{7,15},{8,0},{9,2},... | collective-permute-start | bytes 147464 | tf_op jit(solution)/shard_map/ppermute | solution.py:423
  9.7 6.5 %collective-permute-start.3 = (f32[16,768]{1,0:T(8,128)S(1)}, f32[16,768]{1,0:T(8,128)S(1)}, u32[]{:S(2)}, u32[]{:S(2)}) collective-permute-start(f32[16,768]{1,0:T(8,128)S(1)} %get-tuple-element.44), channel_id=1, source_target_pairs={{0,4},{1,6},{2,5},{3,7},{4,8},{5,10},{6,9},{7,11},{8,12},{9,14},{1... | collective-permute-start | bytes 147464 | tf_op jit(solution)/shard_map/ppermute | solution.py:423
  11.2 5.3 %collective-permute-start.4 = (f32[16,768]{1,0:T(8,128)S(1)}, f32[16,768]{1,0:T(8,128)S(1)}, u32[]{:S(2)}, u32[]{:S(2)}) collective-permute-start(f32[16,768]{1,0:T(8,128)S(1)} %get-tuple-element.45), channel_id=1, source_target_pairs={{0,12},{1,14},{2,13},{3,15},{4,0},{5,2},{6,1},{7,3},{8,4},{9,6},{1... | collective-permute-start | bytes 147464 | tf_op jit(solution)/shard_map/ppermute | solution.py:423
  13.5 3.1 %collective-permute-start.5 = (f32[16,768]{1,0:T(8,128)S(1)}, f32[16,768]{1,0:T(8,128)S(1)}, u32[]{:S(2)}, u32[]{:S(2)}) collective-permute-start(f32[16,768]{1,0:T(8,128)S(1)} %get-tuple-element.46), channel_id=1, source_target_pairs={{0,0},{1,2},{2,1},{3,3},{4,4},{5,6},{6,5},{7,7},{8,8},{9,10},{10,9... | collective-permute-start | bytes 147464 | tf_op jit(solution)/shard_map/ppermute | solution.py:423
  16.5 5.0 %collective-permute-start.6 = (f32[16,768]{1,0:T(8,128)S(1)}, f32[16,768]{1,0:T(8,128)S(1)}, u32[]{:S(2)}, u32[]{:S(2)}) collective-permute-start(f32[16,768]{1,0:T(8,128)S(1)} %add.1.mine_ref), channel_id=1, source_target_pairs={{0,1},{1,0},{2,3},{3,2},{4,5},{5,4},{6,7},{7,6},{8,9},{9,8},{10,11... | collective-permute-start | bytes 147464 | tf_op jit(solution)/shard_map/ppermute | solution.py:405
  21.8 5.9 %copy-start.1 = (bf16[768,768]{1,0:T(8,128)(2,1)S(1)}, bf16[768,768]{1,0:T(8,128)(2,1)}, u32[]{:S(2)}) copy-start(bf16[768,768]{1,0:T(8,128)(2,1)} %w_ref.4) | copy-start | bytes 3538948
  21.8 5.6 %collective-permute-start.10 = (bf16[16,768]{1,0:T(8,128)(2,1)S(1)}, bf16[16,768]{1,0:T(8,128)(2,1)S(1)}, u32[]{:S(2)}, u32[]{:S(2)}) collective-permute-start(bf16[16,768]{1,0:T(8,128)(2,1)S(1)} %row_softmax.1), channel_id=1, source_target_pairs={{0,8},{1,10},{2,9},{3,11},{4,12},{5,14},{6,13},{7,15},{8,0},{9,2},... | collective-permute-start | bytes 73736 | tf_op jit(solution)/shard_map/ppermute | solution.py:423
  21.9 5.8 %collective-permute-start.7 = (bf16[16,768]{1,0:T(8,128)(2,1)S(1)}, bf16[16,768]{1,0:T(8,128)(2,1)S(1)}, u32[]{:S(2)}, u32[]{:S(2)}) collective-permute-start(bf16[16,768]{1,0:T(8,128)(2,1)S(1)} %row_softmax.1), channel_id=1, source_target_pairs={{0,4},{1,6},{2,5},{3,7},{4,8},{5,10},{6,9},{7,11},{8,12},{9,14},{1... | collective-permute-start | bytes 73736 | tf_op jit(solution)/shard_map/ppermute | solution.py:423
  22.5 5.2 %collective-permute-start.8 = (bf16[16,768]{1,0:T(8,128)(2,1)S(1)}, bf16[16,768]{1,0:T(8,128)(2,1)S(1)}, u32[]{:S(2)}, u32[]{:S(2)}) collective-permute-start(bf16[16,768]{1,0:T(8,128)(2,1)S(1)} %row_softmax.1), channel_id=1, source_target_pairs={{0,12},{1,14},{2,13},{3,15},{4,0},{5,2},{6,1},{7,3},{8,4},{9,6},{1... | collective-permute-start | bytes 73736 | tf_op jit(solution)/shard_map/ppermute | solution.py:423
  25.8 1.9 %collective-permute-start.9 = (bf16[16,768]{1,0:T(8,128)(2,1)S(1)}, bf16[16,768]{1,0:T(8,128)(2,1)S(1)}, u32[]{:S(2)}, u32[]{:S(2)}) collective-permute-start(bf16[16,768]{1,0:T(8,128)(2,1)S(1)} %row_softmax.1), channel_id=1, source_target_pairs={{0,0},{1,2},{2,1},{3,3},{4,4},{5,6},{6,5},{7,7},{8,8},{9,10},{10,9... | collective-permute-start | bytes 73736 | tf_op jit(solution)/shard_map/ppermute | solution.py:423
  26.5 19.7 %copy-start.8 = (bf16[768,768]{1,0:T(8,128)(2,1)S(1)}, bf16[768,768]{1,0:T(8,128)(2,1)}, u32[]{:S(2)}) copy-start(bf16[768,768]{1,0:T(8,128)(2,1)} %wv_ref) | copy-start | bytes 3538948
  27.7 18.5 %copy-start.4 = (s32[4]{0:T(128)S(1)}, s32[4]{0:T(128)}, u32[]{:S(2)}) copy-start(s32[4]{0:T(128)} %depth_ref.1) | copy-start | bytes 52
  27.7 18.5 %copy-start.5 = (s32[128]{0:T(128)S(1)}, s32[128]{0:T(128)}, u32[]{:S(2)}) copy-start(s32[128]{0:T(128)} %prot_ref.1) | copy-start | bytes 1540
  27.7 18.5 %copy-start.6 = (bf16[768,768]{1,0:T(8,128)(2,1)S(1)}, bf16[768,768]{1,0:T(8,128)(2,1)}, u32[]{:S(2)}) copy-start(bf16[768,768]{1,0:T(8,128)(2,1)} %wq_ref) | copy-start | bytes 3538948
  27.7 18.5 %copy-start.7 = (bf16[768,768]{1,0:T(8,128)(2,1)S(1)}, bf16[768,768]{1,0:T(8,128)(2,1)}, u32[]{:S(2)}) copy-start(bf16[768,768]{1,0:T(8,128)(2,1)} %wk_ref) | copy-start | bytes 3538948
  29.0 5.6 %collective-permute-start.11 = (bf16[64,768]{1,0:T(8,128)(2,1)S(1)}, bf16[64,768]{1,0:T(8,128)(2,1)S(1)}, u32[]{:S(2)}, u32[]{:S(2)}) collective-permute-start(bf16[64,768]{1,0:T(8,128)(2,1)S(1)} %get-tuple-element.51), channel_id=1, source_target_pairs={{0,8},{1,10},{2,9},{3,11},{4,12},{5,14},{6,13},{7,15},{8,0},{9,2},... | collective-permute-start | bytes 294920 | tf_op jit(solution)/shard_map/ppermute | solution.py:423
  30.0 11.6 %collective-permute-start.12 = (bf16[64,768]{1,0:T(8,128)(2,1)S(1)}, bf16[64,768]{1,0:T(8,128)(2,1)S(1)}, u32[]{:S(2)}, u32[]{:S(2)}) collective-permute-start(bf16[64,768]{1,0:T(8,128)(2,1)S(1)} %get-tuple-element.52), channel_id=1, source_target_pairs={{0,4},{1,6},{2,5},{3,7},{4,8},{5,10},{6,9},{7,11},{8,12},{9,14},{1... | collective-permute-start | bytes 294920 | tf_op jit(solution)/shard_map/ppermute | solution.py:423
  33.3 8.4 %collective-permute-start.13 = (bf16[64,768]{1,0:T(8,128)(2,1)S(1)}, bf16[64,768]{1,0:T(8,128)(2,1)S(1)}, u32[]{:S(2)}, u32[]{:S(2)}) collective-permute-start(bf16[64,768]{1,0:T(8,128)(2,1)S(1)} %get-tuple-element.53), channel_id=1, source_target_pairs={{0,12},{1,14},{2,13},{3,15},{4,0},{5,2},{6,1},{7,3},{8,4},{9,6},{1... | collective-permute-start | bytes 294920 | tf_op jit(solution)/shard_map/ppermute | solution.py:423
  33.8 8.3 %collective-permute-start.14 = (bf16[64,768]{1,0:T(8,128)(2,1)S(1)}, bf16[64,768]{1,0:T(8,128)(2,1)S(1)}, u32[]{:S(2)}, u32[]{:S(2)}) collective-permute-start(bf16[64,768]{1,0:T(8,128)(2,1)S(1)} %get-tuple-element.54), channel_id=1, source_target_pairs={{0,0},{1,2},{2,1},{3,3},{4,4},{5,6},{6,5},{7,7},{8,8},{9,10},{10,9... | collective-permute-start | bytes 294920 | tf_op jit(solution)/shard_map/ppermute | solution.py:423
  34.5 10.7 %collective-permute-start.15 = (bf16[64,768]{1,0:T(8,128)(2,1)S(1)}, bf16[64,768]{1,0:T(8,128)(2,1)S(1)}, u32[]{:S(2)}, u32[]{:S(2)}) collective-permute-start(bf16[64,768]{1,0:T(8,128)(2,1)S(1)} %collective-permute-done.11.refs_0_), channel_id=1, source_target_pairs={{0,1},{1,0},{2,3},{3,2},{4,5},{5,4},{6,7},{7,6},{8,9},{9,8},{10,11... | collective-permute-start | bytes 294920 | tf_op jit(solution)/shard_map/ppermute | solution.py:405
  41.5 3.7 %collective-permute-start.16 = (bf16[64,768]{1,0:T(8,128)(2,1)S(1)}, bf16[64,768]{1,0:T(8,128)(2,1)S(1)}, u32[]{:S(2)}, u32[]{:S(2)}) collective-permute-start(bf16[64,768]{1,0:T(8,128)(2,1)S(1)} %collective-permute-done.12.refs_1_), channel_id=1, source_target_pairs={{0,1},{1,0},{2,3},{3,2},{4,5},{5,4},{6,7},{7,6},{8,9},{9,8},{10,11... | collective-permute-start | bytes 294920 | tf_op jit(solution)/shard_map/ppermute | solution.py:405
  41.7 3.5 %collective-permute-start.17 = (bf16[64,768]{1,0:T(8,128)(2,1)S(1)}, bf16[64,768]{1,0:T(8,128)(2,1)S(1)}, u32[]{:S(2)}, u32[]{:S(2)}) collective-permute-start(bf16[64,768]{1,0:T(8,128)(2,1)S(1)} %collective-permute-done.13.refs_2_), channel_id=1, source_target_pairs={{0,1},{1,0},{2,3},{3,2},{4,5},{5,4},{6,7},{7,6},{8,9},{9,8},{10,11... | collective-permute-start | bytes 294920 | tf_op jit(solution)/shard_map/ppermute | solution.py:405
  42.1 4.1 %collective-permute-start.18 = (bf16[64,768]{1,0:T(8,128)(2,1)S(1)}, bf16[64,768]{1,0:T(8,128)(2,1)S(1)}, u32[]{:S(2)}, u32[]{:S(2)}) collective-permute-start(bf16[64,768]{1,0:T(8,128)(2,1)S(1)} %collective-permute-done.14.refs_3_), channel_id=1, source_target_pairs={{0,1},{1,0},{2,3},{3,2},{4,5},{5,4},{6,7},{7,6},{8,9},{9,8},{10,11... | collective-permute-start | bytes 294920 | tf_op jit(solution)/shard_map/ppermute | solution.py:405
  46.2 14.4 %copy-start.2 = (bf16[768,768]{1,0:T(8,128)(2,1)S(1)}, bf16[768,768]{1,0:T(8,128)(2,1)}, u32[]{:S(2)}) copy-start(bf16[768,768]{1,0:T(8,128)(2,1)} %w_ref.5) | copy-start | bytes 3538948
  49.0 1.5 %collective-permute-start.19 = (bf16[4,64,384]{2,1,0:T(8,128)(2,1)S(1)}, bf16[4,64,384]{2,1,0:T(8,128)(2,1)S(1)}, u32[]{:S(2)}, u32[]{:S(2)}) collective-permute-start(bf16[4,64,384]{2,1,0:T(8,128)(2,1)S(1)} %get-tuple-element.56), channel_id=1, source_target_pairs={{0,1},{1,0},{2,3},{3,2},{4,5},{5,4},{6,7},{7,6},{8,9},{9,8},{10,11... | collective-permute-start | bytes 589832 | tf_op jit(solution)/shard_map/ppermute | solution.py:405
  50.6 7.2 %collective-permute-start.20 = (bf16[64,768]{1,0:T(8,128)(2,1)S(1)}, bf16[64,768]{1,0:T(8,128)(2,1)S(1)}, u32[]{:S(2)}, u32[]{:S(2)}) collective-permute-start(bf16[64,768]{1,0:T(8,128)(2,1)S(1)} %get-tuple-element.57), channel_id=1, source_target_pairs={{8,0},{10,1},{9,2},{11,3},{12,4},{14,5},{13,6},{15,7},{0,8},{2,9},... | collective-permute-start | bytes 294920 | tf_op jit(solution)/shard_map/ppermute | solution.py:427
  50.7 7.2 %collective-permute-start.21 = (bf16[64,768]{1,0:T(8,128)(2,1)S(1)}, bf16[64,768]{1,0:T(8,128)(2,1)S(1)}, u32[]{:S(2)}, u32[]{:S(2)}) collective-permute-start(bf16[64,768]{1,0:T(8,128)(2,1)S(1)} %get-tuple-element.58), channel_id=1, source_target_pairs={{4,0},{6,1},{5,2},{7,3},{8,4},{10,5},{9,6},{11,7},{12,8},{14,9},{1... | collective-permute-start | bytes 294920 | tf_op jit(solution)/shard_map/ppermute | solution.py:427
  52.1 8.5 %collective-permute-start.22 = (bf16[64,768]{1,0:T(8,128)(2,1)S(1)}, bf16[64,768]{1,0:T(8,128)(2,1)S(1)}, u32[]{:S(2)}, u32[]{:S(2)}) collective-permute-start(bf16[64,768]{1,0:T(8,128)(2,1)S(1)} %get-tuple-element.59), channel_id=1, source_target_pairs={{12,0},{14,1},{13,2},{15,3},{0,4},{2,5},{1,6},{3,7},{4,8},{6,9},{5... | collective-permute-start | bytes 294920 | tf_op jit(solution)/shard_map/ppermute | solution.py:427
  52.8 7.9 %collective-permute-start.23 = (bf16[64,768]{1,0:T(8,128)(2,1)S(1)}, bf16[64,768]{1,0:T(8,128)(2,1)S(1)}, u32[]{:S(2)}, u32[]{:S(2)}) collective-permute-start(bf16[64,768]{1,0:T(8,128)(2,1)S(1)} %get-tuple-element.60), channel_id=1, source_target_pairs={{0,0},{2,1},{1,2},{3,3},{4,4},{6,5},{5,6},{7,7},{8,8},{10,9},{9,10... | collective-permute-start | bytes 294920 | tf_op jit(solution)/shard_map/ppermute | solution.py:427
  61.3 1.6 %collective-permute-start.24 = (bf16[2,64,768]{2,1,0:T(8,128)(2,1)S(1)}, bf16[2,64,768]{2,1,0:T(8,128)(2,1)S(1)}, u32[]{:S(2)}, u32[]{:S(2)}) collective-permute-start(bf16[2,64,768]{2,1,0:T(8,128)(2,1)S(1)} %get-tuple-element.62), channel_id=1, source_target_pairs={{0,1},{1,0},{2,3},{3,2},{4,5},{5,4},{6,7},{7,6},{8,9},{9,8},{10,11... | collective-permute-start | bytes 589832 | tf_op jit(solution)/shard_map/ppermute | solution.py:405

commit v7 on v6

--- a/solution.py
+++ b/solution.py
@@ -63,30 +63,41 @@
     return jnp.where(low, 1.0, 0.0), jnp.where(low, 0.0, 1.0)
 
 
-def row_scores_kernel(
-    depth_hbm,
+def own_columns(array, core, quarter):
+    pieces = []
+    for y in range(PLANE // 2):
+        left, right = (array[(2 * y + k) * quarter : (2 * y + k + 1) * quarter] for k in range(2))
+        pieces.append(jnp.where(core, left, right))
+    return jnp.concatenate(pieces, axis=0)
+
+
+def query_tokens(normed_ref, place_ref, columns):
+    quarter = columns // PLANE
+    core = place_ref[0] % 2
+    pieces = []
+    for start in range(0, normed_ref.shape[0], columns // 2):
+        pieces.append(normed_ref[pl.ds(pl.multiple_of(start + core * quarter, quarter), quarter), :])
+    return jnp.concatenate(pieces, axis=0)
+
+
+def row_own_kernel(
+    columns,
     place_ref,
     x_hbm,
     gain_hbm,
-    prot_hbm,
     wq_hbm,
     wk_hbm,
-    keep_ref,
-    send_ref,
     normed_ref,
-    same_ref,
-    depth_ref,
+    query_ref,
+    key_ref,
+    wq_ref,
+    wk_ref,
     x_ref,
     gain_ref,
-    prot_ref,
-    wq_ref,
-    wk_ref,
     sems,
 ):
-    columns = prot_ref.shape[0]
     tokens, width = x_ref.shape
-    rows = tokens // columns
-    pairs = [(x_hbm, x_ref), (gain_hbm, gain_ref), (prot_hbm, prot_ref), (depth_hbm, depth_ref)]
+    pairs = [(x_hbm, x_ref), (gain_hbm, gain_ref)]
     for n in range(width // 256):
         for source, target in ((wq_hbm, wq_ref), (wk_hbm, wk_ref)):
             pairs.append((source.at[256 * n : 256 * n + 256], target.at[256 * n : 256 * n + 256]))
@@ -95,10 +106,33 @@
         copy.start()
     for copy in copies[:2]:
         copy.wait()
-    normed = norm(x_ref[...].astype(F32), gain_ref[...].reshape(1, width)).astype(BF16)
-    normed_ref[...] = normed
-    for copy in copies[2:4]:
+    normed_ref[...] = norm(x_ref[...].astype(F32), gain_ref[...].reshape(1, width)).astype(BF16)
+    for copy in copies[2:]:
         copy.wait()
+    query_ref[...] = dot(query_tokens(normed_ref, place_ref, columns), wq_ref[...]).astype(BF16)
+    key_ref[...] = dot(normed_ref[...], wk_ref[...]).astype(BF16)
+
+
+def row_scores_kernel(
+    depth_ref,
+    place_ref,
+    x_ref,
+    gain_ref,
+    prot_ref,
+    wq_ref,
+    wk_ref,
+    query_ref,
+    key_ref,
+    *refs,
+):
+    outs, (normed_ref, same_ref, part_ref) = refs[:-3], refs[-3:]
+    columns = prot_ref.shape[0]
+    tokens, width = x_ref.shape
+    rows, local, quarter = tokens // columns, columns // 2, columns // PLANE
+    planes, own = part_ref.shape[:2]
+    place = place_ref[0]
+    core = (place % 2) == 0
+    normed_ref[...] = norm(x_ref[...].astype(F32), gain_ref[...].reshape(1, width)).astype(BF16)
     prot = prot_ref[...].reshape(1, columns).astype(F32)
     depth = jnp.zeros((1, columns), F32)
     for p in range(depth_ref.shape[0]):
@@ -108,53 +142,43 @@
     same = jnp.broadcast_to(prot_col, (columns, columns)) == jnp.broadcast_to(prot, (columns, columns))
     same_f = jnp.where(same, 1.0, 0.0)
     same_ref[...] = same_f
-    low = iota((columns, columns), 1) < 64
-    first = jnp.where(low, same_f, pltpu.roll(same_f, 64, 1)) > 0.5
-    valid = [
-        jnp.where((place_ref[0] * rows + r).astype(F32) < depth_col, 1.0, 0.0) for r in range(rows)
-    ]
-    valid = jnp.concatenate(valid, axis=0)
+    same_l = own_columns(same_f, core, quarter)
+    depth_l = own_columns(depth_col, core, quarter)
+    low = iota((local, columns), 1) < 64
+    first = jnp.where(low, same_l, pltpu.roll(same_l, 64, 1)) > 0.5
     even, odd = half_masks(256)
-    quarter = columns // PLANE
-    core = (place_ref[0] % 2) == 0
-    own = keep_ref.shape[1]
-    for copy in copies[4:]:
-        copy.wait()
+    other = place + 1 - 2 * (place % 2)
+    ids = [place * rows + r for r in range(rows)] + [other * rows + r for r in range(rows)]
+    seen_q = [jnp.where(i.astype(F32) < depth_l, 1.0, 0.0) for i in ids]
+    seen_k = [jnp.where(i.astype(F32) < depth_col, 1.0, 0.0) for i in ids]
+    tokens_q = query_tokens(normed_ref, place_ref, columns)
     for n in range(width // 256):
         cols = slice(256 * n, 256 * n + 256)
-        query = dot(normed, wq_ref[:, cols]).astype(BF16).astype(F32) * valid
-        key = (dot(normed, wk_ref[:, cols]) * valid).astype(BF16)
-        query_even, query_odd = (query * even).astype(BF16), (query * odd).astype(BF16)
+        queries = (query_ref[:, cols].astype(F32), dot(tokens_q, wq_ref[:, cols]).astype(BF16).astype(F32))
+        keys = (key_ref[:, cols].astype(F32), dot(normed_ref[...], wk_ref[:, cols]))
+        query, key = [], []
+        for i in range(2 * rows):
+            r = i % rows
+            query.append(queries[i // rows][r * local : (r + 1) * local] * seen_q[i])
+            key.append((keys[i // rows][r * columns : (r + 1) * columns] * seen_k[i]).astype(BF16))
+        query_sides = [[(q * side).astype(BF16) for q in query] for side in (even, odd)]
         for q in range(2):
             lanes = slice(128 * q, 128 * q + 128)
-
-            def side(array, lanes=lanes):
-                return jnp.concatenate(
-                    [array[r * columns : (r + 1) * columns, lanes] for r in range(rows)], axis=1
-                )
-
-            both = jnp.concatenate([side(query_even), side(query_odd)], axis=0)
-            logits = dot_t(both, side(key))
-            one, two = logits[:columns], logits[columns:]
+            both = [jnp.concatenate([a[:, lanes] for a in side], axis=1) for side in query_sides]
+            both = jnp.concatenate(both, axis=0)
+            logits = dot_t(both, jnp.concatenate([a[:, lanes] for a in key], axis=1))
+            one, two = logits[:local], logits[local:]
             folded = jnp.where(
                 low,
                 jnp.where(first, one, pltpu.roll(one, 64, 1)),
                 jnp.where(first, pltpu.roll(two, 64, 1), two),
             )
             out = slice(256 * n + 128 * q, 256 * n + 128 * q + 128)
-            for y in range(PLANE // 2):
-                start = 2 * y * quarter
-                left, right = folded[start : start + quarter], folded[start + quarter : start + 2 * quarter]
-                for target, value in ((keep_ref, jnp.where(core, left, right)), (send_ref, jnp.where(core, right, left))):
-                    for i in range(quarter // own):
-                        target[y * (quarter // own) + i, :, out] = value[i * own : (i + 1) * own]
-
-
-def core_sum_kernel(place_ref, mine_ref, other_ref, *outs):
-    plane, planes = place_ref[0] // PLANE, len(outs)
-    for s, out in enumerate(outs):
-        index = (plane + s) % planes
-        out[...] = mine_ref[index] + other_ref[index]
+            for i in range(planes):
+                part_ref[i, :, out] = folded[i * own : (i + 1) * own]
+    plane = place // PLANE
+    for s, target in enumerate(outs):
+        target[...] = part_ref[(plane + s) % planes]
 
 
 def add_kernel(*refs):
@@ -165,12 +189,11 @@
 
 
 def row_value_kernel(
-    columns, place_ref, x_ref, w_ref, gain_ref, mine_ref, other_ref, out_ref, next_ref, spread_ref
+    columns, place_ref, x_ref, y_ref, w_ref, mine_ref, other_ref, out_ref, next_ref, spread_ref
 ):
     core = place_ref[0] % 2
     out_ref[...] = dot(x_ref[...], w_ref[...]).astype(BF16)
-    normed = norm(other_ref[...].astype(F32), gain_ref[...]).astype(BF16)
-    next_ref[...] = dot(normed, w_ref[...]).astype(BF16)
+    next_ref[...] = dot(y_ref[...], w_ref[...]).astype(BF16)
     rows = x_ref.shape[0] // columns
     quarter = columns // PLANE
     for source, index in ((mine_ref, core), (other_ref, 1 - core)):
@@ -265,15 +288,62 @@
         out[...] = normed_ref[pl.ds(start, size), :].astype(BF16)
 
 
-def column_kernel(scale, steps, columns, depth_ref, prot_ref, place_ref, wq_ref, wk_ref, wv_ref, *refs):
-    planes = len(steps)
-    ins, (keep_ref, send_ref, all_ref, mixed_ref) = refs[: 2 * planes], refs[2 * planes :]
-    size, width = ins[0].shape
+def pack_kernel(*refs):
+    for i, source in enumerate(refs[:-1]):
+        refs[-1][i] = source[...]
+
+
+def block_of(own):
+    return 4 if own % 4 == 0 else own
+
+
+def heads_of(place_ref, wide):
+    return pl.ds(pl.multiple_of(place_ref[0] % 2 * wide, 128), wide)
+
+
+def column_project_kernel(planes, columns, place_ref, wq_ref, wk_ref, wv_ref, *refs):
+    ins, (query_ref, key_ref, value_ref, all_ref) = refs[:planes], refs[planes:]
+    gather_tokens(ins, columns, all_ref)
+    heads = heads_of(place_ref, query_ref.shape[1])
+    for w_ref, out in ((wq_ref, query_ref), (wk_ref, key_ref), (wv_ref, value_ref)):
+        out[...] = dot(all_ref[...], w_ref[:, heads]).astype(BF16)
+
+
+def gather_tokens(sources, columns, all_ref):
+    planes = len(sources)
+    own = columns // 2 // planes
+    piece = block_of(own) * sources[0].shape[0] // own
+    for g in range(own // block_of(own)):
+        for i, source in enumerate(sources):
+            start = (g * planes + i) * piece
+            all_ref[start : start + piece, :] = source[g * piece : (g + 1) * piece, :]
+
+
+def column_kernel(
+    scale,
+    steps,
+    columns,
+    depth_ref,
+    prot_ref,
+    place_ref,
+    wq_ref,
+    wk_ref,
+    wv_ref,
+    query_ref,
+    key_ref,
+    value_ref,
+    other_ref,
+    keep_ref,
+    send_ref,
+    all_ref,
+    mixed_ref,
+):
+    planes, size, width = other_ref.shape
     wide = width // 2
     slots, local = 2 * planes, columns // 2
     own = local // planes
     rows = size // own
-    block = 4 if own % 4 == 0 else own
+    block = block_of(own)
     piece = block * rows
     chunk = slots * piece
     chunks = own // block
@@ -281,15 +351,19 @@
     pair = 8 // rows
     place = place_ref[0]
     core, line, plane = place % 2, (place // 2) % 2, place // PLANE
-    for g in range(chunks):
-        for i, source in enumerate(ins):
-            all_ref[g * chunk + i * piece : g * chunk + (i + 1) * piece, :] = source[g * piece : (g + 1) * piece, :]
-    x = all_ref[...]
-    heads = pl.ds(pl.multiple_of(core * wide, 128), wide)
+    gather_tokens([other_ref.at[i] for i in range(planes)], columns, all_ref)
+    heads = heads_of(place_ref, wide)
+    full = []
+    for mine_ref, w_ref in ((query_ref, wq_ref), (key_ref, wk_ref), (value_ref, wv_ref)):
+        other = dot(all_ref[...], w_ref[:, heads]).astype(BF16)
+        mine = mine_ref[...]
+        parts = []
+        for start in range(0, planes * size, chunk // 2):
+            parts += [mine[start : start + chunk // 2], other[start : start + chunk // 2]]
+        full.append(jnp.concatenate(parts, axis=0))
+    query, key, value = full
+    query = query.astype(F32) * scale
     even, odd = half_masks(wide)
-    query = dot(x, wq_ref[:, heads]).astype(BF16).astype(F32) * scale
-    key = dot(x, wk_ref[:, heads]).astype(BF16)
-    value = dot(x, wv_ref[:, heads]).astype(BF16)
     sides = [(query * side).astype(BF16) for side in (even, odd)]
     unit = jnp.where(iota((128, 128), 0) == iota((128, 128), 1), 1.0, 0.0).astype(BF16)
     lane = (iota((8, 2 * chunk), 1) % piece) // rows
@@ -452,44 +526,38 @@
     size = tokens // planes
     sum_steps = move_steps = back_steps = far_first(planes)
     share_steps = far_first(planes)
-    share_steps = share_steps[1:] + share_steps[:1]
     x = alignment.reshape(tokens, width)
     shape = jax.ShapeDtypeStruct
     square = 2 * tokens * width * width
 
-    half = shape((planes, local // planes, width), F32)
     part = shape((local // planes, width), F32)
-    keep, send, normed, same = call(
-        row_scores_kernel,
-        (half, half, shape((tokens, width), BF16), shape((columns, columns), F32)),
-        "hshhhhh",
-        "vvvv",
+    matrix = shape((width, width), BF16)
+    sibling = swap(x, 1)
+    normed, query, key, row_query, row_key = call(
+        functools.partial(row_own_kernel, columns),
+        (shape((tokens, width), BF16), shape((tokens // 2, width), BF16), shape((tokens, width), BF16), matrix, matrix),
+        "shhhh",
+        "vvvvv",
         [
-            pltpu.SMEM(row_depth.shape, jnp.int32),
             pltpu.VMEM((tokens, width), BF16),
             pltpu.VMEM((width,), F32),
-            pltpu.VMEM((columns,), jnp.int32),
-            pltpu.VMEM((width, width), BF16),
-            pltpu.VMEM((width, width), BF16),
-            pltpu.SemaphoreType.DMA((4 + 2 * (width // 256),)),
+            pltpu.SemaphoreType.DMA((2 + 2 * (width // 256),)),
         ],
-        (2 * square, 4 * width * width, tokens),
+        (3 * square // 2, 4 * width * width, tokens),
+        "row_own",
+    )(place, hbm(x), hbm(row_gain), hbm(row_query), hbm(row_key))
+    *pieces, normed_other, same = call(
+        row_scores_kernel,
+        (part,) * planes + (shape((tokens, width), BF16), shape((columns, columns), F32)),
+        "ss" + "v" * 7,
+        "v" * (planes + 2),
+        [pltpu.VMEM((planes, local // planes, width), F32)],
+        (3 * square // 2, 4 * width * width, tokens),
         "row_scores",
-    )(hbm(row_depth), place, hbm(x), hbm(row_gain), hbm(protein_id), hbm(row_query), hbm(row_key))
+    )(row_depth, place, sibling, row_gain, protein_id, row_query, row_key, query, key)
     column_query, column_key, column_value, late, normed = lax.optimization_barrier(
         (column_query, column_key, column_value, x, normed)
     )
-    other = swap(send, 1)
-    sibling = swap(late, 1)
-    pieces = call(
-        core_sum_kernel,
-        (part,) * planes,
-        "svv",
-        "v" * planes,
-        [],
-        (columns * width, 6 * columns * width, 0),
-        "core_sum",
-    )(place, keep, other)
     (total,) = call(
         add_kernel, (part,), "v" * planes, "v", [], (columns * width, 2 * columns * width, 0), "add"
     )(*[spin(pieces[s], s) for s in sum_steps])
@@ -501,7 +569,7 @@
         [],
         (2 * square, 2 * width * width, 0),
         "row_value",
-    )(place, normed, row_value, row_gain[None], late, sibling)
+    )(place, normed, normed_other, row_value, late, sibling)
     (weights,) = call(
         functools.partial(row_softmax_kernel, 1.0 / (math.sqrt(head_size) * math.sqrt(total_rows))),
         (shape((local // planes, width), BF16),),
@@ -526,18 +594,35 @@
         "row_output",
     )(place, same, value, value_other, spread, row_output, column_gain[None], *shared)
     moved = [spin(blocks[s], s) for s in move_steps]
-    moved += [swap(block, 1) for block in moved]
     wide = width // 2
+    (packed,) = call(
+        pack_kernel,
+        (shape((planes, size, width), BF16),),
+        "v" * planes,
+        "v",
+        [],
+        (tokens * width, 4 * tokens * width, 0),
+        "pack",
+    )(*moved)
+    ours = call(
+        functools.partial(column_project_kernel, planes, columns),
+        (shape((tokens, wide), BF16),) * 3,
+        "svvv" + "v" * planes,
+        "vvv",
+        [pltpu.VMEM((tokens, width), BF16)],
+        (3 * square // 2, 3 * width * width, 0),
+        "column_project",
+    )(place, column_query, column_key, column_value, *moved)
     halves = shape((planes, size, wide), BF16)
     keep, send = call(
         functools.partial(column_kernel, 1.0 / math.sqrt(head_size), move_steps, columns),
         (halves, halves),
-        "sss" + "v" * (3 + 2 * planes),
+        "sss" + "v" * 7,
         "vv",
-        [pltpu.VMEM((2 * tokens, width), BF16), pltpu.VMEM((wide, 2 * tokens), BF16)],
+        [pltpu.VMEM((tokens, width), BF16), pltpu.VMEM((wide, 2 * tokens), BF16)],
         (4 * square, 6 * width * width, H * tokens * tokens // 4),
         "column_attention",
-    )(row_depth, protein_id, place, column_query, column_key, column_value, *moved)
+    )(row_depth, protein_id, place, column_query, column_key, column_value, *ours, swap(packed, 1))
     joined = call(
         join_kernel,
         (shape((size, width), BF16),) * planes,

time: 63.9 us -> 63.3 us (level)
  starting transfers between devices: 37.8 us -> 33.7 us
  waiting for transfers between devices: 15.4 us -> 17.5 us
  Pallas kernels: 10.1 us -> 11.6 us
    ppermute x12, waiting for transfers between devices: 2.75 us -> 6.74 us  [spin(): return lax.ppermute(array, 'seq', spin_pairs(step))]
    ppermute x9 -> x5, starting transfers between devices: 16.4 us -> 12.7 us  [swap(): return lax.ppermute(array, 'seq', [(i, i ^ offset) for i in range(devices)])]
    pallas_call x2 -> x4, Pallas kernels: 3.44 us -> 5.6 us  [the longest x1 2.48 us: per_device(): call(functools.partial(row_own_kernel, columns), (shape((tokens, width),...]
    ppermute x9 -> x5, waiting for transfers between devices: 5.5 us -> 3.57 us  [swap(): return lax.ppermute(array, 'seq', [(i, i ^ offset) for i in range(devices)])]
  transfers between devices with their start and end apart: 25 -> 21, of which waited for: 11 -> 13; matrix products, arithmetic and copies ran while one was open for 0% -> 0% of each run, Pallas kernels for 2% -> 6%
where the time goes in v7:
time: 63.3 us; the launch traced here: 63.1 us
  starting transfers between devices  33.7 us (53%)
  waiting for transfers between devices  17.5 us (28%)
  Pallas kernels  11.6 us (18%)
    ppermute x12, starting transfers between devices, spin(): return lax.ppermute(array, 'seq', spin_pairs(step))  18.3 us
    ppermute x5, starting transfers between devices, swap(): return lax.ppermute(array, 'seq', [(i, i ^ offset) for i in range(devices)])  12.7 us
    ppermute x4, waiting for transfers between devices, spin_back(): return lax.ppermute(array, 'seq', [(b, a) for a, b in spin_pairs(step)])  7.19 us
    ppermute x12, waiting for transfers between devices, spin(): return lax.ppermute(array, 'seq', spin_pairs(step))  6.74 us
    ppermute x5, waiting for transfers between devices, swap(): return lax.ppermute(array, 'seq', [(i, i ^ offset) for i in range(devices)])  3.57 us
    ppermute x4, starting transfers between devices, spin_back(): return lax.ppermute(array, 'seq', [(b, a) for a, b in spin_pairs(step)])  2.8 us
    pallas_call x1, Pallas kernels, per_device(): call(functools.partial(row_own_kernel, columns), (shape((tokens, width),...  2.48 us
    pallas_call x1, Pallas kernels, per_device(): call(row_scores_kernel, (part,) * planes + (shape((tokens, width), BF16),...  2.31 us
  transfers between devices with their start and end apart: 21, of which 13 were waited for; matrix products, arithmetic and copies ran while one was open for 0% of the time, Pallas kernels for 6%

profile of v7, /device:TPU:0, one launch (start us, length us, event | category | flops | bytes accessed | tf_op | source)
XLA Modules:
  0.0 63.1 jit_solution(15928544670221328860)
XLA Ops:
  0.0 0.5 collective-permute-start
  0.5 2.5 %row_own.1 = (bf16[256,768]{1,0:T(8,128)(2,1)S(1)}, bf16[128,768]{1,0:T(8,128)(2,1)S(1)}, bf16[256,768]{1,0:T(8,128)(2,1)S(1)}, bf16[768,768]{1,0:T(8,128)(2,1)S(1)}, bf16[768,768]{1,0:T(8,128)(2,1)S(1)}) custom-call(s32[1]{0:T(128)} %bitcast.place_ref, bf16[256,768]{1,0:T(8,128)(2,1)} %bitcast.3, f32[768]{0:T(1024)} %gain_ref.1, bf16[768,768]{1,0:T(8,128)(2,1)} %wq_hbm.1, ...), custom_call_target="tpu_custom_call" | custom-call | flops 452984832 | bytes 2359296 | tf_op jit(solution)/shard_map/row_own/pallas_call | solution.py:536
  3.0 0.0 copy-start.10
  3.0 0.0 copy-start.3
  3.0 0.0 copy-start.5
  3.0 2.3 %row_scores.1 = (f32[16,768]{1,0:T(8,128)S(1)}, f32[16,768]{1,0:T(8,128)S(1)}, f32[16,768]{1,0:T(8,128)S(1)}, f32[16,768]{1,0:T(8,128)S(1)}, bf16[256,768]{1,0:T(8,128)(2,1)S(1)}, /*index=5*/f32[128,128]{1,0:T(8,128)S(1)}) custom-call(s32[4]{0:T(128)S(1)} %copy-done.8, s32[1]{0:T(128)} %bitcast.place_ref, ...), custom_call_target="tpu_custom_call" | custom-call | flops 452984832 | bytes 2359296 | tf_op jit(solution)/shard_map/row_scores/pallas_call | solution.py:549
  5.3 3.6 %collective-permute-start.1 = (f32[16,768]{1,0:T(8,128)S(1)}, f32[16,768]{1,0:T(8,128)S(1)}, u32[]{:S(2)}, u32[]{:S(2)}) collective-permute-start(f32[16,768]{1,0:T(8,128)S(1)} %get-tuple-element.52), channel_id=1, source_target_pairs={{0,8},{1,10},{2,9},{3,11},{4,12},{5,14},{6,13},{7,15},{8,0},{9,2},... | collective-permute-start | bytes 147464 | tf_op jit(solution)/shard_map/ppermute | solution.py:497
  9.0 1.6 %collective-permute-start.2 = (f32[16,768]{1,0:T(8,128)S(1)}, f32[16,768]{1,0:T(8,128)S(1)}, u32[]{:S(2)}, u32[]{:S(2)}) collective-permute-start(f32[16,768]{1,0:T(8,128)S(1)} %get-tuple-element.53), channel_id=1, source_target_pairs={{0,4},{1,6},{2,5},{3,7},{4,8},{5,10},{6,9},{7,11},{8,12},{9,14},{1... | collective-permute-start | bytes 147464 | tf_op jit(solution)/shard_map/ppermute | solution.py:497
  10.6 2.2 %collective-permute-start.3 = (f32[16,768]{1,0:T(8,128)S(1)}, f32[16,768]{1,0:T(8,128)S(1)}, u32[]{:S(2)}, u32[]{:S(2)}) collective-permute-start(f32[16,768]{1,0:T(8,128)S(1)} %get-tuple-element.54), channel_id=1, source_target_pairs={{0,12},{1,14},{2,13},{3,15},{4,0},{5,2},{6,1},{7,3},{8,4},{9,6},{1... | collective-permute-start | bytes 147464 | tf_op jit(solution)/shard_map/ppermute | solution.py:497
  12.8 0.7 %collective-permute-start.4 = (f32[16,768]{1,0:T(8,128)S(1)}, f32[16,768]{1,0:T(8,128)S(1)}, u32[]{:S(2)}, u32[]{:S(2)}) collective-permute-start(f32[16,768]{1,0:T(8,128)S(1)} %get-tuple-element.55), channel_id=1, source_target_pairs={{0,0},{1,2},{2,1},{3,3},{4,4},{5,6},{6,5},{7,7},{8,8},{9,10},{10,9... | collective-permute-start | bytes 147464 | tf_op jit(solution)/shard_map/ppermute | solution.py:497
  13.5 1.7 %collective-permute-done.2.refs_1_ = f32[16,768]{1,0:T(8,128)S(1)} collective-permute-done((f32[16,768]{1,0:T(8,128)S(1)}, f32[16,768]{1,0:T(8,128)S(1)}, u32[]{:S(2)}, u32[]{:S(2)}) %collective-permute-start.2) | collective-permute-done | bytes 49184 | tf_op jit(solution)/shard_map/ppermute | solution.py:497
  15.2 0.7 %collective-permute-done.3.refs_2_ = f32[16,768]{1,0:T(8,128)S(1)} collective-permute-done((f32[16,768]{1,0:T(8,128)S(1)}, f32[16,768]{1,0:T(8,128)S(1)}, u32[]{:S(2)}, u32[]{:S(2)}) %collective-permute-start.3) | collective-permute-done | bytes 49184 | tf_op jit(solution)/shard_map/ppermute | solution.py:497
  15.9 4.1 %collective-permute-start.5 = (f32[16,768]{1,0:T(8,128)S(1)}, f32[16,768]{1,0:T(8,128)S(1)}, u32[]{:S(2)}, u32[]{:S(2)}) collective-permute-start(f32[16,768]{1,0:T(8,128)S(1)} %add.1.mine_ref), channel_id=1, source_target_pairs={{0,1},{1,0},{2,3},{3,2},{4,5},{5,4},{6,7},{7,6},{8,9},{9,8},{10,11... | collective-permute-start | bytes 147464 | tf_op jit(solution)/shard_map/ppermute | solution.py:479
  20.0 0.9 %collective-permute-done.5.other_ref = f32[16,768]{1,0:T(8,128)S(1)} collective-permute-done((f32[16,768]{1,0:T(8,128)S(1)}, f32[16,768]{1,0:T(8,128)S(1)}, u32[]{:S(2)}, u32[]{:S(2)}) %collective-permute-start.5) | collective-permute-done | bytes 49184 | tf_op jit(solution)/shard_map/ppermute | solution.py:479
  20.9 0.3 row_softmax.1
  21.2 0.1 collective-permute-start.6
  21.2 0.8 %collective-permute-start.7 = (bf16[16,768]{1,0:T(8,128)(2,1)S(1)}, bf16[16,768]{1,0:T(8,128)(2,1)S(1)}, u32[]{:S(2)}, u32[]{:S(2)}) collective-permute-start(bf16[16,768]{1,0:T(8,128)(2,1)S(1)} %row_softmax.1), channel_id=1, source_target_pairs={{0,4},{1,6},{2,5},{3,7},{4,8},{5,10},{6,9},{7,11},{8,12},{9,14},{1... | collective-permute-start | bytes 73736 | tf_op jit(solution)/shard_map/ppermute | solution.py:497
  22.0 3.1 %collective-permute-start.8 = (bf16[16,768]{1,0:T(8,128)(2,1)S(1)}, bf16[16,768]{1,0:T(8,128)(2,1)S(1)}, u32[]{:S(2)}, u32[]{:S(2)}) collective-permute-start(bf16[16,768]{1,0:T(8,128)(2,1)S(1)} %row_softmax.1), channel_id=1, source_target_pairs={{0,12},{1,14},{2,13},{3,15},{4,0},{5,2},{6,1},{7,3},{8,4},{9,6},{1... | collective-permute-start | bytes 73736 | tf_op jit(solution)/shard_map/ppermute | solution.py:497
  25.1 0.7 %collective-permute-start.9 = (bf16[16,768]{1,0:T(8,128)(2,1)S(1)}, bf16[16,768]{1,0:T(8,128)(2,1)S(1)}, u32[]{:S(2)}, u32[]{:S(2)}) collective-permute-start(bf16[16,768]{1,0:T(8,128)(2,1)S(1)} %row_softmax.1), channel_id=1, source_target_pairs={{0,0},{1,2},{2,1},{3,3},{4,4},{5,6},{6,5},{7,7},{8,8},{9,10},{10,9... | collective-permute-start | bytes 73736 | tf_op jit(solution)/shard_map/ppermute | solution.py:497
  25.8 0.0 copy-start.4
  25.8 0.8 %row_value.1 = (bf16[256,768]{1,0:T(8,128)(2,1)S(1)}, bf16[256,768]{1,0:T(8,128)(2,1)S(1)}, f32[6,256,128]{2,1,0:T(8,128)S(1)}) custom-call(s32[1]{0:T(128)} %bitcast.place_ref, bf16[256,768]{1,0:T(8,128)(2,1)S(1)} %get-tuple-element.46.x_ref, bf16[256,768]{1,0:T(8,128)(2,1)S(1)} %get-tuple-element.47.y_ref, bf16[768,768]{1,0:T(8,128)(2,1)S(1)} %copy-done.5, ...), custom_call_target="tpu_custom_call" | custom-call | flops 603979776 | bytes 1179648 | tf_op jit(solution)/shard_map/row_value/pallas_call | solution.py:564
  26.6 0.4 collective-permute-done.7.refs_1_
  27.0 0.1 collective-permute-done.8.refs_2_
  27.1 0.0 copy-start.1
  27.1 1.2 %row_output.1 = (bf16[256,768]{1,0:T(8,128)(2,1)S(1)}, bf16[64,768]{1,0:T(8,128)(2,1)S(1)}, bf16[64,768]{1,0:T(8,128)(2,1)S(1)}, bf16[64,768]{1,0:T(8,128)(2,1)S(1)}, bf16[64,768]{1,0:T(8,128)(2,1)S(1)}) custom-call(s32[1]{0:T(128)} %bitcast.place_ref, f32[128,128]{1,0:T(8,128)S(1)} %get-tuple-element.44.same_ref, ...), custom_call_target="tpu_custom_call" | custom-call | flops 301989888 | bytes 1179648 | tf_op jit(solution)/shard_map/row_output/pallas_call | solution.py:583
  28.3 1.1 %collective-permute-start.10 = (bf16[64,768]{1,0:T(8,128)(2,1)S(1)}, bf16[64,768]{1,0:T(8,128)(2,1)S(1)}, u32[]{:S(2)}, u32[]{:S(2)}) collective-permute-start(bf16[64,768]{1,0:T(8,128)(2,1)S(1)} %get-tuple-element.60), channel_id=1, source_target_pairs={{0,8},{1,10},{2,9},{3,11},{4,12},{5,14},{6,13},{7,15},{8,0},{9,2},... | collective-permute-start | bytes 294920 | tf_op jit(solution)/shard_map/ppermute | solution.py:497
  29.4 3.2 %collective-permute-start.11 = (bf16[64,768]{1,0:T(8,128)(2,1)S(1)}, bf16[64,768]{1,0:T(8,128)(2,1)S(1)}, u32[]{:S(2)}, u32[]{:S(2)}) collective-permute-start(bf16[64,768]{1,0:T(8,128)(2,1)S(1)} %get-tuple-element.61), channel_id=1, source_target_pairs={{0,4},{1,6},{2,5},{3,7},{4,8},{5,10},{6,9},{7,11},{8,12},{9,14},{1... | collective-permute-start | bytes 294920 | tf_op jit(solution)/shard_map/ppermute | solution.py:497
  32.6 0.6 collective-permute-start.12
  33.2 0.7 %collective-permute-start.13 = (bf16[64,768]{1,0:T(8,128)(2,1)S(1)}, bf16[64,768]{1,0:T(8,128)(2,1)S(1)}, u32[]{:S(2)}, u32[]{:S(2)}) collective-permute-start(bf16[64,768]{1,0:T(8,128)(2,1)S(1)} %get-tuple-element.63), channel_id=1, source_target_pairs={{0,0},{1,2},{2,1},{3,3},{4,4},{5,6},{6,5},{7,7},{8,8},{9,10},{10,9... | collective-permute-start | bytes 294920 | tf_op jit(solution)/shard_map/ppermute | solution.py:497
  33.9 2.7 %collective-permute-done.10.refs_0_ = bf16[64,768]{1,0:T(8,128)(2,1)S(1)} collective-permute-done((bf16[64,768]{1,0:T(8,128)(2,1)S(1)}, bf16[64,768]{1,0:T(8,128)(2,1)S(1)}, u32[]{:S(2)}, u32[]{:S(2)}) %collective-permute-start.10) | collective-permute-done | bytes 98336 | tf_op jit(solution)/shard_map/ppermute | solution.py:497
  36.6 1.1 %collective-permute-done.12.refs_2_ = bf16[64,768]{1,0:T(8,128)(2,1)S(1)} collective-permute-done((bf16[64,768]{1,0:T(8,128)(2,1)S(1)}, bf16[64,768]{1,0:T(8,128)(2,1)S(1)}, u32[]{:S(2)}, u32[]{:S(2)}) %collective-permute-start.12) | collective-permute-done | bytes 98336 | tf_op jit(solution)/shard_map/ppermute | solution.py:497
  37.8 6.9 %collective-permute-start.14 = (bf16[4,64,768]{2,1,0:T(8,128)(2,1)S(1)}, bf16[4,64,768]{2,1,0:T(8,128)(2,1)S(1)}, u32[]{:S(2)}, u32[]{:S(2)}) collective-permute-start(bf16[4,64,768]{2,1,0:T(8,128)(2,1)S(1)} %pack.1), channel_id=1, source_target_pairs={{0,1},{1,0},{2,3},{3,2},{4,5},{5,4},{6,7},{7,6},{8,9},{9,8},{10,11... | collective-permute-start | bytes 1179656 | tf_op jit(solution)/shard_map/ppermute | solution.py:479
  44.7 0.8 %column_project.1 = (bf16[256,384]{1,0:T(8,128)(2,1)S(1)}, bf16[256,384]{1,0:T(8,128)(2,1)S(1)}, bf16[256,384]{1,0:T(8,128)(2,1)S(1)}) custom-call(s32[1]{0:T(128)} %bitcast.place_ref, bf16[768,768]{1,0:T(8,128)(2,1)S(1)} %copy-done, bf16[768,768]{1,0:T(8,128)(2,1)S(1)} %copy-done.1, bf16[768,768]{1,0:T(8,128)(2,1)S(1)} %copy-done.2, ...), custom_call_target="tpu_custom_call" | custom-call | flops 452984832 | bytes 1769472 | tf_op jit(solution)/shard_map/column_project/pallas_call | solution.py:607
  45.4 0.6 collective-permute-done.14.other_ref
  46.0 2.2 %column_attention.1 = (bf16[4,64,384]{2,1,0:T(8,128)(2,1)S(1)}, bf16[4,64,384]{2,1,0:T(8,128)(2,1)S(1)}) custom-call(s32[4]{0:T(128)S(1)} %copy-done.8, s32[128]{0:T(128)S(1)} %copy-done.9, s32[1]{0:T(128)} %bitcast.place_ref, bf16[768,768]{1,0:T(8,128)(2,1)S(1)} %copy-done, bf16[768,768]{1,0:T(8,128)(2,1)S(1)} %copy-done.1, bf16[768,768]{1,0:T(8,128)(2,1)S(1)} %copy-done.2, ...), custom_call_target="tpu_custom_call" | custom-call | flops 1207959552 | bytes 3538944 | tf_op jit(solution)/shard_map/column_attention/pallas_call | solution.py:617
  48.2 0.5 collective-permute-start.15
  48.7 1.1 %collective-permute-done.15.other_ref = bf16[4,64,384]{2,1,0:T(8,128)(2,1)S(1)} collective-permute-done((bf16[4,64,384]{2,1,0:T(8,128)(2,1)S(1)}, bf16[4,64,384]{2,1,0:T(8,128)(2,1)S(1)}, u32[]{:S(2)}, u32[]{:S(2)}) %collective-permute-start.15) | collective-permute-done | bytes 196640 | tf_op jit(solution)/shard_map/ppermute | solution.py:479
  49.8 0.1 collective-permute-start.16
  49.9 1.4 %collective-permute-start.17 = (bf16[64,768]{1,0:T(8,128)(2,1)S(1)}, bf16[64,768]{1,0:T(8,128)(2,1)S(1)}, u32[]{:S(2)}, u32[]{:S(2)}) collective-permute-start(bf16[64,768]{1,0:T(8,128)(2,1)S(1)} %get-tuple-element.70), channel_id=1, source_target_pairs={{4,0},{6,1},{5,2},{7,3},{8,4},{10,5},{9,6},{11,7},{12,8},{14,9},{1... | collective-permute-start | bytes 294920 | tf_op jit(solution)/shard_map/ppermute | solution.py:501
  51.3 0.7 %collective-permute-start.18 = (bf16[64,768]{1,0:T(8,128)(2,1)S(1)}, bf16[64,768]{1,0:T(8,128)(2,1)S(1)}, u32[]{:S(2)}, u32[]{:S(2)}) collective-permute-start(bf16[64,768]{1,0:T(8,128)(2,1)S(1)} %get-tuple-element.71), channel_id=1, source_target_pairs={{12,0},{14,1},{13,2},{15,3},{0,4},{2,5},{1,6},{3,7},{4,8},{6,9},{5... | collective-permute-start | bytes 294920 | tf_op jit(solution)/shard_map/ppermute | solution.py:501
  52.0 0.7 %collective-permute-start.19 = (bf16[64,768]{1,0:T(8,128)(2,1)S(1)}, bf16[64,768]{1,0:T(8,128)(2,1)S(1)}, u32[]{:S(2)}, u32[]{:S(2)}) collective-permute-start(bf16[64,768]{1,0:T(8,128)(2,1)S(1)} %get-tuple-element.72), channel_id=1, source_target_pairs={{0,0},{2,1},{1,2},{3,3},{4,4},{6,5},{5,6},{7,7},{8,8},{10,9},{9,10... | collective-permute-start | bytes 294920 | tf_op jit(solution)/shard_map/ppermute | solution.py:501
  52.6 4.4 %collective-permute-done.16.refs_0_ = bf16[64,768]{1,0:T(8,128)(2,1)S(1)} collective-permute-done((bf16[64,768]{1,0:T(8,128)(2,1)S(1)}, bf16[64,768]{1,0:T(8,128)(2,1)S(1)}, u32[]{:S(2)}, u32[]{:S(2)}) %collective-permute-start.16) | collective-permute-done | bytes 98336 | tf_op jit(solution)/shard_map/ppermute | solution.py:501
  57.0 0.4 collective-permute-done.17.refs_1_
  57.4 2.4 %collective-permute-done.18.refs_2_ = bf16[64,768]{1,0:T(8,128)(2,1)S(1)} collective-permute-done((bf16[64,768]{1,0:T(8,128)(2,1)S(1)}, bf16[64,768]{1,0:T(8,128)(2,1)S(1)}, u32[]{:S(2)}, u32[]{:S(2)}) %collective-permute-start.18) | collective-permute-done | bytes 98336 | tf_op jit(solution)/shard_map/ppermute | solution.py:501
  59.8 0.6 %column_output.1 = (bf16[2,64,768]{2,1,0:T(8,128)(2,1)S(1)}, bf16[2,64,768]{2,1,0:T(8,128)(2,1)S(1)}) custom-call(s32[1]{0:T(128)} %bitcast.place_ref, bf16[768,768]{1,0:T(8,128)(2,1)S(1)} %copy-done.6, bf16[256,768]{1,0:T(8,128)(2,1)S(1)} %get-tuple-element.56.after_ref, bf16[64,768]{1,0:T(8,128)(2,1)S(1)} %collective-permute-done.16.refs_0_, ...), custom_call_target="tpu_custom_call" | custom-call | flops 301989888 | bytes 1179648 | tf_op jit(solution)/shard_map/column_output/pallas_call | solution.py:637
  60.5 0.8 %collective-permute-start.20 = (bf16[2,64,768]{2,1,0:T(8,128)(2,1)S(1)}, bf16[2,64,768]{2,1,0:T(8,128)(2,1)S(1)}, u32[]{:S(2)}, u32[]{:S(2)}) collective-permute-start(bf16[2,64,768]{2,1,0:T(8,128)(2,1)S(1)} %get-tuple-element.74), channel_id=1, source_target_pairs={{0,1},{1,0},{2,3},{3,2},{4,5},{5,4},{6,7},{7,6},{8,9},{9,8},{10,11... | collective-permute-start | bytes 589832 | tf_op jit(solution)/shard_map/ppermute | solution.py:479
  61.3 1.1 %collective-permute-done.20.other_ref = bf16[2,64,768]{2,1,0:T(8,128)(2,1)S(1)} collective-permute-done((bf16[2,64,768]{2,1,0:T(8,128)(2,1)S(1)}, bf16[2,64,768]{2,1,0:T(8,128)(2,1)S(1)}, u32[]{:S(2)}, u32[]{:S(2)}) %collective-permute-start.20) | collective-permute-done | bytes 196640 | tf_op jit(solution)/shard_map/ppermute | solution.py:479
  62.4 0.8 %assemble.1 = bf16[2,128,768]{2,1,0:T(8,128)(2,1)} custom-call(s32[1]{0:T(128)} %bitcast.place_ref, bf16[2,64,768]{2,1,0:T(8,128)(2,1)S(1)} %get-tuple-element.73.mine_ref, bf16[2,64,768]{2,1,0:T(8,128)(2,1)S(1)} %collective-permute-done.20.other_ref), custom_call_target="tpu_custom_call" | custom-call | flops 196608 | bytes 786432 | tf_op jit(solution)/shard_map/assemble/pallas_call | solution.py:646
  (29 shorter events, 0.1 us)
Async XLA Ops:
  0.0 2.9 %collective-permute-start = (bf16[256,768]{1,0:T(8,128)(2,1)}, bf16[256,768]{1,0:T(8,128)(2,1)S(1)}, u32[]{:S(2)}, u32[]{:S(2)}) collective-permute-start(bf16[256,768]{1,0:T(8,128)(2,1)} %bitcast.2), channel_id=1, source_target_pairs={{0,1},{1,0},{2,3},{3,2},{4,5},{5,4},{6,7},{7,6},{8,9},{9,8},{10,11... | collective-permute-start | bytes 1179656 | tf_op jit(solution)/shard_map/ppermute | solution.py:479
  0.5 2.5 %copy-start.7 = (f32[768]{0:T(1024)S(1)}, f32[768]{0:T(1024)}, u32[]{:S(2)}) copy-start(f32[768]{0:T(1024)} %gain_ref.1) | copy-start | bytes 9220
  0.5 2.5 %copy-start.8 = (s32[4]{0:T(128)S(1)}, s32[4]{0:T(128)}, u32[]{:S(2)}) copy-start(s32[4]{0:T(128)} %depth_ref.3) | copy-start | bytes 52
  0.5 2.5 %copy-start.9 = (s32[128]{0:T(128)S(1)}, s32[128]{0:T(128)}, u32[]{:S(2)}) copy-start(s32[128]{0:T(128)} %prot_ref.3) | copy-start | bytes 1540
  3.0 17.0 %copy-start.10 = (f32[768]{0:T(1024)S(1)}, f32[768]{0:T(1024)}, u32[]{:S(2)}) copy-start(f32[768]{0:T(1024)} %param.21) | copy-start | bytes 9220
  3.0 22.8 %copy-start.3 = (bf16[2,128,768]{2,1,0:T(8,128)(2,1)S(1)}, bf16[2,128,768]{2,1,0:T(8,128)(2,1)}, u32[]{:S(2)}) copy-start(bf16[2,128,768]{2,1,0:T(8,128)(2,1)} %param.13) | copy-start | bytes 1179652
  3.0 22.8 %copy-start.5 = (bf16[768,768]{1,0:T(8,128)(2,1)S(1)}, bf16[768,768]{1,0:T(8,128)(2,1)}, u32[]{:S(2)}) copy-start(bf16[768,768]{1,0:T(8,128)(2,1)} %w_ref.3) | copy-start | bytes 3538948
  5.3 8.1 %collective-permute-start.1 = (f32[16,768]{1,0:T(8,128)S(1)}, f32[16,768]{1,0:T(8,128)S(1)}, u32[]{:S(2)}, u32[]{:S(2)}) collective-permute-start(f32[16,768]{1,0:T(8,128)S(1)} %get-tuple-element.52), channel_id=1, source_target_pairs={{0,8},{1,10},{2,9},{3,11},{4,12},{5,14},{6,13},{7,15},{8,0},{9,2},... | collective-permute-start | bytes 147464 | tf_op jit(solution)/shard_map/ppermute | solution.py:497
  9.0 6.2 %collective-permute-start.2 = (f32[16,768]{1,0:T(8,128)S(1)}, f32[16,768]{1,0:T(8,128)S(1)}, u32[]{:S(2)}, u32[]{:S(2)}) collective-permute-start(f32[16,768]{1,0:T(8,128)S(1)} %get-tuple-element.53), channel_id=1, source_target_pairs={{0,4},{1,6},{2,5},{3,7},{4,8},{5,10},{6,9},{7,11},{8,12},{9,14},{1... | collective-permute-start | bytes 147464 | tf_op jit(solution)/shard_map/ppermute | solution.py:497
  10.6 5.3 %collective-permute-start.3 = (f32[16,768]{1,0:T(8,128)S(1)}, f32[16,768]{1,0:T(8,128)S(1)}, u32[]{:S(2)}, u32[]{:S(2)}) collective-permute-start(f32[16,768]{1,0:T(8,128)S(1)} %get-tuple-element.54), channel_id=1, source_target_pairs={{0,12},{1,14},{2,13},{3,15},{4,0},{5,2},{6,1},{7,3},{8,4},{9,6},{1... | collective-permute-start | bytes 147464 | tf_op jit(solution)/shard_map/ppermute | solution.py:497
  12.8 3.1 %collective-permute-start.4 = (f32[16,768]{1,0:T(8,128)S(1)}, f32[16,768]{1,0:T(8,128)S(1)}, u32[]{:S(2)}, u32[]{:S(2)}) collective-permute-start(f32[16,768]{1,0:T(8,128)S(1)} %get-tuple-element.55), channel_id=1, source_target_pairs={{0,0},{1,2},{2,1},{3,3},{4,4},{5,6},{6,5},{7,7},{8,8},{9,10},{10,9... | collective-permute-start | bytes 147464 | tf_op jit(solution)/shard_map/ppermute | solution.py:497
  15.9 5.0 %collective-permute-start.5 = (f32[16,768]{1,0:T(8,128)S(1)}, f32[16,768]{1,0:T(8,128)S(1)}, u32[]{:S(2)}, u32[]{:S(2)}) collective-permute-start(f32[16,768]{1,0:T(8,128)S(1)} %add.1.mine_ref), channel_id=1, source_target_pairs={{0,1},{1,0},{2,3},{3,2},{4,5},{5,4},{6,7},{7,6},{8,9},{9,8},{10,11... | collective-permute-start | bytes 147464 | tf_op jit(solution)/shard_map/ppermute | solution.py:479
  21.2 5.5 %collective-permute-start.6 = (bf16[16,768]{1,0:T(8,128)(2,1)S(1)}, bf16[16,768]{1,0:T(8,128)(2,1)S(1)}, u32[]{:S(2)}, u32[]{:S(2)}) collective-permute-start(bf16[16,768]{1,0:T(8,128)(2,1)S(1)} %row_softmax.1), channel_id=1, source_target_pairs={{0,8},{1,10},{2,9},{3,11},{4,12},{5,14},{6,13},{7,15},{8,0},{9,2},... | collective-permute-start | bytes 73736 | tf_op jit(solution)/shard_map/ppermute | solution.py:497
  21.2 5.8 %collective-permute-start.7 = (bf16[16,768]{1,0:T(8,128)(2,1)S(1)}, bf16[16,768]{1,0:T(8,128)(2,1)S(1)}, u32[]{:S(2)}, u32[]{:S(2)}) collective-permute-start(bf16[16,768]{1,0:T(8,128)(2,1)S(1)} %row_softmax.1), channel_id=1, source_target_pairs={{0,4},{1,6},{2,5},{3,7},{4,8},{5,10},{6,9},{7,11},{8,12},{9,14},{1... | collective-permute-start | bytes 73736 | tf_op jit(solution)/shard_map/ppermute | solution.py:497
  22.0 5.0 %collective-permute-start.8 = (bf16[16,768]{1,0:T(8,128)(2,1)S(1)}, bf16[16,768]{1,0:T(8,128)(2,1)S(1)}, u32[]{:S(2)}, u32[]{:S(2)}) collective-permute-start(bf16[16,768]{1,0:T(8,128)(2,1)S(1)} %row_softmax.1), channel_id=1, source_target_pairs={{0,12},{1,14},{2,13},{3,15},{4,0},{5,2},{6,1},{7,3},{8,4},{9,6},{1... | collective-permute-start | bytes 73736 | tf_op jit(solution)/shard_map/ppermute | solution.py:497
  25.1 2.0 %collective-permute-start.9 = (bf16[16,768]{1,0:T(8,128)(2,1)S(1)}, bf16[16,768]{1,0:T(8,128)(2,1)S(1)}, u32[]{:S(2)}, u32[]{:S(2)}) collective-permute-start(bf16[16,768]{1,0:T(8,128)(2,1)S(1)} %row_softmax.1), channel_id=1, source_target_pairs={{0,0},{1,2},{2,1},{3,3},{4,4},{5,6},{6,5},{7,7},{8,8},{9,10},{10,9... | collective-permute-start | bytes 73736 | tf_op jit(solution)/shard_map/ppermute | solution.py:497
  25.8 1.3 %copy-start.4 = (bf16[768,768]{1,0:T(8,128)(2,1)S(1)}, bf16[768,768]{1,0:T(8,128)(2,1)}, u32[]{:S(2)}) copy-start(bf16[768,768]{1,0:T(8,128)(2,1)} %w_ref.4) | copy-start | bytes 3538948
  27.1 17.6 %copy-start = (bf16[768,768]{1,0:T(8,128)(2,1)S(1)}, bf16[768,768]{1,0:T(8,128)(2,1)}, u32[]{:S(2)}) copy-start(bf16[768,768]{1,0:T(8,128)(2,1)} %wq_ref.1) | copy-start | bytes 3538948
  27.1 17.6 %copy-start.1 = (bf16[768,768]{1,0:T(8,128)(2,1)S(1)}, bf16[768,768]{1,0:T(8,128)(2,1)}, u32[]{:S(2)}) copy-start(bf16[768,768]{1,0:T(8,128)(2,1)} %wk_ref.1) | copy-start | bytes 3538948
  27.1 17.5 %copy-start.2 = (bf16[768,768]{1,0:T(8,128)(2,1)S(1)}, bf16[768,768]{1,0:T(8,128)(2,1)}, u32[]{:S(2)}) copy-start(bf16[768,768]{1,0:T(8,128)(2,1)} %wv_ref.1) | copy-start | bytes 3538948
  28.3 8.3 %collective-permute-start.10 = (bf16[64,768]{1,0:T(8,128)(2,1)S(1)}, bf16[64,768]{1,0:T(8,128)(2,1)S(1)}, u32[]{:S(2)}, u32[]{:S(2)}) collective-permute-start(bf16[64,768]{1,0:T(8,128)(2,1)S(1)} %get-tuple-element.60), channel_id=1, source_target_pairs={{0,8},{1,10},{2,9},{3,11},{4,12},{5,14},{6,13},{7,15},{8,0},{9,2},... | collective-permute-start | bytes 294920 | tf_op jit(solution)/shard_map/ppermute | solution.py:497
  29.4 7.2 %collective-permute-start.11 = (bf16[64,768]{1,0:T(8,128)(2,1)S(1)}, bf16[64,768]{1,0:T(8,128)(2,1)S(1)}, u32[]{:S(2)}, u32[]{:S(2)}) collective-permute-start(bf16[64,768]{1,0:T(8,128)(2,1)S(1)} %get-tuple-element.61), channel_id=1, source_target_pairs={{0,4},{1,6},{2,5},{3,7},{4,8},{5,10},{6,9},{7,11},{8,12},{9,14},{1... | collective-permute-start | bytes 294920 | tf_op jit(solution)/shard_map/ppermute | solution.py:497
  32.6 5.1 %collective-permute-start.12 = (bf16[64,768]{1,0:T(8,128)(2,1)S(1)}, bf16[64,768]{1,0:T(8,128)(2,1)S(1)}, u32[]{:S(2)}, u32[]{:S(2)}) collective-permute-start(bf16[64,768]{1,0:T(8,128)(2,1)S(1)} %get-tuple-element.62), channel_id=1, source_target_pairs={{0,12},{1,14},{2,13},{3,15},{4,0},{5,2},{6,1},{7,3},{8,4},{9,6},{1... | collective-permute-start | bytes 294920 | tf_op jit(solution)/shard_map/ppermute | solution.py:497
  33.2 4.5 %collective-permute-start.13 = (bf16[64,768]{1,0:T(8,128)(2,1)S(1)}, bf16[64,768]{1,0:T(8,128)(2,1)S(1)}, u32[]{:S(2)}, u32[]{:S(2)}) collective-permute-start(bf16[64,768]{1,0:T(8,128)(2,1)S(1)} %get-tuple-element.63), channel_id=1, source_target_pairs={{0,0},{1,2},{2,1},{3,3},{4,4},{5,6},{6,5},{7,7},{8,8},{9,10},{10,9... | collective-permute-start | bytes 294920 | tf_op jit(solution)/shard_map/ppermute | solution.py:497
  37.8 8.2 %collective-permute-start.14 = (bf16[4,64,768]{2,1,0:T(8,128)(2,1)S(1)}, bf16[4,64,768]{2,1,0:T(8,128)(2,1)S(1)}, u32[]{:S(2)}, u32[]{:S(2)}) collective-permute-start(bf16[4,64,768]{2,1,0:T(8,128)(2,1)S(1)} %pack.1), channel_id=1, source_target_pairs={{0,1},{1,0},{2,3},{3,2},{4,5},{5,4},{6,7},{7,6},{8,9},{9,8},{10,11... | collective-permute-start | bytes 1179656 | tf_op jit(solution)/shard_map/ppermute | solution.py:479
  46.0 13.8 %copy-start.6 = (bf16[768,768]{1,0:T(8,128)(2,1)S(1)}, bf16[768,768]{1,0:T(8,128)(2,1)}, u32[]{:S(2)}) copy-start(bf16[768,768]{1,0:T(8,128)(2,1)} %w_ref.5) | copy-start | bytes 3538948
  48.2 1.5 %collective-permute-start.15 = (bf16[4,64,384]{2,1,0:T(8,128)(2,1)S(1)}, bf16[4,64,384]{2,1,0:T(8,128)(2,1)S(1)}, u32[]{:S(2)}, u32[]{:S(2)}) collective-permute-start(bf16[4,64,384]{2,1,0:T(8,128)(2,1)S(1)} %get-tuple-element.68), channel_id=1, source_target_pairs={{0,1},{1,0},{2,3},{3,2},{4,5},{5,4},{6,7},{7,6},{8,9},{9,8},{10,11... | collective-permute-start | bytes 589832 | tf_op jit(solution)/shard_map/ppermute | solution.py:479
  49.8 7.2 %collective-permute-start.16 = (bf16[64,768]{1,0:T(8,128)(2,1)S(1)}, bf16[64,768]{1,0:T(8,128)(2,1)S(1)}, u32[]{:S(2)}, u32[]{:S(2)}) collective-permute-start(bf16[64,768]{1,0:T(8,128)(2,1)S(1)} %get-tuple-element.69), channel_id=1, source_target_pairs={{8,0},{10,1},{9,2},{11,3},{12,4},{14,5},{13,6},{15,7},{0,8},{2,9},... | collective-permute-start | bytes 294920 | tf_op jit(solution)/shard_map/ppermute | solution.py:501
  49.9 7.6 %collective-permute-start.17 = (bf16[64,768]{1,0:T(8,128)(2,1)S(1)}, bf16[64,768]{1,0:T(8,128)(2,1)S(1)}, u32[]{:S(2)}, u32[]{:S(2)}) collective-permute-start(bf16[64,768]{1,0:T(8,128)(2,1)S(1)} %get-tuple-element.70), channel_id=1, source_target_pairs={{4,0},{6,1},{5,2},{7,3},{8,4},{10,5},{9,6},{11,7},{12,8},{14,9},{1... | collective-permute-start | bytes 294920 | tf_op jit(solution)/shard_map/ppermute | solution.py:501
  51.3 8.5 %collective-permute-start.18 = (bf16[64,768]{1,0:T(8,128)(2,1)S(1)}, bf16[64,768]{1,0:T(8,128)(2,1)S(1)}, u32[]{:S(2)}, u32[]{:S(2)}) collective-permute-start(bf16[64,768]{1,0:T(8,128)(2,1)S(1)} %get-tuple-element.71), channel_id=1, source_target_pairs={{12,0},{14,1},{13,2},{15,3},{0,4},{2,5},{1,6},{3,7},{4,8},{6,9},{5... | collective-permute-start | bytes 294920 | tf_op jit(solution)/shard_map/ppermute | solution.py:501
  52.0 7.9 %collective-permute-start.19 = (bf16[64,768]{1,0:T(8,128)(2,1)S(1)}, bf16[64,768]{1,0:T(8,128)(2,1)S(1)}, u32[]{:S(2)}, u32[]{:S(2)}) collective-permute-start(bf16[64,768]{1,0:T(8,128)(2,1)S(1)} %get-tuple-element.72), channel_id=1, source_target_pairs={{0,0},{2,1},{1,2},{3,3},{4,4},{6,5},{5,6},{7,7},{8,8},{10,9},{9,10... | collective-permute-start | bytes 294920 | tf_op jit(solution)/shard_map/ppermute | solution.py:501
  60.5 1.9 %collective-permute-start.20 = (bf16[2,64,768]{2,1,0:T(8,128)(2,1)S(1)}, bf16[2,64,768]{2,1,0:T(8,128)(2,1)S(1)}, u32[]{:S(2)}, u32[]{:S(2)}) collective-permute-start(bf16[2,64,768]{2,1,0:T(8,128)(2,1)S(1)} %get-tuple-element.74), channel_id=1, source_target_pairs={{0,1},{1,0},{2,3},{3,2},{4,5},{5,4},{6,7},{7,6},{8,9},{9,8},{10,11... | collective-permute-start | bytes 589832 | tf_op jit(solution)/shard_map/ppermute | solution.py:479

commit v8 on v7

--- a/solution.py
+++ b/solution.py
@@ -210,13 +210,13 @@
     own, width = out_ref.shape
     columns = same_ref.shape[0]
     quarter, local = columns // PLANE, columns // 2
-    line, plane = (place_ref[0] // 2) % 2, place_ref[0] // PLANE
+    core, plane = place_ref[0] % 2, place_ref[0] // PLANE
     same = same_ref[...]
     mask = jnp.maximum(same, pltpu.roll(same, 64, 1))
     for i in range(columns // own):
         mask_ref[i] = mask[i * own : (i + 1) * own]
     first = plane * own
-    live = mask_ref[(first % quarter + quarter * line + local * (first // quarter)) // own] > 0.5
+    live = mask_ref[(first % quarter + quarter * core + local * (first // quarter)) // own] > 0.5
     low = iota((own, 128), 1) < 64
     for p in range(width // 128):
         lanes = slice(128 * p, 128 * p + 128)
@@ -493,6 +493,13 @@
     return sorted(range(planes), key=lambda s: (-min(s, planes - s), s))
 
 
+def shift(array, step):
+    devices = lax.axis_size("seq")
+    if step == 0:
+        return array
+    return lax.ppermute(array, "seq", [(i, (i + PLANE * step) % devices) for i in range(devices)])
+
+
 def spin(array, step):
     return lax.ppermute(array, "seq", spin_pairs(step))
 
@@ -525,6 +532,7 @@
     planes, local = devices // PLANE, columns // 2
     size = tokens // planes
     sum_steps = move_steps = back_steps = far_first(planes)
+    move_steps = move_steps[2:] + move_steps[:2]
     share_steps = far_first(planes)
     x = alignment.reshape(tokens, width)
     shape = jax.ShapeDtypeStruct
@@ -560,7 +568,7 @@
     )
     (total,) = call(
         add_kernel, (part,), "v" * planes, "v", [], (columns * width, 2 * columns * width, 0), "add"
-    )(*[spin(pieces[s], s) for s in sum_steps])
+    )(*[shift(pieces[s], s) for s in sum_steps])
     value, value_other, spread = call(
         functools.partial(row_value_kernel, columns),
         (shape((tokens, width), BF16),) * 2 + (shape((width // 128, tokens, 128), F32),),
@@ -578,8 +586,8 @@
         [pltpu.VMEM((columns * planes // local, local // planes, columns), F32)],
         (columns * width, 2 * columns * width, columns * width // 8),
         "row_softmax",
-    )(place, total, swap(total, 1), same)
-    shared = [spin(weights, s) for s in share_steps]
+    )(place, total, swap(total, 2), same)
+    shared = [shift(weights, s) for s in share_steps]
     after, *blocks = call(
         functools.partial(row_output_kernel, share_steps),
         (shape((tokens, width), BF16),) + (shape((size, width), BF16),) * planes,

time: 63.3 us -> 61.1 us (0.965)
  starting transfers between devices: 33.7 us -> 24 us
  waiting for transfers between devices: 17.5 us -> 25.1 us
    ppermute x12 -> x4, starting transfers between devices: 18.3 us -> 4.61 us  [spin(): return lax.ppermute(array, 'seq', spin_pairs(step))]
    ppermute x0 -> x6, starting transfers between devices: none -> 12.4 us  [shift(): lax.ppermute(array, 'seq', [(i, (i + PLANE * step) % devices) for i in ra...]
    ppermute x5, starting transfers between devices: 12.7 us -> 3.26 us  [swap(): return lax.ppermute(array, 'seq', [(i, i ^ offset) for i in range(devices)])]
    ppermute x0 -> x6, waiting for transfers between devices: none -> 4.64 us  [shift(): lax.ppermute(array, 'seq', [(i, (i + PLANE * step) % devices) for i in ra...]
    ppermute x5, waiting for transfers between devices: 3.57 us -> 5.82 us  [swap(): return lax.ppermute(array, 'seq', [(i, i ^ offset) for i in range(devices)])]
    ppermute x12 -> x4, waiting for transfers between devices: 6.74 us -> 7.96 us  [spin(): return lax.ppermute(array, 'seq', spin_pairs(step))]
    ppermute x4, starting transfers between devices: 2.8 us -> 3.76 us  [spin_back(): return lax.ppermute(array, 'seq', [(b, a) for a, b in spin_pairs(step)])]
  transfers between devices with their start and end apart: 21 -> 19, of which waited for: 13 -> 12; matrix products, arithmetic and copies ran while one was open for 0% -> 0% of each run, Pallas kernels for 6% -> 7%
where the time goes in v8:
time: 61.1 us; the launch traced here: 61 us
  waiting for transfers between devices  25.1 us (41%)
  starting transfers between devices  24 us (39%)
  Pallas kernels  11.6 us (19%)
    ppermute x6, starting transfers between devices, shift(): lax.ppermute(array, 'seq', [(i, (i + PLANE * step) % devices) for i in ra...  12.4 us
    ppermute x4, waiting for transfers between devices, spin(): return lax.ppermute(array, 'seq', spin_pairs(step))  7.96 us
    ppermute x4, waiting for transfers between devices, spin_back(): return lax.ppermute(array, 'seq', [(b, a) for a, b in spin_pairs(step)])  6.72 us
    ppermute x5, waiting for transfers between devices, swap(): return lax.ppermute(array, 'seq', [(i, i ^ offset) for i in range(devices)])  5.82 us
    ppermute x6, waiting for transfers between devices, shift(): lax.ppermute(array, 'seq', [(i, (i + PLANE * step) % devices) for i in ra...  4.64 us
    ppermute x4, starting transfers between devices, spin(): return lax.ppermute(array, 'seq', spin_pairs(step))  4.61 us
    ppermute x4, starting transfers between devices, spin_back(): return lax.ppermute(array, 'seq', [(b, a) for a, b in spin_pairs(step)])  3.76 us
    ppermute x5, starting transfers between devices, swap(): return lax.ppermute(array, 'seq', [(i, i ^ offset) for i in range(devices)])  3.26 us
  transfers between devices with their start and end apart: 19, of which 12 were waited for; matrix products, arithmetic and copies ran while one was open for 0% of the time, Pallas kernels for 7%

profile of v8, /device:TPU:0, one launch (start us, length us, event | category | flops | bytes accessed | tf_op | source)
XLA Modules:
  0.0 61.0 jit_solution(16486139934397656644)
XLA Ops:
  0.0 0.5 collective-permute-start
  0.5 2.5 %row_own.1 = (bf16[256,768]{1,0:T(8,128)(2,1)S(1)}, bf16[128,768]{1,0:T(8,128)(2,1)S(1)}, bf16[256,768]{1,0:T(8,128)(2,1)S(1)}, bf16[768,768]{1,0:T(8,128)(2,1)S(1)}, bf16[768,768]{1,0:T(8,128)(2,1)S(1)}) custom-call(s32[1]{0:T(128)} %bitcast.place_ref, bf16[256,768]{1,0:T(8,128)(2,1)} %bitcast.3, f32[768]{0:T(1024)} %gain_ref.1, bf16[768,768]{1,0:T(8,128)(2,1)} %wq_hbm.1, ...), custom_call_target="tpu_custom_call" | custom-call | flops 452984832 | bytes 2359296 | tf_op jit(solution)/shard_map/row_own/pallas_call | solution.py:544
  2.9 0.0 collective-permute-done.x_ref.other_ref
  3.0 0.0 copy-start.10
  3.0 0.0 copy-start.3
  3.0 0.0 copy-start.5
  3.0 2.3 %row_scores.1 = (f32[16,768]{1,0:T(8,128)S(1)}, f32[16,768]{1,0:T(8,128)S(1)}, f32[16,768]{1,0:T(8,128)S(1)}, f32[16,768]{1,0:T(8,128)S(1)}, bf16[256,768]{1,0:T(8,128)(2,1)S(1)}, /*index=5*/f32[128,128]{1,0:T(8,128)S(1)}) custom-call(s32[4]{0:T(128)S(1)} %copy-done.8, s32[1]{0:T(128)} %bitcast.place_ref, ...), custom_call_target="tpu_custom_call" | custom-call | flops 452984832 | bytes 2359296 | tf_op jit(solution)/shard_map/row_scores/pallas_call | solution.py:557
  5.4 3.6 %collective-permute-start.1 = (f32[16,768]{1,0:T(8,128)S(1)}, f32[16,768]{1,0:T(8,128)S(1)}, u32[]{:S(2)}, u32[]{:S(2)}) collective-permute-start(f32[16,768]{1,0:T(8,128)S(1)} %get-tuple-element.52), channel_id=1, source_target_pairs={{0,8},{1,9},{2,10},{3,11},{4,12},{5,13},{6,14},{7,15},{8,0},{9,1},... | collective-permute-start | bytes 147464 | tf_op jit(solution)/shard_map/ppermute | solution.py:500
  9.0 1.6 %collective-permute-start.2 = (f32[16,768]{1,0:T(8,128)S(1)}, f32[16,768]{1,0:T(8,128)S(1)}, u32[]{:S(2)}, u32[]{:S(2)}) collective-permute-start(f32[16,768]{1,0:T(8,128)S(1)} %get-tuple-element.53), channel_id=1, source_target_pairs={{0,4},{1,5},{2,6},{3,7},{4,8},{5,9},{6,10},{7,11},{8,12},{9,13},{1... | collective-permute-start | bytes 147464 | tf_op jit(solution)/shard_map/ppermute | solution.py:500
  10.6 2.2 %collective-permute-start.3 = (f32[16,768]{1,0:T(8,128)S(1)}, f32[16,768]{1,0:T(8,128)S(1)}, u32[]{:S(2)}, u32[]{:S(2)}) collective-permute-start(f32[16,768]{1,0:T(8,128)S(1)} %get-tuple-element.54), channel_id=1, source_target_pairs={{0,12},{1,13},{2,14},{3,15},{4,0},{5,1},{6,2},{7,3},{8,4},{9,5},{1... | collective-permute-start | bytes 147464 | tf_op jit(solution)/shard_map/ppermute | solution.py:500
  12.8 0.0 collective-permute-done.1.refs_0_
  12.8 2.4 %collective-permute-done.2.refs_1_ = f32[16,768]{1,0:T(8,128)S(1)} collective-permute-done((f32[16,768]{1,0:T(8,128)S(1)}, f32[16,768]{1,0:T(8,128)S(1)}, u32[]{:S(2)}, u32[]{:S(2)}) %collective-permute-start.2) | collective-permute-done | bytes 49184 | tf_op jit(solution)/shard_map/ppermute | solution.py:500
  15.2 0.1 collective-permute-done.3.refs_2_
  15.3 1.6 %collective-permute-start.4 = (f32[16,768]{1,0:T(8,128)S(1)}, f32[16,768]{1,0:T(8,128)S(1)}, u32[]{:S(2)}, u32[]{:S(2)}) collective-permute-start(f32[16,768]{1,0:T(8,128)S(1)} %add.1.mine_ref), channel_id=1, source_target_pairs={{0,2},{1,3},{2,0},{3,1},{4,6},{5,7},{6,4},{7,5},{8,10},{9,11},{10,... | collective-permute-start | bytes 147464 | tf_op jit(solution)/shard_map/ppermute | solution.py:479
  16.9 2.6 %collective-permute-done.4.other_ref = f32[16,768]{1,0:T(8,128)S(1)} collective-permute-done((f32[16,768]{1,0:T(8,128)S(1)}, f32[16,768]{1,0:T(8,128)S(1)}, u32[]{:S(2)}, u32[]{:S(2)}) %collective-permute-start.4) | collective-permute-done | bytes 49184 | tf_op jit(solution)/shard_map/ppermute | solution.py:479
  19.5 0.3 row_softmax.1.refs_3_
  19.8 1.1 %collective-permute-start.5 = (bf16[16,768]{1,0:T(8,128)(2,1)S(1)}, bf16[16,768]{1,0:T(8,128)(2,1)S(1)}, u32[]{:S(2)}, u32[]{:S(2)}) collective-permute-start(bf16[16,768]{1,0:T(8,128)(2,1)S(1)} %row_softmax.1.refs_3_), channel_id=1, source_target_pairs={{0,8},{1,9},{2,10},{3,11},{4,12},{5,13},{6,14},{7,15},{8,0},{9,1},... | collective-permute-start | bytes 73736 | tf_op jit(solution)/shard_map/ppermute | solution.py:500
  20.8 3.0 %collective-permute-start.6 = (bf16[16,768]{1,0:T(8,128)(2,1)S(1)}, bf16[16,768]{1,0:T(8,128)(2,1)S(1)}, u32[]{:S(2)}, u32[]{:S(2)}) collective-permute-start(bf16[16,768]{1,0:T(8,128)(2,1)S(1)} %row_softmax.1.refs_3_), channel_id=1, source_target_pairs={{0,4},{1,5},{2,6},{3,7},{4,8},{5,9},{6,10},{7,11},{8,12},{9,13},{1... | collective-permute-start | bytes 73736 | tf_op jit(solution)/shard_map/ppermute | solution.py:500
  23.8 0.8 %collective-permute-start.7 = (bf16[16,768]{1,0:T(8,128)(2,1)S(1)}, bf16[16,768]{1,0:T(8,128)(2,1)S(1)}, u32[]{:S(2)}, u32[]{:S(2)}) collective-permute-start(bf16[16,768]{1,0:T(8,128)(2,1)S(1)} %row_softmax.1.refs_3_), channel_id=1, source_target_pairs={{0,12},{1,13},{2,14},{3,15},{4,0},{5,1},{6,2},{7,3},{8,4},{9,5},{1... | collective-permute-start | bytes 73736 | tf_op jit(solution)/shard_map/ppermute | solution.py:500
  24.6 0.8 %row_value.1 = (bf16[256,768]{1,0:T(8,128)(2,1)S(1)}, bf16[256,768]{1,0:T(8,128)(2,1)S(1)}, f32[6,256,128]{2,1,0:T(8,128)S(1)}) custom-call(s32[1]{0:T(128)} %bitcast.place_ref, bf16[256,768]{1,0:T(8,128)(2,1)S(1)} %get-tuple-element.46.x_ref, bf16[256,768]{1,0:T(8,128)(2,1)S(1)} %get-tuple-element.47.y_ref, bf16[768,768]{1,0:T(8,128)(2,1)S(1)} %copy-done.5, ...), custom_call_target="tpu_custom_call" | custom-call | flops 603979776 | bytes 1179648 | tf_op jit(solution)/shard_map/row_value/pallas_call | solution.py:572
  25.5 0.0 collective-permute-done.5.refs_0_
  25.5 1.0 %collective-permute-done.6.refs_1_ = bf16[16,768]{1,0:T(8,128)(2,1)S(1)} collective-permute-done((bf16[16,768]{1,0:T(8,128)(2,1)S(1)}, bf16[16,768]{1,0:T(8,128)(2,1)S(1)}, u32[]{:S(2)}, u32[]{:S(2)}) %collective-permute-start.6) | collective-permute-done | bytes 24608 | tf_op jit(solution)/shard_map/ppermute | solution.py:500
  26.4 1.2 %collective-permute-done.7.refs_2_ = bf16[16,768]{1,0:T(8,128)(2,1)S(1)} collective-permute-done((bf16[16,768]{1,0:T(8,128)(2,1)S(1)}, bf16[16,768]{1,0:T(8,128)(2,1)S(1)}, u32[]{:S(2)}, u32[]{:S(2)}) %collective-permute-start.7) | collective-permute-done | bytes 24608 | tf_op jit(solution)/shard_map/ppermute | solution.py:500
  27.6 1.2 %row_output.1 = (bf16[256,768]{1,0:T(8,128)(2,1)S(1)}, bf16[64,768]{1,0:T(8,128)(2,1)S(1)}, bf16[64,768]{1,0:T(8,128)(2,1)S(1)}, bf16[64,768]{1,0:T(8,128)(2,1)S(1)}, bf16[64,768]{1,0:T(8,128)(2,1)S(1)}) custom-call(s32[1]{0:T(128)} %bitcast.place_ref, f32[128,128]{1,0:T(8,128)S(1)} %get-tuple-element.44.same_ref, ...), custom_call_target="tpu_custom_call" | custom-call | flops 301989888 | bytes 1179648 | tf_op jit(solution)/shard_map/row_output/pallas_call | solution.py:591
  28.9 0.1 collective-permute-start.10
  29.0 3.1 %collective-permute-start.11 = (bf16[64,768]{1,0:T(8,128)(2,1)S(1)}, bf16[64,768]{1,0:T(8,128)(2,1)S(1)}, u32[]{:S(2)}, u32[]{:S(2)}) collective-permute-start(bf16[64,768]{1,0:T(8,128)(2,1)S(1)} %get-tuple-element.63), channel_id=1, source_target_pairs={{0,4},{1,6},{2,5},{3,7},{4,8},{5,10},{6,9},{7,11},{8,12},{9,14},{1... | collective-permute-start | bytes 294920 | tf_op jit(solution)/shard_map/ppermute | solution.py:504
  32.1 0.7 %collective-permute-start.8 = (bf16[64,768]{1,0:T(8,128)(2,1)S(1)}, bf16[64,768]{1,0:T(8,128)(2,1)S(1)}, u32[]{:S(2)}, u32[]{:S(2)}) collective-permute-start(bf16[64,768]{1,0:T(8,128)(2,1)S(1)} %get-tuple-element.60), channel_id=1, source_target_pairs={{0,12},{1,14},{2,13},{3,15},{4,0},{5,2},{6,1},{7,3},{8,4},{9,6},{1... | collective-permute-start | bytes 294920 | tf_op jit(solution)/shard_map/ppermute | solution.py:504
  32.8 0.7 %collective-permute-start.9 = (bf16[64,768]{1,0:T(8,128)(2,1)S(1)}, bf16[64,768]{1,0:T(8,128)(2,1)S(1)}, u32[]{:S(2)}, u32[]{:S(2)}) collective-permute-start(bf16[64,768]{1,0:T(8,128)(2,1)S(1)} %get-tuple-element.61), channel_id=1, source_target_pairs={{0,0},{1,2},{2,1},{3,3},{4,4},{5,6},{6,5},{7,7},{8,8},{9,10},{10,9... | collective-permute-start | bytes 294920 | tf_op jit(solution)/shard_map/ppermute | solution.py:504
  33.5 6.0 %collective-permute-done.10.refs_2_ = bf16[64,768]{1,0:T(8,128)(2,1)S(1)} collective-permute-done((bf16[64,768]{1,0:T(8,128)(2,1)S(1)}, bf16[64,768]{1,0:T(8,128)(2,1)S(1)}, u32[]{:S(2)}, u32[]{:S(2)}) %collective-permute-start.10) | collective-permute-done | bytes 98336 | tf_op jit(solution)/shard_map/ppermute | solution.py:504
  39.5 0.0 collective-permute-done.11.refs_3_
  39.5 1.9 %collective-permute-done.8.refs_0_ = bf16[64,768]{1,0:T(8,128)(2,1)S(1)} collective-permute-done((bf16[64,768]{1,0:T(8,128)(2,1)S(1)}, bf16[64,768]{1,0:T(8,128)(2,1)S(1)}, u32[]{:S(2)}, u32[]{:S(2)}) %collective-permute-start.8) | collective-permute-done | bytes 98336 | tf_op jit(solution)/shard_map/ppermute | solution.py:504
  41.5 0.1 collective-permute-start.12
  41.6 0.8 %column_project.1 = (bf16[256,384]{1,0:T(8,128)(2,1)S(1)}, bf16[256,384]{1,0:T(8,128)(2,1)S(1)}, bf16[256,384]{1,0:T(8,128)(2,1)S(1)}) custom-call(s32[1]{0:T(128)} %bitcast.place_ref, bf16[768,768]{1,0:T(8,128)(2,1)S(1)} %copy-done, bf16[768,768]{1,0:T(8,128)(2,1)S(1)} %copy-done.1, bf16[768,768]{1,0:T(8,128)(2,1)S(1)} %copy-done.2, ...), custom_call_target="tpu_custom_call" | custom-call | flops 452984832 | bytes 1769472 | tf_op jit(solution)/shard_map/column_project/pallas_call | solution.py:615
  42.4 0.9 %collective-permute-done.12.other_ref = bf16[4,64,768]{2,1,0:T(8,128)(2,1)S(1)} collective-permute-done((bf16[4,64,768]{2,1,0:T(8,128)(2,1)S(1)}, bf16[4,64,768]{2,1,0:T(8,128)(2,1)S(1)}, u32[]{:S(2)}, u32[]{:S(2)}) %collective-permute-start.12) | collective-permute-done | bytes 393248 | tf_op jit(solution)/shard_map/ppermute | solution.py:479
  43.3 2.2 %column_attention.1 = (bf16[4,64,384]{2,1,0:T(8,128)(2,1)S(1)}, bf16[4,64,384]{2,1,0:T(8,128)(2,1)S(1)}) custom-call(s32[4]{0:T(128)S(1)} %copy-done.8, s32[128]{0:T(128)S(1)} %copy-done.9, s32[1]{0:T(128)} %bitcast.place_ref, bf16[768,768]{1,0:T(8,128)(2,1)S(1)} %copy-done, bf16[768,768]{1,0:T(8,128)(2,1)S(1)} %copy-done.1, bf16[768,768]{1,0:T(8,128)(2,1)S(1)} %copy-done.2, ...), custom_call_target="tpu_custom_call" | custom-call | flops 1207959552 | bytes 3538944 | tf_op jit(solution)/shard_map/column_attention/pallas_call | solution.py:625
  45.5 0.2 collective-permute-start.13
  45.7 1.3 %collective-permute-done.13.other_ref = bf16[4,64,384]{2,1,0:T(8,128)(2,1)S(1)} collective-permute-done((bf16[4,64,384]{2,1,0:T(8,128)(2,1)S(1)}, bf16[4,64,384]{2,1,0:T(8,128)(2,1)S(1)}, u32[]{:S(2)}, u32[]{:S(2)}) %collective-permute-start.13) | collective-permute-done | bytes 196640 | tf_op jit(solution)/shard_map/ppermute | solution.py:479
  47.0 0.5 collective-permute-start.14
  47.6 2.6 %collective-permute-start.15 = (bf16[64,768]{1,0:T(8,128)(2,1)S(1)}, bf16[64,768]{1,0:T(8,128)(2,1)S(1)}, u32[]{:S(2)}, u32[]{:S(2)}) collective-permute-start(bf16[64,768]{1,0:T(8,128)(2,1)S(1)} %get-tuple-element.70), channel_id=1, source_target_pairs={{4,0},{6,1},{5,2},{7,3},{8,4},{10,5},{9,6},{11,7},{12,8},{14,9},{1... | collective-permute-start | bytes 294920 | tf_op jit(solution)/shard_map/ppermute | solution.py:508
  50.1 0.0 collective-permute-start.16
  50.1 0.7 %collective-permute-start.17 = (bf16[64,768]{1,0:T(8,128)(2,1)S(1)}, bf16[64,768]{1,0:T(8,128)(2,1)S(1)}, u32[]{:S(2)}, u32[]{:S(2)}) collective-permute-start(bf16[64,768]{1,0:T(8,128)(2,1)S(1)} %get-tuple-element.72), channel_id=1, source_target_pairs={{0,0},{2,1},{1,2},{3,3},{4,4},{6,5},{5,6},{7,7},{8,8},{10,9},{9,10... | collective-permute-start | bytes 294920 | tf_op jit(solution)/shard_map/ppermute | solution.py:508
  50.8 4.8 %collective-permute-done.14.refs_0_ = bf16[64,768]{1,0:T(8,128)(2,1)S(1)} collective-permute-done((bf16[64,768]{1,0:T(8,128)(2,1)S(1)}, bf16[64,768]{1,0:T(8,128)(2,1)S(1)}, u32[]{:S(2)}, u32[]{:S(2)}) %collective-permute-start.14) | collective-permute-done | bytes 98336 | tf_op jit(solution)/shard_map/ppermute | solution.py:508
  55.6 0.0 collective-permute-done.15.refs_1_
  55.6 1.9 %collective-permute-done.16.refs_2_ = bf16[64,768]{1,0:T(8,128)(2,1)S(1)} collective-permute-done((bf16[64,768]{1,0:T(8,128)(2,1)S(1)}, bf16[64,768]{1,0:T(8,128)(2,1)S(1)}, u32[]{:S(2)}, u32[]{:S(2)}) %collective-permute-start.16) | collective-permute-done | bytes 98336 | tf_op jit(solution)/shard_map/ppermute | solution.py:508
  57.5 0.6 %column_output.1 = (bf16[2,64,768]{2,1,0:T(8,128)(2,1)S(1)}, bf16[2,64,768]{2,1,0:T(8,128)(2,1)S(1)}) custom-call(s32[1]{0:T(128)} %bitcast.place_ref, bf16[768,768]{1,0:T(8,128)(2,1)S(1)} %copy-done.6, bf16[256,768]{1,0:T(8,128)(2,1)S(1)} %get-tuple-element.56.after_ref, bf16[64,768]{1,0:T(8,128)(2,1)S(1)} %collective-permute-done.14.refs_0_, ...), custom_call_target="tpu_custom_call" | custom-call | flops 301989888 | bytes 1179648 | tf_op jit(solution)/shard_map/column_output/pallas_call | solution.py:645
  58.2 0.9 %collective-permute-start.18 = (bf16[2,64,768]{2,1,0:T(8,128)(2,1)S(1)}, bf16[2,64,768]{2,1,0:T(8,128)(2,1)S(1)}, u32[]{:S(2)}, u32[]{:S(2)}) collective-permute-start(bf16[2,64,768]{2,1,0:T(8,128)(2,1)S(1)} %get-tuple-element.74), channel_id=1, source_target_pairs={{0,1},{1,0},{2,3},{3,2},{4,5},{5,4},{6,7},{7,6},{8,9},{9,8},{10,11... | collective-permute-start | bytes 589832 | tf_op jit(solution)/shard_map/ppermute | solution.py:479
  59.1 1.1 %collective-permute-done.18.other_ref = bf16[2,64,768]{2,1,0:T(8,128)(2,1)S(1)} collective-permute-done((bf16[2,64,768]{2,1,0:T(8,128)(2,1)S(1)}, bf16[2,64,768]{2,1,0:T(8,128)(2,1)S(1)}, u32[]{:S(2)}, u32[]{:S(2)}) %collective-permute-start.18) | collective-permute-done | bytes 196640 | tf_op jit(solution)/shard_map/ppermute | solution.py:479
  60.2 0.8 %assemble.1 = bf16[2,128,768]{2,1,0:T(8,128)(2,1)} custom-call(s32[1]{0:T(128)} %bitcast.place_ref, bf16[2,64,768]{2,1,0:T(8,128)(2,1)S(1)} %get-tuple-element.73.mine_ref, bf16[2,64,768]{2,1,0:T(8,128)(2,1)S(1)} %collective-permute-done.18.other_ref), custom_call_target="tpu_custom_call" | custom-call | flops 196608 | bytes 786432 | tf_op jit(solution)/shard_map/assemble/pallas_call | solution.py:654
  (25 shorter events, 0.1 us)
Async XLA Ops:
  0.0 2.9 %collective-permute-start = (bf16[256,768]{1,0:T(8,128)(2,1)}, bf16[256,768]{1,0:T(8,128)(2,1)S(1)}, u32[]{:S(2)}, u32[]{:S(2)}) collective-permute-start(bf16[256,768]{1,0:T(8,128)(2,1)} %bitcast.2), channel_id=1, source_target_pairs={{0,1},{1,0},{2,3},{3,2},{4,5},{5,4},{6,7},{7,6},{8,9},{9,8},{10,11... | collective-permute-start | bytes 1179656 | tf_op jit(solution)/shard_map/ppermute | solution.py:479
  0.5 2.5 %copy-start.7 = (f32[768]{0:T(1024)S(1)}, f32[768]{0:T(1024)}, u32[]{:S(2)}) copy-start(f32[768]{0:T(1024)} %gain_ref.1) | copy-start | bytes 9220
  0.5 2.5 %copy-start.8 = (s32[4]{0:T(128)S(1)}, s32[4]{0:T(128)}, u32[]{:S(2)}) copy-start(s32[4]{0:T(128)} %depth_ref.3) | copy-start | bytes 52
  0.5 2.5 %copy-start.9 = (s32[128]{0:T(128)S(1)}, s32[128]{0:T(128)}, u32[]{:S(2)}) copy-start(s32[128]{0:T(128)} %prot_ref.3) | copy-start | bytes 1540
  3.0 13.9 %copy-start.10 = (f32[768]{0:T(1024)S(1)}, f32[768]{0:T(1024)}, u32[]{:S(2)}) copy-start(f32[768]{0:T(1024)} %param.21) | copy-start | bytes 9220
  3.0 21.6 %copy-start.3 = (bf16[2,128,768]{2,1,0:T(8,128)(2,1)S(1)}, bf16[2,128,768]{2,1,0:T(8,128)(2,1)}, u32[]{:S(2)}) copy-start(bf16[2,128,768]{2,1,0:T(8,128)(2,1)} %param.13) | copy-start | bytes 1179652
  3.0 21.6 %copy-start.5 = (bf16[768,768]{1,0:T(8,128)(2,1)S(1)}, bf16[768,768]{1,0:T(8,128)(2,1)}, u32[]{:S(2)}) copy-start(bf16[768,768]{1,0:T(8,128)(2,1)} %w_ref.3) | copy-start | bytes 3538948
  5.4 7.5 %collective-permute-start.1 = (f32[16,768]{1,0:T(8,128)S(1)}, f32[16,768]{1,0:T(8,128)S(1)}, u32[]{:S(2)}, u32[]{:S(2)}) collective-permute-start(f32[16,768]{1,0:T(8,128)S(1)} %get-tuple-element.52), channel_id=1, source_target_pairs={{0,8},{1,9},{2,10},{3,11},{4,12},{5,13},{6,14},{7,15},{8,0},{9,1},... | collective-permute-start | bytes 147464 | tf_op jit(solution)/shard_map/ppermute | solution.py:500
  9.0 6.2 %collective-permute-start.2 = (f32[16,768]{1,0:T(8,128)S(1)}, f32[16,768]{1,0:T(8,128)S(1)}, u32[]{:S(2)}, u32[]{:S(2)}) collective-permute-start(f32[16,768]{1,0:T(8,128)S(1)} %get-tuple-element.53), channel_id=1, source_target_pairs={{0,4},{1,5},{2,6},{3,7},{4,8},{5,9},{6,10},{7,11},{8,12},{9,13},{1... | collective-permute-start | bytes 147464 | tf_op jit(solution)/shard_map/ppermute | solution.py:500
  10.6 4.7 %collective-permute-start.3 = (f32[16,768]{1,0:T(8,128)S(1)}, f32[16,768]{1,0:T(8,128)S(1)}, u32[]{:S(2)}, u32[]{:S(2)}) collective-permute-start(f32[16,768]{1,0:T(8,128)S(1)} %get-tuple-element.54), channel_id=1, source_target_pairs={{0,12},{1,13},{2,14},{3,15},{4,0},{5,1},{6,2},{7,3},{8,4},{9,5},{1... | collective-permute-start | bytes 147464 | tf_op jit(solution)/shard_map/ppermute | solution.py:500
  15.3 4.2 %collective-permute-start.4 = (f32[16,768]{1,0:T(8,128)S(1)}, f32[16,768]{1,0:T(8,128)S(1)}, u32[]{:S(2)}, u32[]{:S(2)}) collective-permute-start(f32[16,768]{1,0:T(8,128)S(1)} %add.1.mine_ref), channel_id=1, source_target_pairs={{0,2},{1,3},{2,0},{3,1},{4,6},{5,7},{6,4},{7,5},{8,10},{9,11},{10,... | collective-permute-start | bytes 147464 | tf_op jit(solution)/shard_map/ppermute | solution.py:479
  19.8 5.7 %collective-permute-start.5 = (bf16[16,768]{1,0:T(8,128)(2,1)S(1)}, bf16[16,768]{1,0:T(8,128)(2,1)S(1)}, u32[]{:S(2)}, u32[]{:S(2)}) collective-permute-start(bf16[16,768]{1,0:T(8,128)(2,1)S(1)} %row_softmax.1.refs_3_), channel_id=1, source_target_pairs={{0,8},{1,9},{2,10},{3,11},{4,12},{5,13},{6,14},{7,15},{8,0},{9,1},... | collective-permute-start | bytes 73736 | tf_op jit(solution)/shard_map/ppermute | solution.py:500
  20.8 5.6 %collective-permute-start.6 = (bf16[16,768]{1,0:T(8,128)(2,1)S(1)}, bf16[16,768]{1,0:T(8,128)(2,1)S(1)}, u32[]{:S(2)}, u32[]{:S(2)}) collective-permute-start(bf16[16,768]{1,0:T(8,128)(2,1)S(1)} %row_softmax.1.refs_3_), channel_id=1, source_target_pairs={{0,4},{1,5},{2,6},{3,7},{4,8},{5,9},{6,10},{7,11},{8,12},{9,13},{1... | collective-permute-start | bytes 73736 | tf_op jit(solution)/shard_map/ppermute | solution.py:500
  23.8 3.8 %collective-permute-start.7 = (bf16[16,768]{1,0:T(8,128)(2,1)S(1)}, bf16[16,768]{1,0:T(8,128)(2,1)S(1)}, u32[]{:S(2)}, u32[]{:S(2)}) collective-permute-start(bf16[16,768]{1,0:T(8,128)(2,1)S(1)} %row_softmax.1.refs_3_), channel_id=1, source_target_pairs={{0,12},{1,13},{2,14},{3,15},{4,0},{5,1},{6,2},{7,3},{8,4},{9,5},{1... | collective-permute-start | bytes 73736 | tf_op jit(solution)/shard_map/ppermute | solution.py:500
  24.6 3.0 %copy-start.4 = (bf16[768,768]{1,0:T(8,128)(2,1)S(1)}, bf16[768,768]{1,0:T(8,128)(2,1)}, u32[]{:S(2)}) copy-start(bf16[768,768]{1,0:T(8,128)(2,1)} %w_ref.4) | copy-start | bytes 3538948
  27.6 13.9 %copy-start = (bf16[768,768]{1,0:T(8,128)(2,1)S(1)}, bf16[768,768]{1,0:T(8,128)(2,1)}, u32[]{:S(2)}) copy-start(bf16[768,768]{1,0:T(8,128)(2,1)} %wq_ref.1) | copy-start | bytes 3538948
  27.6 13.9 %copy-start.1 = (bf16[768,768]{1,0:T(8,128)(2,1)S(1)}, bf16[768,768]{1,0:T(8,128)(2,1)}, u32[]{:S(2)}) copy-start(bf16[768,768]{1,0:T(8,128)(2,1)} %wk_ref.1) | copy-start | bytes 3538948
  27.6 13.9 %copy-start.2 = (bf16[768,768]{1,0:T(8,128)(2,1)S(1)}, bf16[768,768]{1,0:T(8,128)(2,1)}, u32[]{:S(2)}) copy-start(bf16[768,768]{1,0:T(8,128)(2,1)} %wv_ref.1) | copy-start | bytes 3538948
  28.9 10.6 %collective-permute-start.10 = (bf16[64,768]{1,0:T(8,128)(2,1)S(1)}, bf16[64,768]{1,0:T(8,128)(2,1)S(1)}, u32[]{:S(2)}, u32[]{:S(2)}) collective-permute-start(bf16[64,768]{1,0:T(8,128)(2,1)S(1)} %get-tuple-element.62), channel_id=1, source_target_pairs={{0,8},{1,10},{2,9},{3,11},{4,12},{5,14},{6,13},{7,15},{8,0},{9,2},... | collective-permute-start | bytes 294920 | tf_op jit(solution)/shard_map/ppermute | solution.py:504
  29.0 10.5 %collective-permute-start.11 = (bf16[64,768]{1,0:T(8,128)(2,1)S(1)}, bf16[64,768]{1,0:T(8,128)(2,1)S(1)}, u32[]{:S(2)}, u32[]{:S(2)}) collective-permute-start(bf16[64,768]{1,0:T(8,128)(2,1)S(1)} %get-tuple-element.63), channel_id=1, source_target_pairs={{0,4},{1,6},{2,5},{3,7},{4,8},{5,10},{6,9},{7,11},{8,12},{9,14},{1... | collective-permute-start | bytes 294920 | tf_op jit(solution)/shard_map/ppermute | solution.py:504
  32.1 9.3 %collective-permute-start.8 = (bf16[64,768]{1,0:T(8,128)(2,1)S(1)}, bf16[64,768]{1,0:T(8,128)(2,1)S(1)}, u32[]{:S(2)}, u32[]{:S(2)}) collective-permute-start(bf16[64,768]{1,0:T(8,128)(2,1)S(1)} %get-tuple-element.60), channel_id=1, source_target_pairs={{0,12},{1,14},{2,13},{3,15},{4,0},{5,2},{6,1},{7,3},{8,4},{9,6},{1... | collective-permute-start | bytes 294920 | tf_op jit(solution)/shard_map/ppermute | solution.py:504
  32.8 8.6 %collective-permute-start.9 = (bf16[64,768]{1,0:T(8,128)(2,1)S(1)}, bf16[64,768]{1,0:T(8,128)(2,1)S(1)}, u32[]{:S(2)}, u32[]{:S(2)}) collective-permute-start(bf16[64,768]{1,0:T(8,128)(2,1)S(1)} %get-tuple-element.61), channel_id=1, source_target_pairs={{0,0},{1,2},{2,1},{3,3},{4,4},{5,6},{6,5},{7,7},{8,8},{9,10},{10,9... | collective-permute-start | bytes 294920 | tf_op jit(solution)/shard_map/ppermute | solution.py:504
  41.5 1.8 %collective-permute-start.12 = (bf16[4,64,768]{2,1,0:T(8,128)(2,1)S(1)}, bf16[4,64,768]{2,1,0:T(8,128)(2,1)S(1)}, u32[]{:S(2)}, u32[]{:S(2)}) collective-permute-start(bf16[4,64,768]{2,1,0:T(8,128)(2,1)S(1)} %pack.1), channel_id=1, source_target_pairs={{0,1},{1,0},{2,3},{3,2},{4,5},{5,4},{6,7},{7,6},{8,9},{9,8},{10,11... | collective-permute-start | bytes 1179656 | tf_op jit(solution)/shard_map/ppermute | solution.py:479
  43.3 14.3 %copy-start.6 = (bf16[768,768]{1,0:T(8,128)(2,1)S(1)}, bf16[768,768]{1,0:T(8,128)(2,1)}, u32[]{:S(2)}) copy-start(bf16[768,768]{1,0:T(8,128)(2,1)} %w_ref.5) | copy-start | bytes 3538948
  45.5 1.5 %collective-permute-start.13 = (bf16[4,64,384]{2,1,0:T(8,128)(2,1)S(1)}, bf16[4,64,384]{2,1,0:T(8,128)(2,1)S(1)}, u32[]{:S(2)}, u32[]{:S(2)}) collective-permute-start(bf16[4,64,384]{2,1,0:T(8,128)(2,1)S(1)} %get-tuple-element.68), channel_id=1, source_target_pairs={{0,1},{1,0},{2,3},{3,2},{4,5},{5,4},{6,7},{7,6},{8,9},{9,8},{10,11... | collective-permute-start | bytes 589832 | tf_op jit(solution)/shard_map/ppermute | solution.py:479
  47.0 8.5 %collective-permute-start.14 = (bf16[64,768]{1,0:T(8,128)(2,1)S(1)}, bf16[64,768]{1,0:T(8,128)(2,1)S(1)}, u32[]{:S(2)}, u32[]{:S(2)}) collective-permute-start(bf16[64,768]{1,0:T(8,128)(2,1)S(1)} %get-tuple-element.69), channel_id=1, source_target_pairs={{8,0},{10,1},{9,2},{11,3},{12,4},{14,5},{13,6},{15,7},{0,8},{2,9},... | collective-permute-start | bytes 294920 | tf_op jit(solution)/shard_map/ppermute | solution.py:508
  47.6 8.0 %collective-permute-start.15 = (bf16[64,768]{1,0:T(8,128)(2,1)S(1)}, bf16[64,768]{1,0:T(8,128)(2,1)S(1)}, u32[]{:S(2)}, u32[]{:S(2)}) collective-permute-start(bf16[64,768]{1,0:T(8,128)(2,1)S(1)} %get-tuple-element.70), channel_id=1, source_target_pairs={{4,0},{6,1},{5,2},{7,3},{8,4},{10,5},{9,6},{11,7},{12,8},{14,9},{1... | collective-permute-start | bytes 294920 | tf_op jit(solution)/shard_map/ppermute | solution.py:508
  50.1 7.4 %collective-permute-start.16 = (bf16[64,768]{1,0:T(8,128)(2,1)S(1)}, bf16[64,768]{1,0:T(8,128)(2,1)S(1)}, u32[]{:S(2)}, u32[]{:S(2)}) collective-permute-start(bf16[64,768]{1,0:T(8,128)(2,1)S(1)} %get-tuple-element.71), channel_id=1, source_target_pairs={{12,0},{14,1},{13,2},{15,3},{0,4},{2,5},{1,6},{3,7},{4,8},{6,9},{5... | collective-permute-start | bytes 294920 | tf_op jit(solution)/shard_map/ppermute | solution.py:508
  50.1 7.4 %collective-permute-start.17 = (bf16[64,768]{1,0:T(8,128)(2,1)S(1)}, bf16[64,768]{1,0:T(8,128)(2,1)S(1)}, u32[]{:S(2)}, u32[]{:S(2)}) collective-permute-start(bf16[64,768]{1,0:T(8,128)(2,1)S(1)} %get-tuple-element.72), channel_id=1, source_target_pairs={{0,0},{2,1},{1,2},{3,3},{4,4},{6,5},{5,6},{7,7},{8,8},{10,9},{9,10... | collective-permute-start | bytes 294920 | tf_op jit(solution)/shard_map/ppermute | solution.py:508
  58.2 2.0 %collective-permute-start.18 = (bf16[2,64,768]{2,1,0:T(8,128)(2,1)S(1)}, bf16[2,64,768]{2,1,0:T(8,128)(2,1)S(1)}, u32[]{:S(2)}, u32[]{:S(2)}) collective-permute-start(bf16[2,64,768]{2,1,0:T(8,128)(2,1)S(1)} %get-tuple-element.74), channel_id=1, source_target_pairs={{0,1},{1,0},{2,3},{3,2},{4,5},{5,4},{6,7},{7,6},{8,9},{9,8},{10,11... | collective-permute-start | bytes 589832 | tf_op jit(solution)/shard_map/ppermute | solution.py:479

commit v9 on v8

--- a/solution.py
+++ b/solution.py
@@ -87,17 +87,23 @@
     gain_hbm,
     wq_hbm,
     wk_hbm,
+    depth_hbm,
+    prot_hbm,
     normed_ref,
     query_ref,
     key_ref,
     wq_ref,
     wk_ref,
+    same_ref,
+    seen_ref,
     x_ref,
     gain_ref,
+    depth_ref,
+    prot_ref,
     sems,
 ):
     tokens, width = x_ref.shape
-    pairs = [(x_hbm, x_ref), (gain_hbm, gain_ref)]
+    pairs = [(x_hbm, x_ref), (gain_hbm, gain_ref), (depth_hbm, depth_ref), (prot_hbm, prot_ref)]
     for n in range(width // 256):
         for source, target in ((wq_hbm, wq_ref), (wk_hbm, wk_ref)):
             pairs.append((source.at[256 * n : 256 * n + 256], target.at[256 * n : 256 * n + 256]))
@@ -107,50 +113,53 @@
     for copy in copies[:2]:
         copy.wait()
     normed_ref[...] = norm(x_ref[...].astype(F32), gain_ref[...].reshape(1, width)).astype(BF16)
-    for copy in copies[2:]:
+    for copy in copies[2:4]:
+        copy.wait()
+    prot = prot_ref[...].reshape(1, columns).astype(F32)
+    depth = jnp.zeros((1, columns), F32)
+    for p in range(depth_ref.shape[0]):
+        depth = jnp.where(prot == float(p), depth_ref[p].astype(F32), depth)
+    square = (columns, columns)
+    same = jnp.broadcast_to(to_column(prot, columns), square) == jnp.broadcast_to(prot, square)
+    same_ref[...] = jnp.where(same, 1.0, 0.0)
+    seen_ref[...] = jnp.broadcast_to(to_column(depth, columns), square)
+    for copy in copies[4:]:
         copy.wait()
     query_ref[...] = dot(query_tokens(normed_ref, place_ref, columns), wq_ref[...]).astype(BF16)
     key_ref[...] = dot(normed_ref[...], wk_ref[...]).astype(BF16)
 
 
 def row_scores_kernel(
-    depth_ref,
     place_ref,
     x_ref,
     gain_ref,
-    prot_ref,
     wq_ref,
     wk_ref,
     query_ref,
     key_ref,
+    same_ref,
+    seen_ref,
     *refs,
 ):
-    outs, (normed_ref, same_ref, part_ref) = refs[:-3], refs[-3:]
-    columns = prot_ref.shape[0]
+    outs, (normed_ref, part_ref) = refs[:-2], refs[-2:]
+    columns = same_ref.shape[0]
     tokens, width = x_ref.shape
     rows, local, quarter = tokens // columns, columns // 2, columns // PLANE
     planes, own = part_ref.shape[:2]
     place = place_ref[0]
     core = (place % 2) == 0
     normed_ref[...] = norm(x_ref[...].astype(F32), gain_ref[...].reshape(1, width)).astype(BF16)
-    prot = prot_ref[...].reshape(1, columns).astype(F32)
-    depth = jnp.zeros((1, columns), F32)
-    for p in range(depth_ref.shape[0]):
-        depth = jnp.where(prot == float(p), depth_ref[p].astype(F32), depth)
-    prot_col = to_column(prot, columns)
-    depth_col = to_column(depth, columns)
-    same = jnp.broadcast_to(prot_col, (columns, columns)) == jnp.broadcast_to(prot, (columns, columns))
-    same_f = jnp.where(same, 1.0, 0.0)
-    same_ref[...] = same_f
-    same_l = own_columns(same_f, core, quarter)
-    depth_l = own_columns(depth_col, core, quarter)
+    same_l = own_columns(same_ref[...], core, quarter)
+    seen = seen_ref[...]
+    depth_l = own_columns(seen, core, quarter)
     low = iota((local, columns), 1) < 64
     first = jnp.where(low, same_l, pltpu.roll(same_l, 64, 1)) > 0.5
     even, odd = half_masks(256)
     other = place + 1 - 2 * (place % 2)
     ids = [place * rows + r for r in range(rows)] + [other * rows + r for r in range(rows)]
     seen_q = [jnp.where(i.astype(F32) < depth_l, 1.0, 0.0) for i in ids]
-    seen_k = [jnp.where(i.astype(F32) < depth_col, 1.0, 0.0) for i in ids]
+    seen_k = [jnp.where(i.astype(F32) < seen, 1.0, 0.0) for i in ids]
+    seen_q, seen_k = ([jnp.concatenate([m, m], axis=1) for m in masks] for masks in (seen_q, seen_k))
     tokens_q = query_tokens(normed_ref, place_ref, columns)
     for n in range(width // 256):
         cols = slice(256 * n, 256 * n + 256)
@@ -531,9 +540,8 @@
     tokens = rows * columns
     planes, local = devices // PLANE, columns // 2
     size = tokens // planes
-    sum_steps = move_steps = back_steps = far_first(planes)
-    move_steps = move_steps[2:] + move_steps[:2]
-    share_steps = far_first(planes)
+    sum_steps = back_steps = share_steps = far_first(planes)
+    move_steps = [s for s in (1, 0) if s < planes] + [s for s in back_steps if s > 1]
     x = alignment.reshape(tokens, width)
     shape = jax.ShapeDtypeStruct
     square = 2 * tokens * width * width
@@ -541,28 +549,31 @@
     part = shape((local // planes, width), F32)
     matrix = shape((width, width), BF16)
     sibling = swap(x, 1)
-    normed, query, key, row_query, row_key = call(
+    normed, query, key, row_query, row_key, same, seen = call(
         functools.partial(row_own_kernel, columns),
-        (shape((tokens, width), BF16), shape((tokens // 2, width), BF16), shape((tokens, width), BF16), matrix, matrix),
-        "shhhh",
-        "vvvvv",
+        (shape((tokens, width), BF16), shape((tokens // 2, width), BF16), shape((tokens, width), BF16), matrix, matrix)
+        + (shape((columns, columns), F32),) * 2,
+        "shhhhhh",
+        "v" * 7,
         [
             pltpu.VMEM((tokens, width), BF16),
             pltpu.VMEM((width,), F32),
-            pltpu.SemaphoreType.DMA((2 + 2 * (width // 256),)),
+            pltpu.SMEM(row_depth.shape, jnp.int32),
+            pltpu.VMEM((columns,), jnp.int32),
+            pltpu.SemaphoreType.DMA((4 + 2 * (width // 256),)),
         ],
         (3 * square // 2, 4 * width * width, tokens),
         "row_own",
-    )(place, hbm(x), hbm(row_gain), hbm(row_query), hbm(row_key))
-    *pieces, normed_other, same = call(
+    )(place, hbm(x), hbm(row_gain), hbm(row_query), hbm(row_key), hbm(row_depth), hbm(protein_id))
+    *pieces, normed_other = call(
         row_scores_kernel,
-        (part,) * planes + (shape((tokens, width), BF16), shape((columns, columns), F32)),
-        "ss" + "v" * 7,
-        "v" * (planes + 2),
+        (part,) * planes + (shape((tokens, width), BF16),),
+        "s" + "v" * 8,
+        "v" * (planes + 1),
         [pltpu.VMEM((planes, local // planes, width), F32)],
         (3 * square // 2, 4 * width * width, tokens),
         "row_scores",
-    )(row_depth, place, sibling, row_gain, protein_id, row_query, row_key, query, key)
+    )(place, sibling, row_gain, row_query, row_key, query, key, same, seen)
     column_query, column_key, column_value, late, normed = lax.optimization_barrier(
         (column_query, column_key, column_value, x, normed)
     )

time: 61.1 us -> 60.5 us (level)
  waiting for transfers between devices: 25.1 us -> 23.9 us
  starting transfers between devices: 24 us -> 25 us
    ppermute x4, starting transfers between devices: 3.76 us -> 5.57 us  [spin_back(): return lax.ppermute(array, 'seq', [(b, a) for a, b in spin_pairs(step)])]
    ppermute x4, waiting for transfers between devices: 7.96 us -> 6.83 us  [spin(): return lax.ppermute(array, 'seq', spin_pairs(step))]
    ppermute x4, starting transfers between devices: 4.61 us -> 3.92 us  [spin(): return lax.ppermute(array, 'seq', spin_pairs(step))]
  transfers between devices with their start and end apart: 19 -> 19, of which waited for: 12 -> 13; matrix products, arithmetic and copies ran while one was open for 0% -> 0% of each run, Pallas kernels for 7% -> 7%
where the time goes in v9:
time: 60.5 us; the launch traced here: 60.3 us
  starting transfers between devices  25 us (41%)
  waiting for transfers between devices  23.9 us (40%)
  Pallas kernels  11 us (18%)
    ppermute x6, starting transfers between devices, shift(): lax.ppermute(array, 'seq', [(i, (i + PLANE * step) % devices) for i in ra...  12.4 us
    ppermute x4, waiting for transfers between devices, spin(): return lax.ppermute(array, 'seq', spin_pairs(step))  6.83 us
    ppermute x4, waiting for transfers between devices, spin_back(): return lax.ppermute(array, 'seq', [(b, a) for a, b in spin_pairs(step)])  6.72 us
    ppermute x5, waiting for transfers between devices, swap(): return lax.ppermute(array, 'seq', [(i, i ^ offset) for i in range(devices)])  5.75 us
    ppermute x4, starting transfers between devices, spin_back(): return lax.ppermute(array, 'seq', [(b, a) for a, b in spin_pairs(step)])  5.57 us
    ppermute x6, waiting for transfers between devices, shift(): lax.ppermute(array, 'seq', [(i, (i + PLANE * step) % devices) for i in ra...  4.64 us
    ppermute x4, starting transfers between devices, spin(): return lax.ppermute(array, 'seq', spin_pairs(step))  3.92 us
    ppermute x5, starting transfers between devices, swap(): return lax.ppermute(array, 'seq', [(i, i ^ offset) for i in range(devices)])  3.19 us
  transfers between devices with their start and end apart: 19, of which 13 were waited for; matrix products, arithmetic and copies ran while one was open for 0% of the time, Pallas kernels for 7%

profile of v9, /device:TPU:0, one launch (start us, length us, event | category | flops | bytes accessed | tf_op | source)
XLA Modules:
  0.0 60.3 jit_solution(8965774768405945589)
XLA Ops:
  0.0 0.5 collective-permute-start
  0.5 2.5 %row_own.1 = (bf16[256,768]{1,0:T(8,128)(2,1)S(1)}, bf16[128,768]{1,0:T(8,128)(2,1)S(1)}, bf16[256,768]{1,0:T(8,128)(2,1)S(1)}, bf16[768,768]{1,0:T(8,128)(2,1)S...) custom-call(s32[1]{0:T(128)} %bitcast.place_ref, bf16[256,768]{1,0:T(8,128)(2,1)} %bitcast.3, ...), custom_call_target="tpu_custom_call" | custom-call | flops 452984832 | bytes 2359296 | tf_op jit(solution)/shard_map/row_own/pallas_call | solution.py:552
  3.0 0.0 copy-start.10
  3.0 0.0 copy-start.3
  3.0 0.0 copy-start.5
  3.0 1.8 %row_scores.1 = (f32[16,768]{1,0:T(8,128)S(1)}, f32[16,768]{1,0:T(8,128)S(1)}, f32[16,768]{1,0:T(8,128)S(1)}, f32[16,768]{1,0:T(8,128)S(1)}, bf16[256,768]{1,0:T(8,128)(2,1)S(1)}) custom-call(s32[1]{0:T(128)} %bitcast.place_ref, bf16[256,768]{1,0:T(8,128)(2,1)S(1)} %collective-permute-done.x_ref.other_ref, f32[768]{0:T(1024)S(1)} %copy-done.7, ...), custom_call_target="tpu_custom_call" | custom-call | flops 452984832 | bytes 2359296 | tf_op jit(solution)/shard_map/row_scores/pallas_call | solution.py:568
  4.8 3.7 %collective-permute-start.1 = (f32[16,768]{1,0:T(8,128)S(1)}, f32[16,768]{1,0:T(8,128)S(1)}, u32[]{:S(2)}, u32[]{:S(2)}) collective-permute-start(f32[16,768]{1,0:T(8,128)S(1)} %get-tuple-element.54), channel_id=1, source_target_pairs={{0,8},{1,9},{2,10},{3,11},{4,12},{5,13},{6,14},{7,15},{8,0},{9,1},... | collective-permute-start | bytes 147464 | tf_op jit(solution)/shard_map/ppermute | solution.py:509
  8.4 1.6 %collective-permute-start.2 = (f32[16,768]{1,0:T(8,128)S(1)}, f32[16,768]{1,0:T(8,128)S(1)}, u32[]{:S(2)}, u32[]{:S(2)}) collective-permute-start(f32[16,768]{1,0:T(8,128)S(1)} %get-tuple-element.55), channel_id=1, source_target_pairs={{0,4},{1,5},{2,6},{3,7},{4,8},{5,9},{6,10},{7,11},{8,12},{9,13},{1... | collective-permute-start | bytes 147464 | tf_op jit(solution)/shard_map/ppermute | solution.py:509
  10.0 2.2 %collective-permute-start.3 = (f32[16,768]{1,0:T(8,128)S(1)}, f32[16,768]{1,0:T(8,128)S(1)}, u32[]{:S(2)}, u32[]{:S(2)}) collective-permute-start(f32[16,768]{1,0:T(8,128)S(1)} %get-tuple-element.56), channel_id=1, source_target_pairs={{0,12},{1,13},{2,14},{3,15},{4,0},{5,1},{6,2},{7,3},{8,4},{9,5},{1... | collective-permute-start | bytes 147464 | tf_op jit(solution)/shard_map/ppermute | solution.py:509
  12.3 0.0 collective-permute-done.1.refs_0_
  12.3 2.4 %collective-permute-done.2.refs_1_ = f32[16,768]{1,0:T(8,128)S(1)} collective-permute-done((f32[16,768]{1,0:T(8,128)S(1)}, f32[16,768]{1,0:T(8,128)S(1)}, u32[]{:S(2)}, u32[]{:S(2)}) %collective-permute-start.2) | collective-permute-done | bytes 49184 | tf_op jit(solution)/shard_map/ppermute | solution.py:509
  14.7 0.1 collective-permute-done.3.refs_2_
  14.8 1.6 %collective-permute-start.4 = (f32[16,768]{1,0:T(8,128)S(1)}, f32[16,768]{1,0:T(8,128)S(1)}, u32[]{:S(2)}, u32[]{:S(2)}) collective-permute-start(f32[16,768]{1,0:T(8,128)S(1)} %add.1.mine_ref), channel_id=1, source_target_pairs={{0,2},{1,3},{2,0},{3,1},{4,6},{5,7},{6,4},{7,5},{8,10},{9,11},{10,... | collective-permute-start | bytes 147464 | tf_op jit(solution)/shard_map/ppermute | solution.py:488
  16.4 2.6 %collective-permute-done.4.other_ref = f32[16,768]{1,0:T(8,128)S(1)} collective-permute-done((f32[16,768]{1,0:T(8,128)S(1)}, f32[16,768]{1,0:T(8,128)S(1)}, u32[]{:S(2)}, u32[]{:S(2)}) %collective-permute-start.4) | collective-permute-done | bytes 49184 | tf_op jit(solution)/shard_map/ppermute | solution.py:488
  18.9 0.3 row_softmax.1.refs_3_
  19.2 1.1 %collective-permute-start.5 = (bf16[16,768]{1,0:T(8,128)(2,1)S(1)}, bf16[16,768]{1,0:T(8,128)(2,1)S(1)}, u32[]{:S(2)}, u32[]{:S(2)}) collective-permute-start(bf16[16,768]{1,0:T(8,128)(2,1)S(1)} %row_softmax.1.refs_3_), channel_id=1, source_target_pairs={{0,8},{1,9},{2,10},{3,11},{4,12},{5,13},{6,14},{7,15},{8,0},{9,1},... | collective-permute-start | bytes 73736 | tf_op jit(solution)/shard_map/ppermute | solution.py:509
  20.3 3.0 %collective-permute-start.6 = (bf16[16,768]{1,0:T(8,128)(2,1)S(1)}, bf16[16,768]{1,0:T(8,128)(2,1)S(1)}, u32[]{:S(2)}, u32[]{:S(2)}) collective-permute-start(bf16[16,768]{1,0:T(8,128)(2,1)S(1)} %row_softmax.1.refs_3_), channel_id=1, source_target_pairs={{0,4},{1,5},{2,6},{3,7},{4,8},{5,9},{6,10},{7,11},{8,12},{9,13},{1... | collective-permute-start | bytes 73736 | tf_op jit(solution)/shard_map/ppermute | solution.py:509
  23.2 0.8 %collective-permute-start.7 = (bf16[16,768]{1,0:T(8,128)(2,1)S(1)}, bf16[16,768]{1,0:T(8,128)(2,1)S(1)}, u32[]{:S(2)}, u32[]{:S(2)}) collective-permute-start(bf16[16,768]{1,0:T(8,128)(2,1)S(1)} %row_softmax.1.refs_3_), channel_id=1, source_target_pairs={{0,12},{1,13},{2,14},{3,15},{4,0},{5,1},{6,2},{7,3},{8,4},{9,5},{1... | collective-permute-start | bytes 73736 | tf_op jit(solution)/shard_map/ppermute | solution.py:509
  24.1 0.8 %row_value.1 = (bf16[256,768]{1,0:T(8,128)(2,1)S(1)}, bf16[256,768]{1,0:T(8,128)(2,1)S(1)}, f32[6,256,128]{2,1,0:T(8,128)S(1)}) custom-call(s32[1]{0:T(128)} %bitcast.place_ref, bf16[256,768]{1,0:T(8,128)(2,1)S(1)} %get-tuple-element.43.x_ref, bf16[256,768]{1,0:T(8,128)(2,1)S(1)} %get-tuple-element.49.y_ref, bf16[768,768]{1,0:T(8,128)(2,1)S(1)} %copy-done.5, ...), custom_call_target="tpu_custom_call" | custom-call | flops 603979776 | bytes 1179648 | tf_op jit(solution)/shard_map/row_value/pallas_call | solution.py:583
  24.9 1.0 %collective-permute-done.6.refs_1_ = bf16[16,768]{1,0:T(8,128)(2,1)S(1)} collective-permute-done((bf16[16,768]{1,0:T(8,128)(2,1)S(1)}, bf16[16,768]{1,0:T(8,128)(2,1)S(1)}, u32[]{:S(2)}, u32[]{:S(2)}) %collective-permute-start.6) | collective-permute-done | bytes 24608 | tf_op jit(solution)/shard_map/ppermute | solution.py:509
  25.9 1.2 %collective-permute-done.7.refs_2_ = bf16[16,768]{1,0:T(8,128)(2,1)S(1)} collective-permute-done((bf16[16,768]{1,0:T(8,128)(2,1)S(1)}, bf16[16,768]{1,0:T(8,128)(2,1)S(1)}, u32[]{:S(2)}, u32[]{:S(2)}) %collective-permute-start.7) | collective-permute-done | bytes 24608 | tf_op jit(solution)/shard_map/ppermute | solution.py:509
  27.1 1.2 %row_output.1 = (bf16[256,768]{1,0:T(8,128)(2,1)S(1)}, bf16[64,768]{1,0:T(8,128)(2,1)S(1)}, bf16[64,768]{1,0:T(8,128)(2,1)S(1)}, bf16[64,768]{1,0:T(8,128)(2,1)S(1)}, bf16[64,768]{1,0:T(8,128)(2,1)S(1)}) custom-call(s32[1]{0:T(128)} %bitcast.place_ref, f32[128,128]{1,0:T(8,128)S(1)} %get-tuple-element.41.same_ref, ...), custom_call_target="tpu_custom_call" | custom-call | flops 301989888 | bytes 1179648 | tf_op jit(solution)/shard_map/row_output/pallas_call | solution.py:602
  28.3 0.1 collective-permute-start.10
  28.4 2.6 %collective-permute-start.11 = (bf16[64,768]{1,0:T(8,128)(2,1)S(1)}, bf16[64,768]{1,0:T(8,128)(2,1)S(1)}, u32[]{:S(2)}, u32[]{:S(2)}) collective-permute-start(bf16[64,768]{1,0:T(8,128)(2,1)S(1)} %get-tuple-element.65), channel_id=1, source_target_pairs={{0,12},{1,14},{2,13},{3,15},{4,0},{5,2},{6,1},{7,3},{8,4},{9,6},{1... | collective-permute-start | bytes 294920 | tf_op jit(solution)/shard_map/ppermute | solution.py:513
  31.1 0.5 collective-permute-start.8
  31.6 0.7 %collective-permute-start.9 = (bf16[64,768]{1,0:T(8,128)(2,1)S(1)}, bf16[64,768]{1,0:T(8,128)(2,1)S(1)}, u32[]{:S(2)}, u32[]{:S(2)}) collective-permute-start(bf16[64,768]{1,0:T(8,128)(2,1)S(1)} %get-tuple-element.63), channel_id=1, source_target_pairs={{0,0},{1,2},{2,1},{3,3},{4,4},{5,6},{6,5},{7,7},{8,8},{9,10},{10,9... | collective-permute-start | bytes 294920 | tf_op jit(solution)/shard_map/ppermute | solution.py:513
  32.2 4.7 %collective-permute-done.10.refs_2_ = bf16[64,768]{1,0:T(8,128)(2,1)S(1)} collective-permute-done((bf16[64,768]{1,0:T(8,128)(2,1)S(1)}, bf16[64,768]{1,0:T(8,128)(2,1)S(1)}, u32[]{:S(2)}, u32[]{:S(2)}) %collective-permute-start.10) | collective-permute-done | bytes 98336 | tf_op jit(solution)/shard_map/ppermute | solution.py:513
  36.9 2.1 %collective-permute-done.11.refs_3_ = bf16[64,768]{1,0:T(8,128)(2,1)S(1)} collective-permute-done((bf16[64,768]{1,0:T(8,128)(2,1)S(1)}, bf16[64,768]{1,0:T(8,128)(2,1)S(1)}, u32[]{:S(2)}, u32[]{:S(2)}) %collective-permute-start.11) | collective-permute-done | bytes 98336 | tf_op jit(solution)/shard_map/ppermute | solution.py:513
  39.1 0.0 collective-permute-done.9.refs_1_
  39.1 0.0 copy-start.8
  39.1 0.0 copy-start.9
  39.1 0.2 collective-permute-start.12
  39.3 0.8 %column_project.1 = (bf16[256,384]{1,0:T(8,128)(2,1)S(1)}, bf16[256,384]{1,0:T(8,128)(2,1)S(1)}, bf16[256,384]{1,0:T(8,128)(2,1)S(1)}) custom-call(s32[1]{0:T(128)} %bitcast.place_ref, bf16[768,768]{1,0:T(8,128)(2,1)S(1)} %copy-done, bf16[768,768]{1,0:T(8,128)(2,1)S(1)} %copy-done.1, bf16[768,768]{1,0:T(8,128)(2,1)S(1)} %copy-done.2, ...), custom_call_target="tpu_custom_call" | custom-call | flops 452984832 | bytes 1769472 | tf_op jit(solution)/shard_map/column_project/pallas_call | solution.py:626
  40.1 0.8 %collective-permute-done.12.other_ref = bf16[4,64,768]{2,1,0:T(8,128)(2,1)S(1)} collective-permute-done((bf16[4,64,768]{2,1,0:T(8,128)(2,1)S(1)}, bf16[4,64,768]{2,1,0:T(8,128)(2,1)S(1)}, u32[]{:S(2)}, u32[]{:S(2)}) %collective-permute-start.12) | collective-permute-done | bytes 393248 | tf_op jit(solution)/shard_map/ppermute | solution.py:488
  40.9 2.2 %column_attention.1 = (bf16[4,64,384]{2,1,0:T(8,128)(2,1)S(1)}, bf16[4,64,384]{2,1,0:T(8,128)(2,1)S(1)}) custom-call(s32[4]{0:T(128)S(1)} %copy-done.8, s32[128]{0:T(128)S(1)} %copy-done.9, s32[1]{0:T(128)} %bitcast.place_ref, bf16[768,768]{1,0:T(8,128)(2,1)S(1)} %copy-done, bf16[768,768]{1,0:T(8,128)(2,1)S(1)} %copy-done.1, bf16[768,768]{1,0:T(8,128)(2,1)S(1)} %copy-done.2, ...), custom_call_target="tpu_custom_call" | custom-call | flops 1207959552 | bytes 3538944 | tf_op jit(solution)/shard_map/column_attention/pallas_call | solution.py:636
  43.1 0.2 collective-permute-start.13
  43.4 1.3 %collective-permute-done.13.other_ref = bf16[4,64,384]{2,1,0:T(8,128)(2,1)S(1)} collective-permute-done((bf16[4,64,384]{2,1,0:T(8,128)(2,1)S(1)}, bf16[4,64,384]{2,1,0:T(8,128)(2,1)S(1)}, u32[]{:S(2)}, u32[]{:S(2)}) %collective-permute-start.13) | collective-permute-done | bytes 196640 | tf_op jit(solution)/shard_map/ppermute | solution.py:488
  44.7 2.3 %collective-permute-start.14 = (bf16[64,768]{1,0:T(8,128)(2,1)S(1)}, bf16[64,768]{1,0:T(8,128)(2,1)S(1)}, u32[]{:S(2)}, u32[]{:S(2)}) collective-permute-start(bf16[64,768]{1,0:T(8,128)(2,1)S(1)} %get-tuple-element.71), channel_id=1, source_target_pairs={{8,0},{10,1},{9,2},{11,3},{12,4},{14,5},{13,6},{15,7},{0,8},{2,9},... | collective-permute-start | bytes 294920 | tf_op jit(solution)/shard_map/ppermute | solution.py:517
  47.0 2.6 %collective-permute-start.15 = (bf16[64,768]{1,0:T(8,128)(2,1)S(1)}, bf16[64,768]{1,0:T(8,128)(2,1)S(1)}, u32[]{:S(2)}, u32[]{:S(2)}) collective-permute-start(bf16[64,768]{1,0:T(8,128)(2,1)S(1)} %get-tuple-element.72), channel_id=1, source_target_pairs={{4,0},{6,1},{5,2},{7,3},{8,4},{10,5},{9,6},{11,7},{12,8},{14,9},{1... | collective-permute-start | bytes 294920 | tf_op jit(solution)/shard_map/ppermute | solution.py:517
  49.6 0.0 collective-permute-start.16
  49.6 0.7 %collective-permute-start.17 = (bf16[64,768]{1,0:T(8,128)(2,1)S(1)}, bf16[64,768]{1,0:T(8,128)(2,1)S(1)}, u32[]{:S(2)}, u32[]{:S(2)}) collective-permute-start(bf16[64,768]{1,0:T(8,128)(2,1)S(1)} %get-tuple-element.74), channel_id=1, source_target_pairs={{0,0},{2,1},{1,2},{3,3},{4,4},{6,5},{5,6},{7,7},{8,8},{10,9},{9,10... | collective-permute-start | bytes 294920 | tf_op jit(solution)/shard_map/ppermute | solution.py:517
  50.3 0.2 collective-permute-done.14.refs_0_
  50.5 2.9 %collective-permute-done.15.refs_1_ = bf16[64,768]{1,0:T(8,128)(2,1)S(1)} collective-permute-done((bf16[64,768]{1,0:T(8,128)(2,1)S(1)}, bf16[64,768]{1,0:T(8,128)(2,1)S(1)}, u32[]{:S(2)}, u32[]{:S(2)}) %collective-permute-start.15) | collective-permute-done | bytes 98336 | tf_op jit(solution)/shard_map/ppermute | solution.py:517
  53.4 3.6 %collective-permute-done.16.refs_2_ = bf16[64,768]{1,0:T(8,128)(2,1)S(1)} collective-permute-done((bf16[64,768]{1,0:T(8,128)(2,1)S(1)}, bf16[64,768]{1,0:T(8,128)(2,1)S(1)}, u32[]{:S(2)}, u32[]{:S(2)}) %collective-permute-start.16) | collective-permute-done | bytes 98336 | tf_op jit(solution)/shard_map/ppermute | solution.py:517
  57.0 0.6 %column_output.1 = (bf16[2,64,768]{2,1,0:T(8,128)(2,1)S(1)}, bf16[2,64,768]{2,1,0:T(8,128)(2,1)S(1)}) custom-call(s32[1]{0:T(128)} %bitcast.place_ref, bf16[768,768]{1,0:T(8,128)(2,1)S(1)} %copy-done.6, bf16[256,768]{1,0:T(8,128)(2,1)S(1)} %get-tuple-element.58.after_ref, bf16[64,768]{1,0:T(8,128)(2,1)S(1)} %collective-permute-done.14.refs_0_, ...), custom_call_target="tpu_custom_call" | custom-call | flops 301989888 | bytes 1179648 | tf_op jit(solution)/shard_map/column_output/pallas_call | solution.py:656
  57.7 0.8 %collective-permute-start.18 = (bf16[2,64,768]{2,1,0:T(8,128)(2,1)S(1)}, bf16[2,64,768]{2,1,0:T(8,128)(2,1)S(1)}, u32[]{:S(2)}, u32[]{:S(2)}) collective-permute-start(bf16[2,64,768]{2,1,0:T(8,128)(2,1)S(1)} %get-tuple-element.76), channel_id=1, source_target_pairs={{0,1},{1,0},{2,3},{3,2},{4,5},{5,4},{6,7},{7,6},{8,9},{9,8},{10,11... | collective-permute-start | bytes 589832 | tf_op jit(solution)/shard_map/ppermute | solution.py:488
  58.4 1.1 %collective-permute-done.18.other_ref = bf16[2,64,768]{2,1,0:T(8,128)(2,1)S(1)} collective-permute-done((bf16[2,64,768]{2,1,0:T(8,128)(2,1)S(1)}, bf16[2,64,768]{2,1,0:T(8,128)(2,1)S(1)}, u32[]{:S(2)}, u32[]{:S(2)}) %collective-permute-start.18) | collective-permute-done | bytes 196640 | tf_op jit(solution)/shard_map/ppermute | solution.py:488
  59.5 0.8 %assemble.1 = bf16[2,128,768]{2,1,0:T(8,128)(2,1)} custom-call(s32[1]{0:T(128)} %bitcast.place_ref, bf16[2,64,768]{2,1,0:T(8,128)(2,1)S(1)} %get-tuple-element.75.mine_ref, bf16[2,64,768]{2,1,0:T(8,128)(2,1)S(1)} %collective-permute-done.18.other_ref), custom_call_target="tpu_custom_call" | custom-call | flops 196608 | bytes 786432 | tf_op jit(solution)/shard_map/assemble/pallas_call | solution.py:665
  (25 shorter events, 0.1 us)
Async XLA Ops:
  0.0 3.0 %collective-permute-start = (bf16[256,768]{1,0:T(8,128)(2,1)}, bf16[256,768]{1,0:T(8,128)(2,1)S(1)}, u32[]{:S(2)}, u32[]{:S(2)}) collective-permute-start(bf16[256,768]{1,0:T(8,128)(2,1)} %bitcast.2), channel_id=1, source_target_pairs={{0,1},{1,0},{2,3},{3,2},{4,5},{5,4},{6,7},{7,6},{8,9},{9,8},{10,11... | collective-permute-start | bytes 1179656 | tf_op jit(solution)/shard_map/ppermute | solution.py:488
  0.5 2.5 %copy-start.7 = (f32[768]{0:T(1024)S(1)}, f32[768]{0:T(1024)}, u32[]{:S(2)}) copy-start(f32[768]{0:T(1024)} %gain_ref.1) | copy-start | bytes 9220
  3.0 13.4 %copy-start.10 = (f32[768]{0:T(1024)S(1)}, f32[768]{0:T(1024)}, u32[]{:S(2)}) copy-start(f32[768]{0:T(1024)} %param.21) | copy-start | bytes 9220
  3.0 21.1 %copy-start.3 = (bf16[2,128,768]{2,1,0:T(8,128)(2,1)S(1)}, bf16[2,128,768]{2,1,0:T(8,128)(2,1)}, u32[]{:S(2)}) copy-start(bf16[2,128,768]{2,1,0:T(8,128)(2,1)} %param.13) | copy-start | bytes 1179652
  3.0 21.1 %copy-start.5 = (bf16[768,768]{1,0:T(8,128)(2,1)S(1)}, bf16[768,768]{1,0:T(8,128)(2,1)}, u32[]{:S(2)}) copy-start(bf16[768,768]{1,0:T(8,128)(2,1)} %w_ref.3) | copy-start | bytes 3538948
  4.8 7.5 %collective-permute-start.1 = (f32[16,768]{1,0:T(8,128)S(1)}, f32[16,768]{1,0:T(8,128)S(1)}, u32[]{:S(2)}, u32[]{:S(2)}) collective-permute-start(f32[16,768]{1,0:T(8,128)S(1)} %get-tuple-element.54), channel_id=1, source_target_pairs={{0,8},{1,9},{2,10},{3,11},{4,12},{5,13},{6,14},{7,15},{8,0},{9,1},... | collective-permute-start | bytes 147464 | tf_op jit(solution)/shard_map/ppermute | solution.py:509
  8.4 6.2 %collective-permute-start.2 = (f32[16,768]{1,0:T(8,128)S(1)}, f32[16,768]{1,0:T(8,128)S(1)}, u32[]{:S(2)}, u32[]{:S(2)}) collective-permute-start(f32[16,768]{1,0:T(8,128)S(1)} %get-tuple-element.55), channel_id=1, source_target_pairs={{0,4},{1,5},{2,6},{3,7},{4,8},{5,9},{6,10},{7,11},{8,12},{9,13},{1... | collective-permute-start | bytes 147464 | tf_op jit(solution)/shard_map/ppermute | solution.py:509
  10.0 4.7 %collective-permute-start.3 = (f32[16,768]{1,0:T(8,128)S(1)}, f32[16,768]{1,0:T(8,128)S(1)}, u32[]{:S(2)}, u32[]{:S(2)}) collective-permute-start(f32[16,768]{1,0:T(8,128)S(1)} %get-tuple-element.56), channel_id=1, source_target_pairs={{0,12},{1,13},{2,14},{3,15},{4,0},{5,1},{6,2},{7,3},{8,4},{9,5},{1... | collective-permute-start | bytes 147464 | tf_op jit(solution)/shard_map/ppermute | solution.py:509
  14.8 4.2 %collective-permute-start.4 = (f32[16,768]{1,0:T(8,128)S(1)}, f32[16,768]{1,0:T(8,128)S(1)}, u32[]{:S(2)}, u32[]{:S(2)}) collective-permute-start(f32[16,768]{1,0:T(8,128)S(1)} %add.1.mine_ref), channel_id=1, source_target_pairs={{0,2},{1,3},{2,0},{3,1},{4,6},{5,7},{6,4},{7,5},{8,10},{9,11},{10,... | collective-permute-start | bytes 147464 | tf_op jit(solution)/shard_map/ppermute | solution.py:488
  19.2 5.7 %collective-permute-start.5 = (bf16[16,768]{1,0:T(8,128)(2,1)S(1)}, bf16[16,768]{1,0:T(8,128)(2,1)S(1)}, u32[]{:S(2)}, u32[]{:S(2)}) collective-permute-start(bf16[16,768]{1,0:T(8,128)(2,1)S(1)} %row_softmax.1.refs_3_), channel_id=1, source_target_pairs={{0,8},{1,9},{2,10},{3,11},{4,12},{5,13},{6,14},{7,15},{8,0},{9,1},... | collective-permute-start | bytes 73736 | tf_op jit(solution)/shard_map/ppermute | solution.py:509
  20.3 5.6 %collective-permute-start.6 = (bf16[16,768]{1,0:T(8,128)(2,1)S(1)}, bf16[16,768]{1,0:T(8,128)(2,1)S(1)}, u32[]{:S(2)}, u32[]{:S(2)}) collective-permute-start(bf16[16,768]{1,0:T(8,128)(2,1)S(1)} %row_softmax.1.refs_3_), channel_id=1, source_target_pairs={{0,4},{1,5},{2,6},{3,7},{4,8},{5,9},{6,10},{7,11},{8,12},{9,13},{1... | collective-permute-start | bytes 73736 | tf_op jit(solution)/shard_map/ppermute | solution.py:509
  23.2 3.8 %collective-permute-start.7 = (bf16[16,768]{1,0:T(8,128)(2,1)S(1)}, bf16[16,768]{1,0:T(8,128)(2,1)S(1)}, u32[]{:S(2)}, u32[]{:S(2)}) collective-permute-start(bf16[16,768]{1,0:T(8,128)(2,1)S(1)} %row_softmax.1.refs_3_), channel_id=1, source_target_pairs={{0,12},{1,13},{2,14},{3,15},{4,0},{5,1},{6,2},{7,3},{8,4},{9,5},{1... | collective-permute-start | bytes 73736 | tf_op jit(solution)/shard_map/ppermute | solution.py:509
  24.1 3.0 %copy-start.4 = (bf16[768,768]{1,0:T(8,128)(2,1)S(1)}, bf16[768,768]{1,0:T(8,128)(2,1)}, u32[]{:S(2)}) copy-start(bf16[768,768]{1,0:T(8,128)(2,1)} %w_ref.4) | copy-start | bytes 3538948
  27.1 12.2 %copy-start = (bf16[768,768]{1,0:T(8,128)(2,1)S(1)}, bf16[768,768]{1,0:T(8,128)(2,1)}, u32[]{:S(2)}) copy-start(bf16[768,768]{1,0:T(8,128)(2,1)} %wq_ref.1) | copy-start | bytes 3538948
  27.1 12.2 %copy-start.1 = (bf16[768,768]{1,0:T(8,128)(2,1)S(1)}, bf16[768,768]{1,0:T(8,128)(2,1)}, u32[]{:S(2)}) copy-start(bf16[768,768]{1,0:T(8,128)(2,1)} %wk_ref.1) | copy-start | bytes 3538948
  27.1 12.2 %copy-start.2 = (bf16[768,768]{1,0:T(8,128)(2,1)S(1)}, bf16[768,768]{1,0:T(8,128)(2,1)}, u32[]{:S(2)}) copy-start(bf16[768,768]{1,0:T(8,128)(2,1)} %wv_ref.1) | copy-start | bytes 3538948
  28.3 8.6 %collective-permute-start.10 = (bf16[64,768]{1,0:T(8,128)(2,1)S(1)}, bf16[64,768]{1,0:T(8,128)(2,1)S(1)}, u32[]{:S(2)}, u32[]{:S(2)}) collective-permute-start(bf16[64,768]{1,0:T(8,128)(2,1)S(1)} %get-tuple-element.64), channel_id=1, source_target_pairs={{0,8},{1,10},{2,9},{3,11},{4,12},{5,14},{6,13},{7,15},{8,0},{9,2},... | collective-permute-start | bytes 294920 | tf_op jit(solution)/shard_map/ppermute | solution.py:513
  28.4 10.6 %collective-permute-start.11 = (bf16[64,768]{1,0:T(8,128)(2,1)S(1)}, bf16[64,768]{1,0:T(8,128)(2,1)S(1)}, u32[]{:S(2)}, u32[]{:S(2)}) collective-permute-start(bf16[64,768]{1,0:T(8,128)(2,1)S(1)} %get-tuple-element.65), channel_id=1, source_target_pairs={{0,12},{1,14},{2,13},{3,15},{4,0},{5,2},{6,1},{7,3},{8,4},{9,6},{1... | collective-permute-start | bytes 294920 | tf_op jit(solution)/shard_map/ppermute | solution.py:513
  31.1 8.0 %collective-permute-start.8 = (bf16[64,768]{1,0:T(8,128)(2,1)S(1)}, bf16[64,768]{1,0:T(8,128)(2,1)S(1)}, u32[]{:S(2)}, u32[]{:S(2)}) collective-permute-start(bf16[64,768]{1,0:T(8,128)(2,1)S(1)} %get-tuple-element.62), channel_id=1, source_target_pairs={{0,4},{1,6},{2,5},{3,7},{4,8},{5,10},{6,9},{7,11},{8,12},{9,14},{1... | collective-permute-start | bytes 294920 | tf_op jit(solution)/shard_map/ppermute | solution.py:513
  31.6 7.5 %collective-permute-start.9 = (bf16[64,768]{1,0:T(8,128)(2,1)S(1)}, bf16[64,768]{1,0:T(8,128)(2,1)S(1)}, u32[]{:S(2)}, u32[]{:S(2)}) collective-permute-start(bf16[64,768]{1,0:T(8,128)(2,1)S(1)} %get-tuple-element.63), channel_id=1, source_target_pairs={{0,0},{1,2},{2,1},{3,3},{4,4},{5,6},{6,5},{7,7},{8,8},{9,10},{10,9... | collective-permute-start | bytes 294920 | tf_op jit(solution)/shard_map/ppermute | solution.py:513
  39.1 1.8 %copy-start.8 = (s32[4]{0:T(128)S(1)}, s32[4]{0:T(128)}, u32[]{:S(2)}) copy-start(s32[4]{0:T(128)} %depth_ref.1) | copy-start | bytes 52
  39.1 1.8 %copy-start.9 = (s32[128]{0:T(128)S(1)}, s32[128]{0:T(128)}, u32[]{:S(2)}) copy-start(s32[128]{0:T(128)} %prot_ref.1) | copy-start | bytes 1540
  39.1 1.8 %collective-permute-start.12 = (bf16[4,64,768]{2,1,0:T(8,128)(2,1)S(1)}, bf16[4,64,768]{2,1,0:T(8,128)(2,1)S(1)}, u32[]{:S(2)}, u32[]{:S(2)}) collective-permute-start(bf16[4,64,768]{2,1,0:T(8,128)(2,1)S(1)} %pack.1), channel_id=1, source_target_pairs={{0,1},{1,0},{2,3},{3,2},{4,5},{5,4},{6,7},{7,6},{8,9},{9,8},{10,11... | collective-permute-start | bytes 1179656 | tf_op jit(solution)/shard_map/ppermute | solution.py:488
  40.9 16.1 %copy-start.6 = (bf16[768,768]{1,0:T(8,128)(2,1)S(1)}, bf16[768,768]{1,0:T(8,128)(2,1)}, u32[]{:S(2)}) copy-start(bf16[768,768]{1,0:T(8,128)(2,1)} %w_ref.5) | copy-start | bytes 3538948
  43.1 1.5 %collective-permute-start.13 = (bf16[4,64,384]{2,1,0:T(8,128)(2,1)S(1)}, bf16[4,64,384]{2,1,0:T(8,128)(2,1)S(1)}, u32[]{:S(2)}, u32[]{:S(2)}) collective-permute-start(bf16[4,64,384]{2,1,0:T(8,128)(2,1)S(1)} %get-tuple-element.70), channel_id=1, source_target_pairs={{0,1},{1,0},{2,3},{3,2},{4,5},{5,4},{6,7},{7,6},{8,9},{9,8},{10,11... | collective-permute-start | bytes 589832 | tf_op jit(solution)/shard_map/ppermute | solution.py:488
  44.7 5.8 %collective-permute-start.14 = (bf16[64,768]{1,0:T(8,128)(2,1)S(1)}, bf16[64,768]{1,0:T(8,128)(2,1)S(1)}, u32[]{:S(2)}, u32[]{:S(2)}) collective-permute-start(bf16[64,768]{1,0:T(8,128)(2,1)S(1)} %get-tuple-element.71), channel_id=1, source_target_pairs={{8,0},{10,1},{9,2},{11,3},{12,4},{14,5},{13,6},{15,7},{0,8},{2,9},... | collective-permute-start | bytes 294920 | tf_op jit(solution)/shard_map/ppermute | solution.py:517
  47.0 6.4 %collective-permute-start.15 = (bf16[64,768]{1,0:T(8,128)(2,1)S(1)}, bf16[64,768]{1,0:T(8,128)(2,1)S(1)}, u32[]{:S(2)}, u32[]{:S(2)}) collective-permute-start(bf16[64,768]{1,0:T(8,128)(2,1)S(1)} %get-tuple-element.72), channel_id=1, source_target_pairs={{4,0},{6,1},{5,2},{7,3},{8,4},{10,5},{9,6},{11,7},{12,8},{14,9},{1... | collective-permute-start | bytes 294920 | tf_op jit(solution)/shard_map/ppermute | solution.py:517
  49.6 7.4 %collective-permute-start.16 = (bf16[64,768]{1,0:T(8,128)(2,1)S(1)}, bf16[64,768]{1,0:T(8,128)(2,1)S(1)}, u32[]{:S(2)}, u32[]{:S(2)}) collective-permute-start(bf16[64,768]{1,0:T(8,128)(2,1)S(1)} %get-tuple-element.73), channel_id=1, source_target_pairs={{12,0},{14,1},{13,2},{15,3},{0,4},{2,5},{1,6},{3,7},{4,8},{6,9},{5... | collective-permute-start | bytes 294920 | tf_op jit(solution)/shard_map/ppermute | solution.py:517
  49.6 7.4 %collective-permute-start.17 = (bf16[64,768]{1,0:T(8,128)(2,1)S(1)}, bf16[64,768]{1,0:T(8,128)(2,1)S(1)}, u32[]{:S(2)}, u32[]{:S(2)}) collective-permute-start(bf16[64,768]{1,0:T(8,128)(2,1)S(1)} %get-tuple-element.74), channel_id=1, source_target_pairs={{0,0},{2,1},{1,2},{3,3},{4,4},{6,5},{5,6},{7,7},{8,8},{10,9},{9,10... | collective-permute-start | bytes 294920 | tf_op jit(solution)/shard_map/ppermute | solution.py:517
  57.7 1.8 %collective-permute-start.18 = (bf16[2,64,768]{2,1,0:T(8,128)(2,1)S(1)}, bf16[2,64,768]{2,1,0:T(8,128)(2,1)S(1)}, u32[]{:S(2)}, u32[]{:S(2)}) collective-permute-start(bf16[2,64,768]{2,1,0:T(8,128)(2,1)S(1)} %get-tuple-element.76), channel_id=1, source_target_pairs={{0,1},{1,0},{2,3},{3,2},{4,5},{5,4},{6,7},{7,6},{8,9},{9,8},{10,11... | collective-permute-start | bytes 589832 | tf_op jit(solution)/shard_map/ppermute | solution.py:488

commit v10 on v9

--- a/solution.py
+++ b/solution.py
@@ -310,12 +310,38 @@
     return pl.ds(pl.multiple_of(place_ref[0] % 2 * wide, 128), wide)
 
 
-def column_project_kernel(planes, columns, place_ref, wq_ref, wk_ref, wv_ref, *refs):
-    ins, (query_ref, key_ref, value_ref, all_ref) = refs[:planes], refs[planes:]
+def column_project_kernel(scale, steps, columns, depth_ref, prot_ref, place_ref, wq_ref, wk_ref, wv_ref, *refs):
+    planes = len(steps)
+    ins, (live_ref, even_ref, odd_ref, key_ref, value_ref, all_ref) = refs[:planes], refs[planes:]
     gather_tokens(ins, columns, all_ref)
-    heads = heads_of(place_ref, query_ref.shape[1])
-    for w_ref, out in ((wq_ref, query_ref), (wk_ref, key_ref), (wv_ref, value_ref)):
+    wide = key_ref.shape[1]
+    heads = heads_of(place_ref, wide)
+    query = dot(all_ref[...], wq_ref[:, heads]).astype(BF16).astype(F32) * scale
+    for side, out in zip(half_masks(wide), (even_ref, odd_ref)):
+        out[...] = (query * side).astype(BF16)
+    for w_ref, out in ((wk_ref, key_ref), (wv_ref, value_ref)):
         out[...] = dot(all_ref[...], w_ref[:, heads]).astype(BF16)
+    slots, local = 2 * planes, columns // 2
+    own = local // planes
+    rows = ins[0].shape[0] // own
+    block = block_of(own)
+    piece = block * rows
+    chunk = slots * piece
+    pair = 8 // rows
+    place = place_ref[0]
+    core, line, plane = place % 2, (place // 2) % 2, place // PLANE
+    lane = (iota((8, 2 * chunk), 1) % piece) // rows
+    level = iota((8, 2 * chunk), 0)
+    fits = level // rows == lane % pair
+    for g in range(own // block):
+        depth = jnp.zeros((8, 2 * chunk), jnp.int32)
+        for c in range(block):
+            index = plane * own + g * block + c
+            column = index % (local // 2) + (local // 2) * line + local * (index // (local // 2))
+            depth = jnp.where(lane == c, depth_ref[prot_ref[column]], depth)
+        for i in range(slots):
+            away = ((plane + planes - steps[i % planes]) % planes) * 2 + (core if i < planes else 1 - core)
+            live_ref[g, i] = jnp.where(fits & (level % rows + away * rows < depth), 1.0, 0.0)
 
 
 def gather_tokens(sources, columns, all_ref):
@@ -330,15 +356,14 @@
 
 def column_kernel(
     scale,
-    steps,
     columns,
-    depth_ref,
-    prot_ref,
     place_ref,
     wq_ref,
     wk_ref,
     wv_ref,
-    query_ref,
+    live_ref,
+    even_ref,
+    odd_ref,
     key_ref,
     value_ref,
     other_ref,
@@ -358,39 +383,27 @@
     chunks = own // block
     fold = piece // 8
     pair = 8 // rows
-    place = place_ref[0]
-    core, line, plane = place % 2, (place // 2) % 2, place // PLANE
     gather_tokens([other_ref.at[i] for i in range(planes)], columns, all_ref)
     heads = heads_of(place_ref, wide)
-    full = []
-    for mine_ref, w_ref in ((query_ref, wq_ref), (key_ref, wk_ref), (value_ref, wv_ref)):
-        other = dot(all_ref[...], w_ref[:, heads]).astype(BF16)
-        mine = mine_ref[...]
+    half = chunk // 2
+
+    def woven(mine, other):
         parts = []
-        for start in range(0, planes * size, chunk // 2):
-            parts += [mine[start : start + chunk // 2], other[start : start + chunk // 2]]
-        full.append(jnp.concatenate(parts, axis=0))
-    query, key, value = full
-    query = query.astype(F32) * scale
-    even, odd = half_masks(wide)
-    sides = [(query * side).astype(BF16) for side in (even, odd)]
+        for start in range(0, planes * size, half):
+            parts += [mine[start : start + half], other[start : start + half]]
+        return jnp.concatenate(parts, axis=0)
+
+    query = dot(all_ref[...], wq_ref[:, heads]).astype(BF16).astype(F32) * scale
+    sides = [
+        woven(mine_ref[...], (query * side).astype(BF16))
+        for mine_ref, side in zip((even_ref, odd_ref), half_masks(wide))
+    ]
+    key = woven(key_ref[...], dot(all_ref[...], wk_ref[:, heads]).astype(BF16))
+    value = woven(value_ref[...], dot(all_ref[...], wv_ref[:, heads]).astype(BF16))
     unit = jnp.where(iota((128, 128), 0) == iota((128, 128), 1), 1.0, 0.0).astype(BF16)
     lane = (iota((8, 2 * chunk), 1) % piece) // rows
-    level = iota((8, 2 * chunk), 0)
-    fits = level // rows == lane % pair
     mine = [jnp.where(lane // pair == v, 1.0, 0.0)[None] for v in range(fold)]
-    lives = []
-    for g in range(chunks):
-        depth = jnp.zeros((8, 2 * chunk), jnp.int32)
-        for c in range(block):
-            index = plane * own + g * block + c
-            column = index % (local // 2) + (local // 2) * line + local * (index // (local // 2))
-            depth = jnp.where(lane == c, depth_ref[prot_ref[column]], depth)
-        live = []
-        for i in range(slots):
-            away = ((plane + planes - steps[i % planes]) % planes) * 2 + (core if i < planes else 1 - core)
-            live.append((fits & (level % rows + away * rows < depth))[None])
-        lives.append(jnp.concatenate([jnp.where(l, 1.0, 0.0) for l in live], axis=0) > 0.5)
+    lives = [live_ref[g] > 0.5 for g in range(chunks)]
     packs, values = [], []
     for q in range(wide // 128):
         lanes = slice(128 * q, 128 * q + 128)
@@ -623,25 +636,28 @@
         (tokens * width, 4 * tokens * width, 0),
         "pack",
     )(*moved)
+    block = block_of(local // planes)
+    chunk = 2 * planes * block * 2 * rows
+    scale = 1.0 / math.sqrt(head_size)
     ours = call(
-        functools.partial(column_project_kernel, planes, columns),
-        (shape((tokens, wide), BF16),) * 3,
-        "svvv" + "v" * planes,
-        "vvv",
+        functools.partial(column_project_kernel, scale, move_steps, columns),
+        (shape((local // planes // block, 2 * planes, 8, 2 * chunk), F32),) + (shape((tokens, wide), BF16),) * 4,
+        "sssvvv" + "v" * planes,
+        "v" * 5,
         [pltpu.VMEM((tokens, width), BF16)],
         (3 * square // 2, 3 * width * width, 0),
         "column_project",
-    )(place, column_query, column_key, column_value, *moved)
+    )(row_depth, protein_id, place, column_query, column_key, column_value, *moved)
     halves = shape((planes, size, wide), BF16)
     keep, send = call(
-        functools.partial(column_kernel, 1.0 / math.sqrt(head_size), move_steps, columns),
+        functools.partial(column_kernel, scale, columns),
         (halves, halves),
-        "sss" + "v" * 7,
+        "s" + "v" * 9,
         "vv",
         [pltpu.VMEM((tokens, width), BF16), pltpu.VMEM((wide, 2 * tokens), BF16)],
         (4 * square, 6 * width * width, H * tokens * tokens // 4),
         "column_attention",
-    )(row_depth, protein_id, place, column_query, column_key, column_value, *ours, swap(packed, 1))
+    )(place, column_query, column_key, column_value, *ours, swap(packed, 1))
     joined = call(
         join_kernel,
         (shape((size, width), BF16),) * planes,

time: 60.5 us -> 59.8 us (0.988)
    ppermute x5, waiting for transfers between devices: 5.75 us -> 5.12 us  [swap(): return lax.ppermute(array, 'seq', [(i, i ^ offset) for i in range(devices)])]
  transfers between devices with their start and end apart: 19 -> 19, of which waited for: 13 -> 13; matrix products, arithmetic and copies ran while one was open for 0% -> 0% of each run, Pallas kernels for 7% -> 8%
where the time goes in v10:
time: 59.8 us; the launch traced here: 59.6 us
  starting transfers between devices  25.1 us (42%)
  waiting for transfers between devices  23.3 us (39%)
  Pallas kernels  11 us (18%)
    ppermute x6, starting transfers between devices, shift(): lax.ppermute(array, 'seq', [(i, (i + PLANE * step) % devices) for i in ra...  12.4 us
    ppermute x4, waiting for transfers between devices, spin(): return lax.ppermute(array, 'seq', spin_pairs(step))  6.83 us
    ppermute x4, waiting for transfers between devices, spin_back(): return lax.ppermute(array, 'seq', [(b, a) for a, b in spin_pairs(step)])  6.73 us
    ppermute x4, starting transfers between devices, spin_back(): return lax.ppermute(array, 'seq', [(b, a) for a, b in spin_pairs(step)])  5.58 us
    ppermute x5, waiting for transfers between devices, swap(): return lax.ppermute(array, 'seq', [(i, i ^ offset) for i in range(devices)])  5.12 us
    ppermute x6, waiting for transfers between devices, shift(): lax.ppermute(array, 'seq', [(i, (i + PLANE * step) % devices) for i in ra...  4.64 us
    ppermute x4, starting transfers between devices, spin(): return lax.ppermute(array, 'seq', spin_pairs(step))  3.92 us
    ppermute x5, starting transfers between devices, swap(): return lax.ppermute(array, 'seq', [(i, i ^ offset) for i in range(devices)])  3.24 us
  transfers between devices with their start and end apart: 19, of which 13 were waited for; matrix products, arithmetic and copies ran while one was open for 0% of the time, Pallas kernels for 8%

profile of v10, /device:TPU:0, one launch (start us, length us, event | category | flops | bytes accessed | tf_op | source)
XLA Modules:
  0.0 59.6 jit_solution(6856367628626758814)
XLA Ops:
  0.0 0.5 collective-permute-start
  0.5 2.5 %row_own.1 = (bf16[256,768]{1,0:T(8,128)(2,1)S(1)}, bf16[128,768]{1,0:T(8,128)(2,1)S(1)}, bf16[256,768]{1,0:T(8,128)(2,1)S(1)}, bf16[768,768]{1,0:T(8,128)(2,1)S...) custom-call(s32[1]{0:T(128)} %bitcast.place_ref, bf16[256,768]{1,0:T(8,128)(2,1)} %bitcast.3, ...), custom_call_target="tpu_custom_call" | custom-call | flops 452984832 | bytes 2359296 | tf_op jit(solution)/shard_map/row_own/pallas_call | solution.py:565
  3.0 0.0 collective-permute-done.x_ref.other_ref
  3.0 0.0 copy-start.10
  3.0 0.0 copy-start.3
  3.0 0.0 copy-start.5
  3.0 1.8 %row_scores.1 = (f32[16,768]{1,0:T(8,128)S(1)}, f32[16,768]{1,0:T(8,128)S(1)}, f32[16,768]{1,0:T(8,128)S(1)}, f32[16,768]{1,0:T(8,128)S(1)}, bf16[256,768]{1,0:T(8,128)(2,1)S(1)}) custom-call(s32[1]{0:T(128)} %bitcast.place_ref, bf16[256,768]{1,0:T(8,128)(2,1)S(1)} %collective-permute-done.x_ref.other_ref, f32[768]{0:T(1024)S(1)} %copy-done.7, ...), custom_call_target="tpu_custom_call" | custom-call | flops 452984832 | bytes 2359296 | tf_op jit(solution)/shard_map/row_scores/pallas_call | solution.py:581
  4.8 3.7 %collective-permute-start.1 = (f32[16,768]{1,0:T(8,128)S(1)}, f32[16,768]{1,0:T(8,128)S(1)}, u32[]{:S(2)}, u32[]{:S(2)}) collective-permute-start(f32[16,768]{1,0:T(8,128)S(1)} %get-tuple-element.56), channel_id=1, source_target_pairs={{0,8},{1,9},{2,10},{3,11},{4,12},{5,13},{6,14},{7,15},{8,0},{9,1},... | collective-permute-start | bytes 147464 | tf_op jit(solution)/shard_map/ppermute | solution.py:522
  8.4 1.6 %collective-permute-start.2 = (f32[16,768]{1,0:T(8,128)S(1)}, f32[16,768]{1,0:T(8,128)S(1)}, u32[]{:S(2)}, u32[]{:S(2)}) collective-permute-start(f32[16,768]{1,0:T(8,128)S(1)} %get-tuple-element.57), channel_id=1, source_target_pairs={{0,4},{1,5},{2,6},{3,7},{4,8},{5,9},{6,10},{7,11},{8,12},{9,13},{1... | collective-permute-start | bytes 147464 | tf_op jit(solution)/shard_map/ppermute | solution.py:522
  10.0 2.2 %collective-permute-start.3 = (f32[16,768]{1,0:T(8,128)S(1)}, f32[16,768]{1,0:T(8,128)S(1)}, u32[]{:S(2)}, u32[]{:S(2)}) collective-permute-start(f32[16,768]{1,0:T(8,128)S(1)} %get-tuple-element.58), channel_id=1, source_target_pairs={{0,12},{1,13},{2,14},{3,15},{4,0},{5,1},{6,2},{7,3},{8,4},{9,5},{1... | collective-permute-start | bytes 147464 | tf_op jit(solution)/shard_map/ppermute | solution.py:522
  12.3 2.4 %collective-permute-done.2.refs_1_ = f32[16,768]{1,0:T(8,128)S(1)} collective-permute-done((f32[16,768]{1,0:T(8,128)S(1)}, f32[16,768]{1,0:T(8,128)S(1)}, u32[]{:S(2)}, u32[]{:S(2)}) %collective-permute-start.2) | collective-permute-done | bytes 49184 | tf_op jit(solution)/shard_map/ppermute | solution.py:522
  14.7 0.1 collective-permute-done.3.refs_2_
  14.8 1.6 %collective-permute-start.4 = (f32[16,768]{1,0:T(8,128)S(1)}, f32[16,768]{1,0:T(8,128)S(1)}, u32[]{:S(2)}, u32[]{:S(2)}) collective-permute-start(f32[16,768]{1,0:T(8,128)S(1)} %add.1.mine_ref), channel_id=1, source_target_pairs={{0,2},{1,3},{2,0},{3,1},{4,6},{5,7},{6,4},{7,5},{8,10},{9,11},{10,... | collective-permute-start | bytes 147464 | tf_op jit(solution)/shard_map/ppermute | solution.py:501
  16.4 2.6 %collective-permute-done.4.other_ref = f32[16,768]{1,0:T(8,128)S(1)} collective-permute-done((f32[16,768]{1,0:T(8,128)S(1)}, f32[16,768]{1,0:T(8,128)S(1)}, u32[]{:S(2)}, u32[]{:S(2)}) %collective-permute-start.4) | collective-permute-done | bytes 49184 | tf_op jit(solution)/shard_map/ppermute | solution.py:501
  18.9 0.3 row_softmax.1.refs_3_
  19.2 1.1 %collective-permute-start.5 = (bf16[16,768]{1,0:T(8,128)(2,1)S(1)}, bf16[16,768]{1,0:T(8,128)(2,1)S(1)}, u32[]{:S(2)}, u32[]{:S(2)}) collective-permute-start(bf16[16,768]{1,0:T(8,128)(2,1)S(1)} %row_softmax.1.refs_3_), channel_id=1, source_target_pairs={{0,8},{1,9},{2,10},{3,11},{4,12},{5,13},{6,14},{7,15},{8,0},{9,1},... | collective-permute-start | bytes 73736 | tf_op jit(solution)/shard_map/ppermute | solution.py:522
  20.3 3.0 %collective-permute-start.6 = (bf16[16,768]{1,0:T(8,128)(2,1)S(1)}, bf16[16,768]{1,0:T(8,128)(2,1)S(1)}, u32[]{:S(2)}, u32[]{:S(2)}) collective-permute-start(bf16[16,768]{1,0:T(8,128)(2,1)S(1)} %row_softmax.1.refs_3_), channel_id=1, source_target_pairs={{0,4},{1,5},{2,6},{3,7},{4,8},{5,9},{6,10},{7,11},{8,12},{9,13},{1... | collective-permute-start | bytes 73736 | tf_op jit(solution)/shard_map/ppermute | solution.py:522
  23.2 0.8 %collective-permute-start.7 = (bf16[16,768]{1,0:T(8,128)(2,1)S(1)}, bf16[16,768]{1,0:T(8,128)(2,1)S(1)}, u32[]{:S(2)}, u32[]{:S(2)}) collective-permute-start(bf16[16,768]{1,0:T(8,128)(2,1)S(1)} %row_softmax.1.refs_3_), channel_id=1, source_target_pairs={{0,12},{1,13},{2,14},{3,15},{4,0},{5,1},{6,2},{7,3},{8,4},{9,5},{1... | collective-permute-start | bytes 73736 | tf_op jit(solution)/shard_map/ppermute | solution.py:522
  24.1 0.8 %row_value.1 = (bf16[256,768]{1,0:T(8,128)(2,1)S(1)}, bf16[256,768]{1,0:T(8,128)(2,1)S(1)}, f32[6,256,128]{2,1,0:T(8,128)S(1)}) custom-call(s32[1]{0:T(128)} %bitcast.place_ref, bf16[256,768]{1,0:T(8,128)(2,1)S(1)} %get-tuple-element.45.x_ref, bf16[256,768]{1,0:T(8,128)(2,1)S(1)} %get-tuple-element.51.y_ref, bf16[768,768]{1,0:T(8,128)(2,1)S(1)} %copy-done.5, ...), custom_call_target="tpu_custom_call" | custom-call | flops 603979776 | bytes 1179648 | tf_op jit(solution)/shard_map/row_value/pallas_call | solution.py:596
  24.9 0.0 collective-permute-done.5.refs_0_
  24.9 1.0 %collective-permute-done.6.refs_1_ = bf16[16,768]{1,0:T(8,128)(2,1)S(1)} collective-permute-done((bf16[16,768]{1,0:T(8,128)(2,1)S(1)}, bf16[16,768]{1,0:T(8,128)(2,1)S(1)}, u32[]{:S(2)}, u32[]{:S(2)}) %collective-permute-start.6) | collective-permute-done | bytes 24608 | tf_op jit(solution)/shard_map/ppermute | solution.py:522
  25.9 1.2 %collective-permute-done.7.refs_2_ = bf16[16,768]{1,0:T(8,128)(2,1)S(1)} collective-permute-done((bf16[16,768]{1,0:T(8,128)(2,1)S(1)}, bf16[16,768]{1,0:T(8,128)(2,1)S(1)}, u32[]{:S(2)}, u32[]{:S(2)}) %collective-permute-start.7) | collective-permute-done | bytes 24608 | tf_op jit(solution)/shard_map/ppermute | solution.py:522
  27.1 0.0 copy-start.8
  27.1 0.0 copy-start.9
  27.1 1.2 %row_output.1 = (bf16[256,768]{1,0:T(8,128)(2,1)S(1)}, bf16[64,768]{1,0:T(8,128)(2,1)S(1)}, bf16[64,768]{1,0:T(8,128)(2,1)S(1)}, bf16[64,768]{1,0:T(8,128)(2,1)S(1)}, bf16[64,768]{1,0:T(8,128)(2,1)S(1)}) custom-call(s32[1]{0:T(128)} %bitcast.place_ref, f32[128,128]{1,0:T(8,128)S(1)} %get-tuple-element.43.same_ref, ...), custom_call_target="tpu_custom_call" | custom-call | flops 301989888 | bytes 1179648 | tf_op jit(solution)/shard_map/row_output/pallas_call | solution.py:615
  28.3 0.1 collective-permute-start.10
  28.5 2.6 %collective-permute-start.11 = (bf16[64,768]{1,0:T(8,128)(2,1)S(1)}, bf16[64,768]{1,0:T(8,128)(2,1)S(1)}, u32[]{:S(2)}, u32[]{:S(2)}) collective-permute-start(bf16[64,768]{1,0:T(8,128)(2,1)S(1)} %get-tuple-element.67), channel_id=1, source_target_pairs={{0,12},{1,14},{2,13},{3,15},{4,0},{5,2},{6,1},{7,3},{8,4},{9,6},{1... | collective-permute-start | bytes 294920 | tf_op jit(solution)/shard_map/ppermute | solution.py:526
  31.1 0.5 collective-permute-start.8
  31.6 0.7 %collective-permute-start.9 = (bf16[64,768]{1,0:T(8,128)(2,1)S(1)}, bf16[64,768]{1,0:T(8,128)(2,1)S(1)}, u32[]{:S(2)}, u32[]{:S(2)}) collective-permute-start(bf16[64,768]{1,0:T(8,128)(2,1)S(1)} %get-tuple-element.65), channel_id=1, source_target_pairs={{0,0},{1,2},{2,1},{3,3},{4,4},{5,6},{6,5},{7,7},{8,8},{9,10},{10,9... | collective-permute-start | bytes 294920 | tf_op jit(solution)/shard_map/ppermute | solution.py:526
  32.3 4.7 %collective-permute-done.10.refs_2_ = bf16[64,768]{1,0:T(8,128)(2,1)S(1)} collective-permute-done((bf16[64,768]{1,0:T(8,128)(2,1)S(1)}, bf16[64,768]{1,0:T(8,128)(2,1)S(1)}, u32[]{:S(2)}, u32[]{:S(2)}) %collective-permute-start.10) | collective-permute-done | bytes 98336 | tf_op jit(solution)/shard_map/ppermute | solution.py:526
  37.0 2.1 %collective-permute-done.11.refs_3_ = bf16[64,768]{1,0:T(8,128)(2,1)S(1)} collective-permute-done((bf16[64,768]{1,0:T(8,128)(2,1)S(1)}, bf16[64,768]{1,0:T(8,128)(2,1)S(1)}, u32[]{:S(2)}, u32[]{:S(2)}) %collective-permute-start.11) | collective-permute-done | bytes 98336 | tf_op jit(solution)/shard_map/ppermute | solution.py:526
  39.1 0.2 collective-permute-start.12
  39.3 1.3 %column_project.1 = (f32[4,8,8,256]{3,2,1,0:T(8,128)S(1)}, bf16[256,384]{1,0:T(8,128)(2,1)S(1)}, bf16[256,384]{1,0:T(8,128)(2,1)S(1)}, bf16[256,384]{1,0:T(8,128)(2,1)S(1)}, bf16[256,384]{1,0:T(8,128)(2,1)S(1)}) custom-call(s32[4]{0:T(128)S(1)} %copy-done.8, s32[128]{0:T(128)S(1)} %copy-done.9, s32[1]{0:T(128)} %bitcast.place_ref, ...), custom_call_target="tpu_custom_call" | custom-call | flops 452984832 | bytes 1769472 | tf_op jit(solution)/shard_map/column_project/pallas_call | solution.py:642
  40.7 0.2 collective-permute-done.12.other_ref
  40.9 1.6 %column_attention.1 = (bf16[4,64,384]{2,1,0:T(8,128)(2,1)S(1)}, bf16[4,64,384]{2,1,0:T(8,128)(2,1)S(1)}) custom-call(s32[1]{0:T(128)} %bitcast.place_ref, bf16[768,768]{1,0:T(8,128)(2,1)S(1)} %copy-done, bf16[768,768]{1,0:T(8,128)(2,1)S(1)} %copy-done.1, bf16[768,768]{1,0:T(8,128)(2,1)S(1)} %copy-done.2, f32[4,8,8,256]{3,2,1,0:T(8,128)S(1)} %get-tuple-element.68.live_ref, ...), custom_call_target="tpu_custom_call" | custom-call | flops 1207959552 | bytes 3538944 | tf_op jit(solution)/shard_map/column_attention/pallas_call | solution.py:652
  42.5 0.3 collective-permute-start.13
  42.8 1.2 %collective-permute-done.13.other_ref = bf16[4,64,384]{2,1,0:T(8,128)(2,1)S(1)} collective-permute-done((bf16[4,64,384]{2,1,0:T(8,128)(2,1)S(1)}, bf16[4,64,384]{2,1,0:T(8,128)(2,1)S(1)}, u32[]{:S(2)}, u32[]{:S(2)}) %collective-permute-start.13) | collective-permute-done | bytes 196640 | tf_op jit(solution)/shard_map/ppermute | solution.py:501
  44.1 2.3 %collective-permute-start.14 = (bf16[64,768]{1,0:T(8,128)(2,1)S(1)}, bf16[64,768]{1,0:T(8,128)(2,1)S(1)}, u32[]{:S(2)}, u32[]{:S(2)}) collective-permute-start(bf16[64,768]{1,0:T(8,128)(2,1)S(1)} %get-tuple-element.75), channel_id=1, source_target_pairs={{8,0},{10,1},{9,2},{11,3},{12,4},{14,5},{13,6},{15,7},{0,8},{2,9},... | collective-permute-start | bytes 294920 | tf_op jit(solution)/shard_map/ppermute | solution.py:530
  46.4 2.6 %collective-permute-start.15 = (bf16[64,768]{1,0:T(8,128)(2,1)S(1)}, bf16[64,768]{1,0:T(8,128)(2,1)S(1)}, u32[]{:S(2)}, u32[]{:S(2)}) collective-permute-start(bf16[64,768]{1,0:T(8,128)(2,1)S(1)} %get-tuple-element.76), channel_id=1, source_target_pairs={{4,0},{6,1},{5,2},{7,3},{8,4},{10,5},{9,6},{11,7},{12,8},{14,9},{1... | collective-permute-start | bytes 294920 | tf_op jit(solution)/shard_map/ppermute | solution.py:530
  49.0 0.0 collective-permute-start.16
  49.0 0.7 %collective-permute-start.17 = (bf16[64,768]{1,0:T(8,128)(2,1)S(1)}, bf16[64,768]{1,0:T(8,128)(2,1)S(1)}, u32[]{:S(2)}, u32[]{:S(2)}) collective-permute-start(bf16[64,768]{1,0:T(8,128)(2,1)S(1)} %get-tuple-element.78), channel_id=1, source_target_pairs={{0,0},{2,1},{1,2},{3,3},{4,4},{6,5},{5,6},{7,7},{8,8},{10,9},{9,10... | collective-permute-start | bytes 294920 | tf_op jit(solution)/shard_map/ppermute | solution.py:530
  49.7 0.2 collective-permute-done.14.refs_0_
  49.9 2.9 %collective-permute-done.15.refs_1_ = bf16[64,768]{1,0:T(8,128)(2,1)S(1)} collective-permute-done((bf16[64,768]{1,0:T(8,128)(2,1)S(1)}, bf16[64,768]{1,0:T(8,128)(2,1)S(1)}, u32[]{:S(2)}, u32[]{:S(2)}) %collective-permute-start.15) | collective-permute-done | bytes 98336 | tf_op jit(solution)/shard_map/ppermute | solution.py:530
  52.8 3.6 %collective-permute-done.16.refs_2_ = bf16[64,768]{1,0:T(8,128)(2,1)S(1)} collective-permute-done((bf16[64,768]{1,0:T(8,128)(2,1)S(1)}, bf16[64,768]{1,0:T(8,128)(2,1)S(1)}, u32[]{:S(2)}, u32[]{:S(2)}) %collective-permute-start.16) | collective-permute-done | bytes 98336 | tf_op jit(solution)/shard_map/ppermute | solution.py:530
  56.4 0.6 %column_output.1 = (bf16[2,64,768]{2,1,0:T(8,128)(2,1)S(1)}, bf16[2,64,768]{2,1,0:T(8,128)(2,1)S(1)}) custom-call(s32[1]{0:T(128)} %bitcast.place_ref, bf16[768,768]{1,0:T(8,128)(2,1)S(1)} %copy-done.6, bf16[256,768]{1,0:T(8,128)(2,1)S(1)} %get-tuple-element.60.after_ref, bf16[64,768]{1,0:T(8,128)(2,1)S(1)} %collective-permute-done.14.refs_0_, ...), custom_call_target="tpu_custom_call" | custom-call | flops 301989888 | bytes 1179648 | tf_op jit(solution)/shard_map/column_output/pallas_call | solution.py:672
  57.0 0.8 %collective-permute-start.18 = (bf16[2,64,768]{2,1,0:T(8,128)(2,1)S(1)}, bf16[2,64,768]{2,1,0:T(8,128)(2,1)S(1)}, u32[]{:S(2)}, u32[]{:S(2)}) collective-permute-start(bf16[2,64,768]{2,1,0:T(8,128)(2,1)S(1)} %get-tuple-element.80), channel_id=1, source_target_pairs={{0,1},{1,0},{2,3},{3,2},{4,5},{5,4},{6,7},{7,6},{8,9},{9,8},{10,11... | collective-permute-start | bytes 589832 | tf_op jit(solution)/shard_map/ppermute | solution.py:501
  57.8 1.1 %collective-permute-done.18.other_ref = bf16[2,64,768]{2,1,0:T(8,128)(2,1)S(1)} collective-permute-done((bf16[2,64,768]{2,1,0:T(8,128)(2,1)S(1)}, bf16[2,64,768]{2,1,0:T(8,128)(2,1)S(1)}, u32[]{:S(2)}, u32[]{:S(2)}) %collective-permute-start.18) | collective-permute-done | bytes 196640 | tf_op jit(solution)/shard_map/ppermute | solution.py:501
  58.9 0.8 %assemble.1 = bf16[2,128,768]{2,1,0:T(8,128)(2,1)} custom-call(s32[1]{0:T(128)} %bitcast.place_ref, bf16[2,64,768]{2,1,0:T(8,128)(2,1)S(1)} %get-tuple-element.79.mine_ref, bf16[2,64,768]{2,1,0:T(8,128)(2,1)S(1)} %collective-permute-done.18.other_ref), custom_call_target="tpu_custom_call" | custom-call | flops 196608 | bytes 786432 | tf_op jit(solution)/shard_map/assemble/pallas_call | solution.py:681
  (25 shorter events, 0.1 us)
Async XLA Ops:
  0.0 3.0 %collective-permute-start = (bf16[256,768]{1,0:T(8,128)(2,1)}, bf16[256,768]{1,0:T(8,128)(2,1)S(1)}, u32[]{:S(2)}, u32[]{:S(2)}) collective-permute-start(bf16[256,768]{1,0:T(8,128)(2,1)} %bitcast.2), channel_id=1, source_target_pairs={{0,1},{1,0},{2,3},{3,2},{4,5},{5,4},{6,7},{7,6},{8,9},{9,8},{10,11... | collective-permute-start | bytes 1179656 | tf_op jit(solution)/shard_map/ppermute | solution.py:501
  0.5 2.5 %copy-start.7 = (f32[768]{0:T(1024)S(1)}, f32[768]{0:T(1024)}, u32[]{:S(2)}) copy-start(f32[768]{0:T(1024)} %gain_ref.1) | copy-start | bytes 9220
  3.0 13.4 %copy-start.10 = (f32[768]{0:T(1024)S(1)}, f32[768]{0:T(1024)}, u32[]{:S(2)}) copy-start(f32[768]{0:T(1024)} %param.21) | copy-start | bytes 9220
  3.0 21.1 %copy-start.3 = (bf16[2,128,768]{2,1,0:T(8,128)(2,1)S(1)}, bf16[2,128,768]{2,1,0:T(8,128)(2,1)}, u32[]{:S(2)}) copy-start(bf16[2,128,768]{2,1,0:T(8,128)(2,1)} %param.13) | copy-start | bytes 1179652
  3.0 21.1 %copy-start.5 = (bf16[768,768]{1,0:T(8,128)(2,1)S(1)}, bf16[768,768]{1,0:T(8,128)(2,1)}, u32[]{:S(2)}) copy-start(bf16[768,768]{1,0:T(8,128)(2,1)} %w_ref.3) | copy-start | bytes 3538948
  4.8 7.5 %collective-permute-start.1 = (f32[16,768]{1,0:T(8,128)S(1)}, f32[16,768]{1,0:T(8,128)S(1)}, u32[]{:S(2)}, u32[]{:S(2)}) collective-permute-start(f32[16,768]{1,0:T(8,128)S(1)} %get-tuple-element.56), channel_id=1, source_target_pairs={{0,8},{1,9},{2,10},{3,11},{4,12},{5,13},{6,14},{7,15},{8,0},{9,1},... | collective-permute-start | bytes 147464 | tf_op jit(solution)/shard_map/ppermute | solution.py:522
  8.4 6.2 %collective-permute-start.2 = (f32[16,768]{1,0:T(8,128)S(1)}, f32[16,768]{1,0:T(8,128)S(1)}, u32[]{:S(2)}, u32[]{:S(2)}) collective-permute-start(f32[16,768]{1,0:T(8,128)S(1)} %get-tuple-element.57), channel_id=1, source_target_pairs={{0,4},{1,5},{2,6},{3,7},{4,8},{5,9},{6,10},{7,11},{8,12},{9,13},{1... | collective-permute-start | bytes 147464 | tf_op jit(solution)/shard_map/ppermute | solution.py:522
  10.0 4.7 %collective-permute-start.3 = (f32[16,768]{1,0:T(8,128)S(1)}, f32[16,768]{1,0:T(8,128)S(1)}, u32[]{:S(2)}, u32[]{:S(2)}) collective-permute-start(f32[16,768]{1,0:T(8,128)S(1)} %get-tuple-element.58), channel_id=1, source_target_pairs={{0,12},{1,13},{2,14},{3,15},{4,0},{5,1},{6,2},{7,3},{8,4},{9,5},{1... | collective-permute-start | bytes 147464 | tf_op jit(solution)/shard_map/ppermute | solution.py:522
  14.8 4.2 %collective-permute-start.4 = (f32[16,768]{1,0:T(8,128)S(1)}, f32[16,768]{1,0:T(8,128)S(1)}, u32[]{:S(2)}, u32[]{:S(2)}) collective-permute-start(f32[16,768]{1,0:T(8,128)S(1)} %add.1.mine_ref), channel_id=1, source_target_pairs={{0,2},{1,3},{2,0},{3,1},{4,6},{5,7},{6,4},{7,5},{8,10},{9,11},{10,... | collective-permute-start | bytes 147464 | tf_op jit(solution)/shard_map/ppermute | solution.py:501
  19.2 5.7 %collective-permute-start.5 = (bf16[16,768]{1,0:T(8,128)(2,1)S(1)}, bf16[16,768]{1,0:T(8,128)(2,1)S(1)}, u32[]{:S(2)}, u32[]{:S(2)}) collective-permute-start(bf16[16,768]{1,0:T(8,128)(2,1)S(1)} %row_softmax.1.refs_3_), channel_id=1, source_target_pairs={{0,8},{1,9},{2,10},{3,11},{4,12},{5,13},{6,14},{7,15},{8,0},{9,1},... | collective-permute-start | bytes 73736 | tf_op jit(solution)/shard_map/ppermute | solution.py:522
  20.3 5.6 %collective-permute-start.6 = (bf16[16,768]{1,0:T(8,128)(2,1)S(1)}, bf16[16,768]{1,0:T(8,128)(2,1)S(1)}, u32[]{:S(2)}, u32[]{:S(2)}) collective-permute-start(bf16[16,768]{1,0:T(8,128)(2,1)S(1)} %row_softmax.1.refs_3_), channel_id=1, source_target_pairs={{0,4},{1,5},{2,6},{3,7},{4,8},{5,9},{6,10},{7,11},{8,12},{9,13},{1... | collective-permute-start | bytes 73736 | tf_op jit(solution)/shard_map/ppermute | solution.py:522
  23.2 3.8 %collective-permute-start.7 = (bf16[16,768]{1,0:T(8,128)(2,1)S(1)}, bf16[16,768]{1,0:T(8,128)(2,1)S(1)}, u32[]{:S(2)}, u32[]{:S(2)}) collective-permute-start(bf16[16,768]{1,0:T(8,128)(2,1)S(1)} %row_softmax.1.refs_3_), channel_id=1, source_target_pairs={{0,12},{1,13},{2,14},{3,15},{4,0},{5,1},{6,2},{7,3},{8,4},{9,5},{1... | collective-permute-start | bytes 73736 | tf_op jit(solution)/shard_map/ppermute | solution.py:522
  24.1 3.0 %copy-start.4 = (bf16[768,768]{1,0:T(8,128)(2,1)S(1)}, bf16[768,768]{1,0:T(8,128)(2,1)}, u32[]{:S(2)}) copy-start(bf16[768,768]{1,0:T(8,128)(2,1)} %w_ref.4) | copy-start | bytes 3538948
  27.1 12.2 %copy-start = (bf16[768,768]{1,0:T(8,128)(2,1)S(1)}, bf16[768,768]{1,0:T(8,128)(2,1)}, u32[]{:S(2)}) copy-start(bf16[768,768]{1,0:T(8,128)(2,1)} %wq_ref.1) | copy-start | bytes 3538948
  27.1 12.2 %copy-start.1 = (bf16[768,768]{1,0:T(8,128)(2,1)S(1)}, bf16[768,768]{1,0:T(8,128)(2,1)}, u32[]{:S(2)}) copy-start(bf16[768,768]{1,0:T(8,128)(2,1)} %wk_ref.1) | copy-start | bytes 3538948
  27.1 12.2 %copy-start.2 = (bf16[768,768]{1,0:T(8,128)(2,1)S(1)}, bf16[768,768]{1,0:T(8,128)(2,1)}, u32[]{:S(2)}) copy-start(bf16[768,768]{1,0:T(8,128)(2,1)} %wv_ref.1) | copy-start | bytes 3538948
  27.1 12.2 %copy-start.8 = (s32[4]{0:T(128)S(1)}, s32[4]{0:T(128)}, u32[]{:S(2)}) copy-start(s32[4]{0:T(128)} %depth_ref.1) | copy-start | bytes 52
  27.1 12.2 %copy-start.9 = (s32[128]{0:T(128)S(1)}, s32[128]{0:T(128)}, u32[]{:S(2)}) copy-start(s32[128]{0:T(128)} %prot_ref.1) | copy-start | bytes 1540
  28.3 8.6 %collective-permute-start.10 = (bf16[64,768]{1,0:T(8,128)(2,1)S(1)}, bf16[64,768]{1,0:T(8,128)(2,1)S(1)}, u32[]{:S(2)}, u32[]{:S(2)}) collective-permute-start(bf16[64,768]{1,0:T(8,128)(2,1)S(1)} %get-tuple-element.66), channel_id=1, source_target_pairs={{0,8},{1,10},{2,9},{3,11},{4,12},{5,14},{6,13},{7,15},{8,0},{9,2},... | collective-permute-start | bytes 294920 | tf_op jit(solution)/shard_map/ppermute | solution.py:526
  28.5 10.6 %collective-permute-start.11 = (bf16[64,768]{1,0:T(8,128)(2,1)S(1)}, bf16[64,768]{1,0:T(8,128)(2,1)S(1)}, u32[]{:S(2)}, u32[]{:S(2)}) collective-permute-start(bf16[64,768]{1,0:T(8,128)(2,1)S(1)} %get-tuple-element.67), channel_id=1, source_target_pairs={{0,12},{1,14},{2,13},{3,15},{4,0},{5,2},{6,1},{7,3},{8,4},{9,6},{1... | collective-permute-start | bytes 294920 | tf_op jit(solution)/shard_map/ppermute | solution.py:526
  31.1 8.0 %collective-permute-start.8 = (bf16[64,768]{1,0:T(8,128)(2,1)S(1)}, bf16[64,768]{1,0:T(8,128)(2,1)S(1)}, u32[]{:S(2)}, u32[]{:S(2)}) collective-permute-start(bf16[64,768]{1,0:T(8,128)(2,1)S(1)} %get-tuple-element.64), channel_id=1, source_target_pairs={{0,4},{1,6},{2,5},{3,7},{4,8},{5,10},{6,9},{7,11},{8,12},{9,14},{1... | collective-permute-start | bytes 294920 | tf_op jit(solution)/shard_map/ppermute | solution.py:526
  31.6 7.5 %collective-permute-start.9 = (bf16[64,768]{1,0:T(8,128)(2,1)S(1)}, bf16[64,768]{1,0:T(8,128)(2,1)S(1)}, u32[]{:S(2)}, u32[]{:S(2)}) collective-permute-start(bf16[64,768]{1,0:T(8,128)(2,1)S(1)} %get-tuple-element.65), channel_id=1, source_target_pairs={{0,0},{1,2},{2,1},{3,3},{4,4},{5,6},{6,5},{7,7},{8,8},{9,10},{10,9... | collective-permute-start | bytes 294920 | tf_op jit(solution)/shard_map/ppermute | solution.py:526
  39.1 1.8 %collective-permute-start.12 = (bf16[4,64,768]{2,1,0:T(8,128)(2,1)S(1)}, bf16[4,64,768]{2,1,0:T(8,128)(2,1)S(1)}, u32[]{:S(2)}, u32[]{:S(2)}) collective-permute-start(bf16[4,64,768]{2,1,0:T(8,128)(2,1)S(1)} %pack.1), channel_id=1, source_target_pairs={{0,1},{1,0},{2,3},{3,2},{4,5},{5,4},{6,7},{7,6},{8,9},{9,8},{10,11... | collective-permute-start | bytes 1179656 | tf_op jit(solution)/shard_map/ppermute | solution.py:501
  40.9 15.5 %copy-start.6 = (bf16[768,768]{1,0:T(8,128)(2,1)S(1)}, bf16[768,768]{1,0:T(8,128)(2,1)}, u32[]{:S(2)}) copy-start(bf16[768,768]{1,0:T(8,128)(2,1)} %w_ref.5) | copy-start | bytes 3538948
  42.5 1.5 %collective-permute-start.13 = (bf16[4,64,384]{2,1,0:T(8,128)(2,1)S(1)}, bf16[4,64,384]{2,1,0:T(8,128)(2,1)S(1)}, u32[]{:S(2)}, u32[]{:S(2)}) collective-permute-start(bf16[4,64,384]{2,1,0:T(8,128)(2,1)S(1)} %get-tuple-element.74), channel_id=1, source_target_pairs={{0,1},{1,0},{2,3},{3,2},{4,5},{5,4},{6,7},{7,6},{8,9},{9,8},{10,11... | collective-permute-start | bytes 589832 | tf_op jit(solution)/shard_map/ppermute | solution.py:501
  44.1 5.8 %collective-permute-start.14 = (bf16[64,768]{1,0:T(8,128)(2,1)S(1)}, bf16[64,768]{1,0:T(8,128)(2,1)S(1)}, u32[]{:S(2)}, u32[]{:S(2)}) collective-permute-start(bf16[64,768]{1,0:T(8,128)(2,1)S(1)} %get-tuple-element.75), channel_id=1, source_target_pairs={{8,0},{10,1},{9,2},{11,3},{12,4},{14,5},{13,6},{15,7},{0,8},{2,9},... | collective-permute-start | bytes 294920 | tf_op jit(solution)/shard_map/ppermute | solution.py:530
  46.4 6.4 %collective-permute-start.15 = (bf16[64,768]{1,0:T(8,128)(2,1)S(1)}, bf16[64,768]{1,0:T(8,128)(2,1)S(1)}, u32[]{:S(2)}, u32[]{:S(2)}) collective-permute-start(bf16[64,768]{1,0:T(8,128)(2,1)S(1)} %get-tuple-element.76), channel_id=1, source_target_pairs={{4,0},{6,1},{5,2},{7,3},{8,4},{10,5},{9,6},{11,7},{12,8},{14,9},{1... | collective-permute-start | bytes 294920 | tf_op jit(solution)/shard_map/ppermute | solution.py:530
  49.0 7.4 %collective-permute-start.16 = (bf16[64,768]{1,0:T(8,128)(2,1)S(1)}, bf16[64,768]{1,0:T(8,128)(2,1)S(1)}, u32[]{:S(2)}, u32[]{:S(2)}) collective-permute-start(bf16[64,768]{1,0:T(8,128)(2,1)S(1)} %get-tuple-element.77), channel_id=1, source_target_pairs={{12,0},{14,1},{13,2},{15,3},{0,4},{2,5},{1,6},{3,7},{4,8},{6,9},{5... | collective-permute-start | bytes 294920 | tf_op jit(solution)/shard_map/ppermute | solution.py:530
  49.0 7.4 %collective-permute-start.17 = (bf16[64,768]{1,0:T(8,128)(2,1)S(1)}, bf16[64,768]{1,0:T(8,128)(2,1)S(1)}, u32[]{:S(2)}, u32[]{:S(2)}) collective-permute-start(bf16[64,768]{1,0:T(8,128)(2,1)S(1)} %get-tuple-element.78), channel_id=1, source_target_pairs={{0,0},{2,1},{1,2},{3,3},{4,4},{6,5},{5,6},{7,7},{8,8},{10,9},{9,10... | collective-permute-start | bytes 294920 | tf_op jit(solution)/shard_map/ppermute | solution.py:530
  57.0 1.8 %collective-permute-start.18 = (bf16[2,64,768]{2,1,0:T(8,128)(2,1)S(1)}, bf16[2,64,768]{2,1,0:T(8,128)(2,1)S(1)}, u32[]{:S(2)}, u32[]{:S(2)}) collective-permute-start(bf16[2,64,768]{2,1,0:T(8,128)(2,1)S(1)} %get-tuple-element.80), channel_id=1, source_target_pairs={{0,1},{1,0},{2,3},{3,2},{4,5},{5,4},{6,7},{7,6},{8,9},{9,8},{10,11... | collective-permute-start | bytes 589832 | tf_op jit(solution)/shard_map/ppermute | solution.py:501

commit v11 on v10

--- a/solution.py
+++ b/solution.py
@@ -96,10 +96,12 @@
     wk_ref,
     same_ref,
     seen_ref,
+    live_ref,
     x_ref,
     gain_ref,
     depth_ref,
     prot_ref,
+    mask_ref,
     sems,
 ):
     tokens, width = x_ref.shape
@@ -121,7 +123,15 @@
         depth = jnp.where(prot == float(p), depth_ref[p].astype(F32), depth)
     square = (columns, columns)
     same = jnp.broadcast_to(to_column(prot, columns), square) == jnp.broadcast_to(prot, square)
-    same_ref[...] = jnp.where(same, 1.0, 0.0)
+    same = jnp.where(same, 1.0, 0.0)
+    core, quarter = place_ref[0] % 2, columns // PLANE
+    same = own_columns(same, core == 0, quarter)
+    same_ref[...] = same
+    mask = jnp.maximum(same, pltpu.roll(same, 64, 1))
+    own = live_ref.shape[0]
+    for i in range(mask_ref.shape[0]):
+        mask_ref[i] = mask[i * own : (i + 1) * own]
+    live_ref[...] = mask_ref[place_ref[0] // PLANE]
     seen_ref[...] = jnp.broadcast_to(to_column(depth, columns), square)
     for copy in copies[4:]:
         copy.wait()
@@ -142,14 +152,14 @@
     *refs,
 ):
     outs, (normed_ref, part_ref) = refs[:-2], refs[-2:]
-    columns = same_ref.shape[0]
+    columns = same_ref.shape[1]
     tokens, width = x_ref.shape
     rows, local, quarter = tokens // columns, columns // 2, columns // PLANE
     planes, own = part_ref.shape[:2]
     place = place_ref[0]
     core = (place % 2) == 0
     normed_ref[...] = norm(x_ref[...].astype(F32), gain_ref[...].reshape(1, width)).astype(BF16)
-    same_l = own_columns(same_ref[...], core, quarter)
+    same_l = same_ref[...]
     seen = seen_ref[...]
     depth_l = own_columns(seen, core, quarter)
     low = iota((local, columns), 1) < 64
@@ -215,17 +225,9 @@
                     spread_ref[p, target, :] = piece[:, 128 * p : 128 * p + 128]
 
 
-def row_softmax_kernel(scale, place_ref, mine_ref, other_ref, same_ref, out_ref, mask_ref):
+def row_softmax_kernel(scale, mine_ref, other_ref, live_ref, out_ref):
     own, width = out_ref.shape
-    columns = same_ref.shape[0]
-    quarter, local = columns // PLANE, columns // 2
-    core, plane = place_ref[0] % 2, place_ref[0] // PLANE
-    same = same_ref[...]
-    mask = jnp.maximum(same, pltpu.roll(same, 64, 1))
-    for i in range(columns // own):
-        mask_ref[i] = mask[i * own : (i + 1) * own]
-    first = plane * own
-    live = mask_ref[(first % quarter + quarter * core + local * (first // quarter)) // own] > 0.5
+    live = live_ref[...] > 0.5
     low = iota((own, 128), 1) < 64
     for p in range(width // 128):
         lanes = slice(128 * p, 128 * p + 128)
@@ -252,7 +254,7 @@
     planes = (len(refs) - 4) // 2
     pieces, after_ref, outs = refs[:planes], refs[planes], refs[planes + 1 : -3]
     mixed_ref, folded_ref, normed_ref = refs[-3:]
-    columns = same_ref.shape[0]
+    columns = same_ref.shape[1]
     tokens, width = after_ref.shape
     rows = tokens // columns
     quarter, local = columns // PLANE, columns // 2
@@ -261,10 +263,7 @@
     own = local // planes
     for s, piece in zip(steps, pieces):
         folded_ref[(plane + planes - s) % planes] = piece[...].astype(F32)
-    same = [
-        same_ref[pl.ds(pl.multiple_of(y * local + core * quarter, quarter), quarter), :] for y in range(2)
-    ]
-    same = jnp.concatenate(same, axis=0) > 0.5
+    same = same_ref[...] > 0.5
     low = iota((local, columns), 1) < 64
     even, odd = half_masks(256 * rows)
     even, odd = even.astype(BF16), odd.astype(BF16)
@@ -562,17 +561,18 @@
     part = shape((local // planes, width), F32)
     matrix = shape((width, width), BF16)
     sibling = swap(x, 1)
-    normed, query, key, row_query, row_key, same, seen = call(
+    normed, query, key, row_query, row_key, same, seen, live = call(
         functools.partial(row_own_kernel, columns),
         (shape((tokens, width), BF16), shape((tokens // 2, width), BF16), shape((tokens, width), BF16), matrix, matrix)
-        + (shape((columns, columns), F32),) * 2,
+        + (shape((local, columns), F32), shape((columns, columns), F32), shape((local // planes, columns), F32)),
         "shhhhhh",
-        "v" * 7,
+        "v" * 8,
         [
             pltpu.VMEM((tokens, width), BF16),
             pltpu.VMEM((width,), F32),
             pltpu.SMEM(row_depth.shape, jnp.int32),
             pltpu.VMEM((columns,), jnp.int32),
+            pltpu.VMEM((planes, local // planes, columns), F32),
             pltpu.SemaphoreType.DMA((4 + 2 * (width // 256),)),
         ],
         (3 * square // 2, 4 * width * width, tokens),
@@ -593,6 +593,8 @@
     (total,) = call(
         add_kernel, (part,), "v" * planes, "v", [], (columns * width, 2 * columns * width, 0), "add"
     )(*[shift(pieces[s], s) for s in sum_steps])
+    other_total = swap(total, 2)
+    normed, _ = lax.optimization_barrier((normed, total))
     value, value_other, spread = call(
         functools.partial(row_value_kernel, columns),
         (shape((tokens, width), BF16),) * 2 + (shape((width // 128, tokens, 128), F32),),
@@ -602,15 +604,16 @@
         (2 * square, 2 * width * width, 0),
         "row_value",
     )(place, normed, normed_other, row_value, late, sibling)
+    live, value = lax.optimization_barrier((live, value))
     (weights,) = call(
         functools.partial(row_softmax_kernel, 1.0 / (math.sqrt(head_size) * math.sqrt(total_rows))),
         (shape((local // planes, width), BF16),),
-        "svvv",
+        "vvv",
         "v",
-        [pltpu.VMEM((columns * planes // local, local // planes, columns), F32)],
+        [],
         (columns * width, 2 * columns * width, columns * width // 8),
         "row_softmax",
-    )(place, total, swap(total, 2), same)
+    )(total, other_total, live)
     shared = [shift(weights, s) for s in share_steps]
     after, *blocks = call(
         functools.partial(row_output_kernel, share_steps),

time: 59.8 us -> 59.7 us (level)
    ppermute x6, waiting for transfers between devices: 4.64 us -> 5.46 us  [shift(): lax.ppermute(array, 'seq', [(i, (i + PLANE * step) % devices) for i in ra...]
    ppermute x5, waiting for transfers between devices: 5.12 us -> 4.32 us  [swap(): return lax.ppermute(array, 'seq', [(i, i ^ offset) for i in range(devices)])]
where the time goes in v11:
time: 59.7 us; the launch traced here: 59.5 us
  starting transfers between devices  25.1 us (42%)
  waiting for transfers between devices  23.3 us (39%)
  Pallas kernels  10.9 us (18%)
    ppermute x6, starting transfers between devices, shift(): lax.ppermute(array, 'seq', [(i, (i + PLANE * step) % devices) for i in ra...  12.3 us
    ppermute x4, waiting for transfers between devices, spin(): return lax.ppermute(array, 'seq', spin_pairs(step))  6.83 us
    ppermute x4, waiting for transfers between devices, spin_back(): return lax.ppermute(array, 'seq', [(b, a) for a, b in spin_pairs(step)])  6.72 us
    ppermute x4, starting transfers between devices, spin_back(): return lax.ppermute(array, 'seq', [(b, a) for a, b in spin_pairs(step)])  5.57 us
    ppermute x6, waiting for transfers between devices, shift(): lax.ppermute(array, 'seq', [(i, (i + PLANE * step) % devices) for i in ra...  5.46 us
    ppermute x5, waiting for transfers between devices, swap(): return lax.ppermute(array, 'seq', [(i, i ^ offset) for i in range(devices)])  4.32 us
    ppermute x4, starting transfers between devices, spin(): return lax.ppermute(array, 'seq', spin_pairs(step))  3.92 us
    ppermute x5, starting transfers between devices, swap(): return lax.ppermute(array, 'seq', [(i, i ^ offset) for i in range(devices)])  3.24 us
  transfers between devices with their start and end apart: 19, of which 13 were waited for; matrix products, arithmetic and copies ran while one was open for 0% of the time, Pallas kernels for 8%

profile of v11, /device:TPU:0, one launch (start us, length us, event | category | flops | bytes accessed | tf_op | source)
XLA Modules:
  0.0 59.5 jit_solution(14358020761576090098)
XLA Ops:
  0.0 0.5 collective-permute-start
  0.5 2.5 %row_own.1 = (bf16[256,768]{1,0:T(8,128)(2,1)S(1)}, bf16[128,768]{1,0:T(8,128)(2,1)S(1)}, bf16[256,768]{1,0:T(8,128)(2,1)S(1)}, bf16[768,768]{1,0:T(8,128)(2,1)S...) custom-call(s32[1]{0:T(128)} %bitcast.place_ref, ...), custom_call_target="tpu_custom_call" | custom-call | flops 452984832 | bytes 2359296 | tf_op jit(solution)/shard_map/row_own/pallas_call | solution.py:564
  3.0 0.0 copy-start.3
  3.0 0.0 copy-start.5
  3.0 1.8 %row_scores.1 = (f32[16,768]{1,0:T(8,128)S(1)}, f32[16,768]{1,0:T(8,128)S(1)}, f32[16,768]{1,0:T(8,128)S(1)}, f32[16,768]{1,0:T(8,128)S(1)}, bf16[256,768]{1,0:T(8,128)(2,1)S(1)}) custom-call(s32[1]{0:T(128)} %bitcast.place_ref, bf16[256,768]{1,0:T(8,128)(2,1)S(1)} %collective-permute-done.x_ref.other_ref, f32[768]{0:T(1024)S(1)} %copy-done.7, ...), custom_call_target="tpu_custom_call" | custom-call | flops 452984832 | bytes 2359296 | tf_op jit(solution)/shard_map/row_scores/pallas_call | solution.py:581
  4.8 3.7 %collective-permute-start.1 = (f32[16,768]{1,0:T(8,128)S(1)}, f32[16,768]{1,0:T(8,128)S(1)}, u32[]{:S(2)}, u32[]{:S(2)}) collective-permute-start(f32[16,768]{1,0:T(8,128)S(1)} %get-tuple-element.56), channel_id=1, source_target_pairs={{0,8},{1,9},{2,10},{3,11},{4,12},{5,13},{6,14},{7,15},{8,0},{9,1},... | collective-permute-start | bytes 147464 | tf_op jit(solution)/shard_map/ppermute | solution.py:521
  8.4 1.6 %collective-permute-start.2 = (f32[16,768]{1,0:T(8,128)S(1)}, f32[16,768]{1,0:T(8,128)S(1)}, u32[]{:S(2)}, u32[]{:S(2)}) collective-permute-start(f32[16,768]{1,0:T(8,128)S(1)} %get-tuple-element.57), channel_id=1, source_target_pairs={{0,4},{1,5},{2,6},{3,7},{4,8},{5,9},{6,10},{7,11},{8,12},{9,13},{1... | collective-permute-start | bytes 147464 | tf_op jit(solution)/shard_map/ppermute | solution.py:521
  10.0 2.2 %collective-permute-start.3 = (f32[16,768]{1,0:T(8,128)S(1)}, f32[16,768]{1,0:T(8,128)S(1)}, u32[]{:S(2)}, u32[]{:S(2)}) collective-permute-start(f32[16,768]{1,0:T(8,128)S(1)} %get-tuple-element.58), channel_id=1, source_target_pairs={{0,12},{1,13},{2,14},{3,15},{4,0},{5,1},{6,2},{7,3},{8,4},{9,5},{1... | collective-permute-start | bytes 147464 | tf_op jit(solution)/shard_map/ppermute | solution.py:521
  12.2 0.0 collective-permute-done.1.refs_0_
  12.2 2.4 %collective-permute-done.2.refs_1_ = f32[16,768]{1,0:T(8,128)S(1)} collective-permute-done((f32[16,768]{1,0:T(8,128)S(1)}, f32[16,768]{1,0:T(8,128)S(1)}, u32[]{:S(2)}, u32[]{:S(2)}) %collective-permute-start.2) | collective-permute-done | bytes 49184 | tf_op jit(solution)/shard_map/ppermute | solution.py:521
  14.6 0.1 collective-permute-done.3.refs_2_
  14.7 1.6 %collective-permute-start.4 = (f32[16,768]{1,0:T(8,128)S(1)}, f32[16,768]{1,0:T(8,128)S(1)}, u32[]{:S(2)}, u32[]{:S(2)}) collective-permute-start(f32[16,768]{1,0:T(8,128)S(1)} %add.1.mine_ref), channel_id=1, source_target_pairs={{0,2},{1,3},{2,0},{3,1},{4,6},{5,7},{6,4},{7,5},{8,10},{9,11},{10,... | collective-permute-start | bytes 147464 | tf_op jit(solution)/shard_map/ppermute | solution.py:500
  16.3 0.8 %row_value.1 = (bf16[256,768]{1,0:T(8,128)(2,1)S(1)}, bf16[256,768]{1,0:T(8,128)(2,1)S(1)}, f32[6,256,128]{2,1,0:T(8,128)S(1)}) custom-call(s32[1]{0:T(128)} %bitcast.place_ref, bf16[256,768]{1,0:T(8,128)(2,1)S(1)} %get-tuple-element.60.x_ref, bf16[256,768]{1,0:T(8,128)(2,1)S(1)} %get-tuple-element.61.y_ref, bf16[768,768]{1,0:T(8,128)(2,1)S(1)} %copy-done.5, ...), custom_call_target="tpu_custom_call" | custom-call | flops 603979776 | bytes 1179648 | tf_op jit(solution)/shard_map/row_value/pallas_call | solution.py:598
  17.1 1.8 %collective-permute-done.4.other_ref = f32[16,768]{1,0:T(8,128)S(1)} collective-permute-done((f32[16,768]{1,0:T(8,128)S(1)}, f32[16,768]{1,0:T(8,128)S(1)}, u32[]{:S(2)}, u32[]{:S(2)}) %collective-permute-start.4) | collective-permute-done | bytes 49184 | tf_op jit(solution)/shard_map/ppermute | solution.py:500
  18.9 0.2 row_softmax.1.refs_3_
  19.1 1.1 %collective-permute-start.5 = (bf16[16,768]{1,0:T(8,128)(2,1)S(1)}, bf16[16,768]{1,0:T(8,128)(2,1)S(1)}, u32[]{:S(2)}, u32[]{:S(2)}) collective-permute-start(bf16[16,768]{1,0:T(8,128)(2,1)S(1)} %row_softmax.1.refs_3_), channel_id=1, source_target_pairs={{0,8},{1,9},{2,10},{3,11},{4,12},{5,13},{6,14},{7,15},{8,0},{9,1},... | collective-permute-start | bytes 73736 | tf_op jit(solution)/shard_map/ppermute | solution.py:521
  20.2 3.0 %collective-permute-start.6 = (bf16[16,768]{1,0:T(8,128)(2,1)S(1)}, bf16[16,768]{1,0:T(8,128)(2,1)S(1)}, u32[]{:S(2)}, u32[]{:S(2)}) collective-permute-start(bf16[16,768]{1,0:T(8,128)(2,1)S(1)} %row_softmax.1.refs_3_), channel_id=1, source_target_pairs={{0,4},{1,5},{2,6},{3,7},{4,8},{5,9},{6,10},{7,11},{8,12},{9,13},{1... | collective-permute-start | bytes 73736 | tf_op jit(solution)/shard_map/ppermute | solution.py:521
  23.1 0.8 %collective-permute-start.7 = (bf16[16,768]{1,0:T(8,128)(2,1)S(1)}, bf16[16,768]{1,0:T(8,128)(2,1)S(1)}, u32[]{:S(2)}, u32[]{:S(2)}) collective-permute-start(bf16[16,768]{1,0:T(8,128)(2,1)S(1)} %row_softmax.1.refs_3_), channel_id=1, source_target_pairs={{0,12},{1,13},{2,14},{3,15},{4,0},{5,1},{6,2},{7,3},{8,4},{9,5},{1... | collective-permute-start | bytes 73736 | tf_op jit(solution)/shard_map/ppermute | solution.py:521
  24.0 0.0 collective-permute-done.5.refs_0_
  24.0 1.8 %collective-permute-done.6.refs_1_ = bf16[16,768]{1,0:T(8,128)(2,1)S(1)} collective-permute-done((bf16[16,768]{1,0:T(8,128)(2,1)S(1)}, bf16[16,768]{1,0:T(8,128)(2,1)S(1)}, u32[]{:S(2)}, u32[]{:S(2)}) %collective-permute-start.6) | collective-permute-done | bytes 24608 | tf_op jit(solution)/shard_map/ppermute | solution.py:521
  25.8 1.2 %collective-permute-done.7.refs_2_ = bf16[16,768]{1,0:T(8,128)(2,1)S(1)} collective-permute-done((bf16[16,768]{1,0:T(8,128)(2,1)S(1)}, bf16[16,768]{1,0:T(8,128)(2,1)S(1)}, u32[]{:S(2)}, u32[]{:S(2)}) %collective-permute-start.7) | collective-permute-done | bytes 24608 | tf_op jit(solution)/shard_map/ppermute | solution.py:521
  27.0 0.0 copy-start.8
  27.0 0.0 copy-start.9
  27.0 1.2 %row_output.1 = (bf16[256,768]{1,0:T(8,128)(2,1)S(1)}, bf16[64,768]{1,0:T(8,128)(2,1)S(1)}, bf16[64,768]{1,0:T(8,128)(2,1)S(1)}, bf16[64,768]{1,0:T(8,128)(2,1)S(1)}, bf16[64,768]{1,0:T(8,128)(2,1)S(1)}) custom-call(s32[1]{0:T(128)} %bitcast.place_ref, f32[64,128]{1,0:T(8,128)S(1)} %get-tuple-element.47.same_ref, ...), custom_call_target="tpu_custom_call" | custom-call | flops 301989888 | bytes 1179648 | tf_op jit(solution)/shard_map/row_output/pallas_call | solution.py:618
  28.2 0.1 collective-permute-start.10
  28.3 2.6 %collective-permute-start.11 = (bf16[64,768]{1,0:T(8,128)(2,1)S(1)}, bf16[64,768]{1,0:T(8,128)(2,1)S(1)}, u32[]{:S(2)}, u32[]{:S(2)}) collective-permute-start(bf16[64,768]{1,0:T(8,128)(2,1)S(1)} %get-tuple-element.75), channel_id=1, source_target_pairs={{0,12},{1,14},{2,13},{3,15},{4,0},{5,2},{6,1},{7,3},{8,4},{9,6},{1... | collective-permute-start | bytes 294920 | tf_op jit(solution)/shard_map/ppermute | solution.py:525
  31.0 0.5 collective-permute-start.8
  31.5 0.7 %collective-permute-start.9 = (bf16[64,768]{1,0:T(8,128)(2,1)S(1)}, bf16[64,768]{1,0:T(8,128)(2,1)S(1)}, u32[]{:S(2)}, u32[]{:S(2)}) collective-permute-start(bf16[64,768]{1,0:T(8,128)(2,1)S(1)} %get-tuple-element.73), channel_id=1, source_target_pairs={{0,0},{1,2},{2,1},{3,3},{4,4},{5,6},{6,5},{7,7},{8,8},{9,10},{10,9... | collective-permute-start | bytes 294920 | tf_op jit(solution)/shard_map/ppermute | solution.py:525
  32.1 4.7 %collective-permute-done.10.refs_2_ = bf16[64,768]{1,0:T(8,128)(2,1)S(1)} collective-permute-done((bf16[64,768]{1,0:T(8,128)(2,1)S(1)}, bf16[64,768]{1,0:T(8,128)(2,1)S(1)}, u32[]{:S(2)}, u32[]{:S(2)}) %collective-permute-start.10) | collective-permute-done | bytes 98336 | tf_op jit(solution)/shard_map/ppermute | solution.py:525
  36.9 2.1 %collective-permute-done.11.refs_3_ = bf16[64,768]{1,0:T(8,128)(2,1)S(1)} collective-permute-done((bf16[64,768]{1,0:T(8,128)(2,1)S(1)}, bf16[64,768]{1,0:T(8,128)(2,1)S(1)}, u32[]{:S(2)}, u32[]{:S(2)}) %collective-permute-start.11) | collective-permute-done | bytes 98336 | tf_op jit(solution)/shard_map/ppermute | solution.py:525
  39.0 0.2 collective-permute-start.12
  39.2 1.3 %column_project.1 = (f32[4,8,8,256]{3,2,1,0:T(8,128)S(1)}, bf16[256,384]{1,0:T(8,128)(2,1)S(1)}, bf16[256,384]{1,0:T(8,128)(2,1)S(1)}, bf16[256,384]{1,0:T(8,128)(2,1)S(1)}, bf16[256,384]{1,0:T(8,128)(2,1)S(1)}) custom-call(s32[4]{0:T(128)S(1)} %copy-done.8, s32[128]{0:T(128)S(1)} %copy-done.9, s32[1]{0:T(128)} %bitcast.place_ref, ...), custom_call_target="tpu_custom_call" | custom-call | flops 452984832 | bytes 1769472 | tf_op jit(solution)/shard_map/column_project/pallas_call | solution.py:645
  40.6 0.2 collective-permute-done.12.other_ref
  40.8 1.6 %column_attention.1 = (bf16[4,64,384]{2,1,0:T(8,128)(2,1)S(1)}, bf16[4,64,384]{2,1,0:T(8,128)(2,1)S(1)}) custom-call(s32[1]{0:T(128)} %bitcast.place_ref, bf16[768,768]{1,0:T(8,128)(2,1)S(1)} %copy-done, bf16[768,768]{1,0:T(8,128)(2,1)S(1)} %copy-done.1, bf16[768,768]{1,0:T(8,128)(2,1)S(1)} %copy-done.2, f32[4,8,8,256]{3,2,1,0:T(8,128)S(1)} %get-tuple-element.76.live_ref, ...), custom_call_target="tpu_custom_call" | custom-call | flops 1207959552 | bytes 3538944 | tf_op jit(solution)/shard_map/column_attention/pallas_call | solution.py:655
  42.4 0.3 collective-permute-start.13
  42.7 1.2 %collective-permute-done.13.other_ref = bf16[4,64,384]{2,1,0:T(8,128)(2,1)S(1)} collective-permute-done((bf16[4,64,384]{2,1,0:T(8,128)(2,1)S(1)}, bf16[4,64,384]{2,1,0:T(8,128)(2,1)S(1)}, u32[]{:S(2)}, u32[]{:S(2)}) %collective-permute-start.13) | collective-permute-done | bytes 196640 | tf_op jit(solution)/shard_map/ppermute | solution.py:500
  44.0 2.3 %collective-permute-start.14 = (bf16[64,768]{1,0:T(8,128)(2,1)S(1)}, bf16[64,768]{1,0:T(8,128)(2,1)S(1)}, u32[]{:S(2)}, u32[]{:S(2)}) collective-permute-start(bf16[64,768]{1,0:T(8,128)(2,1)S(1)} %get-tuple-element.83), channel_id=1, source_target_pairs={{8,0},{10,1},{9,2},{11,3},{12,4},{14,5},{13,6},{15,7},{0,8},{2,9},... | collective-permute-start | bytes 294920 | tf_op jit(solution)/shard_map/ppermute | solution.py:529
  46.3 2.6 %collective-permute-start.15 = (bf16[64,768]{1,0:T(8,128)(2,1)S(1)}, bf16[64,768]{1,0:T(8,128)(2,1)S(1)}, u32[]{:S(2)}, u32[]{:S(2)}) collective-permute-start(bf16[64,768]{1,0:T(8,128)(2,1)S(1)} %get-tuple-element.84), channel_id=1, source_target_pairs={{4,0},{6,1},{5,2},{7,3},{8,4},{10,5},{9,6},{11,7},{12,8},{14,9},{1... | collective-permute-start | bytes 294920 | tf_op jit(solution)/shard_map/ppermute | solution.py:529
  48.9 0.0 collective-permute-start.16
  48.9 0.7 %collective-permute-start.17 = (bf16[64,768]{1,0:T(8,128)(2,1)S(1)}, bf16[64,768]{1,0:T(8,128)(2,1)S(1)}, u32[]{:S(2)}, u32[]{:S(2)}) collective-permute-start(bf16[64,768]{1,0:T(8,128)(2,1)S(1)} %get-tuple-element.86), channel_id=1, source_target_pairs={{0,0},{2,1},{1,2},{3,3},{4,4},{6,5},{5,6},{7,7},{8,8},{10,9},{9,10... | collective-permute-start | bytes 294920 | tf_op jit(solution)/shard_map/ppermute | solution.py:529
  49.6 0.2 collective-permute-done.14.refs_0_
  49.8 2.9 %collective-permute-done.15.refs_1_ = bf16[64,768]{1,0:T(8,128)(2,1)S(1)} collective-permute-done((bf16[64,768]{1,0:T(8,128)(2,1)S(1)}, bf16[64,768]{1,0:T(8,128)(2,1)S(1)}, u32[]{:S(2)}, u32[]{:S(2)}) %collective-permute-start.15) | collective-permute-done | bytes 98336 | tf_op jit(solution)/shard_map/ppermute | solution.py:529
  52.7 3.6 %collective-permute-done.16.refs_2_ = bf16[64,768]{1,0:T(8,128)(2,1)S(1)} collective-permute-done((bf16[64,768]{1,0:T(8,128)(2,1)S(1)}, bf16[64,768]{1,0:T(8,128)(2,1)S(1)}, u32[]{:S(2)}, u32[]{:S(2)}) %collective-permute-start.16) | collective-permute-done | bytes 98336 | tf_op jit(solution)/shard_map/ppermute | solution.py:529
  56.3 0.0 collective-permute-done.17.refs_3_
  56.3 0.6 %column_output.1 = (bf16[2,64,768]{2,1,0:T(8,128)(2,1)S(1)}, bf16[2,64,768]{2,1,0:T(8,128)(2,1)S(1)}) custom-call(s32[1]{0:T(128)} %bitcast.place_ref, bf16[768,768]{1,0:T(8,128)(2,1)S(1)} %copy-done.6, bf16[256,768]{1,0:T(8,128)(2,1)S(1)} %get-tuple-element.68.after_ref, bf16[64,768]{1,0:T(8,128)(2,1)S(1)} %collective-permute-done.14.refs_0_, ...), custom_call_target="tpu_custom_call" | custom-call | flops 301989888 | bytes 1179648 | tf_op jit(solution)/shard_map/column_output/pallas_call | solution.py:675
  56.9 0.8 %collective-permute-start.18 = (bf16[2,64,768]{2,1,0:T(8,128)(2,1)S(1)}, bf16[2,64,768]{2,1,0:T(8,128)(2,1)S(1)}, u32[]{:S(2)}, u32[]{:S(2)}) collective-permute-start(bf16[2,64,768]{2,1,0:T(8,128)(2,1)S(1)} %get-tuple-element.88), channel_id=1, source_target_pairs={{0,1},{1,0},{2,3},{3,2},{4,5},{5,4},{6,7},{7,6},{8,9},{9,8},{10,11... | collective-permute-start | bytes 589832 | tf_op jit(solution)/shard_map/ppermute | solution.py:500
  57.7 1.1 %collective-permute-done.18.other_ref = bf16[2,64,768]{2,1,0:T(8,128)(2,1)S(1)} collective-permute-done((bf16[2,64,768]{2,1,0:T(8,128)(2,1)S(1)}, bf16[2,64,768]{2,1,0:T(8,128)(2,1)S(1)}, u32[]{:S(2)}, u32[]{:S(2)}) %collective-permute-start.18) | collective-permute-done | bytes 196640 | tf_op jit(solution)/shard_map/ppermute | solution.py:500
  58.8 0.8 %assemble.1 = bf16[2,128,768]{2,1,0:T(8,128)(2,1)} custom-call(s32[1]{0:T(128)} %bitcast.place_ref, bf16[2,64,768]{2,1,0:T(8,128)(2,1)S(1)} %get-tuple-element.87.mine_ref, bf16[2,64,768]{2,1,0:T(8,128)(2,1)S(1)} %collective-permute-done.18.other_ref), custom_call_target="tpu_custom_call" | custom-call | flops 196608 | bytes 786432 | tf_op jit(solution)/shard_map/assemble/pallas_call | solution.py:684
  (25 shorter events, 0.1 us)
Async XLA Ops:
  0.0 2.9 %collective-permute-start = (bf16[256,768]{1,0:T(8,128)(2,1)}, bf16[256,768]{1,0:T(8,128)(2,1)S(1)}, u32[]{:S(2)}, u32[]{:S(2)}) collective-permute-start(bf16[256,768]{1,0:T(8,128)(2,1)} %bitcast.2), channel_id=1, source_target_pairs={{0,1},{1,0},{2,3},{3,2},{4,5},{5,4},{6,7},{7,6},{8,9},{9,8},{10,11... | collective-permute-start | bytes 1179656 | tf_op jit(solution)/shard_map/ppermute | solution.py:500
  0.5 2.5 %copy-start.7 = (f32[768]{0:T(1024)S(1)}, f32[768]{0:T(1024)}, u32[]{:S(2)}) copy-start(f32[768]{0:T(1024)} %gain_ref.1) | copy-start | bytes 9220
  3.0 13.4 %copy-start.3 = (bf16[2,128,768]{2,1,0:T(8,128)(2,1)S(1)}, bf16[2,128,768]{2,1,0:T(8,128)(2,1)}, u32[]{:S(2)}) copy-start(bf16[2,128,768]{2,1,0:T(8,128)(2,1)} %param.13) | copy-start | bytes 1179652
  3.0 13.4 %copy-start.5 = (bf16[768,768]{1,0:T(8,128)(2,1)S(1)}, bf16[768,768]{1,0:T(8,128)(2,1)}, u32[]{:S(2)}) copy-start(bf16[768,768]{1,0:T(8,128)(2,1)} %w_ref.3) | copy-start | bytes 3538948
  4.8 7.5 %collective-permute-start.1 = (f32[16,768]{1,0:T(8,128)S(1)}, f32[16,768]{1,0:T(8,128)S(1)}, u32[]{:S(2)}, u32[]{:S(2)}) collective-permute-start(f32[16,768]{1,0:T(8,128)S(1)} %get-tuple-element.56), channel_id=1, source_target_pairs={{0,8},{1,9},{2,10},{3,11},{4,12},{5,13},{6,14},{7,15},{8,0},{9,1},... | collective-permute-start | bytes 147464 | tf_op jit(solution)/shard_map/ppermute | solution.py:521
  8.4 6.2 %collective-permute-start.2 = (f32[16,768]{1,0:T(8,128)S(1)}, f32[16,768]{1,0:T(8,128)S(1)}, u32[]{:S(2)}, u32[]{:S(2)}) collective-permute-start(f32[16,768]{1,0:T(8,128)S(1)} %get-tuple-element.57), channel_id=1, source_target_pairs={{0,4},{1,5},{2,6},{3,7},{4,8},{5,9},{6,10},{7,11},{8,12},{9,13},{1... | collective-permute-start | bytes 147464 | tf_op jit(solution)/shard_map/ppermute | solution.py:521
  10.0 4.7 %collective-permute-start.3 = (f32[16,768]{1,0:T(8,128)S(1)}, f32[16,768]{1,0:T(8,128)S(1)}, u32[]{:S(2)}, u32[]{:S(2)}) collective-permute-start(f32[16,768]{1,0:T(8,128)S(1)} %get-tuple-element.58), channel_id=1, source_target_pairs={{0,12},{1,13},{2,14},{3,15},{4,0},{5,1},{6,2},{7,3},{8,4},{9,5},{1... | collective-permute-start | bytes 147464 | tf_op jit(solution)/shard_map/ppermute | solution.py:521
  14.7 4.2 %collective-permute-start.4 = (f32[16,768]{1,0:T(8,128)S(1)}, f32[16,768]{1,0:T(8,128)S(1)}, u32[]{:S(2)}, u32[]{:S(2)}) collective-permute-start(f32[16,768]{1,0:T(8,128)S(1)} %add.1.mine_ref), channel_id=1, source_target_pairs={{0,2},{1,3},{2,0},{3,1},{4,6},{5,7},{6,4},{7,5},{8,10},{9,11},{10,... | collective-permute-start | bytes 147464 | tf_op jit(solution)/shard_map/ppermute | solution.py:500
  16.3 7.7 %copy-start.10 = (f32[768]{0:T(1024)S(1)}, f32[768]{0:T(1024)}, u32[]{:S(2)}) copy-start(f32[768]{0:T(1024)} %param.21) | copy-start | bytes 9220
  16.3 10.6 %copy-start.4 = (bf16[768,768]{1,0:T(8,128)(2,1)S(1)}, bf16[768,768]{1,0:T(8,128)(2,1)}, u32[]{:S(2)}) copy-start(bf16[768,768]{1,0:T(8,128)(2,1)} %w_ref.4) | copy-start | bytes 3538948
  19.1 4.9 %collective-permute-start.5 = (bf16[16,768]{1,0:T(8,128)(2,1)S(1)}, bf16[16,768]{1,0:T(8,128)(2,1)S(1)}, u32[]{:S(2)}, u32[]{:S(2)}) collective-permute-start(bf16[16,768]{1,0:T(8,128)(2,1)S(1)} %row_softmax.1.refs_3_), channel_id=1, source_target_pairs={{0,8},{1,9},{2,10},{3,11},{4,12},{5,13},{6,14},{7,15},{8,0},{9,1},... | collective-permute-start | bytes 73736 | tf_op jit(solution)/shard_map/ppermute | solution.py:521
  20.2 5.6 %collective-permute-start.6 = (bf16[16,768]{1,0:T(8,128)(2,1)S(1)}, bf16[16,768]{1,0:T(8,128)(2,1)S(1)}, u32[]{:S(2)}, u32[]{:S(2)}) collective-permute-start(bf16[16,768]{1,0:T(8,128)(2,1)S(1)} %row_softmax.1.refs_3_), channel_id=1, source_target_pairs={{0,4},{1,5},{2,6},{3,7},{4,8},{5,9},{6,10},{7,11},{8,12},{9,13},{1... | collective-permute-start | bytes 73736 | tf_op jit(solution)/shard_map/ppermute | solution.py:521
  23.1 3.8 %collective-permute-start.7 = (bf16[16,768]{1,0:T(8,128)(2,1)S(1)}, bf16[16,768]{1,0:T(8,128)(2,1)S(1)}, u32[]{:S(2)}, u32[]{:S(2)}) collective-permute-start(bf16[16,768]{1,0:T(8,128)(2,1)S(1)} %row_softmax.1.refs_3_), channel_id=1, source_target_pairs={{0,12},{1,13},{2,14},{3,15},{4,0},{5,1},{6,2},{7,3},{8,4},{9,5},{1... | collective-permute-start | bytes 73736 | tf_op jit(solution)/shard_map/ppermute | solution.py:521
  27.0 12.2 %copy-start = (bf16[768,768]{1,0:T(8,128)(2,1)S(1)}, bf16[768,768]{1,0:T(8,128)(2,1)}, u32[]{:S(2)}) copy-start(bf16[768,768]{1,0:T(8,128)(2,1)} %wq_ref.1) | copy-start | bytes 3538948
  27.0 12.2 %copy-start.1 = (bf16[768,768]{1,0:T(8,128)(2,1)S(1)}, bf16[768,768]{1,0:T(8,128)(2,1)}, u32[]{:S(2)}) copy-start(bf16[768,768]{1,0:T(8,128)(2,1)} %wk_ref.1) | copy-start | bytes 3538948
  27.0 12.2 %copy-start.2 = (bf16[768,768]{1,0:T(8,128)(2,1)S(1)}, bf16[768,768]{1,0:T(8,128)(2,1)}, u32[]{:S(2)}) copy-start(bf16[768,768]{1,0:T(8,128)(2,1)} %wv_ref.1) | copy-start | bytes 3538948
  27.0 12.2 %copy-start.8 = (s32[4]{0:T(128)S(1)}, s32[4]{0:T(128)}, u32[]{:S(2)}) copy-start(s32[4]{0:T(128)} %depth_ref.1) | copy-start | bytes 52
  27.0 12.2 %copy-start.9 = (s32[128]{0:T(128)S(1)}, s32[128]{0:T(128)}, u32[]{:S(2)}) copy-start(s32[128]{0:T(128)} %prot_ref.1) | copy-start | bytes 1540
  28.2 8.6 %collective-permute-start.10 = (bf16[64,768]{1,0:T(8,128)(2,1)S(1)}, bf16[64,768]{1,0:T(8,128)(2,1)S(1)}, u32[]{:S(2)}, u32[]{:S(2)}) collective-permute-start(bf16[64,768]{1,0:T(8,128)(2,1)S(1)} %get-tuple-element.74), channel_id=1, source_target_pairs={{0,8},{1,10},{2,9},{3,11},{4,12},{5,14},{6,13},{7,15},{8,0},{9,2},... | collective-permute-start | bytes 294920 | tf_op jit(solution)/shard_map/ppermute | solution.py:525
  28.3 10.6 %collective-permute-start.11 = (bf16[64,768]{1,0:T(8,128)(2,1)S(1)}, bf16[64,768]{1,0:T(8,128)(2,1)S(1)}, u32[]{:S(2)}, u32[]{:S(2)}) collective-permute-start(bf16[64,768]{1,0:T(8,128)(2,1)S(1)} %get-tuple-element.75), channel_id=1, source_target_pairs={{0,12},{1,14},{2,13},{3,15},{4,0},{5,2},{6,1},{7,3},{8,4},{9,6},{1... | collective-permute-start | bytes 294920 | tf_op jit(solution)/shard_map/ppermute | solution.py:525
  31.0 8.0 %collective-permute-start.8 = (bf16[64,768]{1,0:T(8,128)(2,1)S(1)}, bf16[64,768]{1,0:T(8,128)(2,1)S(1)}, u32[]{:S(2)}, u32[]{:S(2)}) collective-permute-start(bf16[64,768]{1,0:T(8,128)(2,1)S(1)} %get-tuple-element.72), channel_id=1, source_target_pairs={{0,4},{1,6},{2,5},{3,7},{4,8},{5,10},{6,9},{7,11},{8,12},{9,14},{1... | collective-permute-start | bytes 294920 | tf_op jit(solution)/shard_map/ppermute | solution.py:525
  31.5 7.5 %collective-permute-start.9 = (bf16[64,768]{1,0:T(8,128)(2,1)S(1)}, bf16[64,768]{1,0:T(8,128)(2,1)S(1)}, u32[]{:S(2)}, u32[]{:S(2)}) collective-permute-start(bf16[64,768]{1,0:T(8,128)(2,1)S(1)} %get-tuple-element.73), channel_id=1, source_target_pairs={{0,0},{1,2},{2,1},{3,3},{4,4},{5,6},{6,5},{7,7},{8,8},{9,10},{10,9... | collective-permute-start | bytes 294920 | tf_op jit(solution)/shard_map/ppermute | solution.py:525
  39.0 1.8 %collective-permute-start.12 = (bf16[4,64,768]{2,1,0:T(8,128)(2,1)S(1)}, bf16[4,64,768]{2,1,0:T(8,128)(2,1)S(1)}, u32[]{:S(2)}, u32[]{:S(2)}) collective-permute-start(bf16[4,64,768]{2,1,0:T(8,128)(2,1)S(1)} %pack.1), channel_id=1, source_target_pairs={{0,1},{1,0},{2,3},{3,2},{4,5},{5,4},{6,7},{7,6},{8,9},{9,8},{10,11... | collective-permute-start | bytes 1179656 | tf_op jit(solution)/shard_map/ppermute | solution.py:500
  40.8 15.5 %copy-start.6 = (bf16[768,768]{1,0:T(8,128)(2,1)S(1)}, bf16[768,768]{1,0:T(8,128)(2,1)}, u32[]{:S(2)}) copy-start(bf16[768,768]{1,0:T(8,128)(2,1)} %w_ref.5) | copy-start | bytes 3538948
  42.4 1.5 %collective-permute-start.13 = (bf16[4,64,384]{2,1,0:T(8,128)(2,1)S(1)}, bf16[4,64,384]{2,1,0:T(8,128)(2,1)S(1)}, u32[]{:S(2)}, u32[]{:S(2)}) collective-permute-start(bf16[4,64,384]{2,1,0:T(8,128)(2,1)S(1)} %get-tuple-element.82), channel_id=1, source_target_pairs={{0,1},{1,0},{2,3},{3,2},{4,5},{5,4},{6,7},{7,6},{8,9},{9,8},{10,11... | collective-permute-start | bytes 589832 | tf_op jit(solution)/shard_map/ppermute | solution.py:500
  44.0 5.8 %collective-permute-start.14 = (bf16[64,768]{1,0:T(8,128)(2,1)S(1)}, bf16[64,768]{1,0:T(8,128)(2,1)S(1)}, u32[]{:S(2)}, u32[]{:S(2)}) collective-permute-start(bf16[64,768]{1,0:T(8,128)(2,1)S(1)} %get-tuple-element.83), channel_id=1, source_target_pairs={{8,0},{10,1},{9,2},{11,3},{12,4},{14,5},{13,6},{15,7},{0,8},{2,9},... | collective-permute-start | bytes 294920 | tf_op jit(solution)/shard_map/ppermute | solution.py:529
  46.3 6.4 %collective-permute-start.15 = (bf16[64,768]{1,0:T(8,128)(2,1)S(1)}, bf16[64,768]{1,0:T(8,128)(2,1)S(1)}, u32[]{:S(2)}, u32[]{:S(2)}) collective-permute-start(bf16[64,768]{1,0:T(8,128)(2,1)S(1)} %get-tuple-element.84), channel_id=1, source_target_pairs={{4,0},{6,1},{5,2},{7,3},{8,4},{10,5},{9,6},{11,7},{12,8},{14,9},{1... | collective-permute-start | bytes 294920 | tf_op jit(solution)/shard_map/ppermute | solution.py:529
  48.9 7.4 %collective-permute-start.16 = (bf16[64,768]{1,0:T(8,128)(2,1)S(1)}, bf16[64,768]{1,0:T(8,128)(2,1)S(1)}, u32[]{:S(2)}, u32[]{:S(2)}) collective-permute-start(bf16[64,768]{1,0:T(8,128)(2,1)S(1)} %get-tuple-element.85), channel_id=1, source_target_pairs={{12,0},{14,1},{13,2},{15,3},{0,4},{2,5},{1,6},{3,7},{4,8},{6,9},{5... | collective-permute-start | bytes 294920 | tf_op jit(solution)/shard_map/ppermute | solution.py:529
  48.9 7.4 %collective-permute-start.17 = (bf16[64,768]{1,0:T(8,128)(2,1)S(1)}, bf16[64,768]{1,0:T(8,128)(2,1)S(1)}, u32[]{:S(2)}, u32[]{:S(2)}) collective-permute-start(bf16[64,768]{1,0:T(8,128)(2,1)S(1)} %get-tuple-element.86), channel_id=1, source_target_pairs={{0,0},{2,1},{1,2},{3,3},{4,4},{6,5},{5,6},{7,7},{8,8},{10,9},{9,10... | collective-permute-start | bytes 294920 | tf_op jit(solution)/shard_map/ppermute | solution.py:529
  56.9 1.8 %collective-permute-start.18 = (bf16[2,64,768]{2,1,0:T(8,128)(2,1)S(1)}, bf16[2,64,768]{2,1,0:T(8,128)(2,1)S(1)}, u32[]{:S(2)}, u32[]{:S(2)}) collective-permute-start(bf16[2,64,768]{2,1,0:T(8,128)(2,1)S(1)} %get-tuple-element.88), channel_id=1, source_target_pairs={{0,1},{1,0},{2,3},{3,2},{4,5},{5,4},{6,7},{7,6},{8,9},{9,8},{10,11... | collective-permute-start | bytes 589832 | tf_op jit(solution)/shard_map/ppermute | solution.py:500

commit v12 on v11

--- a/solution.py
+++ b/solution.py
@@ -17,14 +17,15 @@
 PLANE = 4
 
 
-def call(kernel, out_shape, ins, outs, scratch, cost, name):
-    spaces = {"v": pltpu.VMEM, "s": pltpu.SMEM, "h": pltpu.HBM, "a": pl.ANY}
+def call(kernel, out_shape, ins, outs, scratch, cost, name, aliases=None):
+    spaces = {"v": pltpu.VMEM, "s": pltpu.SMEM, "h": pltpu.HBM}
     return pl.pallas_call(
         kernel,
         out_shape=out_shape,
         in_specs=[pl.BlockSpec(memory_space=spaces[c]) for c in ins],
         out_specs=[pl.BlockSpec(memory_space=spaces[c]) for c in outs],
         scratch_shapes=scratch,
+        input_output_aliases=aliases or {},
         compiler_params=pltpu.CompilerParams(vmem_limit_bytes=LIMIT),
         cost_estimate=pl.CostEstimate(flops=cost[0], bytes_accessed=cost[1], transcendentals=cost[2]),
         name=name,
@@ -470,25 +471,30 @@
                 target[r, :, lanes] = row.astype(BF16)
 
 
-def assemble_kernel(place_ref, mine_ref, other_ref, out_ref, sems):
-    core = place_ref[0] % 2
-    local = mine_ref.shape[1]
-    quarter = local // 2
+def place_half(source, out_ref, index, sems):
+    quarter = source.shape[1] // 2
     copies = []
-    for source, index in ((mine_ref, core), (other_ref, 1 - core)):
-        for y in range(2):
-            start = pl.multiple_of(y * local + index * quarter, quarter)
-            copies.append(
-                pltpu.make_async_copy(
-                    source.at[:, y * quarter : (y + 1) * quarter, :],
-                    out_ref.at[:, pl.ds(start, quarter), :],
-                    sems.at[len(copies)],
-                )
+    for y in range(2):
+        start = pl.multiple_of(y * 2 * quarter + index * quarter, quarter)
+        copies.append(
+            pltpu.make_async_copy(
+                source.at[:, y * quarter : (y + 1) * quarter, :],
+                out_ref.at[:, pl.ds(start, quarter), :],
+                sems.at[y],
             )
+        )
     for copy in copies:
         copy.start()
     for copy in copies:
         copy.wait()
+
+
+def own_half_kernel(place_ref, mine_ref, out_ref, sems):
+    place_half(mine_ref, out_ref, place_ref[0] % 2, sems)
+
+
+def assemble_kernel(place_ref, other_ref, half_ref, out_ref, sems):
+    place_half(other_ref, out_ref, 1 - place_ref[0] % 2, sems)
 
 
 def hbm(array):
@@ -681,15 +687,13 @@
         (square, 2 * width * width, 0),
         "column_output",
     )(place, column_output, after, *returned)
-    (out,) = call(
-        assemble_kernel,
-        (shape((rows, columns, width), BF16),),
-        "svv",
-        "a",
-        [pltpu.SemaphoreType.DMA((4,))],
-        (tokens * width, 4 * tokens * width, 0),
-        "assemble",
-    )(place, keep, swap(send, 1))
+    whole = shape((rows, columns, width), BF16)
+    cost = (tokens * width, 2 * tokens * width, 0)
+    two = [pltpu.SemaphoreType.DMA((2,))]
+    (begun,) = call(own_half_kernel, (whole,), "sv", "h", two, cost, "own_half")(place, keep)
+    (out,) = call(assemble_kernel, (whole,), "svh", "h", two, cost, "assemble", {2: 0})(
+        place, swap(send, 1), begun
+    )
     return out
 
 

time: 59.7 us -> 59.6 us (level)
  waiting for transfers between devices: 23.3 us -> 22.6 us
  Pallas kernels: 10.9 us -> 11.5 us
    ppermute x5, waiting for transfers between devices: 4.32 us -> 3.62 us  [swap(): return lax.ppermute(array, 'seq', [(i, i ^ offset) for i in range(devices)])]
    pallas_call x1 -> x2, Pallas kernels: 0.77 us -> 1.38 us  [the longest x1 0.69 us: per_device(): call(own_half_kernel, (whole,), 'sv', 'h', two, cost, 'own_half')]
  transfers between devices with their start and end apart: 19 -> 19, of which waited for: 13 -> 13; matrix products, arithmetic and copies ran while one was open for 0% -> 0% of each run, Pallas kernels for 8% -> 9%
where the time goes in v12:
time: 59.6 us; the launch traced here: 59.5 us
  starting transfers between devices  25.1 us (42%)
  waiting for transfers between devices  22.6 us (38%)
  Pallas kernels  11.5 us (19%)
    ppermute x6, starting transfers between devices, shift(): lax.ppermute(array, 'seq', [(i, (i + PLANE * step) % devices) for i in ra...  12.3 us
    ppermute x4, waiting for transfers between devices, spin(): return lax.ppermute(array, 'seq', spin_pairs(step))  6.83 us
    ppermute x4, waiting for transfers between devices, spin_back(): return lax.ppermute(array, 'seq', [(b, a) for a, b in spin_pairs(step)])  6.72 us
    ppermute x4, starting transfers between devices, spin_back(): return lax.ppermute(array, 'seq', [(b, a) for a, b in spin_pairs(step)])  5.57 us
    ppermute x6, waiting for transfers between devices, shift(): lax.ppermute(array, 'seq', [(i, (i + PLANE * step) % devices) for i in ra...  5.46 us
    ppermute x4, starting transfers between devices, spin(): return lax.ppermute(array, 'seq', spin_pairs(step))  3.92 us
    ppermute x5, waiting for transfers between devices, swap(): return lax.ppermute(array, 'seq', [(i, i ^ offset) for i in range(devices)])  3.62 us
    ppermute x5, starting transfers between devices, swap(): return lax.ppermute(array, 'seq', [(i, i ^ offset) for i in range(devices)])  3.24 us
  transfers between devices with their start and end apart: 19, of which 13 were waited for; matrix products, arithmetic and copies ran while one was open for 0% of the time, Pallas kernels for 9%

profile of v12, /device:TPU:0, one launch (start us, length us, event | category | flops | bytes accessed | tf_op | source)
XLA Modules:
  0.0 59.5 jit_solution(7877875444450070133)
XLA Ops:
  0.0 0.5 collective-permute-start
  0.5 2.5 %row_own.1 = (bf16[256,768]{1,0:T(8,128)(2,1)S(1)}, bf16[128,768]{1,0:T(8,128)(2,1)S(1)}, bf16[256,768]{1,0:T(8,128)(2,1)S(1)}, bf16[768,768]{1,0:T(8,128)(2,1)S...) custom-call(s32[1]{0:T(128)} %bitcast.place_ref, ...), custom_call_target="tpu_custom_call" | custom-call | flops 452984832 | bytes 2359296 | tf_op jit(solution)/shard_map/row_own/pallas_call | solution.py:570
  3.0 0.0 copy-start.3
  3.0 0.0 copy-start.5
  3.0 1.8 %row_scores.1 = (f32[16,768]{1,0:T(8,128)S(1)}, f32[16,768]{1,0:T(8,128)S(1)}, f32[16,768]{1,0:T(8,128)S(1)}, f32[16,768]{1,0:T(8,128)S(1)}, bf16[256,768]{1,0:T(8,128)(2,1)S(1)}) custom-call(s32[1]{0:T(128)} %bitcast.place_ref, bf16[256,768]{1,0:T(8,128)(2,1)S(1)} %collective-permute-done.x_ref.other_ref, f32[768]{0:T(1024)S(1)} %copy-done.7, ...), custom_call_target="tpu_custom_call" | custom-call | flops 452984832 | bytes 2359296 | tf_op jit(solution)/shard_map/row_scores/pallas_call | solution.py:587
  4.8 3.7 %collective-permute-start.1 = (f32[16,768]{1,0:T(8,128)S(1)}, f32[16,768]{1,0:T(8,128)S(1)}, u32[]{:S(2)}, u32[]{:S(2)}) collective-permute-start(f32[16,768]{1,0:T(8,128)S(1)} %get-tuple-element.56), channel_id=1, source_target_pairs={{0,8},{1,9},{2,10},{3,11},{4,12},{5,13},{6,14},{7,15},{8,0},{9,1},... | collective-permute-start | bytes 147464 | tf_op jit(solution)/shard_map/ppermute | solution.py:527
  8.4 1.6 %collective-permute-start.2 = (f32[16,768]{1,0:T(8,128)S(1)}, f32[16,768]{1,0:T(8,128)S(1)}, u32[]{:S(2)}, u32[]{:S(2)}) collective-permute-start(f32[16,768]{1,0:T(8,128)S(1)} %get-tuple-element.57), channel_id=1, source_target_pairs={{0,4},{1,5},{2,6},{3,7},{4,8},{5,9},{6,10},{7,11},{8,12},{9,13},{1... | collective-permute-start | bytes 147464 | tf_op jit(solution)/shard_map/ppermute | solution.py:527
  10.0 2.2 %collective-permute-start.3 = (f32[16,768]{1,0:T(8,128)S(1)}, f32[16,768]{1,0:T(8,128)S(1)}, u32[]{:S(2)}, u32[]{:S(2)}) collective-permute-start(f32[16,768]{1,0:T(8,128)S(1)} %get-tuple-element.58), channel_id=1, source_target_pairs={{0,12},{1,13},{2,14},{3,15},{4,0},{5,1},{6,2},{7,3},{8,4},{9,5},{1... | collective-permute-start | bytes 147464 | tf_op jit(solution)/shard_map/ppermute | solution.py:527
  12.2 0.0 collective-permute-done.1.refs_0_
  12.2 2.4 %collective-permute-done.2.refs_1_ = f32[16,768]{1,0:T(8,128)S(1)} collective-permute-done((f32[16,768]{1,0:T(8,128)S(1)}, f32[16,768]{1,0:T(8,128)S(1)}, u32[]{:S(2)}, u32[]{:S(2)}) %collective-permute-start.2) | collective-permute-done | bytes 49184 | tf_op jit(solution)/shard_map/ppermute | solution.py:527
  14.6 0.1 collective-permute-done.3.refs_2_
  14.7 1.6 %collective-permute-start.4 = (f32[16,768]{1,0:T(8,128)S(1)}, f32[16,768]{1,0:T(8,128)S(1)}, u32[]{:S(2)}, u32[]{:S(2)}) collective-permute-start(f32[16,768]{1,0:T(8,128)S(1)} %add.1.mine_ref), channel_id=1, source_target_pairs={{0,2},{1,3},{2,0},{3,1},{4,6},{5,7},{6,4},{7,5},{8,10},{9,11},{10,... | collective-permute-start | bytes 147464 | tf_op jit(solution)/shard_map/ppermute | solution.py:506
  16.3 0.8 %row_value.1 = (bf16[256,768]{1,0:T(8,128)(2,1)S(1)}, bf16[256,768]{1,0:T(8,128)(2,1)S(1)}, f32[6,256,128]{2,1,0:T(8,128)S(1)}) custom-call(s32[1]{0:T(128)} %bitcast.place_ref, bf16[256,768]{1,0:T(8,128)(2,1)S(1)} %get-tuple-element.60.x_ref, bf16[256,768]{1,0:T(8,128)(2,1)S(1)} %get-tuple-element.61.y_ref, bf16[768,768]{1,0:T(8,128)(2,1)S(1)} %copy-done.5, ...), custom_call_target="tpu_custom_call" | custom-call | flops 603979776 | bytes 1179648 | tf_op jit(solution)/shard_map/row_value/pallas_call | solution.py:604
  17.1 1.8 %collective-permute-done.4.other_ref = f32[16,768]{1,0:T(8,128)S(1)} collective-permute-done((f32[16,768]{1,0:T(8,128)S(1)}, f32[16,768]{1,0:T(8,128)S(1)}, u32[]{:S(2)}, u32[]{:S(2)}) %collective-permute-start.4) | collective-permute-done | bytes 49184 | tf_op jit(solution)/shard_map/ppermute | solution.py:506
  18.9 0.2 row_softmax.1.refs_3_
  19.1 1.1 %collective-permute-start.5 = (bf16[16,768]{1,0:T(8,128)(2,1)S(1)}, bf16[16,768]{1,0:T(8,128)(2,1)S(1)}, u32[]{:S(2)}, u32[]{:S(2)}) collective-permute-start(bf16[16,768]{1,0:T(8,128)(2,1)S(1)} %row_softmax.1.refs_3_), channel_id=1, source_target_pairs={{0,8},{1,9},{2,10},{3,11},{4,12},{5,13},{6,14},{7,15},{8,0},{9,1},... | collective-permute-start | bytes 73736 | tf_op jit(solution)/shard_map/ppermute | solution.py:527
  20.2 3.0 %collective-permute-start.6 = (bf16[16,768]{1,0:T(8,128)(2,1)S(1)}, bf16[16,768]{1,0:T(8,128)(2,1)S(1)}, u32[]{:S(2)}, u32[]{:S(2)}) collective-permute-start(bf16[16,768]{1,0:T(8,128)(2,1)S(1)} %row_softmax.1.refs_3_), channel_id=1, source_target_pairs={{0,4},{1,5},{2,6},{3,7},{4,8},{5,9},{6,10},{7,11},{8,12},{9,13},{1... | collective-permute-start | bytes 73736 | tf_op jit(solution)/shard_map/ppermute | solution.py:527
  23.1 0.8 %collective-permute-start.7 = (bf16[16,768]{1,0:T(8,128)(2,1)S(1)}, bf16[16,768]{1,0:T(8,128)(2,1)S(1)}, u32[]{:S(2)}, u32[]{:S(2)}) collective-permute-start(bf16[16,768]{1,0:T(8,128)(2,1)S(1)} %row_softmax.1.refs_3_), channel_id=1, source_target_pairs={{0,12},{1,13},{2,14},{3,15},{4,0},{5,1},{6,2},{7,3},{8,4},{9,5},{1... | collective-permute-start | bytes 73736 | tf_op jit(solution)/shard_map/ppermute | solution.py:527
  24.0 0.0 collective-permute-done.5.refs_0_
  24.0 1.8 %collective-permute-done.6.refs_1_ = bf16[16,768]{1,0:T(8,128)(2,1)S(1)} collective-permute-done((bf16[16,768]{1,0:T(8,128)(2,1)S(1)}, bf16[16,768]{1,0:T(8,128)(2,1)S(1)}, u32[]{:S(2)}, u32[]{:S(2)}) %collective-permute-start.6) | collective-permute-done | bytes 24608 | tf_op jit(solution)/shard_map/ppermute | solution.py:527
  25.8 1.2 %collective-permute-done.7.refs_2_ = bf16[16,768]{1,0:T(8,128)(2,1)S(1)} collective-permute-done((bf16[16,768]{1,0:T(8,128)(2,1)S(1)}, bf16[16,768]{1,0:T(8,128)(2,1)S(1)}, u32[]{:S(2)}, u32[]{:S(2)}) %collective-permute-start.7) | collective-permute-done | bytes 24608 | tf_op jit(solution)/shard_map/ppermute | solution.py:527
  27.0 0.0 copy-start.8
  27.0 0.0 copy-start.9
  27.0 1.2 %row_output.1 = (bf16[256,768]{1,0:T(8,128)(2,1)S(1)}, bf16[64,768]{1,0:T(8,128)(2,1)S(1)}, bf16[64,768]{1,0:T(8,128)(2,1)S(1)}, bf16[64,768]{1,0:T(8,128)(2,1)S(1)}, bf16[64,768]{1,0:T(8,128)(2,1)S(1)}) custom-call(s32[1]{0:T(128)} %bitcast.place_ref, f32[64,128]{1,0:T(8,128)S(1)} %get-tuple-element.47.same_ref, ...), custom_call_target="tpu_custom_call" | custom-call | flops 301989888 | bytes 1179648 | tf_op jit(solution)/shard_map/row_output/pallas_call | solution.py:624
  28.2 0.1 collective-permute-start.10
  28.3 2.6 %collective-permute-start.11 = (bf16[64,768]{1,0:T(8,128)(2,1)S(1)}, bf16[64,768]{1,0:T(8,128)(2,1)S(1)}, u32[]{:S(2)}, u32[]{:S(2)}) collective-permute-start(bf16[64,768]{1,0:T(8,128)(2,1)S(1)} %get-tuple-element.75), channel_id=1, source_target_pairs={{0,12},{1,14},{2,13},{3,15},{4,0},{5,2},{6,1},{7,3},{8,4},{9,6},{1... | collective-permute-start | bytes 294920 | tf_op jit(solution)/shard_map/ppermute | solution.py:531
  31.0 0.5 collective-permute-start.8
  31.5 0.7 %collective-permute-start.9 = (bf16[64,768]{1,0:T(8,128)(2,1)S(1)}, bf16[64,768]{1,0:T(8,128)(2,1)S(1)}, u32[]{:S(2)}, u32[]{:S(2)}) collective-permute-start(bf16[64,768]{1,0:T(8,128)(2,1)S(1)} %get-tuple-element.73), channel_id=1, source_target_pairs={{0,0},{1,2},{2,1},{3,3},{4,4},{5,6},{6,5},{7,7},{8,8},{9,10},{10,9... | collective-permute-start | bytes 294920 | tf_op jit(solution)/shard_map/ppermute | solution.py:531
  32.1 4.7 %collective-permute-done.10.refs_2_ = bf16[64,768]{1,0:T(8,128)(2,1)S(1)} collective-permute-done((bf16[64,768]{1,0:T(8,128)(2,1)S(1)}, bf16[64,768]{1,0:T(8,128)(2,1)S(1)}, u32[]{:S(2)}, u32[]{:S(2)}) %collective-permute-start.10) | collective-permute-done | bytes 98336 | tf_op jit(solution)/shard_map/ppermute | solution.py:531
  36.9 2.1 %collective-permute-done.11.refs_3_ = bf16[64,768]{1,0:T(8,128)(2,1)S(1)} collective-permute-done((bf16[64,768]{1,0:T(8,128)(2,1)S(1)}, bf16[64,768]{1,0:T(8,128)(2,1)S(1)}, u32[]{:S(2)}, u32[]{:S(2)}) %collective-permute-start.11) | collective-permute-done | bytes 98336 | tf_op jit(solution)/shard_map/ppermute | solution.py:531
  39.0 0.2 collective-permute-start.12
  39.2 1.3 %column_project.1 = (f32[4,8,8,256]{3,2,1,0:T(8,128)S(1)}, bf16[256,384]{1,0:T(8,128)(2,1)S(1)}, bf16[256,384]{1,0:T(8,128)(2,1)S(1)}, bf16[256,384]{1,0:T(8,128)(2,1)S(1)}, bf16[256,384]{1,0:T(8,128)(2,1)S(1)}) custom-call(s32[4]{0:T(128)S(1)} %copy-done.8, s32[128]{0:T(128)S(1)} %copy-done.9, s32[1]{0:T(128)} %bitcast.place_ref, ...), custom_call_target="tpu_custom_call" | custom-call | flops 452984832 | bytes 1769472 | tf_op jit(solution)/shard_map/column_project/pallas_call | solution.py:651
  40.6 0.2 collective-permute-done.12.other_ref
  40.8 1.6 %column_attention.1 = (bf16[4,64,384]{2,1,0:T(8,128)(2,1)S(1)}, bf16[4,64,384]{2,1,0:T(8,128)(2,1)S(1)}) custom-call(s32[1]{0:T(128)} %bitcast.place_ref, bf16[768,768]{1,0:T(8,128)(2,1)S(1)} %copy-done, bf16[768,768]{1,0:T(8,128)(2,1)S(1)} %copy-done.1, bf16[768,768]{1,0:T(8,128)(2,1)S(1)} %copy-done.2, f32[4,8,8,256]{3,2,1,0:T(8,128)S(1)} %get-tuple-element.76.live_ref, ...), custom_call_target="tpu_custom_call" | custom-call | flops 1207959552 | bytes 3538944 | tf_op jit(solution)/shard_map/column_attention/pallas_call | solution.py:661
  42.4 0.3 collective-permute-start.13
  42.7 1.2 %collective-permute-done.13.other_ref = bf16[4,64,384]{2,1,0:T(8,128)(2,1)S(1)} collective-permute-done((bf16[4,64,384]{2,1,0:T(8,128)(2,1)S(1)}, bf16[4,64,384]{2,1,0:T(8,128)(2,1)S(1)}, u32[]{:S(2)}, u32[]{:S(2)}) %collective-permute-start.13) | collective-permute-done | bytes 196640 | tf_op jit(solution)/shard_map/ppermute | solution.py:506
  44.0 2.3 %collective-permute-start.14 = (bf16[64,768]{1,0:T(8,128)(2,1)S(1)}, bf16[64,768]{1,0:T(8,128)(2,1)S(1)}, u32[]{:S(2)}, u32[]{:S(2)}) collective-permute-start(bf16[64,768]{1,0:T(8,128)(2,1)S(1)} %get-tuple-element.83), channel_id=1, source_target_pairs={{8,0},{10,1},{9,2},{11,3},{12,4},{14,5},{13,6},{15,7},{0,8},{2,9},... | collective-permute-start | bytes 294920 | tf_op jit(solution)/shard_map/ppermute | solution.py:535
  46.3 2.6 %collective-permute-start.15 = (bf16[64,768]{1,0:T(8,128)(2,1)S(1)}, bf16[64,768]{1,0:T(8,128)(2,1)S(1)}, u32[]{:S(2)}, u32[]{:S(2)}) collective-permute-start(bf16[64,768]{1,0:T(8,128)(2,1)S(1)} %get-tuple-element.84), channel_id=1, source_target_pairs={{4,0},{6,1},{5,2},{7,3},{8,4},{10,5},{9,6},{11,7},{12,8},{14,9},{1... | collective-permute-start | bytes 294920 | tf_op jit(solution)/shard_map/ppermute | solution.py:535
  48.9 0.0 collective-permute-start.16
  48.9 0.7 %collective-permute-start.17 = (bf16[64,768]{1,0:T(8,128)(2,1)S(1)}, bf16[64,768]{1,0:T(8,128)(2,1)S(1)}, u32[]{:S(2)}, u32[]{:S(2)}) collective-permute-start(bf16[64,768]{1,0:T(8,128)(2,1)S(1)} %get-tuple-element.86), channel_id=1, source_target_pairs={{0,0},{2,1},{1,2},{3,3},{4,4},{6,5},{5,6},{7,7},{8,8},{10,9},{9,10... | collective-permute-start | bytes 294920 | tf_op jit(solution)/shard_map/ppermute | solution.py:535
  49.6 0.2 collective-permute-done.14.refs_0_
  49.8 2.9 %collective-permute-done.15.refs_1_ = bf16[64,768]{1,0:T(8,128)(2,1)S(1)} collective-permute-done((bf16[64,768]{1,0:T(8,128)(2,1)S(1)}, bf16[64,768]{1,0:T(8,128)(2,1)S(1)}, u32[]{:S(2)}, u32[]{:S(2)}) %collective-permute-start.15) | collective-permute-done | bytes 98336 | tf_op jit(solution)/shard_map/ppermute | solution.py:535
  52.7 3.6 %collective-permute-done.16.refs_2_ = bf16[64,768]{1,0:T(8,128)(2,1)S(1)} collective-permute-done((bf16[64,768]{1,0:T(8,128)(2,1)S(1)}, bf16[64,768]{1,0:T(8,128)(2,1)S(1)}, u32[]{:S(2)}, u32[]{:S(2)}) %collective-permute-start.16) | collective-permute-done | bytes 98336 | tf_op jit(solution)/shard_map/ppermute | solution.py:535
  56.3 0.6 %column_output.1 = (bf16[2,64,768]{2,1,0:T(8,128)(2,1)S(1)}, bf16[2,64,768]{2,1,0:T(8,128)(2,1)S(1)}) custom-call(s32[1]{0:T(128)} %bitcast.place_ref, bf16[768,768]{1,0:T(8,128)(2,1)S(1)} %copy-done.6, bf16[256,768]{1,0:T(8,128)(2,1)S(1)} %get-tuple-element.68.after_ref, bf16[64,768]{1,0:T(8,128)(2,1)S(1)} %collective-permute-done.14.refs_0_, ...), custom_call_target="tpu_custom_call" | custom-call | flops 301989888 | bytes 1179648 | tf_op jit(solution)/shard_map/column_output/pallas_call | solution.py:681
  56.9 0.8 %collective-permute-start.18 = (bf16[2,64,768]{2,1,0:T(8,128)(2,1)S(1)}, bf16[2,64,768]{2,1,0:T(8,128)(2,1)S(1)}, u32[]{:S(2)}, u32[]{:S(2)}) collective-permute-start(bf16[2,64,768]{2,1,0:T(8,128)(2,1)S(1)} %get-tuple-element.87), channel_id=1, source_target_pairs={{0,1},{1,0},{2,3},{3,2},{4,5},{5,4},{6,7},{7,6},{8,9},{9,8},{10,11... | collective-permute-start | bytes 589832 | tf_op jit(solution)/shard_map/ppermute | solution.py:506
  57.7 0.7 %own_half.1.half_ref = bf16[2,128,768]{2,1,0:T(8,128)(2,1)} custom-call(s32[1]{0:T(128)} %bitcast.place_ref, bf16[2,64,768]{2,1,0:T(8,128)(2,1)S(1)} %get-tuple-element.88.mine_ref), custom_call_target="tpu_custom_call" | custom-call | flops 196608 | bytes 393216 | tf_op jit(solution)/shard_map/own_half/pallas_call | solution.py:693
  58.4 0.4 collective-permute-done.18.other_ref
  58.8 0.7 %assemble.1 = bf16[2,128,768]{2,1,0:T(8,128)(2,1)} custom-call(s32[1]{0:T(128)} %bitcast.place_ref, bf16[2,64,768]{2,1,0:T(8,128)(2,1)S(1)} %collective-permute-done.18.other_ref, bf16[2,128,768]{2,1,0:T(8,128)(2,1)} %own_half.1.half_ref), custom_call_target="tpu_custom_call", output_to_operand_aliasing={{}: (2, {})} | custom-call | flops 196608 | bytes 393216 | tf_op jit(solution)/shard_map/assemble/pallas_call | solution.py:694
  (26 shorter events, 0.1 us)
Async XLA Ops:
  0.0 2.9 %collective-permute-start = (bf16[256,768]{1,0:T(8,128)(2,1)}, bf16[256,768]{1,0:T(8,128)(2,1)S(1)}, u32[]{:S(2)}, u32[]{:S(2)}) collective-permute-start(bf16[256,768]{1,0:T(8,128)(2,1)} %bitcast.2), channel_id=1, source_target_pairs={{0,1},{1,0},{2,3},{3,2},{4,5},{5,4},{6,7},{7,6},{8,9},{9,8},{10,11... | collective-permute-start | bytes 1179656 | tf_op jit(solution)/shard_map/ppermute | solution.py:506
  0.5 2.5 %copy-start.7 = (f32[768]{0:T(1024)S(1)}, f32[768]{0:T(1024)}, u32[]{:S(2)}) copy-start(f32[768]{0:T(1024)} %gain_ref.1) | copy-start | bytes 9220
  3.0 13.4 %copy-start.3 = (bf16[2,128,768]{2,1,0:T(8,128)(2,1)S(1)}, bf16[2,128,768]{2,1,0:T(8,128)(2,1)}, u32[]{:S(2)}) copy-start(bf16[2,128,768]{2,1,0:T(8,128)(2,1)} %param.13) | copy-start | bytes 1179652
  3.0 13.4 %copy-start.5 = (bf16[768,768]{1,0:T(8,128)(2,1)S(1)}, bf16[768,768]{1,0:T(8,128)(2,1)}, u32[]{:S(2)}) copy-start(bf16[768,768]{1,0:T(8,128)(2,1)} %w_ref.3) | copy-start | bytes 3538948
  4.8 7.5 %collective-permute-start.1 = (f32[16,768]{1,0:T(8,128)S(1)}, f32[16,768]{1,0:T(8,128)S(1)}, u32[]{:S(2)}, u32[]{:S(2)}) collective-permute-start(f32[16,768]{1,0:T(8,128)S(1)} %get-tuple-element.56), channel_id=1, source_target_pairs={{0,8},{1,9},{2,10},{3,11},{4,12},{5,13},{6,14},{7,15},{8,0},{9,1},... | collective-permute-start | bytes 147464 | tf_op jit(solution)/shard_map/ppermute | solution.py:527
  8.4 6.2 %collective-permute-start.2 = (f32[16,768]{1,0:T(8,128)S(1)}, f32[16,768]{1,0:T(8,128)S(1)}, u32[]{:S(2)}, u32[]{:S(2)}) collective-permute-start(f32[16,768]{1,0:T(8,128)S(1)} %get-tuple-element.57), channel_id=1, source_target_pairs={{0,4},{1,5},{2,6},{3,7},{4,8},{5,9},{6,10},{7,11},{8,12},{9,13},{1... | collective-permute-start | bytes 147464 | tf_op jit(solution)/shard_map/ppermute | solution.py:527
  10.0 4.7 %collective-permute-start.3 = (f32[16,768]{1,0:T(8,128)S(1)}, f32[16,768]{1,0:T(8,128)S(1)}, u32[]{:S(2)}, u32[]{:S(2)}) collective-permute-start(f32[16,768]{1,0:T(8,128)S(1)} %get-tuple-element.58), channel_id=1, source_target_pairs={{0,12},{1,13},{2,14},{3,15},{4,0},{5,1},{6,2},{7,3},{8,4},{9,5},{1... | collective-permute-start | bytes 147464 | tf_op jit(solution)/shard_map/ppermute | solution.py:527
  14.7 4.2 %collective-permute-start.4 = (f32[16,768]{1,0:T(8,128)S(1)}, f32[16,768]{1,0:T(8,128)S(1)}, u32[]{:S(2)}, u32[]{:S(2)}) collective-permute-start(f32[16,768]{1,0:T(8,128)S(1)} %add.1.mine_ref), channel_id=1, source_target_pairs={{0,2},{1,3},{2,0},{3,1},{4,6},{5,7},{6,4},{7,5},{8,10},{9,11},{10,... | collective-permute-start | bytes 147464 | tf_op jit(solution)/shard_map/ppermute | solution.py:506
  16.3 7.7 %copy-start.10 = (f32[768]{0:T(1024)S(1)}, f32[768]{0:T(1024)}, u32[]{:S(2)}) copy-start(f32[768]{0:T(1024)} %param.21) | copy-start | bytes 9220
  16.3 10.6 %copy-start.4 = (bf16[768,768]{1,0:T(8,128)(2,1)S(1)}, bf16[768,768]{1,0:T(8,128)(2,1)}, u32[]{:S(2)}) copy-start(bf16[768,768]{1,0:T(8,128)(2,1)} %w_ref.4) | copy-start | bytes 3538948
  19.1 4.9 %collective-permute-start.5 = (bf16[16,768]{1,0:T(8,128)(2,1)S(1)}, bf16[16,768]{1,0:T(8,128)(2,1)S(1)}, u32[]{:S(2)}, u32[]{:S(2)}) collective-permute-start(bf16[16,768]{1,0:T(8,128)(2,1)S(1)} %row_softmax.1.refs_3_), channel_id=1, source_target_pairs={{0,8},{1,9},{2,10},{3,11},{4,12},{5,13},{6,14},{7,15},{8,0},{9,1},... | collective-permute-start | bytes 73736 | tf_op jit(solution)/shard_map/ppermute | solution.py:527
  20.2 5.6 %collective-permute-start.6 = (bf16[16,768]{1,0:T(8,128)(2,1)S(1)}, bf16[16,768]{1,0:T(8,128)(2,1)S(1)}, u32[]{:S(2)}, u32[]{:S(2)}) collective-permute-start(bf16[16,768]{1,0:T(8,128)(2,1)S(1)} %row_softmax.1.refs_3_), channel_id=1, source_target_pairs={{0,4},{1,5},{2,6},{3,7},{4,8},{5,9},{6,10},{7,11},{8,12},{9,13},{1... | collective-permute-start | bytes 73736 | tf_op jit(solution)/shard_map/ppermute | solution.py:527
  23.1 3.8 %collective-permute-start.7 = (bf16[16,768]{1,0:T(8,128)(2,1)S(1)}, bf16[16,768]{1,0:T(8,128)(2,1)S(1)}, u32[]{:S(2)}, u32[]{:S(2)}) collective-permute-start(bf16[16,768]{1,0:T(8,128)(2,1)S(1)} %row_softmax.1.refs_3_), channel_id=1, source_target_pairs={{0,12},{1,13},{2,14},{3,15},{4,0},{5,1},{6,2},{7,3},{8,4},{9,5},{1... | collective-permute-start | bytes 73736 | tf_op jit(solution)/shard_map/ppermute | solution.py:527
  27.0 12.2 %copy-start = (bf16[768,768]{1,0:T(8,128)(2,1)S(1)}, bf16[768,768]{1,0:T(8,128)(2,1)}, u32[]{:S(2)}) copy-start(bf16[768,768]{1,0:T(8,128)(2,1)} %wq_ref.1) | copy-start | bytes 3538948
  27.0 12.2 %copy-start.1 = (bf16[768,768]{1,0:T(8,128)(2,1)S(1)}, bf16[768,768]{1,0:T(8,128)(2,1)}, u32[]{:S(2)}) copy-start(bf16[768,768]{1,0:T(8,128)(2,1)} %wk_ref.1) | copy-start | bytes 3538948
  27.0 12.2 %copy-start.2 = (bf16[768,768]{1,0:T(8,128)(2,1)S(1)}, bf16[768,768]{1,0:T(8,128)(2,1)}, u32[]{:S(2)}) copy-start(bf16[768,768]{1,0:T(8,128)(2,1)} %wv_ref.1) | copy-start | bytes 3538948
  27.0 12.2 %copy-start.8 = (s32[4]{0:T(128)S(1)}, s32[4]{0:T(128)}, u32[]{:S(2)}) copy-start(s32[4]{0:T(128)} %depth_ref.1) | copy-start | bytes 52
  27.0 12.2 %copy-start.9 = (s32[128]{0:T(128)S(1)}, s32[128]{0:T(128)}, u32[]{:S(2)}) copy-start(s32[128]{0:T(128)} %prot_ref.1) | copy-start | bytes 1540
  28.2 8.6 %collective-permute-start.10 = (bf16[64,768]{1,0:T(8,128)(2,1)S(1)}, bf16[64,768]{1,0:T(8,128)(2,1)S(1)}, u32[]{:S(2)}, u32[]{:S(2)}) collective-permute-start(bf16[64,768]{1,0:T(8,128)(2,1)S(1)} %get-tuple-element.74), channel_id=1, source_target_pairs={{0,8},{1,10},{2,9},{3,11},{4,12},{5,14},{6,13},{7,15},{8,0},{9,2},... | collective-permute-start | bytes 294920 | tf_op jit(solution)/shard_map/ppermute | solution.py:531
  28.3 10.6 %collective-permute-start.11 = (bf16[64,768]{1,0:T(8,128)(2,1)S(1)}, bf16[64,768]{1,0:T(8,128)(2,1)S(1)}, u32[]{:S(2)}, u32[]{:S(2)}) collective-permute-start(bf16[64,768]{1,0:T(8,128)(2,1)S(1)} %get-tuple-element.75), channel_id=1, source_target_pairs={{0,12},{1,14},{2,13},{3,15},{4,0},{5,2},{6,1},{7,3},{8,4},{9,6},{1... | collective-permute-start | bytes 294920 | tf_op jit(solution)/shard_map/ppermute | solution.py:531
  31.0 8.0 %collective-permute-start.8 = (bf16[64,768]{1,0:T(8,128)(2,1)S(1)}, bf16[64,768]{1,0:T(8,128)(2,1)S(1)}, u32[]{:S(2)}, u32[]{:S(2)}) collective-permute-start(bf16[64,768]{1,0:T(8,128)(2,1)S(1)} %get-tuple-element.72), channel_id=1, source_target_pairs={{0,4},{1,6},{2,5},{3,7},{4,8},{5,10},{6,9},{7,11},{8,12},{9,14},{1... | collective-permute-start | bytes 294920 | tf_op jit(solution)/shard_map/ppermute | solution.py:531
  31.5 7.5 %collective-permute-start.9 = (bf16[64,768]{1,0:T(8,128)(2,1)S(1)}, bf16[64,768]{1,0:T(8,128)(2,1)S(1)}, u32[]{:S(2)}, u32[]{:S(2)}) collective-permute-start(bf16[64,768]{1,0:T(8,128)(2,1)S(1)} %get-tuple-element.73), channel_id=1, source_target_pairs={{0,0},{1,2},{2,1},{3,3},{4,4},{5,6},{6,5},{7,7},{8,8},{9,10},{10,9... | collective-permute-start | bytes 294920 | tf_op jit(solution)/shard_map/ppermute | solution.py:531
  39.0 1.8 %collective-permute-start.12 = (bf16[4,64,768]{2,1,0:T(8,128)(2,1)S(1)}, bf16[4,64,768]{2,1,0:T(8,128)(2,1)S(1)}, u32[]{:S(2)}, u32[]{:S(2)}) collective-permute-start(bf16[4,64,768]{2,1,0:T(8,128)(2,1)S(1)} %pack.1), channel_id=1, source_target_pairs={{0,1},{1,0},{2,3},{3,2},{4,5},{5,4},{6,7},{7,6},{8,9},{9,8},{10,11... | collective-permute-start | bytes 1179656 | tf_op jit(solution)/shard_map/ppermute | solution.py:506
  40.8 15.5 %copy-start.6 = (bf16[768,768]{1,0:T(8,128)(2,1)S(1)}, bf16[768,768]{1,0:T(8,128)(2,1)}, u32[]{:S(2)}) copy-start(bf16[768,768]{1,0:T(8,128)(2,1)} %w_ref.5) | copy-start | bytes 3538948
  42.4 1.5 %collective-permute-start.13 = (bf16[4,64,384]{2,1,0:T(8,128)(2,1)S(1)}, bf16[4,64,384]{2,1,0:T(8,128)(2,1)S(1)}, u32[]{:S(2)}, u32[]{:S(2)}) collective-permute-start(bf16[4,64,384]{2,1,0:T(8,128)(2,1)S(1)} %get-tuple-element.82), channel_id=1, source_target_pairs={{0,1},{1,0},{2,3},{3,2},{4,5},{5,4},{6,7},{7,6},{8,9},{9,8},{10,11... | collective-permute-start | bytes 589832 | tf_op jit(solution)/shard_map/ppermute | solution.py:506
  44.0 5.8 %collective-permute-start.14 = (bf16[64,768]{1,0:T(8,128)(2,1)S(1)}, bf16[64,768]{1,0:T(8,128)(2,1)S(1)}, u32[]{:S(2)}, u32[]{:S(2)}) collective-permute-start(bf16[64,768]{1,0:T(8,128)(2,1)S(1)} %get-tuple-element.83), channel_id=1, source_target_pairs={{8,0},{10,1},{9,2},{11,3},{12,4},{14,5},{13,6},{15,7},{0,8},{2,9},... | collective-permute-start | bytes 294920 | tf_op jit(solution)/shard_map/ppermute | solution.py:535
  46.3 6.4 %collective-permute-start.15 = (bf16[64,768]{1,0:T(8,128)(2,1)S(1)}, bf16[64,768]{1,0:T(8,128)(2,1)S(1)}, u32[]{:S(2)}, u32[]{:S(2)}) collective-permute-start(bf16[64,768]{1,0:T(8,128)(2,1)S(1)} %get-tuple-element.84), channel_id=1, source_target_pairs={{4,0},{6,1},{5,2},{7,3},{8,4},{10,5},{9,6},{11,7},{12,8},{14,9},{1... | collective-permute-start | bytes 294920 | tf_op jit(solution)/shard_map/ppermute | solution.py:535
  48.9 7.4 %collective-permute-start.16 = (bf16[64,768]{1,0:T(8,128)(2,1)S(1)}, bf16[64,768]{1,0:T(8,128)(2,1)S(1)}, u32[]{:S(2)}, u32[]{:S(2)}) collective-permute-start(bf16[64,768]{1,0:T(8,128)(2,1)S(1)} %get-tuple-element.85), channel_id=1, source_target_pairs={{12,0},{14,1},{13,2},{15,3},{0,4},{2,5},{1,6},{3,7},{4,8},{6,9},{5... | collective-permute-start | bytes 294920 | tf_op jit(solution)/shard_map/ppermute | solution.py:535
  48.9 7.4 %collective-permute-start.17 = (bf16[64,768]{1,0:T(8,128)(2,1)S(1)}, bf16[64,768]{1,0:T(8,128)(2,1)S(1)}, u32[]{:S(2)}, u32[]{:S(2)}) collective-permute-start(bf16[64,768]{1,0:T(8,128)(2,1)S(1)} %get-tuple-element.86), channel_id=1, source_target_pairs={{0,0},{2,1},{1,2},{3,3},{4,4},{6,5},{5,6},{7,7},{8,8},{10,9},{9,10... | collective-permute-start | bytes 294920 | tf_op jit(solution)/shard_map/ppermute | solution.py:535
  56.9 1.8 %collective-permute-start.18 = (bf16[2,64,768]{2,1,0:T(8,128)(2,1)S(1)}, bf16[2,64,768]{2,1,0:T(8,128)(2,1)S(1)}, u32[]{:S(2)}, u32[]{:S(2)}) collective-permute-start(bf16[2,64,768]{2,1,0:T(8,128)(2,1)S(1)} %get-tuple-element.87), channel_id=1, source_target_pairs={{0,1},{1,0},{2,3},{3,2},{4,5},{5,4},{6,7},{7,6},{8,9},{9,8},{10,11... | collective-permute-start | bytes 589832 | tf_op jit(solution)/shard_map/ppermute | solution.py:506
